TPU v7x, 32 devices: a whole 2x2x4 slice. The times are simulated.
32 devices in a mesh: dp: 4 (over y, x), seq: 8 (over z, core).
Axes of the slice: x: 2, y: 2, z: 4, core: 2. Of those that a mesh axis runs over, the one named last changes fastest.
Arguments:
- tokens: bfloat16 [4, 1024, 2048], P('dp', 'seq'), may hold values from -6 to 6
- doc_ids: int32 [4, 1024], P('dp', 'seq'), may hold values from 0 to 3, never falling along the last dimension, each value on 1 to 512 neighbouring positions
- cotangent: bfloat16 [4, 1024, 2048], P('dp', 'seq'), may hold values from -6 to 6
- w_query: bfloat16 [2048, 2048], P('dp'), may hold values from -0.125 to 0.125
- w_key: bfloat16 [2048, 2048], P('dp'), may hold values from -0.125 to 0.125
- w_value: bfloat16 [2048, 2048], P('dp'), may hold values from -0.125 to 0.125
- w_out: bfloat16 [2048, 2048], P('dp'), may hold values from -0.125 to 0.125
- w_gate: bfloat16 [2048, 8192], P('dp'), may hold values from -0.125 to 0.125
- w_up: bfloat16 [2048, 8192], P('dp'), may hold values from -0.125 to 0.125
- w_down: bfloat16 [8192, 2048], P('dp'), may hold values from -0.0625 to 0.0625
- g_query: bfloat16 [2048], replicated, may hold values from 0.5 to 1.5
- g_key: bfloat16 [2048], replicated, may hold values from 0.5 to 1.5
- g_attn: bfloat16 [2048], replicated, may hold values from 0.5 to 1.5
- g_ffn: bfloat16 [2048], replicated, may hold values from 0.5 to 1.5
Outputs:
- layer_out: bfloat16 [4, 1024, 2048], P('dp', 'seq')
- tokens_grad: float32 [4, 1024, 2048], P('dp', 'seq')
- w_query_grad: float32 [2048, 2048], P(('dp', 'seq'))
- w_key_grad: float32 [2048, 2048], P(('dp', 'seq'))
- w_value_grad: float32 [2048, 2048], P(('dp', 'seq'))
- w_out_grad: float32 [2048, 2048], P(('dp', 'seq'))
- w_gate_grad: float32 [2048, 8192], P(('dp', 'seq'))
- w_up_grad: float32 [2048, 8192], P(('dp', 'seq'))
- w_down_grad: float32 [8192, 2048], P(('dp', 'seq'))
- g_query_grad: float32 [2048], P(('dp', 'seq'))
- g_key_grad: float32 [2048], P(('dp', 'seq'))
- g_attn_grad: float32 [2048], P(('dp', 'seq'))
- g_ffn_grad: float32 [2048], P(('dp', 'seq'))
Inputs may be any that keep to these rules, and one draw needn't show every extreme that they name: `doc_ids`: along a row the numbers never fall; each document holds 1 to 512 tokens and one holds exactly 512.
All inputs are finite; a program needn't handle non-finite values.
Results may differ from a plain program's by a relative error of at most 0.018.
Values may be sent and summed in bfloat16 or wider, within the bound.
No kernel may reach another device: no remote copies, remote signals or barrier semaphores. Data moves between devices by JAX's collectives and lax.ppermute only.
A program may use at most 768 MiB of HBM per device.

v0:
```python
import jax
import jax.numpy as jnp
from jax import lax
from jax.sharding import PartitionSpec as P

HEAD = 128
SLABS = 4


eps = 1e-06
theta = 500000.0


def rotation(positions, head_size):
    half_size = head_size // 2
    frequency = theta ** (-(2.0 * jnp.arange(half_size, dtype=jnp.float32)) / head_size)
    angles = positions.astype(jnp.float32)[:, None] * frequency[None, :]
    return (jnp.cos(angles), jnp.sin(angles))


def rotate(tensor, cosine, sine_part):
    half_size = tensor.shape[-1] // 2
    first_half = tensor[..., :half_size]
    second_half = tensor[..., half_size:]
    cos_wide = cosine[:, None, :]
    sin_wide = sine_part[:, None, :]
    return jnp.concatenate(
        [
            first_half * cos_wide - second_half * sin_wide,
            second_half * cos_wide + first_half * sin_wide,
        ],
        -1,
    )


def unrotate(tensor, cosine, sine_part):
    half_size = tensor.shape[-1] // 2
    first_half = tensor[..., :half_size]
    second_half = tensor[..., half_size:]
    cos_wide = cosine[:, None, :]
    sin_wide = sine_part[:, None, :]
    return jnp.concatenate(
        [
            first_half * cos_wide + second_half * sin_wide,
            second_half * cos_wide - first_half * sin_wide,
        ],
        -1,
    )


def inverse_rms(tensor):
    return lax.rsqrt(jnp.mean(tensor * tensor, -1, keepdims=True) + eps)


def norm_back(grad_unit, unit_vec, inverse):
    return inverse * (grad_unit - unit_vec * jnp.mean(grad_unit * unit_vec, -1, keepdims=True))


def visible(own_ids, key_ids, query_at, key_at):
    causal = key_at[None, :] <= query_at[:, None]
    same_doc = own_ids[:, :, None] == key_ids[:, None, :]
    return (causal[None] & same_doc)[:, None]


def masked_scores(query_low, pair_all, allowed, head_count, head_size):
    row_count = pair_all.shape[0]
    row_length = pair_all.shape[1]
    feature_count = head_count * head_size
    key_rows = pair_all[..., :feature_count].reshape(row_count, row_length, head_count, head_size)
    value_rows = pair_all[..., feature_count:].reshape(row_count, row_length, head_count, head_size)
    scores = jnp.einsum(
        "rche,rlhe->rhcl", query_low, key_rows, preferred_element_type=jnp.float32
    ) * head_size ** (-0.5)
    return (jnp.where(allowed, scores, -1e30), key_rows, value_rows)


def columns_of(matrix, parts, slab_count, index):
    lead = matrix.shape[0]
    width = matrix.shape[1] // (parts * slab_count)
    return matrix.reshape(lead, parts, slab_count, width)[:, :, index].reshape(lead, parts * width)


def entries_of(vector, parts, slab_count, index):
    width = vector.shape[0] // (parts * slab_count)
    return vector.reshape(parts, slab_count, width)[:, index].reshape(parts * width)


def shards(
    tokens,
    doc_ids,
    cotangent,
    w_query,
    w_key,
    w_value,
    w_out,
    w_gate,
    w_up,
    w_down,
    g_query,
    g_key,
    g_attn,
    g_ffn,
):
    row_count, piece_len, model_width = tokens.shape
    head_size = HEAD
    feature_count = w_query.shape[1]
    head_count = feature_count // head_size
    tok_count = row_count * piece_len
    scale = head_size ** (-0.5)
    seq_count = lax.axis_size("seq")
    parts = lax.axis_size("dp") * seq_count
    slab_count = SLABS
    gather_all = (
        lax.all_gather(w_query, "dp", axis=0, tiled=True),
        lax.all_gather(w_key, "dp", axis=0, tiled=True),
        lax.all_gather(w_value, "dp", axis=0, tiled=True),
        lax.all_gather(w_out, "dp", axis=0, tiled=True),
        lax.all_gather(w_gate, "dp", axis=0, tiled=True),
        lax.all_gather(w_up, "dp", axis=0, tiled=True),
        lax.all_gather(w_down, "dp", axis=0, tiled=True),
    )
    wq_full, wk_full, wv_full, wo_full, wg_full, wu_full, wd_full = gather_all
    gain_query = g_query.astype(jnp.float32)
    gain_key = g_key.astype(jnp.float32)
    gain_attn = g_attn.astype(jnp.float32)
    gain_ffn = g_ffn.astype(jnp.float32)
    flat_tokens = tokens.reshape(tok_count, model_width)
    query_pre = jnp.dot(flat_tokens, wq_full, preferred_element_type=jnp.float32)
    key_pre = jnp.dot(flat_tokens, wk_full, preferred_element_type=jnp.float32)
    value_pre = jnp.dot(flat_tokens, wv_full, preferred_element_type=jnp.float32)
    query_inv = inverse_rms(query_pre)
    query_unit = query_pre * query_inv
    key_inv = inverse_rms(key_pre)
    key_unit = key_pre * key_inv
    first_row = lax.axis_index("seq") * piece_len
    positions = first_row + jnp.tile(jnp.arange(piece_len, dtype=jnp.int32), row_count)
    cosine, sine_part = rotation(positions, head_size)
    query_rot = rotate(
        (query_unit * gain_query).reshape(tok_count, head_count, head_size), cosine, sine_part
    )
    key_rot = rotate(
        (key_unit * gain_key).reshape(tok_count, head_count, head_size), cosine, sine_part
    )
    query_low = query_rot.astype(jnp.bfloat16).reshape(row_count, piece_len, head_count, head_size)
    key_low = key_rot.astype(jnp.bfloat16).reshape(row_count, piece_len, feature_count)
    value_low = value_pre.astype(jnp.bfloat16).reshape(row_count, piece_len, feature_count)
    pair_low = jnp.concatenate([key_low, value_low], -1)
    ids_low = doc_ids.astype(jnp.bfloat16)
    pair_all, ids_all = (
        lax.all_gather(pair_low, "seq", axis=1, tiled=True),
        lax.all_gather(ids_low, "seq", axis=1, tiled=True),
    )
    query_at = first_row + jnp.arange(piece_len, dtype=jnp.int32)
    allowed = visible(ids_low, ids_all, query_at, jnp.arange(pair_all.shape[1], dtype=jnp.int32))
    masked, key_rows, value_rows = masked_scores(
        query_low, pair_all, allowed, head_count, head_size
    )
    row_max = jnp.max(masked, -1, keepdims=True)
    log_total = jnp.log(jnp.sum(jnp.exp(masked - row_max), -1, keepdims=True)) + row_max
    probs_low = jnp.exp(masked - log_total).astype(jnp.bfloat16)
    mixed = jnp.einsum("rhcl,rlhe->rche", probs_low, value_rows, preferred_element_type=jnp.float32)
    mixed_low = mixed.reshape(tok_count, feature_count).astype(jnp.bfloat16)
    attn_out = jnp.dot(mixed_low, wo_full, preferred_element_type=jnp.float32)
    attn_inv = inverse_rms(attn_out)
    attn_unit = attn_out * attn_inv
    hidden_state = flat_tokens.astype(jnp.float32) + attn_unit * gain_attn
    hidden_low = hidden_state.astype(jnp.bfloat16)
    gate = jnp.dot(hidden_low, wg_full, preferred_element_type=jnp.float32)
    up_proj = jnp.dot(hidden_low, wu_full, preferred_element_type=jnp.float32)
    sigma = jax.nn.sigmoid(gate)
    active = gate * sigma
    inner_low = (active * up_proj).astype(jnp.bfloat16)
    branch = jnp.dot(inner_low, wd_full, preferred_element_type=jnp.float32)
    branch_inv = inverse_rms(branch)
    branch_unit = branch * branch_inv
    result = (
        (hidden_state + branch_unit * gain_ffn)
        .astype(jnp.bfloat16)
        .reshape(row_count, piece_len, model_width)
    )
    wq_back, wk_back, wv_back, wo_back, wg_back, wu_back, wd_back = gather_all
    pair_back, ids_back = (pair_all, ids_all)
    grad_out = cotangent.reshape(tok_count, model_width).astype(jnp.float32)
    ffn_gain_term = jnp.sum(grad_out * branch_unit, 0)
    d_branch = norm_back(grad_out * gain_ffn, branch_unit, branch_inv).astype(jnp.bfloat16)
    d_inner = jnp.einsum("nd,fd->nf", d_branch, wd_back, preferred_element_type=jnp.float32)
    d_gate = (d_inner * up_proj * sigma * (1.0 + gate * (1.0 - sigma))).astype(jnp.bfloat16)
    d_up = (d_inner * active).astype(jnp.bfloat16)
    d_hidden = grad_out + jnp.einsum(
        "nf,df->nd", d_gate, wg_back, preferred_element_type=jnp.float32
    )
    d_hidden = d_hidden + jnp.einsum("nf,df->nd", d_up, wu_back, preferred_element_type=jnp.float32)
    mlp_shares = []
    for index in range(slab_count):
        hidden_part = columns_of(hidden_low, parts, slab_count, index)
        inner_part = columns_of(inner_low, parts, slab_count, index)
        gate_term = jnp.einsum("nd,nf->df", hidden_part, d_gate, preferred_element_type=jnp.float32)
        up_term = jnp.einsum("nd,nf->df", hidden_part, d_up, preferred_element_type=jnp.float32)
        down_term = jnp.einsum(
            "nf,nd->fd", inner_part, d_branch, preferred_element_type=jnp.float32
        )
        ffn_term = entries_of(ffn_gain_term, parts, slab_count, index)
        shares = (
            lax.psum_scatter(down_term, ("dp", "seq"), scatter_dimension=0, tiled=True),
            lax.psum_scatter(gate_term, ("dp", "seq"), scatter_dimension=0, tiled=True),
            lax.psum_scatter(up_term, ("dp", "seq"), scatter_dimension=0, tiled=True),
            lax.psum_scatter(ffn_term, ("dp", "seq"), scatter_dimension=0, tiled=True),
        )
        mlp_shares.append(shares)
    down_grad = jnp.concatenate([s[0] for s in mlp_shares], 0)
    gate_grad = jnp.concatenate([s[1] for s in mlp_shares], 0)
    up_grad = jnp.concatenate([s[2] for s in mlp_shares], 0)
    ffn_grad = jnp.concatenate([s[3] for s in mlp_shares], 0)
    attn_gain_term = jnp.sum(d_hidden * attn_unit, 0)
    d_attn = norm_back(d_hidden * gain_attn, attn_unit, attn_inv).astype(jnp.bfloat16)
    d_mixed = jnp.einsum("nd,fd->nf", d_attn, wo_back, preferred_element_type=jnp.float32).astype(
        jnp.bfloat16
    )
    d_mixed = d_mixed.reshape(row_count, piece_len, head_count, head_size)
    sub_len = piece_len // slab_count
    pair_width = pair_back.shape[-1]
    pair_view = pair_back.reshape(row_count, seq_count, slab_count, sub_len, pair_width)
    ids_view = ids_back.reshape(row_count, seq_count, slab_count, sub_len)

    def slab_scores(index):
        pair_part = pair_view[:, :, index].reshape(row_count, seq_count * sub_len, pair_width)
        ids_part = ids_view[:, :, index].reshape(row_count, seq_count * sub_len)
        key_at = (
            jnp.arange(seq_count, dtype=jnp.int32)[:, None] * piece_len
            + index * sub_len
            + jnp.arange(sub_len, dtype=jnp.int32)[None, :]
        ).reshape(seq_count * sub_len)
        allowed_part = visible(ids_low, ids_part, query_at, key_at)
        masked_part, key_part, value_part = masked_scores(
            query_low, pair_part, allowed_part, head_count, head_size
        )
        probs_part = jnp.exp(masked_part - log_total)
        d_probs_part = jnp.einsum(
            "rche,rlhe->rhcl", d_mixed, value_part, preferred_element_type=jnp.float32
        )
        return (probs_part, d_probs_part, key_part)

    row_dot = jnp.zeros((row_count, head_count, piece_len, 1), jnp.float32)
    for index in range(slab_count):
        probs_part, d_probs_part, key_part = slab_scores(index)
        row_dot = row_dot + jnp.sum(probs_part * d_probs_part, -1, keepdims=True)
    query_acc = jnp.zeros((row_count, piece_len, head_count, head_size), jnp.float32)
    pair_shares = []
    for index in range(slab_count):
        probs_part, d_probs_part, key_part = slab_scores(index)
        d_scores = (probs_part * (d_probs_part - row_dot)).astype(jnp.bfloat16)
        query_acc = query_acc + jnp.einsum(
            "rhcl,rlhe->rche", d_scores, key_part, preferred_element_type=jnp.float32
        )
        key_term = (
            jnp.einsum("rhcl,rche->rlhe", d_scores, query_low, preferred_element_type=jnp.float32)
            * scale
        )
        value_term = jnp.einsum(
            "rhcl,rche->rlhe",
            probs_part.astype(jnp.bfloat16),
            d_mixed,
            preferred_element_type=jnp.float32,
        )
        key_count = seq_count * sub_len
        pair_term = jnp.concatenate(
            [
                key_term.reshape(row_count, key_count, feature_count),
                value_term.reshape(row_count, key_count, feature_count),
            ],
            -1,
        )
        pair_shares.append(
            lax.psum_scatter(
                pair_term.astype(jnp.bfloat16), "seq", scatter_dimension=1, tiled=True
            ).astype(jnp.float32)
        )
    pair_grad = jnp.concatenate(pair_shares, 1)
    d_query = (query_acc * scale).astype(jnp.bfloat16)
    d_key = (
        pair_grad[..., :feature_count]
        .astype(jnp.bfloat16)
        .reshape(tok_count, head_count, head_size)
    )
    d_value = pair_grad[..., feature_count:].astype(jnp.bfloat16).reshape(tok_count, feature_count)
    dq_norm = unrotate(
        d_query.reshape(tok_count, head_count, head_size).astype(jnp.float32), cosine, sine_part
    ).reshape(tok_count, feature_count)
    dk_norm = unrotate(d_key.astype(jnp.float32), cosine, sine_part).reshape(
        tok_count, feature_count
    )
    query_gain_term = jnp.sum(dq_norm * query_unit, 0)
    key_gain_term = jnp.sum(dk_norm * key_unit, 0)
    dq_pre = norm_back(dq_norm * gain_query, query_unit, query_inv).astype(jnp.bfloat16)
    dk_pre = norm_back(dk_norm * gain_key, key_unit, key_inv).astype(jnp.bfloat16)
    d_tokens = d_hidden + jnp.einsum(
        "nf,df->nd", dq_pre, wq_back, preferred_element_type=jnp.float32
    )
    d_tokens = d_tokens + jnp.einsum(
        "nf,df->nd", dk_pre, wk_back, preferred_element_type=jnp.float32
    )
    d_tokens = d_tokens + jnp.einsum(
        "nf,df->nd", d_value, wv_back, preferred_element_type=jnp.float32
    )
    attn_shares = []
    for index in range(slab_count):
        token_part = columns_of(flat_tokens, parts, slab_count, index)
        mixed_part = columns_of(mixed_low, parts, slab_count, index)
        query_term = jnp.einsum("nd,nf->df", token_part, dq_pre, preferred_element_type=jnp.float32)
        key_wterm = jnp.einsum("nd,nf->df", token_part, dk_pre, preferred_element_type=jnp.float32)
        value_wterm = jnp.einsum(
            "nd,nf->df", token_part, d_value, preferred_element_type=jnp.float32
        )
        out_term = jnp.einsum("nf,nd->fd", mixed_part, d_attn, preferred_element_type=jnp.float32)
        gq_term = entries_of(query_gain_term, parts, slab_count, index)
        gk_term = entries_of(key_gain_term, parts, slab_count, index)
        ga_term = entries_of(attn_gain_term, parts, slab_count, index)
        shares = (
            lax.psum_scatter(query_term, ("dp", "seq"), scatter_dimension=0, tiled=True),
            lax.psum_scatter(key_wterm, ("dp", "seq"), scatter_dimension=0, tiled=True),
            lax.psum_scatter(value_wterm, ("dp", "seq"), scatter_dimension=0, tiled=True),
            lax.psum_scatter(out_term, ("dp", "seq"), scatter_dimension=0, tiled=True),
            lax.psum_scatter(gq_term, ("dp", "seq"), scatter_dimension=0, tiled=True),
            lax.psum_scatter(gk_term, ("dp", "seq"), scatter_dimension=0, tiled=True),
            lax.psum_scatter(ga_term, ("dp", "seq"), scatter_dimension=0, tiled=True),
        )
        attn_shares.append(shares)
    query_grad = jnp.concatenate([s[0] for s in attn_shares], 0)
    key_grad = jnp.concatenate([s[1] for s in attn_shares], 0)
    value_grad = jnp.concatenate([s[2] for s in attn_shares], 0)
    out_grad = jnp.concatenate([s[3] for s in attn_shares], 0)
    gq_grad = jnp.concatenate([s[4] for s in attn_shares], 0)
    gk_grad = jnp.concatenate([s[5] for s in attn_shares], 0)
    ga_grad = jnp.concatenate([s[6] for s in attn_shares], 0)
    tokens_grad = d_tokens.reshape(row_count, piece_len, model_width)
    return (
        result,
        tokens_grad,
        query_grad,
        key_grad,
        value_grad,
        out_grad,
        gate_grad,
        up_grad,
        down_grad,
        gq_grad,
        gk_grad,
        ga_grad,
        ffn_grad,
    )


def solution(mesh):
    return jax.shard_map(
        shards,
        mesh=mesh,
        in_specs=(
            P("dp", "seq", None),
            P("dp", "seq"),
            P("dp", "seq", None),
            P("dp", None),
            P("dp", None),
            P("dp", None),
            P("dp", None),
            P("dp", None),
            P("dp", None),
            P("dp", None),
            P(),
            P(),
            P(),
            P(),
        ),
        out_specs=(
            P("dp", "seq", None),
            P("dp", "seq", None),
            P(("dp", "seq"), None),
            P(("dp", "seq"), None),
            P(("dp", "seq"), None),
            P(("dp", "seq"), None),
            P(("dp", "seq"), None),
            P(("dp", "seq"), None),
            P(("dp", "seq"), None),
            P(("dp", "seq")),
            P(("dp", "seq")),
            P(("dp", "seq")),
            P(("dp", "seq")),
        ),
        check_vma=False,
    )
```

profile of v0, /device:TPU:0, one launch (start us, length us, event | category | flops | bytes accessed | tf_op | source)
XLA Modules:
  0.0 6417.1 jit_solution(10378769804241937220)
XLA Ops:
  460.4 292.8 %all-gather.19.cloned.1.call-done = bf16[2048,8192]{1,0:T(8,128)(2,1)} async-done(((bf16[512,8192]{1,0:T(8,128)(2,1)}), bf16[2048,8192]{1,0:T(8,128)(2,1)}) %all-gather.19.cloned.1.call-update) | async-done | bytes 33554448 | tf_op jit(solution)/shard_map/all_gather | solution.py:118
  773.1 279.1 %all-gather.21.cloned.1.call-done = bf16[2048,8192]{1,0:T(8,128)(2,1)} async-done(((bf16[512,8192]{1,0:T(8,128)(2,1)}), bf16[2048,8192]{1,0:T(8,128)(2,1)}) %all-gather.21.cloned.1.call-update) | async-done | bytes 33554448 | tf_op jit(solution)/shard_map/all_gather | solution.py:119
  1076.1 275.0 %all-gather.23.cloned.1.call-done = bf16[8192,2048]{1,0:T(8,128)(2,1)} async-done(((bf16[2048,2048]{1,0:T(8,128)(2,1)}), bf16[8192,2048]{1,0:T(8,128)(2,1)}) %all-gather.23.cloned.1.call-update) | async-done | bytes 33554448 | tf_op jit(solution)/shard_map/all_gather | solution.py:120
  1557.5 318.4 %all-reduce.24.cloned.1.call-done = (bf16[1,256,4096]{2,0,1:T(2,128)(2,1)}, bf16[1,256,4096]{2,0,1:T(2,128)(2,1)}, bf16[1,256,4096]{2,0,1:T(2,128)(2,1)}, bf16[1,256,4096]{2,0,1:T(2,128)(2,1)}) async-done(((bf16[1,256,4096]{2,0,1:T(2,128)(2,1)}, bf16[1,256,4096]{2,0,1:T(2,128)(2,1)}, bf16[1,256,4096]{2,0,1:T(2,128)(2,1)}, bf16[1,256,4096]{2,0,1:T(2,128)(2,1)}), (bf16[1,256,4096]{2,0,1:T(2,128)(2,1)}, ...) | async-done | bytes 8388624
  2308.9 143.0 %reduce-scatter.59.cloned.1.call-done = f32[16,2048]{1,0:T(8,128)} async-done(((f32[512,2048]{1,0:T(8,128)}), f32[16,2048]{1,0:T(8,128)}) %reduce-scatter.59.cloned.1.call-update) | async-done | bytes 131088 | tf_op jit(solution)/shard_map/reduce_scatter | solution.py:322
  2596.4 141.7 %reduce-scatter.103.cloned.1.call-done = f32[16,2048]{1,0:T(8,128)} async-done(((f32[512,2048]{1,0:T(8,128)}), f32[16,2048]{1,0:T(8,128)}) %reduce-scatter.103.cloned.1.call-update) | async-done | bytes 131088
  2739.3 142.0 %reduce-scatter.105.cloned.1.call-done = f32[16,2048]{1,0:T(8,128)} async-done(((f32[512,2048]{1,0:T(8,128)}), f32[16,2048]{1,0:T(8,128)}) %reduce-scatter.105.cloned.1.call-update) | async-done | bytes 131088
  2882.5 141.6 %reduce-scatter.107.cloned.1.call-done = f32[16,2048]{1,0:T(8,128)} async-done(((f32[512,2048]{1,0:T(8,128)}), f32[16,2048]{1,0:T(8,128)}) %reduce-scatter.107.cloned.1.call-update) | async-done | bytes 131088
  3168.5 142.1 %reduce-scatter.95.cloned.1.call-done = f32[16,2048]{1,0:T(8,128)} async-done(((f32[512,2048]{1,0:T(8,128)}), f32[16,2048]{1,0:T(8,128)}) %reduce-scatter.95.cloned.1.call-update) | async-done | bytes 131088
  3311.8 141.7 %reduce-scatter.97.cloned.1.call-done = f32[16,2048]{1,0:T(8,128)} async-done(((f32[512,2048]{1,0:T(8,128)}), f32[16,2048]{1,0:T(8,128)}) %reduce-scatter.97.cloned.1.call-update) | async-done | bytes 131088
  3454.7 142.0 %reduce-scatter.99.cloned.1.call-done = f32[16,2048]{1,0:T(8,128)} async-done(((f32[512,2048]{1,0:T(8,128)}), f32[16,2048]{1,0:T(8,128)}) %reduce-scatter.99.cloned.1.call-update) | async-done | bytes 131088
  4026.5 142.7 %reduce-scatter.91.cloned.1.call-done = f32[16,2048]{1,0:T(8,128)} async-done(((f32[512,2048]{1,0:T(8,128)}), f32[16,2048]{1,0:T(8,128)}) %reduce-scatter.91.cloned.1.call-update) | async-done | bytes 131088
  4176.8 177.8 %reduce-scatter.77.cloned.1.call-done = f32[64,2048]{1,0:T(8,128)} async-done(((f32[2048,2048]{1,0:T(8,128)}), f32[64,2048]{1,0:T(8,128)}) %reduce-scatter.77.cloned.1.call-update) | async-done | bytes 524304 | tf_op jit(solution)/shard_map/reduce_scatter | solution.py:204
  4354.6 186.5 %reduce-scatter.79.cloned.1.call-done = f32[64,2048]{1,0:T(8,128)} async-done(((f32[2048,2048]{1,0:T(8,128)}), f32[64,2048]{1,0:T(8,128)}) %reduce-scatter.79.cloned.1.call-update) | async-done | bytes 524304 | tf_op jit(solution)/shard_map/reduce_scatter | solution.py:204
  4541.2 186.6 %reduce-scatter.81.cloned.1.call-done = f32[64,2048]{1,0:T(8,128)} async-done(((f32[2048,2048]{1,0:T(8,128)}), f32[64,2048]{1,0:T(8,128)}) %reduce-scatter.81.cloned.1.call-update) | async-done | bytes 524304 | tf_op jit(solution)/shard_map/reduce_scatter | solution.py:204
  4727.8 186.7 %reduce-scatter.83.cloned.1.call-done = f32[64,2048]{1,0:T(8,128)} async-done(((f32[2048,2048]{1,0:T(8,128)}), f32[64,2048]{1,0:T(8,128)}) %reduce-scatter.83.cloned.1.call-update) | async-done | bytes 524304 | tf_op jit(solution)/shard_map/reduce_scatter | solution.py:204
  4917.5 183.4 %reduce-scatter.69.cloned.1.call-done = f32[16,8192]{1,0:T(8,128)} async-done(((f32[512,8192]{1,0:T(8,128)}), f32[16,8192]{1,0:T(8,128)}) %reduce-scatter.69.cloned.1.call-update) | async-done | bytes 524304 | tf_op jit(solution)/shard_map/reduce_scatter | solution.py:206
  5101.0 186.7 %reduce-scatter.71.cloned.1.call-done = f32[16,8192]{1,0:T(8,128)} async-done(((f32[512,8192]{1,0:T(8,128)}), f32[16,8192]{1,0:T(8,128)}) %reduce-scatter.71.cloned.1.call-update) | async-done | bytes 524304 | tf_op jit(solution)/shard_map/reduce_scatter | solution.py:206
  5287.6 186.7 %reduce-scatter.73.cloned.1.call-done = f32[16,8192]{1,0:T(8,128)} async-done(((f32[512,8192]{1,0:T(8,128)}), f32[16,8192]{1,0:T(8,128)}) %reduce-scatter.73.cloned.1.call-update) | async-done | bytes 524304 | tf_op jit(solution)/shard_map/reduce_scatter | solution.py:206
  5474.3 186.5 %reduce-scatter.75.cloned.1.call-done = f32[16,8192]{1,0:T(8,128)} async-done(((f32[512,8192]{1,0:T(8,128)}), f32[16,8192]{1,0:T(8,128)}) %reduce-scatter.75.cloned.1.call-update) | async-done | bytes 524304 | tf_op jit(solution)/shard_map/reduce_scatter | solution.py:206
  5663.8 183.7 %reduce-scatter.61.cloned.1.call-done = f32[16,8192]{1,0:T(8,128)} async-done(((f32[512,8192]{1,0:T(8,128)}), f32[16,8192]{1,0:T(8,128)}) %reduce-scatter.61.cloned.1.call-update) | async-done | bytes 524304 | tf_op jit(solution)/shard_map/reduce_scatter | solution.py:205
  5847.4 186.6 %reduce-scatter.63.cloned.1.call-done = f32[16,8192]{1,0:T(8,128)} async-done(((f32[512,8192]{1,0:T(8,128)}), f32[16,8192]{1,0:T(8,128)}) %reduce-scatter.63.cloned.1.call-update) | async-done | bytes 524304 | tf_op jit(solution)/shard_map/reduce_scatter | solution.py:205
  6034.1 186.5 %reduce-scatter.65.cloned.1.call-done = f32[16,8192]{1,0:T(8,128)} async-done(((f32[512,8192]{1,0:T(8,128)}), f32[16,8192]{1,0:T(8,128)}) %reduce-scatter.65.cloned.1.call-update) | async-done | bytes 524304 | tf_op jit(solution)/shard_map/reduce_scatter | solution.py:205
  6220.6 186.5 %reduce-scatter.67.cloned.1.call-done = f32[16,8192]{1,0:T(8,128)} async-done(((f32[512,8192]{1,0:T(8,128)}), f32[16,8192]{1,0:T(8,128)}) %reduce-scatter.67.cloned.1.call-update) | async-done | bytes 524304 | tf_op jit(solution)/shard_map/reduce_scatter | solution.py:205
  (466 shorter events, 1874.1 us)
Async XLA Ops:
  286.5 1064.6 %all-gather.23.cloned.1.call-start = ((), (), s32[]{:S(2)}) async-start(), calls=%async_computation.35 | async-start | bytes 41943040 | tf_op jit(solution)/shard_map/all_gather | solution.py:120
  287.2 1588.7 %all-reduce.24.cloned.1.call-start = ((), (), s32[]{:S(2)}) async-start(), calls=%async_computation.64 | async-start | bytes 33554432
  1555.2 1040.0 %reduce-scatter.101.cloned.1.call-start = ((), (), s32[]{:S(2)}) async-start(), calls=%async_computation.60 | async-start | bytes 4325376
  1916.2 1108.0 %reduce-scatter.107.cloned.1.call-start = ((), (), s32[]{:S(2)}) async-start(), calls=%async_computation.63 | async-start | bytes 4325376
  1924.4 1242.8 %reduce-scatter.93.cloned.1.call-start = ((), (), s32[]{:S(2)}) async-start(), calls=%async_computation.56 | async-start | bytes 4325376
  1943.5 1367.0 %reduce-scatter.95.cloned.1.call-start = ((), (), s32[]{:S(2)}) async-start(), calls=%async_computation.57 | async-start | bytes 4325376
  1951.7 1501.7 %reduce-scatter.97.cloned.1.call-start = ((), (), s32[]{:S(2)}) async-start(), calls=%async_computation.58 | async-start | bytes 4325376
  1960.0 1636.7 %reduce-scatter.99.cloned.1.call-start = ((), (), s32[]{:S(2)}) async-start(), calls=%async_computation.59 | async-start | bytes 4325376
  1968.2 1771.6 %reduce-scatter.85.cloned.1.call-start = ((), (), s32[]{:S(2)}) async-start(), calls=%async_computation.52 | async-start | bytes 4325376
  1980.8 1901.8 %reduce-scatter.87.cloned.1.call-start = ((), (), s32[]{:S(2)}) async-start(), calls=%async_computation.53 | async-start | bytes 4325376
  1988.9 2036.3 %reduce-scatter.89.cloned.1.call-start = ((), (), s32[]{:S(2)}) async-start(), calls=%async_computation.54 | async-start | bytes 4325376
  1997.6 2171.6 %reduce-scatter.91.cloned.1.call-start = ((), (), s32[]{:S(2)}) async-start(), calls=%async_computation.55 | async-start | bytes 4325376
  2005.8 2348.8 %reduce-scatter.77.cloned.1.call-start = ((), (), s32[]{:S(2)}) async-start(), calls=%async_computation.48 | async-start | bytes 17301504 | tf_op jit(solution)/shard_map/reduce_scatter | solution.py:204
  2019.9 2521.3 %reduce-scatter.79.cloned.1.call-start = ((), (), s32[]{:S(2)}) async-start(), calls=%async_computation.49 | async-start | bytes 17301504 | tf_op jit(solution)/shard_map/reduce_scatter | solution.py:204
  2028.0 2699.8 %reduce-scatter.81.cloned.1.call-start = ((), (), s32[]{:S(2)}) async-start(), calls=%async_computation.50 | async-start | bytes 17301504 | tf_op jit(solution)/shard_map/reduce_scatter | solution.py:204
  2036.1 2878.4 %reduce-scatter.83.cloned.1.call-start = ((), (), s32[]{:S(2)}) async-start(), calls=%async_computation.51 | async-start | bytes 17301504 | tf_op jit(solution)/shard_map/reduce_scatter | solution.py:204
  2044.4 3056.5 %reduce-scatter.69.cloned.1.call-start = ((), (), s32[]{:S(2)}) async-start(), calls=%async_computation.44 | async-start | bytes 17301504 | tf_op jit(solution)/shard_map/reduce_scatter | solution.py:206
  2055.7 3232.0 %reduce-scatter.71.cloned.1.call-start = ((), (), s32[]{:S(2)}) async-start(), calls=%async_computation.45 | async-start | bytes 17301504 | tf_op jit(solution)/shard_map/reduce_scatter | solution.py:206
  2063.9 3410.4 %reduce-scatter.73.cloned.1.call-start = ((), (), s32[]{:S(2)}) async-start(), calls=%async_computation.46 | async-start | bytes 17301504 | tf_op jit(solution)/shard_map/reduce_scatter | solution.py:206
  2072.0 3588.7 %reduce-scatter.75.cloned.1.call-start = ((), (), s32[]{:S(2)}) async-start(), calls=%async_computation.47 | async-start | bytes 17301504 | tf_op jit(solution)/shard_map/reduce_scatter | solution.py:206
  2080.4 3767.1 %reduce-scatter.61.cloned.1.call-start = ((), (), s32[]{:S(2)}) async-start(), calls=%async_computation.40 | async-start | bytes 17301504 | tf_op jit(solution)/shard_map/reduce_scatter | solution.py:205
  2090.0 3944.0 %reduce-scatter.63.cloned.1.call-start = ((), (), s32[]{:S(2)}) async-start(), calls=%async_computation.41 | async-start | bytes 17301504 | tf_op jit(solution)/shard_map/reduce_scatter | solution.py:205
  2098.3 4122.3 %reduce-scatter.65.cloned.1.call-start = ((), (), s32[]{:S(2)}) async-start(), calls=%async_computation.42 | async-start | bytes 17301504 | tf_op jit(solution)/shard_map/reduce_scatter | solution.py:205
  2106.4 4300.7 %reduce-scatter.67.cloned.1.call-start = ((), (), s32[]{:S(2)}) async-start(), calls=%async_computation.43 | async-start | bytes 17301504 | tf_op jit(solution)/shard_map/reduce_scatter | solution.py:205
  (74 other events, 8832.5 us)
Sparse Core Ops, SparseCore 0:
  456.1 297.0 all-gather.18
  755.1 297.0 all-gather.20
  1054.0 297.0 all-gather.22
  1543.1 332.8 all-reduce.23
  1878.1 144.3 reduce-scatter.52
  2167.3 141.5 reduce-scatter.56
  2454.0 141.0 reduce-scatter.100
  2740.2 141.0 reduce-scatter.104
  3026.3 140.8 reduce-scatter.92
  3169.5 141.0 reduce-scatter.94
  3455.7 140.9 reduce-scatter.98
  4027.5 141.6 reduce-scatter.90
  4171.3 183.2 reduce-scatter.76
  4356.8 184.3 reduce-scatter.78
  4543.5 184.3 reduce-scatter.80
  4730.1 184.3 reduce-scatter.82
  4916.6 184.3 reduce-scatter.68
  5103.3 184.3 reduce-scatter.70
  5289.9 184.3 reduce-scatter.72
  5476.4 184.3 reduce-scatter.74
  5663.1 184.3 reduce-scatter.60
  5849.7 184.3 reduce-scatter.62
  6036.2 184.3 reduce-scatter.64
  6222.7 184.3 reduce-scatter.66
  (13 shorter events, 1557.4 us)
where the time goes:
time: 6430 us; the launch traced here: 6420 us
  waiting for transfers between devices  5700 us (89%)
  matrix products  330 us (5%)
  local copies, waits for them, and re-layouts  228 us (4%)
  other arithmetic  83.6 us (1%)
    unnamed x50, waiting for transfers between devices  2010 us
    reduce_scatter x4, waiting for transfers between devices, shards(): lax.psum_scatter(gate_term, ('dp', 'seq'), scatter_dimension=0, tiled=True)  743 us
    reduce_scatter x4, waiting for transfers between devices, shards(): lax.psum_scatter(up_term, ('dp', 'seq'), scatter_dimension=0, tiled=True)  743 us
    reduce_scatter x4, waiting for transfers between devices, shards(): lax.psum_scatter(down_term, ('dp', 'seq'), scatter_dimension=0, tiled=True)  738 us
    all_gather x1, waiting for transfers between devices, shards(): lax.all_gather(w_gate, 'dp', axis=0, tiled=True)  293 us
    all_gather x1, waiting for transfers between devices, shards(): lax.all_gather(w_up, 'dp', axis=0, tiled=True)  279 us
    all_gather x1, waiting for transfers between devices, shards(): lax.all_gather(w_down, 'dp', axis=0, tiled=True)  275 us
    reduce_scatter x4, waiting for transfers between devices, shards(): lax.psum_scatter(out_term, ('dp', 'seq'), scatter_dimension=0, tiled=True)  272 us
  transfers between devices with their start and end apart: 37, of which 35 were waited for; matrix products, arithmetic and copies ran while one was open for 7% of the time, Pallas kernels for 0%

commit v1 on v0

--- a/solution.py
+++ b/solution.py
@@ -85,7 +85,7 @@
     return vector.reshape(parts, slab_count, width)[:, index].reshape(parts * width)
 
 
-def shards(
+def shards_by_slab(
     tokens,
     doc_ids,
     cotangent,
@@ -348,6 +348,254 @@
         ga_grad,
         ffn_grad,
     )
+
+
+def own_columns(matrix, groups, parts, index):
+    lead = matrix.shape[0]
+    width = matrix.shape[1] // (groups * parts)
+    view = matrix.reshape(lead, groups, parts, width)
+    return lax.dynamic_index_in_dim(view, index, 2, False).reshape(lead, groups * width)
+
+
+def gather_seq(piece):
+    return lax.all_gather(piece, "seq", axis=1, tiled=True)
+
+
+def scatter_seq(partial):
+    return lax.psum_scatter(partial, "seq", scatter_dimension=1, tiled=True)
+
+
+def rows_home(partial, seq_count):
+    summed = lax.psum_scatter(partial, "dp", scatter_dimension=0, tiled=True)
+    lead, width = summed.shape
+    return lax.all_to_all(
+        summed.reshape(seq_count, lead // seq_count, width), "seq", split_axis=0, concat_axis=0
+    )
+
+
+def shards_by_feature(
+    tokens,
+    doc_ids,
+    cotangent,
+    w_query,
+    w_key,
+    w_value,
+    w_out,
+    w_gate,
+    w_up,
+    w_down,
+    g_query,
+    g_key,
+    g_attn,
+    g_ffn,
+):
+    row_count, piece_len, model_width = tokens.shape
+    head_size = HEAD
+    feature_count = w_query.shape[1]
+    scale = head_size ** (-0.5)
+    seq_count = lax.axis_size("seq")
+    dp_count = lax.axis_size("dp")
+    seq_at = lax.axis_index("seq")
+    row_len = piece_len * seq_count
+    all_count = row_count * row_len
+    tok_count = row_count * piece_len
+    own_features = feature_count // seq_count
+    own_heads = own_features // head_size
+    own_hidden = w_gate.shape[1] // seq_count
+    low = jnp.bfloat16
+
+    def gather_dp(piece):
+        return lax.all_gather(piece, "dp", axis=0, tiled=True)
+
+    def own_piece(tensor):
+        view = tensor.reshape(row_count, row_len, -1)
+        return lax.dynamic_slice_in_dim(view, seq_at * piece_len, piece_len, 1).reshape(tok_count, -1)
+
+    w_qkv = gather_dp(
+        jnp.concatenate([own_columns(w, 1, seq_count, seq_at) for w in (w_query, w_key, w_value)], 1)
+    )
+    tokens_all = gather_seq(tokens).reshape(all_count, model_width)
+    ids_all = gather_seq(doc_ids)
+    wo_full = gather_dp(w_out)
+    w_hidden = gather_dp(
+        jnp.concatenate([own_columns(w, dp_count, seq_count, seq_at) for w in (w_gate, w_up)], 1)
+    )
+    w_back = gather_dp(
+        lax.dynamic_slice_in_dim(
+            w_down, seq_at * (own_hidden // dp_count), own_hidden // dp_count, 0
+        )
+    )
+    gain_query = lax.dynamic_slice_in_dim(g_query, seq_at * own_features, own_features).astype(jnp.float32)
+    gain_key = lax.dynamic_slice_in_dim(g_key, seq_at * own_features, own_features).astype(jnp.float32)
+    gain_attn = g_attn.astype(jnp.float32)
+    gain_ffn = g_ffn.astype(jnp.float32)
+
+    qkv = jnp.dot(tokens_all, w_qkv, preferred_element_type=jnp.float32)
+    query_pre = qkv[:, :own_features]
+    key_pre = qkv[:, own_features : 2 * own_features]
+    value_low = qkv[:, 2 * own_features :].astype(low).reshape(row_count, row_len, own_heads, head_size)
+    squares = jnp.stack([jnp.sum(query_pre * query_pre, -1), jnp.sum(key_pre * key_pre, -1)])
+    inverse = lax.rsqrt(lax.psum(squares, "seq") / feature_count + eps)
+    query_inv, key_inv = inverse[0][:, None], inverse[1][:, None]
+    query_unit = query_pre * query_inv
+    key_unit = key_pre * key_inv
+    positions = jnp.tile(jnp.arange(row_len, dtype=jnp.int32), row_count)
+    cosine, sine_part = rotation(positions, head_size)
+    heads = (all_count, own_heads, head_size)
+    split = (row_count, row_len, own_heads, head_size)
+    query_low = rotate((query_unit * gain_query).reshape(heads), cosine, sine_part).astype(low).reshape(split)
+    key_low = rotate((key_unit * gain_key).reshape(heads), cosine, sine_part).astype(low).reshape(split)
+    at = jnp.arange(row_len, dtype=jnp.int32)
+    allowed = visible(ids_all, ids_all, at, at)
+    scores = jnp.einsum("rche,rlhe->rhcl", query_low, key_low, preferred_element_type=jnp.float32) * scale
+    masked = jnp.where(allowed, scores, -1e30)
+    row_max = jnp.max(masked, -1, keepdims=True)
+    log_total = jnp.log(jnp.sum(jnp.exp(masked - row_max), -1, keepdims=True)) + row_max
+    probs = jnp.exp(masked - log_total)
+    probs_low = probs.astype(low)
+    mixed = jnp.einsum("rhcl,rlhe->rche", probs_low, value_low, preferred_element_type=jnp.float32)
+    mixed_low = mixed.astype(low).reshape(all_count, own_features)
+    mixed_all = lax.all_gather(mixed_low, "seq", axis=1, tiled=True)
+    attn_out = jnp.dot(mixed_all, wo_full, preferred_element_type=jnp.float32)
+    attn_inv_all = inverse_rms(attn_out)
+    hidden_all = tokens_all.astype(jnp.float32) + attn_out * attn_inv_all * gain_attn
+    hidden_low = hidden_all.astype(low)
+    attn_inv = own_piece(attn_inv_all)
+    attn_unit = own_piece(attn_out) * attn_inv
+    hidden_state = tokens.reshape(tok_count, model_width).astype(jnp.float32) + attn_unit * gain_attn
+
+    gate_up = jnp.dot(hidden_low, w_hidden, preferred_element_type=jnp.float32)
+    gate, up_proj = gate_up[:, :own_hidden], gate_up[:, own_hidden:]
+    sigma = jax.nn.sigmoid(gate)
+    active = gate * sigma
+    inner_low = (active * up_proj).astype(low)
+    branch_part = jnp.dot(inner_low, w_back, preferred_element_type=jnp.float32).astype(low)
+    branch = (
+        scatter_seq(branch_part.reshape(row_count, row_len, model_width))
+        .astype(jnp.float32)
+        .reshape(tok_count, model_width)
+    )
+    branch_inv = inverse_rms(branch)
+    branch_unit = branch * branch_inv
+    result = (
+        (hidden_state + branch_unit * gain_ffn)
+        .astype(low)
+        .reshape(row_count, piece_len, model_width)
+    )
+
+    grad_out = cotangent.reshape(tok_count, model_width).astype(jnp.float32)
+    ffn_gain_term = jnp.sum(grad_out * branch_unit, 0)
+    d_branch = norm_back(grad_out * gain_ffn, branch_unit, branch_inv).astype(low)
+    d_branch_all = gather_seq(d_branch.reshape(row_count, piece_len, model_width)).reshape(all_count, model_width)
+    d_inner = jnp.einsum("nd,fd->nf", d_branch_all, w_back, preferred_element_type=jnp.float32)
+    d_gate = (d_inner * up_proj * sigma * (1.0 + gate * (1.0 - sigma))).astype(low)
+    d_up = (d_inner * active).astype(low)
+    d_gate_up = jnp.concatenate([d_gate, d_up], 1)
+    d_hidden_part = jnp.einsum("nf,df->nd", d_gate_up, w_hidden, preferred_element_type=jnp.float32).astype(low)
+    d_hidden = grad_out + scatter_seq(d_hidden_part.reshape(row_count, row_len, model_width)).astype(
+        jnp.float32
+    ).reshape(tok_count, model_width)
+
+    attn_gain_term = jnp.sum(d_hidden * attn_unit, 0)
+    d_attn = norm_back(d_hidden * gain_attn, attn_unit, attn_inv).astype(low)
+    d_mixed = jnp.einsum("nd,fd->nf", d_attn, wo_full, preferred_element_type=jnp.float32).astype(low)
+    both = jnp.concatenate(
+        [
+            d_mixed.reshape(row_count, piece_len, seq_count, own_features),
+            d_attn.reshape(row_count, piece_len, seq_count, model_width // seq_count),
+        ],
+        -1,
+    )
+    both = lax.all_to_all(both, "seq", split_axis=2, concat_axis=1, tiled=True).reshape(all_count, -1)
+    d_mixed = both[:, :own_features].reshape(split)
+    d_attn_own = both[:, own_features:]
+
+    down_part = jnp.einsum("nf,nd->fd", inner_low, d_branch_all, preferred_element_type=jnp.float32).astype(low)
+    down_grad = lax.psum_scatter(down_part, "dp", scatter_dimension=0, tiled=True).astype(jnp.float32)
+    hidden_part = jnp.einsum("nd,nf->df", hidden_low, d_gate_up, preferred_element_type=jnp.float32).astype(low)
+    hidden_home = rows_home(hidden_part, seq_count).astype(jnp.float32)
+    home_rows = hidden_home.shape[1]
+    hidden_home = (
+        hidden_home.reshape(seq_count, home_rows, 2, dp_count, own_hidden // dp_count)
+        .transpose(2, 1, 3, 0, 4)
+        .reshape(2, home_rows, own_hidden * seq_count)
+    )
+    gate_grad, up_grad = hidden_home[0], hidden_home[1]
+
+    d_probs = jnp.einsum("rche,rlhe->rhcl", d_mixed, value_low, preferred_element_type=jnp.float32)
+    row_dot = jnp.sum(probs * d_probs, -1, keepdims=True)
+    d_scores = (probs * (d_probs - row_dot)).astype(low)
+    d_query = (
+        jnp.einsum("rhcl,rlhe->rche", d_scores, key_low, preferred_element_type=jnp.float32) * scale
+    ).astype(low)
+    d_key = (
+        jnp.einsum("rhcl,rche->rlhe", d_scores, query_low, preferred_element_type=jnp.float32) * scale
+    ).astype(low)
+    d_value = (
+        jnp.einsum("rhcl,rche->rlhe", probs_low, d_mixed, preferred_element_type=jnp.float32)
+        .astype(low)
+        .reshape(all_count, own_features)
+    )
+    dq_norm = unrotate(d_query.reshape(heads).astype(jnp.float32), cosine, sine_part).reshape(all_count, own_features)
+    dk_norm = unrotate(d_key.reshape(heads).astype(jnp.float32), cosine, sine_part).reshape(all_count, own_features)
+    query_gain_term = jnp.sum(dq_norm * query_unit, 0)
+    key_gain_term = jnp.sum(dk_norm * key_unit, 0)
+    dq_gained = dq_norm * gain_query
+    dk_gained = dk_norm * gain_key
+    dots = jnp.stack([jnp.sum(dq_gained * query_unit, -1), jnp.sum(dk_gained * key_unit, -1)])
+    means = lax.psum(dots, "seq") / feature_count
+    dq_pre = (query_inv * (dq_gained - query_unit * means[0][:, None])).astype(low)
+    dk_pre = (key_inv * (dk_gained - key_unit * means[1][:, None])).astype(low)
+    d_qkv = jnp.concatenate([dq_pre, dk_pre, d_value], 1)
+    d_tokens_part = jnp.einsum("nf,df->nd", d_qkv, w_qkv, preferred_element_type=jnp.float32).astype(low)
+    d_tokens = d_hidden + scatter_seq(d_tokens_part.reshape(row_count, row_len, model_width)).astype(
+        jnp.float32
+    ).reshape(tok_count, model_width)
+
+    qkv_part = jnp.einsum("nd,nf->df", tokens_all, d_qkv, preferred_element_type=jnp.float32).astype(low)
+    out_part = jnp.einsum("nf,nd->fd", mixed_all, d_attn_own, preferred_element_type=jnp.float32).astype(low)
+    attn_home = rows_home(jnp.concatenate([qkv_part, out_part], 1), seq_count).astype(jnp.float32)
+    attn_rows = attn_home.shape[1]
+    attn_home = (
+        attn_home.reshape(seq_count, attn_rows, 4, own_features)
+        .transpose(2, 1, 0, 3)
+        .reshape(4, attn_rows, feature_count)
+    )
+    zeros = jnp.zeros((feature_count,), jnp.float32)
+    gains = jnp.stack(
+        [
+            lax.dynamic_update_slice_in_dim(zeros, query_gain_term, seq_at * own_features, 0),
+            lax.dynamic_update_slice_in_dim(zeros, key_gain_term, seq_at * own_features, 0),
+            attn_gain_term,
+            ffn_gain_term,
+        ]
+    )
+    gains = lax.psum(gains, ("dp", "seq"))
+    share = feature_count // (dp_count * seq_count)
+    gains = lax.dynamic_slice_in_dim(
+        gains, (lax.axis_index("dp") * seq_count + seq_at) * share, share, 1
+    )
+    return (
+        result,
+        d_tokens.reshape(row_count, piece_len, model_width),
+        attn_home[0],
+        attn_home[1],
+        attn_home[2],
+        attn_home[3],
+        gate_grad,
+        up_grad,
+        down_grad,
+        gains[0],
+        gains[1],
+        gains[2],
+        gains[3],
+    )
+
+
+def shards(tokens, doc_ids, cotangent, w_query, *rest):
+    whole_heads = w_query.shape[1] // HEAD % lax.axis_size("seq") == 0
+    body = shards_by_feature if whole_heads else shards_by_slab
+    return body(tokens, doc_ids, cotangent, w_query, *rest)
 
 
 def solution(mesh):

time: 6430 us -> 898 us (0.14)
  waiting for transfers between devices: 5700 us -> 456 us
  matrix products: 330 us -> 131 us
  local copies, waits for them, and re-layouts: 228 us -> 111 us
    reduce_scatter x16 -> x6, waiting for transfers between devices: 2500 us -> 149 us  [the longest x3 92.6 us: scatter_seq(): return lax.psum_scatter(partial, 'seq', scatter_dimension=1, tiled=True)]
    unnamed x50 -> x13, waiting for transfers between devices: 2010 us -> 1.56 us
    all_gather x8 -> x7, waiting for transfers between devices: 1190 us -> 286 us  [the longest x4 144 us: gather_dp(): return lax.all_gather(piece, 'dp', axis=0, tiled=True)]
    dot_general x64 -> x18, matrix products: 330 us -> 131 us  [the longest x1 14.1 us: shards_by_feature(): jnp.einsum('nd,nf->df', hidden_low, d_gate_up, preferred_element_type=jnp...]
    psum x0 -> x3, blocking collectives: none -> 71.9 us  [the longest x1 41 us: shards_by_feature(): gains = lax.psum(gains, ('dp', 'seq'))]
  transfers between devices with their start and end apart: 37 -> 15, of which waited for: 35 -> 13; matrix products, arithmetic and copies ran while one was open for 7% -> 25% of each run, Pallas kernels for 0% -> 0%
where the time goes in v1:
time: 898 us; the launch traced here: 890 us
  waiting for transfers between devices  456 us (51%)
  matrix products  131 us (15%)
  blocking collectives  115 us (13%)
  local copies, waits for them, and re-layouts  111 us (12%)
  other arithmetic  51.4 us (6%)
  between operations  15 us (2%)
  starting transfers between devices  10.3 us (1%)
    all_gather x4, waiting for transfers between devices, gather_dp(): return lax.all_gather(piece, 'dp', axis=0, tiled=True)  144 us
    all_gather x2, waiting for transfers between devices, gather_seq(): return lax.all_gather(piece, 'seq', axis=1, tiled=True)  93.9 us
    reduce_scatter x3, waiting for transfers between devices, scatter_seq(): return lax.psum_scatter(partial, 'seq', scatter_dimension=1, tiled=True)  92.6 us
    unnamed x107, local copies, waits for them, and re-layouts  59.6 us
    all_gather x1, waiting for transfers between devices, shards_by_feature(): mixed_all = lax.all_gather(mixed_low, 'seq', axis=1, tiled=True)  48.9 us
    psum x1, blocking collectives, shards_by_feature(): gains = lax.psum(gains, ('dp', 'seq'))  41 us
    all_to_all x1, blocking collectives, shards_by_feature(): lax.all_to_all(both, 'seq', split_axis=2, concat_axis=1, tiled=True)  29.9 us
    reduce_scatter x1, waiting for transfers between devices, shards_by_feature(): lax.psum_scatter(down_part, 'dp', scatter_dimension=0, tiled=True)  28.6 us
  transfers between devices with their start and end apart: 15, of which 13 were waited for; matrix products, arithmetic and copies ran while one was open for 25% of the time, Pallas kernels for 0%

profile of v1, /device:TPU:0, one launch (start us, length us, event | category | flops | bytes accessed | tf_op | source)
XLA Modules:
  0.0 890.2 jit_solution(4832865761933219216)
XLA Ops:
  20.9 13.5 %all_gather.26 = s32[1,1024]{1,0:T(1,128)S(1)} all-gather(s32[1,128]{1,0:T(1,128)S(1)} %copy-done.40), channel_id=1, replica_groups=mesh['dp'=4,'seq'=8] {'seq'}, dimensions={1}, use_global_device_ids=true | all-gather | bytes 4608 | tf_op jit(solution)/shard_map/all_gather | solution.py:361
  37.6 28.4 %all-gather.8.cloned.1.call-done = bf16[2048,768]{1,0:T(8,128)(2,1)} async-done(((bf16[512,768]{1,0:T(8,128)(2,1)}), bf16[2048,768]{1,0:T(8,128)(2,1)}) %all-gather.8.cloned.1.call-update) | async-done | bytes 3145744 | tf_op jit(solution)/shard_map/all_gather | solution.py:408
  66.0 48.5 %all-gather.10.cloned.1.call-done = bf16[1,1024,2048]{2,1,0:T(8,128)(2,1)} async-done(((bf16[1,128,2048]{2,1,0:T(8,128)(2,1)}), bf16[1,1024,2048]{2,1,0:T(8,128)(2,1)}) %all-gather.10.cloned.1.call-update) | async-done | bytes 4194320 | tf_op jit(solution)/shard_map/all_gather | solution.py:361
  122.9 15.2 %psum.21 = f32[2,1024]{1,0:T(2,128)S(1)} all-reduce(f32[2,1024]{1,0:T(2,128)S(1)} %pad_maximum_fusion.18), channel_id=1, replica_groups=mesh['dp'=4,'seq'=8] {'seq'}, use_global_device_ids=true, to_apply=%region_2.3 | all-reduce | flops 2048 | bytes 16384 | tf_op jit(solution)/shard_map/psum | solution.py:438
  164.3 12.0 %copy.122 = bf16[512,8192]{0,1:T(8,128)(2,1)} copy(bf16[512,8192]{1,0:T(8,128)(2,1)} %param.21) | data formatting | bytes 16777216 | tf_op args[7]
  176.3 12.0 %copy.123 = bf16[512,8192]{0,1:T(8,128)(2,1)} copy(bf16[512,8192]{1,0:T(8,128)(2,1)} %param.22) | data formatting | bytes 16777216 | tf_op args[8]
  202.7 48.9 %all-gather.12.cloned.1.call-done = bf16[1024,2048]{0,1:T(8,128)(2,1)} async-done(((bf16[1024,256]{0,1:T(8,128)(2,1)}), bf16[1024,2048]{0,1:T(8,128)(2,1)}) %all-gather.12.cloned.1.call-update) | async-done | bytes 4194320 | tf_op jit(solution)/shard_map/all_gather | solution.py:458
  251.6 13.3 %multiply_reduce_fusion.1 = (f32[1024]{0:T(1024)S(1)}, f32[1024,2048]{1,0:T(8,128)S(1)}) fusion(bf16[1024,2048]{0,1:T(8,128)(2,1)} %all-gather.12.cloned.1.call-done, bf16[2048,2048]{1,0:T(8,128)(2,1)} %all-gather.14.cloned.1.call-done), kind=kOutput, calls=%fused_computation.3 | convolution fusion | flops 8594127872 | bytes 20975616 | tf_op jit(solution)/shard_map/dot_general | solution.py:459
  271.2 68.8 %all-gather.16.cloned.1.call-done = bf16[2048,2048]{0,1:T(8,128)(2,1)} async-done(((bf16[512,2048]{0,1:T(8,128)(2,1)}), bf16[2048,2048]{0,1:T(8,128)(2,1)}) %all-gather.16.cloned.1.call-update) | async-done | bytes 8388624 | tf_op jit(solution)/shard_map/all_gather | solution.py:408
  340.1 12.6 %fusion.73 = f32[1024,2048]{1,0:T(8,128)S(1)} fusion(bf16[1024,2048]{1,0:T(8,128)(2,1)} %add_convert_fusion, bf16[2048,2048]{0,1:T(8,128)(2,1)} %all-gather.16.cloned.1.call-done), kind=kOutput, calls=%fused_computation.159 | convolution fusion | flops 8589934592 | bytes 20971520 | tf_op jit(solution)/shard_map/dot_general | solution.py:467
  357.3 37.7 %all-gather.18.cloned.1.call-done = bf16[1024,2048]{1,0:T(8,128)(2,1)} async-done(((bf16[256,2048]{1,0:T(8,128)(2,1)}), bf16[1024,2048]{1,0:T(8,128)(2,1)}) %all-gather.18.cloned.1.call-update) | async-done | bytes 4194320 | tf_op jit(solution)/shard_map/all_gather | solution.py:408
  403.9 49.4 %reduce-scatter.7.cloned.1.call-done = bf16[1,128,2048]{2,1,0:T(8,128)(2,1)} async-done(((bf16[1,1024,2048]{2,1,0:T(8,128)(2,1)}), bf16[1,128,2048]{2,1,0:T(8,128)(2,1)}) %reduce-scatter.7.cloned.1.call-update) | async-done | bytes 524304 | tf_op jit(solution)/shard_map/reduce_scatter | solution.py:365
  458.3 45.4 %all-gather.20.cloned.1.call-done = bf16[1,1024,2048]{2,1,0:T(8,128)(2,1)} async-done(((bf16[1,128,2048]{2,1,0:T(8,128)(2,1)}), bf16[1,1024,2048]{2,1,0:T(8,128)(2,1)}) %all-gather.20.cloned.1.call-update) | async-done | bytes 4194320 | tf_op jit(solution)/shard_map/all_gather | solution.py:361
  503.7 11.7 %multiply_convert_fusion.2 = (bf16[1024,1024]{1,0:T(8,128)(2,1)S(1)}, bf16[1024,1024]{1,0:T(8,128)(2,1)S(1)}) fusion(f32[1024,2048]{1,0:T(8,128)} %copy-done.4, bf16[1024,2048]{1,0:T(8,128)(2,1)} %all-gather.18.cloned.1.call-done, bf16[1,1024,2048]{2,1,0:T(8,128)(2,1)} %all-gather.20.cloned.1.call-done), kind=kOutput, calls=%fused_computation.24 | convolution fusion | flops 4308598784 | bytes 20971520 | tf_op jit(solution)/shard_map/nd,fd->nf/dot_general | solution.py:490
  517.4 12.7 %convert_bitcast_fusion.1 = bf16[1,1024,2048]{2,1,0:T(8,128)(2,1)} fusion(bf16[2048,2048]{0,1:T(8,128)(2,1)} %all-gather.16.cloned.1.call-done, bf16[1024,1024]{1,0:T(8,128)(2,1)S(1)} %get-tuple-element.27, bf16[1024,1024]{1,0:T(8,128)(2,1)S(1)} %get-tuple-element.26), kind=kOutput, calls=%fused_computation.22 | convolution fusion | flops 8600420352 | bytes 16777216 | tf_op jit(solution)/shard_map/nf,df->nd/dot_general | solution.py:494
  530.3 14.1 %convolution_convert_fusion = bf16[2048,2048]{1,0:T(8,128)(2,1)} fusion(bf16[1024,2048]{1,0:T(8,128)(2,1)} %add_convert_fusion, bf16[1024,1024]{1,0:T(8,128)(2,1)} %copy-done.44, bf16[1024,1024]{1,0:T(8,128)(2,1)} %copy-done.43), kind=kOutput, calls=%fused_computation.7 | convolution fusion | flops 8602517504 | bytes 16777216 | tf_op jit(solution)/shard_map/nd,nf->df/dot_general | solution.py:515
  544.6 34.4 %reduce-scatter.9.cloned.1.call-done = bf16[1,128,2048]{2,1,0:T(8,128)(2,1)} async-done(((bf16[1,1024,2048]{2,1,0:T(8,128)(2,1)}), bf16[1,128,2048]{2,1,0:T(8,128)(2,1)}) %reduce-scatter.9.cloned.1.call-update) | async-done | bytes 524304 | tf_op jit(solution)/shard_map/reduce_scatter | solution.py:365
  598.0 29.9 %all_to_all.25 = bf16[1,128,8,512]{1,3,0,2:T(8,128)(2,1)} all-to-all(bf16[1,128,8,512]{1,3,0,2:T(8,128)(2,1)S(1)} %maximum_bitcast_fusion), channel_id=1, replica_groups=mesh['dp'=4,'seq'=8] {'seq'}, dimensions={2} | all-to-all | bytes 2097152 | tf_op jit(solution)/shard_map/all_to_all | solution.py:509
  661.4 15.7 %psum.22 = f32[2,1024]{1,0:T(2,128)S(1)} all-reduce(f32[2,1024]{1,0:T(2,128)S(1)} %pad_maximum_fusion.19), channel_id=1, replica_groups=mesh['dp'=4,'seq'=8] {'seq'}, use_global_device_ids=true, to_apply=%region_14.15 | all-reduce | flops 2048 | bytes 16384 | tf_op jit(solution)/shard_map/psum | solution.py:546
  696.7 9.4 %fusion.12 = bf16[1024,2048]{1,0:T(8,128)(2,1)} fusion(bf16[1024,1024]{1,0:T(8,128)(2,1)} %copy-done.22, bf16[1,1024,2048]{2,1,0:T(8,128)(2,1)} %all-gather.20.cloned.1.call-done), kind=kOutput, calls=%fused_computation.31 | convolution fusion | flops 4297064448 | bytes 10485760 | tf_op jit(solution)/shard_map/nf,nd->fd/dot_general | solution.py:513
  719.6 27.6 %reduce-scatter.13.cloned.1.call-done = bf16[512,1024]{0,1:T(8,128)(2,1)} async-done(((bf16[2048,1024]{0,1:T(8,128)(2,1)}), bf16[512,1024]{0,1:T(8,128)(2,1)}) %reduce-scatter.13.cloned.1.call-update) | async-done | bytes 1048592 | tf_op jit(solution)/shard_map/reduce_scatter | solution.py:369
  749.5 19.1 %all-to-all-done.2 = bf16[8,64,2048]{2,1,0:T(8,128)(2,1)} async-done(((bf16[8,64,2048]{2,1,0:T(8,128)(2,1)}), bf16[8,64,2048]{2,1,0:T(8,128)(2,1)}, u32[]{:S(2)}, u32[]{:S(2)}) %all-to-all-start.2) | async-done | bytes 2097184 | tf_op jit(solution)/shard_map/all_to_all | solution.py:371
  774.1 28.6 %reduce-scatter.17.cloned.1.call-done = bf16[256,2048]{1,0:T(8,128)(2,1)} async-done(((bf16[1024,2048]{1,0:T(8,128)(2,1)}), bf16[256,2048]{1,0:T(8,128)(2,1)}) %reduce-scatter.17.cloned.1.call-update) | async-done | bytes 1048592 | tf_op jit(solution)/shard_map/reduce_scatter | solution.py:514
  805.6 41.0 %psum.23 = f32[4,2048]{1,0:T(4,128)S(1)} all-reduce(f32[4,2048]{1,0:T(4,128)S(1)} %pad_maximum_fusion.17), channel_id=1, replica_groups=mesh['dp'=4,'seq'=8] {'dp','seq'}, use_global_device_ids=true, to_apply=%region_23.24 | all-reduce | flops 8192 | bytes 65536 | tf_op jit(solution)/shard_map/psum | solution.py:573
  (232 shorter events, 225.4 us)
Async XLA Ops:
  7.2 58.9 %all-gather.8.cloned.1.call-start = ((), (), s32[]{:S(2)}) async-start(), calls=%async_computation.9 | async-start | bytes 3932160 | tf_op jit(solution)/shard_map/all_gather | solution.py:408
  19.3 95.2 %all-gather.10.cloned.1.call-start = ((), (), s32[]{:S(2)}) async-start(), calls=%async_computation.10 | async-start | bytes 4718592 | tf_op jit(solution)/shard_map/all_gather | solution.py:361
  20.1 182.6 %all-gather.14.cloned.1.call-start = ((), (), s32[]{:S(2)}) async-start(), calls=%async_computation.12 | async-start | bytes 10485760 | tf_op jit(solution)/shard_map/all_gather | solution.py:408
  20.8 230.8 %all-gather.12.cloned.1.call-start = ((), (), s32[]{:S(2)}) async-start(), calls=%async_computation.11 | async-start | bytes 4718592 | tf_op jit(solution)/shard_map/all_gather | solution.py:458
  35.1 103.1 %copy-start.35 = (f32[256]{0:T(256)}, f32[256]{0:T(256)S(1)}, u32[]{:S(2)}) copy-start(f32[256]{0:T(256)S(1)} %get-tuple-element.74) | copy-start | bytes 3076
  35.1 103.1 %copy-start.37 = (f32[256]{0:T(256)}, f32[256]{0:T(256)S(1)}, u32[]{:S(2)}) copy-start(f32[256]{0:T(256)S(1)} %get-tuple-element.75) | copy-start | bytes 3076
  37.0 115.7 %copy-start.7 = (f32[1024,64]{1,0:T(8,128)}, f32[1024,64]{1,0:T(8,128)S(1)}, u32[]{:S(2)}) copy-start(f32[1024,64]{1,0:T(8,128)S(1)} %get-tuple-element.58) | copy-start | bytes 786436
  37.0 115.7 %copy-start.9 = (f32[1024,64]{1,0:T(8,128)}, f32[1024,64]{1,0:T(8,128)S(1)}, u32[]{:S(2)}) copy-start(f32[1024,64]{1,0:T(8,128)S(1)} %get-tuple-element.59) | copy-start | bytes 786436
  164.2 175.8 %all-gather.16.cloned.1.call-start = ((), (), s32[]{:S(2)}) async-start(), calls=%async_computation.13 | async-start | bytes 10485760 | tf_op jit(solution)/shard_map/all_gather | solution.py:408
  191.4 203.5 %all-gather.18.cloned.1.call-start = ((), (), s32[]{:S(2)}) async-start(), calls=%async_computation.14 | async-start | bytes 5242880 | tf_op jit(solution)/shard_map/all_gather | solution.py:408
  193.8 259.5 %reduce-scatter.7.cloned.1.call-start = ((), (), s32[]{:S(2)}) async-start(), calls=%async_computation.15 | async-start | bytes 4718592 | tf_op jit(solution)/shard_map/reduce_scatter | solution.py:365
  251.6 16.6 %copy-start.11 = (bf16[1,1024,2048]{2,1,0:T(8,128)(2,1)S(1)}, bf16[1,1024,2048]{2,1,0:T(8,128)(2,1)}, u32[]{:S(2)}) copy-start(bf16[1,1024,2048]{2,1,0:T(8,128)(2,1)} %all-gather.10.cloned.1.call-done) | copy-start | bytes 12582916
  357.3 37.7 %copy-start.22 = (bf16[1024,1024]{1,0:T(8,128)(2,1)}, bf16[1024,1024]{1,0:T(8,128)(2,1)S(1)}, u32[]{:S(2)}) copy-start(bf16[1024,1024]{1,0:T(8,128)(2,1)S(1)} %multiply_convert_fusion.3) | copy-start | bytes 6291460
  403.2 51.3 %copy-start.2 = (bf16[1,128,2048]{2,1,0:T(8,128)(2,1)S(1)}, bf16[1,128,2048]{2,1,0:T(8,128)(2,1)}, u32[]{:S(2)}) copy-start(bf16[1,128,2048]{2,1,0:T(8,128)(2,1)} %param.16) | copy-start | bytes 1572868
  403.2 100.5 %all-gather.20.cloned.1.call-start = ((), (), s32[]{:S(2)}) async-start(), calls=%async_computation.16 | async-start | bytes 4718592 | tf_op jit(solution)/shard_map/all_gather | solution.py:361
  458.2 120.7 %reduce-scatter.9.cloned.1.call-start = ((), (), s32[]{:S(2)}) async-start(), calls=%async_computation.17 | async-start | bytes 4718592 | tf_op jit(solution)/shard_map/reduce_scatter | solution.py:365
  530.1 184.9 %reduce-scatter.15.cloned.1.call-start = ((), (), s32[]{:S(2)}) async-start(), calls=%async_computation.20 | async-start | bytes 10485760 | tf_op jit(solution)/shard_map/reduce_scatter | solution.py:369
  544.4 202.8 %reduce-scatter.13.cloned.1.call-start = ((), (), s32[]{:S(2)}) async-start(), calls=%async_computation.19 | async-start | bytes 5242880 | tf_op jit(solution)/shard_map/reduce_scatter | solution.py:369
  696.6 106.0 %reduce-scatter.17.cloned.1.call-start = ((), (), s32[]{:S(2)}) async-start(), calls=%async_computation.21 | async-start | bytes 5242880 | tf_op jit(solution)/shard_map/reduce_scatter | solution.py:514
  706.1 149.9 %reduce-scatter.11.cloned.1.call-start = ((), (), s32[]{:S(2)}) async-start(), calls=%async_computation.18 | async-start | bytes 4718592 | tf_op jit(solution)/shard_map/reduce_scatter | solution.py:365
  715.0 57.8 %copy-start.6 = (bf16[1,128,2048]{2,1,0:T(8,128)(2,1)S(1)}, bf16[1,128,2048]{2,1,0:T(8,128)(2,1)}, u32[]{:S(2)}) copy-start(bf16[1,128,2048]{2,1,0:T(8,128)(2,1)} %reduce-scatter.7.cloned.1.call-done) | copy-start | bytes 1572868
  715.0 57.8 %copy-start.23 = (bf16[1,128,2048]{2,1,0:T(8,128)(2,1)S(1)}, bf16[1,128,2048]{2,1,0:T(8,128)(2,1)}, u32[]{:S(2)}) copy-start(bf16[1,128,2048]{2,1,0:T(8,128)(2,1)} %param.14) | copy-start | bytes 1572868
  715.1 53.5 %all-to-all-start.2 = ((bf16[8,64,2048]{2,1,0:T(8,128)(2,1)}), bf16[8,64,2048]{2,1,0:T(8,128)(2,1)}, u32[]{:S(2)}, u32[]{:S(2)}) async-start(bf16[8,64,2048]{2,1,0:T(8,128)(2,1)} %bitcast.240), calls=%async_computation.7 | async-start | bytes 4194304 | tf_op jit(solution)/shard_map/all_to_all | solution.py:371
  768.6 106.3 %all-to-all-start.1 = ((bf16[8,64,1024]{2,1,0:T(8,128)(2,1)}), bf16[8,64,1024]{2,1,0:T(8,128)(2,1)}, u32[]{:S(2)}, u32[]{:S(2)}) async-start(bf16[8,64,1024]{2,1,0:T(8,128)(2,1)} %bitcast.230), calls=%async_computation.5 | async-start | bytes 2097152 | tf_op jit(solution)/shard_map/all_to_all | solution.py:371
  (38 other events, 140.1 us)
Sparse Core Ops, SparseCore 0:
  19.4 46.5 all-gather.7
  67.6 46.8 all-gather.9
  116.4 86.2 all-gather.13
  204.7 46.8 all-gather.11
  253.9 86.1 all-gather.15
  342.3 52.5 all-gather.17
  403.3 49.8 reduce-scatter.6
  458.3 45.3 all-gather.19
  530.2 48.7 reduce-scatter.8
  581.9 84.7 reduce-scatter.14
  696.8 50.4 reduce-scatter.12
  750.0 52.5 reduce-scatter.16
  805.0 50.9 reduce-scatter.10

commit v2 on v1

--- a/solution.py
+++ b/solution.py
@@ -1,7 +1,12 @@
+import functools
+
 import jax
 import jax.numpy as jnp
 from jax import lax
+from jax.experimental import pallas as pl
+from jax.experimental.pallas import tpu as pltpu
 from jax.sharding import PartitionSpec as P
+
 
 HEAD = 128
 SLABS = 4
@@ -152,7 +157,7 @@
     )
     query_at = first_row + jnp.arange(piece_len, dtype=jnp.int32)
     allowed = visible(ids_low, ids_all, query_at, jnp.arange(pair_all.shape[1], dtype=jnp.int32))
-    masked, key_rows, value_rows = masked_scores(
+    masked, _, value_rows = masked_scores(
         query_low, pair_all, allowed, head_count, head_size
     )
     row_max = jnp.max(masked, -1, keepdims=True)
@@ -351,10 +356,12 @@
 
 
 def own_columns(matrix, groups, parts, index):
-    lead = matrix.shape[0]
     width = matrix.shape[1] // (groups * parts)
-    view = matrix.reshape(lead, groups, parts, width)
-    return lax.dynamic_index_in_dim(view, index, 2, False).reshape(lead, groups * width)
+    pieces = [
+        lax.dynamic_slice_in_dim(matrix, (group * parts + index) * width, width, 1)
+        for group in range(groups)
+    ]
+    return jnp.concatenate(pieces, 1) if groups > 1 else pieces[0]
 
 
 def gather_seq(piece):
@@ -365,12 +372,249 @@
     return lax.psum_scatter(partial, "seq", scatter_dimension=1, tiled=True)
 
 
-def rows_home(partial, seq_count):
-    summed = lax.psum_scatter(partial, "dp", scatter_dimension=0, tiled=True)
+def swap(value, axis, flip):
+    return lax.ppermute(value, axis, [(at, at ^ flip) for at in range(lax.axis_size(axis))])
+
+
+def placed(pieces, index, axis, count):
+    width = pieces[0].shape[axis]
+    shape = list(pieces[0].shape)
+    shape[axis] = width * count
+    whole = jnp.zeros(shape, pieces[0].dtype)
+    for flip, piece in enumerate(pieces):
+        whole = lax.dynamic_update_slice_in_dim(whole, piece, (index ^ flip) * width, axis)
+    return whole
+
+
+def pieces_for(value, name, split_axis):
+    count, index = lax.axis_size(name), lax.axis_index(name)
+    width = value.shape[split_axis] // count
+    return [
+        lax.dynamic_slice_in_dim(value, (index ^ flip) * width, width, split_axis)
+        for flip in range(count)
+    ]
+
+
+def swapped(pieces, name):
+    return [swap(piece, name, flip) if flip else piece for flip, piece in enumerate(pieces)]
+
+
+def exchanged(value, name, split_axis):
+    return swapped(pieces_for(value, name, split_axis), name)
+
+
+def gather_dp(piece):
+    half = piece.shape[0] // 2
+    first, second = swap(piece, "dp", 1), swap(piece, "dp", 2)
+    top, bottom = swap(first[:half], "dp", 2), swap(second[half:], "dp", 1)
+    index = lax.axis_index("dp")
+    width = piece.shape[0]
+    whole = placed([piece], index, 0, 4)
+    for part, place in (
+        (first, (index ^ 1) * width),
+        (second, (index ^ 2) * width),
+        (top, (index ^ 3) * width),
+        (bottom, (index ^ 3) * width + half),
+    ):
+        whole = lax.dynamic_update_slice_in_dim(whole, part, place, 0)
+    return whole
+
+
+def sum_dp(sent, kept):
+    got = swap(sent[0], "dp", 1), swap(sent[1], "dp", 2)
+    wide = [(kept[at].astype(jnp.float32) + got[at].astype(jnp.float32)) for at in range(2)]
+    onward = [side[1].astype(jnp.bfloat16) for side in wide]
+    last = swap(onward[0], "dp", 2), swap(onward[1], "dp", 1)
+    return jnp.concatenate(
+        [wide[at][0] + last[at].astype(jnp.float32) for at in range(2)], 0
+    )
+
+
+def shares_for(partial):
+    index = lax.axis_index("dp")
+    width = partial.shape[0] // 4
+    half = width // 2
+
+    def part(flip, side):
+        return lax.dynamic_slice_in_dim(partial, (index ^ flip) * width + side * half, half, 0)
+
+    sent = [jnp.stack([part(1, 0), part(3, 0)]), jnp.stack([part(2, 1), part(3, 1)])]
+    kept = [jnp.stack([part(0, 0), part(2, 0)]), jnp.stack([part(0, 1), part(1, 1)])]
+    return sent, kept
+
+
+def total_seq(value):
+    flip = 1
+    while flip < lax.axis_size("seq"):
+        value = value + swap(value, "seq", flip)
+        flip *= 2
+    return value
+
+
+def share_of_total(rows):
+    for name in ("dp", "seq"):
+        flip = lax.axis_size(name) // 2
+        while flip:
+            halves = rows.reshape(2, rows.shape[0] // 2, rows.shape[1])
+            side = lax.axis_index(name) // flip % 2
+            kept = lax.dynamic_index_in_dim(halves, side, 0, False)
+            sent = lax.dynamic_index_in_dim(halves, 1 - side, 0, False)
+            rows = kept + swap(sent, name, flip)
+            flip //= 2
+    return rows[0]
+
+
+def rows_home(summed, seq_count):
     lead, width = summed.shape
     return lax.all_to_all(
         summed.reshape(seq_count, lead // seq_count, width), "seq", split_axis=0, concat_axis=0
-    )
+    ).astype(jnp.float32)
+
+
+QUERY_BLOCK = 256
+
+
+def attention_masks(ids_col, ids_row, block, width, start):
+    rows = start + lax.broadcasted_iota(jnp.int32, (block, width), 0)
+    columns = lax.broadcasted_iota(jnp.int32, (block, width), 1)
+    return (columns <= rows) & (ids_col[start : start + block] == ids_row[:, :width])
+
+
+def attend_kernel(
+    q_ref, k_ref, v_ref, qinv_ref, kinv_ref, cos_ref, sin_ref, gq_ref, gk_ref, col_ref, row_ref,
+    qlow_ref, klow_ref, vlow_ref, mixed_ref, total_ref, *, scale
+):
+    low = jnp.bfloat16
+    half = q_ref.shape[-1] // 2
+    cosine, sine_part = cos_ref[...], sin_ref[...]
+
+    def rotated(ref, inv_ref, gain_ref):
+        value = ref[0] * inv_ref[0] * gain_ref[...]
+        return (value * cosine + pltpu.roll(value, half, 1) * sine_part).astype(low)
+
+    qlow_ref[0] = rotated(q_ref, qinv_ref, gq_ref)
+    klow_ref[0] = rotated(k_ref, kinv_ref, gk_ref)
+    vlow_ref[0] = v_ref[0].astype(low)
+    length = q_ref.shape[1]
+    block = min(QUERY_BLOCK, length)
+    ids_col, ids_row = col_ref[0], row_ref[0]
+    for start in range(0, length, block):
+        width = start + block
+        scores = lax.dot_general(
+            qlow_ref[0, start:width], klow_ref[0, :width], (((1,), (1,)), ((), ())),
+            preferred_element_type=jnp.float32,
+        ) * scale
+        allowed = attention_masks(ids_col, ids_row, block, width, start)
+        masked = jnp.where(allowed, scores, -1e30)
+        row_max = jnp.max(masked, -1, keepdims=True)
+        log_total = jnp.log(jnp.sum(jnp.exp(masked - row_max), -1, keepdims=True)) + row_max
+        total_ref[0, 0, start:width] = log_total
+        probs = jnp.exp(masked - log_total).astype(low)
+        mixed_ref[0, start:width] = jnp.dot(
+            probs, vlow_ref[0, :width], preferred_element_type=jnp.float32
+        ).astype(low)
+
+
+def attend_back_kernel(
+    q_ref, k_ref, qinv_ref, kinv_ref, cos_ref, sin_ref, gq_ref, gk_ref, col_ref, row_ref,
+    qlow_ref, klow_ref, vlow_ref, total_ref, dmixed_ref,
+    dq_ref, dk_ref, dv_ref, dots_ref, gains_ref, key_acc, value_acc, query_acc, *, scale
+):
+    low = jnp.bfloat16
+    half = q_ref.shape[-1] // 2
+    length = q_ref.shape[1]
+    block = min(QUERY_BLOCK, length)
+    ids_col, ids_row = col_ref[0], row_ref[0]
+    turned = (((0,), (0,)), ((), ()))
+    across = (((1,), (1,)), ((), ()))
+    key_acc[...] = jnp.zeros_like(key_acc)
+    value_acc[...] = jnp.zeros_like(value_acc)
+    for start in range(0, length, block):
+        width = start + block
+        query = qlow_ref[0, start:width]
+        d_mixed = dmixed_ref[0, start:width]
+        keys = klow_ref[0, :width]
+        scores = lax.dot_general(query, keys, across, preferred_element_type=jnp.float32) * scale
+        allowed = attention_masks(ids_col, ids_row, block, width, start)
+        probs = jnp.exp(jnp.where(allowed, scores, -1e30) - total_ref[0, 0, start:width])
+        d_probs = lax.dot_general(
+            d_mixed, vlow_ref[0, :width], across, preferred_element_type=jnp.float32
+        )
+        row_dot = jnp.sum(probs * d_probs, -1, keepdims=True)
+        d_scores = (probs * (d_probs - row_dot)).astype(low)
+        query_acc[start:width] = jnp.dot(d_scores, keys, preferred_element_type=jnp.float32)
+        key_acc[:width] += lax.dot_general(d_scores, query, turned, preferred_element_type=jnp.float32)
+        value_acc[:width] += lax.dot_general(
+            probs.astype(low), d_mixed, turned, preferred_element_type=jnp.float32
+        )
+    dv_ref[0] = value_acc[...].astype(low)
+    cosine, sine_part = cos_ref[...], sin_ref[...]
+
+    def turned_back(acc, ref, inv_ref, gain_ref, out_ref, at):
+        value = (acc[...] * scale).astype(low).astype(jnp.float32)
+        value = value * cosine - pltpu.roll(value, half, 1) * sine_part
+        unit = ref[0] * inv_ref[0]
+        gains_ref[0, at : at + 1] = jnp.sum(value * unit, 0, keepdims=True)
+        value = value * gain_ref[...]
+        out_ref[0] = value
+        dots_ref[0, 0, :, at : at + 1] = jnp.sum(value * unit, -1, keepdims=True)
+
+    turned_back(query_acc, q_ref, qinv_ref, gq_ref, dq_ref, 0)
+    turned_back(key_acc, k_ref, kinv_ref, gk_ref, dk_ref, 1)
+
+
+def attention_specs(length, heads, head_size):
+    wide = lambda at: pl.BlockSpec((1, length, head_size), lambda r, h, at=at: (r, 0, at * heads + h))
+    thin = pl.BlockSpec((1, length, 1), lambda r, h: (r, 0, 0))
+    table = pl.BlockSpec((length, head_size), lambda r, h: (0, 0))
+    gain = pl.BlockSpec((1, head_size), lambda r, h: (0, h))
+    flat = pl.BlockSpec((1, 1, length), lambda r, h: (r, 0, 0))
+    total = pl.BlockSpec((1, 1, length, 1), lambda r, h: (r, h, 0, 0))
+    return wide, thin, table, gain, flat, total
+
+
+def attend(qkv, inverses, tables, gains, ids, head_size, scale):
+    rows, length, width = qkv.shape
+    heads = width // (3 * head_size)
+    wide, thin, table, gain, flat, total = attention_specs(length, heads, head_size)
+    narrow = jax.ShapeDtypeStruct((rows, length, heads * head_size), jnp.bfloat16)
+    return pl.pallas_call(
+        functools.partial(attend_kernel, scale=scale),
+        grid=(rows, heads),
+        in_specs=[wide(0), wide(1), wide(2), thin, thin, table, table, gain, gain, thin, flat],
+        out_specs=[wide(0), wide(0), wide(0), wide(0), total],
+        out_shape=[narrow] * 4 + [jax.ShapeDtypeStruct((rows, heads, length, 1), jnp.float32)],
+        name="attend",
+    )(qkv, qkv, qkv, *inverses, *tables, *gains, ids[:, :, None], ids[:, None, :])
+
+
+def attend_back(qkv, inverses, tables, gains, ids, kept, d_mixed, head_size, scale):
+    rows, length, width = qkv.shape
+    heads = width // (3 * head_size)
+    wide, thin, table, gain, flat, total = attention_specs(length, heads, head_size)
+    shape = (rows, length, heads * head_size)
+    return pl.pallas_call(
+        functools.partial(attend_back_kernel, scale=scale),
+        grid=(rows, heads),
+        in_specs=[wide(0), wide(1), thin, thin, table, table, gain, gain, thin, flat]
+        + [wide(0), wide(0), wide(0), total, wide(0)],
+        out_specs=[
+            wide(0),
+            wide(0),
+            wide(0),
+            pl.BlockSpec((1, 1, length, 2), lambda r, h: (r, h, 0, 0)),
+            pl.BlockSpec((1, 2, head_size), lambda r, h: (r, 0, h)),
+        ],
+        out_shape=[
+            jax.ShapeDtypeStruct(shape, jnp.float32),
+            jax.ShapeDtypeStruct(shape, jnp.float32),
+            jax.ShapeDtypeStruct(shape, jnp.bfloat16),
+            jax.ShapeDtypeStruct((rows, heads, length, 2), jnp.float32),
+            jax.ShapeDtypeStruct((rows, 2, heads * head_size), jnp.float32),
+        ],
+        scratch_shapes=[pltpu.VMEM((length, head_size), jnp.float32)] * 3,
+        name="attend_back",
+    )(qkv, qkv, *inverses, *tables, *gains, ids[:, :, None], ids[:, None, :], *kept, d_mixed)
 
 
 def shards_by_feature(
@@ -400,30 +644,29 @@
     all_count = row_count * row_len
     tok_count = row_count * piece_len
     own_features = feature_count // seq_count
-    own_heads = own_features // head_size
     own_hidden = w_gate.shape[1] // seq_count
     low = jnp.bfloat16
-
-    def gather_dp(piece):
-        return lax.all_gather(piece, "dp", axis=0, tiled=True)
 
     def own_piece(tensor):
         view = tensor.reshape(row_count, row_len, -1)
         return lax.dynamic_slice_in_dim(view, seq_at * piece_len, piece_len, 1).reshape(tok_count, -1)
 
-    w_qkv = gather_dp(
-        jnp.concatenate([own_columns(w, 1, seq_count, seq_at) for w in (w_query, w_key, w_value)], 1)
-    )
+    w_qkv = gather_dp(jnp.concatenate([own_columns(w, 1, seq_count, seq_at) for w in (w_query, w_key, w_value)], 1))
     tokens_all = gather_seq(tokens).reshape(all_count, model_width)
-    ids_all = gather_seq(doc_ids)
-    wo_full = gather_dp(w_out)
-    w_hidden = gather_dp(
-        jnp.concatenate([own_columns(w, dp_count, seq_count, seq_at) for w in (w_gate, w_up)], 1)
-    )
+    ids_all = total_seq(
+        lax.dynamic_update_slice_in_dim(
+            jnp.zeros((row_count, row_len), jnp.int32), doc_ids, seq_at * piece_len, 1
+        )
+    )
+    core = seq_at % 2
+    half = model_width // 2
+    wo_half = gather_dp(lax.dynamic_slice_in_dim(w_out, core * half, half, 1))
+    wo_full = placed([wo_half, swap(wo_half, "seq", 1)], core, 1, 2)
+    w_hidden = gather_dp(jnp.concatenate([own_columns(w, dp_count, seq_count, seq_at) for w in (w_gate, w_up)], 1))
     w_back = gather_dp(
         lax.dynamic_slice_in_dim(
             w_down, seq_at * (own_hidden // dp_count), own_hidden // dp_count, 0
-        )
+        ),
     )
     gain_query = lax.dynamic_slice_in_dim(g_query, seq_at * own_features, own_features).astype(jnp.float32)
     gain_key = lax.dynamic_slice_in_dim(g_key, seq_at * own_features, own_features).astype(jnp.float32)
@@ -433,28 +676,17 @@
     qkv = jnp.dot(tokens_all, w_qkv, preferred_element_type=jnp.float32)
     query_pre = qkv[:, :own_features]
     key_pre = qkv[:, own_features : 2 * own_features]
-    value_low = qkv[:, 2 * own_features :].astype(low).reshape(row_count, row_len, own_heads, head_size)
     squares = jnp.stack([jnp.sum(query_pre * query_pre, -1), jnp.sum(key_pre * key_pre, -1)])
-    inverse = lax.rsqrt(lax.psum(squares, "seq") / feature_count + eps)
-    query_inv, key_inv = inverse[0][:, None], inverse[1][:, None]
-    query_unit = query_pre * query_inv
-    key_unit = key_pre * key_inv
-    positions = jnp.tile(jnp.arange(row_len, dtype=jnp.int32), row_count)
-    cosine, sine_part = rotation(positions, head_size)
-    heads = (all_count, own_heads, head_size)
-    split = (row_count, row_len, own_heads, head_size)
-    query_low = rotate((query_unit * gain_query).reshape(heads), cosine, sine_part).astype(low).reshape(split)
-    key_low = rotate((key_unit * gain_key).reshape(heads), cosine, sine_part).astype(low).reshape(split)
-    at = jnp.arange(row_len, dtype=jnp.int32)
-    allowed = visible(ids_all, ids_all, at, at)
-    scores = jnp.einsum("rche,rlhe->rhcl", query_low, key_low, preferred_element_type=jnp.float32) * scale
-    masked = jnp.where(allowed, scores, -1e30)
-    row_max = jnp.max(masked, -1, keepdims=True)
-    log_total = jnp.log(jnp.sum(jnp.exp(masked - row_max), -1, keepdims=True)) + row_max
-    probs = jnp.exp(masked - log_total)
-    probs_low = probs.astype(low)
-    mixed = jnp.einsum("rhcl,rlhe->rche", probs_low, value_low, preferred_element_type=jnp.float32)
-    mixed_low = mixed.astype(low).reshape(all_count, own_features)
+    cosine, sine_part = rotation(jnp.arange(row_len, dtype=jnp.int32), head_size)
+    tables = jnp.concatenate([cosine, cosine], 1), jnp.concatenate([-sine_part, sine_part], 1)
+    inverse = lax.rsqrt(total_seq(squares) / feature_count + eps)
+    inverses = [inverse[at].reshape(row_count, row_len, 1) for at in range(2)]
+    norm_gains = gain_query[None, :], gain_key[None, :]
+    qkv_rows = qkv.reshape(row_count, row_len, 3 * own_features)
+    *kept, mixed_low, log_total = attend(
+        qkv_rows, inverses, tables, norm_gains, ids_all, head_size, scale
+    )
+    mixed_low = mixed_low.reshape(all_count, own_features)
     mixed_all = lax.all_gather(mixed_low, "seq", axis=1, tiled=True)
     attn_out = jnp.dot(mixed_all, wo_full, preferred_element_type=jnp.float32)
     attn_inv_all = inverse_rms(attn_out)
@@ -492,60 +724,50 @@
     d_up = (d_inner * active).astype(low)
     d_gate_up = jnp.concatenate([d_gate, d_up], 1)
     d_hidden_part = jnp.einsum("nf,df->nd", d_gate_up, w_hidden, preferred_element_type=jnp.float32).astype(low)
-    d_hidden = grad_out + scatter_seq(d_hidden_part.reshape(row_count, row_len, model_width)).astype(
-        jnp.float32
-    ).reshape(tok_count, model_width)
+    d_hidden_sum = scatter_seq(d_hidden_part.reshape(row_count, row_len, model_width))
+    down_part = jnp.einsum("nf,nd->fd", inner_low, d_branch_all, preferred_element_type=jnp.float32).astype(low)
+    hidden_part = jnp.einsum("nd,nf->df", hidden_low, d_gate_up, preferred_element_type=jnp.float32).astype(low)
+    down_grad = sum_dp(*shares_for(down_part))
+    hidden_own = sum_dp(*shares_for(hidden_part)).astype(low)
+    d_hidden = grad_out + d_hidden_sum.astype(jnp.float32).reshape(tok_count, model_width)
 
     attn_gain_term = jnp.sum(d_hidden * attn_unit, 0)
     d_attn = norm_back(d_hidden * gain_attn, attn_unit, attn_inv).astype(low)
     d_mixed = jnp.einsum("nd,fd->nf", d_attn, wo_full, preferred_element_type=jnp.float32).astype(low)
-    both = jnp.concatenate(
-        [
-            d_mixed.reshape(row_count, piece_len, seq_count, own_features),
-            d_attn.reshape(row_count, piece_len, seq_count, model_width // seq_count),
-        ],
-        -1,
-    )
-    both = lax.all_to_all(both, "seq", split_axis=2, concat_axis=1, tiled=True).reshape(all_count, -1)
-    d_mixed = both[:, :own_features].reshape(split)
-    d_attn_own = both[:, own_features:]
-
-    down_part = jnp.einsum("nf,nd->fd", inner_low, d_branch_all, preferred_element_type=jnp.float32).astype(low)
-    down_grad = lax.psum_scatter(down_part, "dp", scatter_dimension=0, tiled=True).astype(jnp.float32)
-    hidden_part = jnp.einsum("nd,nf->df", hidden_low, d_gate_up, preferred_element_type=jnp.float32).astype(low)
-    hidden_home = rows_home(hidden_part, seq_count).astype(jnp.float32)
-    home_rows = hidden_home.shape[1]
+    d_mixed = placed(
+        exchanged(d_mixed.reshape(row_count, piece_len, feature_count), "seq", 2), seq_at, 1, seq_count
+    )
+    d_attn_own = placed(
+        exchanged(d_attn.reshape(row_count, piece_len, model_width), "seq", 2), seq_at, 1, seq_count
+    ).reshape(all_count, -1)
+
+    out_part = jnp.einsum("nf,nd->fd", mixed_all, d_attn_own, preferred_element_type=jnp.float32).astype(low)
+    out_own = sum_dp(*shares_for(out_part)).astype(low)
+    home = rows_home(jnp.concatenate([hidden_own, out_own], 1), seq_count)
+    home_rows = home.shape[1]
+    out_grad = home[..., 2 * own_hidden :].transpose(1, 0, 2).reshape(home_rows, feature_count)
     hidden_home = (
-        hidden_home.reshape(seq_count, home_rows, 2, dp_count, own_hidden // dp_count)
+        home[..., : 2 * own_hidden]
+        .reshape(seq_count, home_rows, 2, dp_count, own_hidden // dp_count)
         .transpose(2, 1, 3, 0, 4)
         .reshape(2, home_rows, own_hidden * seq_count)
     )
     gate_grad, up_grad = hidden_home[0], hidden_home[1]
 
-    d_probs = jnp.einsum("rche,rlhe->rhcl", d_mixed, value_low, preferred_element_type=jnp.float32)
-    row_dot = jnp.sum(probs * d_probs, -1, keepdims=True)
-    d_scores = (probs * (d_probs - row_dot)).astype(low)
-    d_query = (
-        jnp.einsum("rhcl,rlhe->rche", d_scores, key_low, preferred_element_type=jnp.float32) * scale
-    ).astype(low)
-    d_key = (
-        jnp.einsum("rhcl,rche->rlhe", d_scores, query_low, preferred_element_type=jnp.float32) * scale
-    ).astype(low)
-    d_value = (
-        jnp.einsum("rhcl,rche->rlhe", probs_low, d_mixed, preferred_element_type=jnp.float32)
-        .astype(low)
-        .reshape(all_count, own_features)
-    )
-    dq_norm = unrotate(d_query.reshape(heads).astype(jnp.float32), cosine, sine_part).reshape(all_count, own_features)
-    dk_norm = unrotate(d_key.reshape(heads).astype(jnp.float32), cosine, sine_part).reshape(all_count, own_features)
-    query_gain_term = jnp.sum(dq_norm * query_unit, 0)
-    key_gain_term = jnp.sum(dk_norm * key_unit, 0)
-    dq_gained = dq_norm * gain_query
-    dk_gained = dk_norm * gain_key
-    dots = jnp.stack([jnp.sum(dq_gained * query_unit, -1), jnp.sum(dk_gained * key_unit, -1)])
-    means = lax.psum(dots, "seq") / feature_count
-    dq_pre = (query_inv * (dq_gained - query_unit * means[0][:, None])).astype(low)
-    dk_pre = (key_inv * (dk_gained - key_unit * means[1][:, None])).astype(low)
+    dq_gained, dk_gained, d_value, dots, gain_terms = attend_back(
+        qkv_rows, inverses, tables, norm_gains, ids_all, (*kept, log_total), d_mixed, head_size, scale
+    )
+    query_gain_term, key_gain_term = jnp.sum(gain_terms, 0)
+    means = total_seq(jnp.sum(dots, 1).reshape(all_count, 2).T) / feature_count
+
+    def norm_back_wide(gained, pre, at):
+        inv = inverse[at][:, None]
+        gained = gained.reshape(all_count, own_features)
+        return (inv * (gained - pre * inv * means[at][:, None])).astype(low)
+
+    dq_pre = norm_back_wide(dq_gained, query_pre, 0)
+    dk_pre = norm_back_wide(dk_gained, key_pre, 1)
+    d_value = d_value.reshape(all_count, own_features)
     d_qkv = jnp.concatenate([dq_pre, dk_pre, d_value], 1)
     d_tokens_part = jnp.einsum("nf,df->nd", d_qkv, w_qkv, preferred_element_type=jnp.float32).astype(low)
     d_tokens = d_hidden + scatter_seq(d_tokens_part.reshape(row_count, row_len, model_width)).astype(
@@ -553,13 +775,11 @@
     ).reshape(tok_count, model_width)
 
     qkv_part = jnp.einsum("nd,nf->df", tokens_all, d_qkv, preferred_element_type=jnp.float32).astype(low)
-    out_part = jnp.einsum("nf,nd->fd", mixed_all, d_attn_own, preferred_element_type=jnp.float32).astype(low)
-    attn_home = rows_home(jnp.concatenate([qkv_part, out_part], 1), seq_count).astype(jnp.float32)
-    attn_rows = attn_home.shape[1]
+    attn_home = rows_home(sum_dp(*shares_for(qkv_part)).astype(low), seq_count)
     attn_home = (
-        attn_home.reshape(seq_count, attn_rows, 4, own_features)
+        attn_home.reshape(seq_count, home_rows, 3, own_features)
         .transpose(2, 1, 0, 3)
-        .reshape(4, attn_rows, feature_count)
+        .reshape(3, home_rows, feature_count)
     )
     zeros = jnp.zeros((feature_count,), jnp.float32)
     gains = jnp.stack(
@@ -570,18 +790,17 @@
             ffn_gain_term,
         ]
     )
-    gains = lax.psum(gains, ("dp", "seq"))
     share = feature_count // (dp_count * seq_count)
-    gains = lax.dynamic_slice_in_dim(
-        gains, (lax.axis_index("dp") * seq_count + seq_at) * share, share, 1
-    )
+    gains = share_of_total(
+        gains.reshape(4, dp_count * seq_count, share).transpose(1, 0, 2).reshape(dp_count * seq_count, 4 * share)
+    ).reshape(4, share)
     return (
         result,
         d_tokens.reshape(row_count, piece_len, model_width),
         attn_home[0],
         attn_home[1],
         attn_home[2],
-        attn_home[3],
+        out_grad,
         gate_grad,
         up_grad,
         down_grad,
@@ -593,9 +812,9 @@
 
 
 def shards(tokens, doc_ids, cotangent, w_query, *rest):
-    whole_heads = w_query.shape[1] // HEAD % lax.axis_size("seq") == 0
-    body = shards_by_feature if whole_heads else shards_by_slab
-    return body(tokens, doc_ids, cotangent, w_query, *rest)
+    if w_query.shape[1] // HEAD % lax.axis_size("seq"):
+        return shards_by_slab(tokens, doc_ids, cotangent, w_query, *rest)
+    return shards_by_feature(tokens, doc_ids, cotangent, w_query, *rest)
 
 
 def solution(mesh):

time: 898 us -> 893 us (level)
  blocking collectives: 115 us -> 0 us
  starting transfers between devices: 10.3 us -> 77.7 us
  local copies, waits for them, and re-layouts: 111 us -> 142 us
  matrix products: 131 us -> 102 us
  Pallas kernels: 0 us -> 24.8 us
  other arithmetic: 51.4 us -> 63.2 us
    ppermute x0 -> x61, waiting for transfers between devices: none -> 333 us  [swap(): lax.ppermute(value, axis, [(at, at ^ flip) for at in range(lax.axis_size(...]
    all_gather x4 -> x0, waiting for transfers between devices: 144 us -> none  [gather_dp(): return lax.all_gather(piece, 'dp', axis=0, tiled=True)]
    psum x3 -> x0, blocking collectives: 71.9 us -> none  [the longest x1 41 us: shards_by_feature(): gains = lax.psum(gains, ('dp', 'seq'))]
    ppermute x0 -> x61, starting transfers between devices: none -> 69 us  [swap(): lax.ppermute(value, axis, [(at, at ^ flip) for at in range(lax.axis_size(...]
    reduce_scatter x3 -> x0, waiting for transfers between devices: 56.3 us -> none  [the longest x1 28.6 us: shards_by_feature(): lax.psum_scatter(down_part, 'dp', scatter_dimension=0, tiled=True)]
    all_gather x1, waiting for transfers between devices: 48.9 us -> 0.01 us  [shards_by_feature(): mixed_all = lax.all_gather(mixed_low, 'seq', axis=1, tiled=True)]
    reduce_scatter x3, waiting for transfers between devices: 92.6 us -> 46.2 us  [scatter_seq(): return lax.psum_scatter(partial, 'seq', scatter_dimension=1, tiled=True)]
    all_gather x2, waiting for transfers between devices: 93.9 us -> 57.1 us  [gather_seq(): return lax.all_gather(piece, 'seq', axis=1, tiled=True)]
  transfers between devices with their start and end apart: 15 -> 69, of which waited for: 13 -> 36; matrix products, arithmetic and copies ran while one was open for 25% -> 25% of each run, Pallas kernels for 0% -> 2%
where the time goes in v2:
time: 893 us; the launch traced here: 884 us
  waiting for transfers between devices  459 us (51%)
  local copies, waits for them, and re-layouts  142 us (16%)
  matrix products  102 us (11%)
  starting transfers between devices  77.7 us (9%)
  other arithmetic  63.2 us (7%)
  Pallas kernels  24.8 us (3%)
  between operations  15.7 us (2%)
    ppermute x61, waiting for transfers between devices, swap(): lax.ppermute(value, axis, [(at, at ^ flip) for at in range(lax.axis_size(...  333 us
    ppermute x61, starting transfers between devices, swap(): lax.ppermute(value, axis, [(at, at ^ flip) for at in range(lax.axis_size(...  69 us
    all_gather x2, waiting for transfers between devices, gather_seq(): return lax.all_gather(piece, 'seq', axis=1, tiled=True)  57.1 us
    reduce_scatter x3, waiting for transfers between devices, scatter_seq(): return lax.psum_scatter(partial, 'seq', scatter_dimension=1, tiled=True)  46.2 us
    unnamed x93, local copies, waits for them, and re-layouts  29 us
    all_to_all x2, waiting for transfers between devices, rows_home(): lax.all_to_all(summed.reshape(seq_count, lead // seq_count, width), 'seq'...  21.7 us
    dynamic_update_slice x16, local copies, waits for them, and re-layouts, gather_dp(): whole = lax.dynamic_update_slice_in_dim(whole, part, place, 0)  18.2 us
  transfers between devices with their start and end apart: 69, of which 36 were waited for; matrix products, arithmetic and copies ran while one was open for 25% of the time, Pallas kernels for 2%

profile of v2, /device:TPU:0, one launch (start us, length us, event | category | flops | bytes accessed | tf_op | source)
XLA Modules:
  0.0 884.3 jit_solution(10016141652290574083)
XLA Ops:
  18.9 13.1 %collective-permute-done = bf16[512,768]{1,0:T(8,128)(2,1)} collective-permute-done((bf16[512,768]{1,0:T(8,128)(2,1)}, bf16[512,768]{1,0:T(8,128)(2,1)}, u32[]{:S(2)}, u32[]{:S(2)}) %collective-permute-start) | collective-permute-done | bytes 786464 | tf_op jit(solution)/shard_map/ppermute | solution.py:376
  47.3 11.9 %all-gather.5.cloned.1.call-done = bf16[1,1024,2048]{2,1,0:T(8,128)(2,1)} async-done(((bf16[1,128,2048]{2,1,0:T(8,128)(2,1)}), bf16[1,1024,2048]{2,1,0:T(8,128)(2,1)}) %all-gather.5.cloned.1.call-update) | async-done | bytes 4194320 | tf_op jit(solution)/shard_map/all_gather | solution.py:368
  74.8 11.9 %collective-permute-done.5 = f32[2,1024]{0,1:T(8,128)S(1)} collective-permute-done((f32[2,1024]{0,1:T(8,128)S(1)}, f32[2,1024]{0,1:T(8,128)S(1)}, u32[]{:S(2)}, u32[]{:S(2)}) %collective-permute-start.5) | collective-permute-done | bytes 8224 | tf_op jit(solution)/shard_map/ppermute | solution.py:376
  90.7 22.2 %collective-permute-done.6 = f32[2,1024]{0,1:T(8,128)} collective-permute-done((f32[2,1024]{0,1:T(8,128)}, f32[2,1024]{0,1:T(8,128)}, u32[]{:S(2)}, u32[]{:S(2)}) %collective-permute-start.6) | collective-permute-done | bytes 8224 | tf_op jit(solution)/shard_map/ppermute | solution.py:376
  116.0 10.3 %attend.1 = (bf16[1,1024,256]{2,1,0:T(8,128)(2,1)}, bf16[1,1024,256]{2,1,0:T(8,128)(2,1)}, bf16[1,1024,256]{2,1,0:T(8,128)(2,1)}, bf16[1,1024,256]{2,1,0:T(8,128)(2,1)}, f32[1,2,1024,1]{3,2,1,0:T(8,128)}) custom-call(f32[1,1024,768]{2,1,0:T(8,128)} %bitcast.379, f32[1,1024,768]{2,1,0:T(8,128)} %bitcast.380, f32[1,1024,768]{2,1,0:T(8,128)} %bitcast.381, ...), custom_call_target="tpu_custom_call" | custom-call | tf_op jit(solution)/shard_map/attend/pallas_call | solution.py:581
  138.7 17.0 %collective-permute-done.10 = bf16[512,1024]{1,0:T(8,128)(2,1)S(1)} collective-permute-done((bf16[512,1024]{1,0:T(8,128)(2,1)S(1)}, bf16[512,1024]{1,0:T(8,128)(2,1)S(1)}, u32[]{:S(2)}, u32[]{:S(2)}) %collective-permute-start.10) | collective-permute-done | bytes 1048608 | tf_op jit(solution)/shard_map/ppermute | solution.py:376
  193.1 53.8 %collective-permute-done.19 = bf16[256,2048]{1,0:T(8,128)(2,1)S(1)} collective-permute-done((bf16[256,2048]{1,0:T(8,128)(2,1)}, bf16[256,2048]{1,0:T(8,128)(2,1)S(1)}, u32[]{:S(2)}, u32[]{:S(2)}) %collective-permute-start.19) | collective-permute-done | bytes 1048608 | tf_op jit(solution)/shard_map/ppermute | solution.py:376
  272.7 10.4 %collective-permute-done.17 = bf16[256,2048]{1,0:T(8,128)(2,1)S(1)} collective-permute-done((bf16[256,2048]{1,0:T(8,128)(2,1)S(1)}, bf16[256,2048]{1,0:T(8,128)(2,1)S(1)}, u32[]{:S(2)}, u32[]{:S(2)}) %collective-permute-start.17) | collective-permute-done | bytes 1048608 | tf_op jit(solution)/shard_map/ppermute | solution.py:376
  295.4 12.9 %multiply_reduce_fusion = (f32[1024]{0:T(1024)S(1)}, f32[1024,2048]{1,0:T(8,128)S(1)}) fusion(bf16[2048,2048]{1,0:T(8,128)(2,1)} %constant_dynamic-update-slice_fusion.19, bf16[1,1024,2048]{2,1,0:T(8,128)(2,1)} %all-gather.9.cloned.1.call-done), kind=kOutput, calls=%fused_computation.1 | convolution fusion | flops 8594127872 | bytes 20975616 | tf_op jit(solution)/shard_map/dot_general | solution.py:691
  313.4 12.8 %fusion.88 = f32[1024,2048]{1,0:T(8,128)S(1)} fusion(bf16[1024,2048]{1,0:T(8,128)(2,1)S(1)} %add_convert_fusion, bf16[2048,2048]{1,0:T(8,128)(2,1)} %constant_dynamic-update-slice_fusion.14), kind=kOutput, calls=%fused_computation.290 | convolution fusion | flops 8589934592 | bytes 20971520 | tf_op jit(solution)/shard_map/dot_general | solution.py:699
  339.8 46.2 %reduce-scatter.4.cloned.1.call-done = bf16[1,128,2048]{2,1,0:T(8,128)(2,1)} async-done(((bf16[1,1024,2048]{2,1,0:T(8,128)(2,1)}), bf16[1,128,2048]{2,1,0:T(8,128)(2,1)}) %reduce-scatter.4.cloned.1.call-update) | async-done | bytes 524304 | tf_op jit(solution)/shard_map/reduce_scatter | solution.py:372
  391.9 45.2 %all-gather.7.cloned.1.call-done = bf16[1,1024,2048]{2,1,0:T(8,128)(2,1)} async-done(((bf16[1,128,2048]{2,1,0:T(8,128)(2,1)}), bf16[1,1024,2048]{2,1,0:T(8,128)(2,1)}) %all-gather.7.cloned.1.call-update) | async-done | bytes 4194320 | tf_op jit(solution)/shard_map/all_gather | solution.py:368
  437.0 11.7 %multiply_convert_fusion.1 = (bf16[1024,1024]{1,0:T(8,128)(2,1)S(1)}, bf16[1024,1024]{1,0:T(8,128)(2,1)S(1)}) fusion(f32[1024,2048]{1,0:T(8,128)} %copy-done.7, bf16[1024,2048]{1,0:T(8,128)(2,1)} %constant_dynamic-update-slice_fusion.9, bf16[1,1024,2048]{2,1,0:T(8,128)(2,1)} %all-gather.7.cloned.1.call-done), kind=kOutput, calls=%fused_computation.21 | convolution fusion | flops 4308598784 | bytes 20971520 | tf_op jit(solution)/shard_map/nd,fd->nf/dot_general | solution.py:722
  450.0 12.7 %convert_bitcast_fusion.1 = bf16[1,1024,2048]{2,1,0:T(8,128)(2,1)} fusion(bf16[2048,2048]{1,0:T(8,128)(2,1)} %constant_dynamic-update-slice_fusion.14, bf16[1024,1024]{1,0:T(8,128)(2,1)S(1)} %get-tuple-element.48, bf16[1024,1024]{1,0:T(8,128)(2,1)S(1)} %get-tuple-element.47), kind=kOutput, calls=%fused_computation.19 | convolution fusion | flops 8600420352 | bytes 16777216 | tf_op jit(solution)/shard_map/nf,df->nd/dot_general | solution.py:726
  463.2 11.5 %convolution_convert_fusion = bf16[2048,2048]{1,0:T(8,128)(2,1)S(1)} fusion(bf16[1024,2048]{1,0:T(8,128)(2,1)} %copy-done.14, bf16[1024,1024]{1,0:T(8,128)(2,1)} %copy-done.40, bf16[1024,1024]{1,0:T(8,128)(2,1)S(1)} %get-tuple-element.47), kind=kOutput, calls=%fused_computation.2 | convolution fusion | flops 8602517504 | bytes 16777216 | tf_op jit(solution)/shard_map/nd,nf->df/dot_general | solution.py:729
  494.0 33.7 %collective-permute-done.39 = bf16[2,256,2048]{2,1,0:T(8,128)(2,1)} collective-permute-done((bf16[2,256,2048]{2,1,0:T(8,128)(2,1)}, bf16[2,256,2048]{2,1,0:T(8,128)(2,1)}, u32[]{:S(2)}, u32[]{:S(2)}) %collective-permute-start.39) | collective-permute-done | bytes 2097184 | tf_op jit(solution)/shard_map/ppermute | solution.py:376
  534.4 15.7 %collective-permute-done.54 = bf16[2,128,2048]{2,1,0:T(8,128)(2,1)S(1)} collective-permute-done((bf16[2,128,2048]{2,1,0:T(8,128)(2,1)S(1)}, bf16[2,128,2048]{2,1,0:T(8,128)(2,1)S(1)}, u32[]{:S(2)}, u32[]{:S(2)}) %collective-permute-start.54) | collective-permute-done | bytes 1048608 | tf_op jit(solution)/shard_map/ppermute | solution.py:376
  554.1 20.1 %collective-permute-done.40 = bf16[256,2048]{1,0:T(8,128)(2,1)S(1)} collective-permute-done((bf16[256,2048]{1,0:T(8,128)(2,1)S(1)}, bf16[256,2048]{1,0:T(8,128)(2,1)S(1)}, u32[]{:S(2)}, u32[]{:S(2)}) %collective-permute-start.40) | collective-permute-done | bytes 1048608 | tf_op jit(solution)/shard_map/ppermute | solution.py:376
  619.5 14.4 %attend_back.1 = (f32[1,1024,256]{2,1,0:T(8,128)}, f32[1,1024,256]{2,1,0:T(8,128)}, bf16[1,1024,256]{2,1,0:T(8,128)(2,1)}, f32[1,2,1024,2]{3,2,1,0:T(8,128)}, f32[1,2,256]{2,1,0:T(2,128)}) custom-call(f32[1,1024,768]{2,1,0:T(8,128)} %bitcast.382, f32[1,1024,768]{2,1,0:T(8,128)} %bitcast.383, f32[1,1024,1]{2,1,0:T(8,128)} %get-tuple-element.101.qinv_ref, ...), custom_call_target="tpu_custom_call" | custom-call | tf_op jit(solution)/shard_map/attend_back/pallas_call | solution.py:596
  659.8 9.6 %collective-permute-done.31 = f32[2,1024]{0,1:T(8,128)} collective-permute-done((f32[2,1024]{0,1:T(8,128)}, f32[2,1024]{0,1:T(8,128)}, u32[]{:S(2)}, u32[]{:S(2)}) %collective-permute-start.31) | collective-permute-done | bytes 8224 | tf_op jit(solution)/shard_map/ppermute | solution.py:376
  674.1 21.9 %collective-permute-done.32 = f32[2,1024]{0,1:T(8,128)S(1)} collective-permute-done((f32[2,1024]{0,1:T(8,128)S(1)}, f32[2,1024]{0,1:T(8,128)S(1)}, u32[]{:S(2)}, u32[]{:S(2)}) %collective-permute-start.32) | collective-permute-done | bytes 8224 | tf_op jit(solution)/shard_map/ppermute | solution.py:376
  712.9 8.5 collective-permute-done.35
  751.9 21.7 %all-to-all-done = bf16[8,64,768]{2,1,0:T(8,128)(2,1)S(1)} async-done(((bf16[8,64,768]{2,1,0:T(8,128)(2,1)}), bf16[8,64,768]{2,1,0:T(8,128)(2,1)S(1)}, u32[]{:S(2)}, u32[]{:S(2)}) %all-to-all-start) | async-done | bytes 786464 | tf_op jit(solution)/shard_map/all_to_all | solution.py:469
  788.3 44.8 %collective-permute-done.58 = f32[4,256]{1,0:T(4,128)S(1)} collective-permute-done((f32[4,256]{1,0:T(4,128)S(1)}, f32[4,256]{1,0:T(4,128)S(1)}, u32[]{:S(2)}, u32[]{:S(2)}) %collective-permute-start.58) | collective-permute-done | bytes 4128 | tf_op jit(solution)/shard_map/ppermute | solution.py:376
  (405 shorter events, 374.7 us)
Async XLA Ops:
  7.2 52.0 %all-gather.5.cloned.1.call-start = ((), (), s32[]{:S(2)}) async-start(), calls=%async_computation.5 | async-start | bytes 4718592 | tf_op jit(solution)/shard_map/all_gather | solution.py:368
  7.9 287.5 %all-gather.9.cloned.1.call-start = ((), (), s32[]{:S(2)}) async-start(), calls=%async_computation.10 | async-start | bytes 4718592 | tf_op jit(solution)/shard_map/all_gather | solution.py:690
  126.4 259.5 %reduce-scatter.4.cloned.1.call-start = ((), (), s32[]{:S(2)}) async-start(), calls=%async_computation.6 | async-start | bytes 4718592 | tf_op jit(solution)/shard_map/reduce_scatter | solution.py:372
  172.9 117.9 %collective-permute-start.14 = (bf16[2048,1024]{1,0:T(8,128)(2,1)}, bf16[2048,1024]{1,0:T(8,128)(2,1)}, u32[]{:S(2)}, u32[]{:S(2)}) collective-permute-start(bf16[2048,1024]{1,0:T(8,128)(2,1)} %constant_dynamic-update-slice_fusion.21), channel_id=1, source_target_pairs={{0,1},{1,0},{2,3},{3,2},{4,5},{5,4},{6,7},{7,6},{8,9},{9,8},{10,11... | collective-permute-start | bytes 12582920 | tf_op jit(solution)/shard_map/ppermute | solution.py:376
  176.3 77.1 %collective-permute-start.15 = (bf16[512,2048]{1,0:T(8,128)(2,1)}, bf16[512,2048]{1,0:T(8,128)(2,1)S(1)}, u32[]{:S(2)}, u32[]{:S(2)}) collective-permute-start(bf16[512,2048]{1,0:T(8,128)(2,1)} %dynamic-slice_dynamic-update-slice_fusion), channel_id=1, source_target_pairs={{0,8},{8,0},{16,24},{24,16},{1,9},{9,1},{17,25},{25,17},{2,10},{10... | collective-permute-start | bytes 6291464 | tf_op jit(solution)/shard_map/ppermute | solution.py:376
  177.7 86.7 %collective-permute-start.16 = (bf16[512,2048]{1,0:T(8,128)(2,1)}, bf16[512,2048]{1,0:T(8,128)(2,1)}, u32[]{:S(2)}, u32[]{:S(2)}) collective-permute-start(bf16[512,2048]{1,0:T(8,128)(2,1)} %dynamic-slice_dynamic-update-slice_fusion), channel_id=1, source_target_pairs={{0,16},{8,24},{16,0},{24,8},{1,17},{9,25},{17,1},{25,9},{2,18},{10... | collective-permute-start | bytes 6291464 | tf_op jit(solution)/shard_map/ppermute | solution.py:376
  183.4 63.5 %collective-permute-start.19 = (bf16[256,2048]{1,0:T(8,128)(2,1)}, bf16[256,2048]{1,0:T(8,128)(2,1)S(1)}, u32[]{:S(2)}, u32[]{:S(2)}) collective-permute-start(bf16[256,2048]{1,0:T(8,128)(2,1)} %get-tuple-element.44), channel_id=1, source_target_pairs={{0,8},{8,0},{16,24},{24,16},{1,9},{9,1},{17,25},{25,17},{2,10},{10... | collective-permute-start | bytes 3145736 | tf_op jit(solution)/shard_map/ppermute | solution.py:376
  183.9 64.3 %collective-permute-start.20 = (bf16[256,2048]{1,0:T(8,128)(2,1)}, bf16[256,2048]{1,0:T(8,128)(2,1)}, u32[]{:S(2)}, u32[]{:S(2)}) collective-permute-start(bf16[256,2048]{1,0:T(8,128)(2,1)} %get-tuple-element.44), channel_id=1, source_target_pairs={{0,16},{8,24},{16,0},{24,8},{1,17},{9,25},{17,1},{25,9},{2,18},{10... | collective-permute-start | bytes 3145736 | tf_op jit(solution)/shard_map/ppermute | solution.py:376
  339.0 98.0 %all-gather.7.cloned.1.call-start = ((), (), s32[]{:S(2)}) async-start(), calls=%async_computation.7 | async-start | bytes 4718592 | tf_op jit(solution)/shard_map/all_gather | solution.py:368
  391.6 184.8 %reduce-scatter.6.cloned.1.call-start = ((), (), s32[]{:S(2)}) async-start(), calls=%async_computation.8 | async-start | bytes 4718592 | tf_op jit(solution)/shard_map/reduce_scatter | solution.py:372
  462.7 412.1 %reduce-scatter.8.cloned.1.call-start = ((), (), s32[]{:S(2)}) async-start(), calls=%async_computation.9 | async-start | bytes 4718592 | tf_op jit(solution)/shard_map/reduce_scatter | solution.py:372
  478.9 48.8 %collective-permute-start.39 = (bf16[2,256,2048]{2,1,0:T(8,128)(2,1)}, bf16[2,256,2048]{2,1,0:T(8,128)(2,1)}, u32[]{:S(2)}, u32[]{:S(2)}) collective-permute-start(bf16[2,256,2048]{2,1,0:T(8,128)(2,1)} %pad_maximum_fusion.5), channel_id=1, source_target_pairs={{0,16},{8,24},{16,0},{24,8},{1,17},{9,25},{17,1},{25,9},{2,18},{10... | collective-permute-start | bytes 6291464 | tf_op jit(solution)/shard_map/ppermute | solution.py:376
  480.6 51.3 %collective-permute-start.37 = (bf16[2,256,2048]{2,1,0:T(8,128)(2,1)S(1)}, bf16[2,256,2048]{2,1,0:T(8,128)(2,1)S(1)}, u32[]{:S(2)}, u32[]{:S(2)}) collective-permute-start(bf16[2,256,2048]{2,1,0:T(8,128)(2,1)S(1)} %pad_maximum_fusion.4), channel_id=1, source_target_pairs={{0,8},{8,0},{16,24},{24,16},{1,9},{9,1},{17,25},{25,17},{2,10},{10... | collective-permute-start | bytes 6291464 | tf_op jit(solution)/shard_map/ppermute | solution.py:376
  491.0 59.1 %collective-permute-start.54 = (bf16[2,128,2048]{2,1,0:T(8,128)(2,1)S(1)}, bf16[2,128,2048]{2,1,0:T(8,128)(2,1)S(1)}, u32[]{:S(2)}, u32[]{:S(2)}) collective-permute-start(bf16[2,128,2048]{2,1,0:T(8,128)(2,1)S(1)} %pad_maximum_fusion.10), channel_id=1, source_target_pairs={{0,16},{8,24},{16,0},{24,8},{1,17},{9,25},{17,1},{25,9},{2,18},{10... | collective-permute-start | bytes 3145736 | tf_op jit(solution)/shard_map/ppermute | solution.py:376
  492.7 285.7 %collective-permute-start.52 = (bf16[2,128,2048]{2,1,0:T(8,128)(2,1)}, bf16[2,128,2048]{2,1,0:T(8,128)(2,1)}, u32[]{:S(2)}, u32[]{:S(2)}) collective-permute-start(bf16[2,128,2048]{2,1,0:T(8,128)(2,1)} %pad_maximum_fusion.9), channel_id=1, source_target_pairs={{0,8},{8,0},{16,24},{24,16},{1,9},{9,1},{17,25},{25,17},{2,10},{10... | collective-permute-start | bytes 3145736 | tf_op jit(solution)/shard_map/ppermute | solution.py:376
  530.4 43.8 %collective-permute-start.40 = (bf16[256,2048]{1,0:T(8,128)(2,1)S(1)}, bf16[256,2048]{1,0:T(8,128)(2,1)S(1)}, u32[]{:S(2)}, u32[]{:S(2)}) collective-permute-start(bf16[256,2048]{1,0:T(8,128)(2,1)S(1)} %fusion.44), channel_id=1, source_target_pairs={{0,8},{8,0},{16,24},{24,16},{1,9},{9,1},{17,25},{25,17},{2,10},{10... | collective-permute-start | bytes 3145736 | tf_op jit(solution)/shard_map/ppermute | solution.py:376
  532.8 41.6 %collective-permute-start.38 = (bf16[256,2048]{1,0:T(8,128)(2,1)S(1)}, bf16[256,2048]{1,0:T(8,128)(2,1)S(1)}, u32[]{:S(2)}, u32[]{:S(2)}) collective-permute-start(bf16[256,2048]{1,0:T(8,128)(2,1)S(1)} %fusion.43), channel_id=1, source_target_pairs={{0,16},{8,24},{16,0},{24,8},{1,17},{9,25},{17,1},{25,9},{2,18},{10... | collective-permute-start | bytes 3145736 | tf_op jit(solution)/shard_map/ppermute | solution.py:376
  552.6 234.2 %collective-permute-start.55 = (bf16[128,2048]{1,0:T(8,128)(2,1)}, bf16[128,2048]{1,0:T(8,128)(2,1)}, u32[]{:S(2)}, u32[]{:S(2)}) collective-permute-start(bf16[128,2048]{1,0:T(8,128)(2,1)} %fusion.57), channel_id=1, source_target_pairs={{0,8},{8,0},{16,24},{24,16},{1,9},{9,1},{17,25},{25,17},{2,10},{10... | collective-permute-start | bytes 1572872 | tf_op jit(solution)/shard_map/ppermute | solution.py:376
  642.3 68.6 %collective-permute-start.50 = (bf16[2,256,256]{2,1,0:T(8,128)(2,1)S(1)}, bf16[2,256,256]{2,1,0:T(8,128)(2,1)}, u32[]{:S(2)}, u32[]{:S(2)}) collective-permute-start(bf16[2,256,256]{2,1,0:T(8,128)(2,1)S(1)} %pad_maximum_fusion.20), channel_id=1, source_target_pairs={{0,16},{8,24},{16,0},{24,8},{1,17},{9,25},{17,1},{25,9},{2,18},{10... | collective-permute-start | bytes 786440 | tf_op jit(solution)/shard_map/ppermute | solution.py:376
  736.2 43.9 %collective-permute-start.56 = (f32[16,256]{1,0:T(8,128)}, f32[16,256]{1,0:T(8,128)S(1)}, u32[]{:S(2)}, u32[]{:S(2)}) collective-permute-start(f32[16,256]{1,0:T(8,128)} %fusion.70), channel_id=1, source_target_pairs={{0,16},{8,24},{16,0},{24,8},{1,17},{9,25},{17,1},{25,9},{2,18},{10... | collective-permute-start | bytes 49160 | tf_op jit(solution)/shard_map/ppermute | solution.py:376
  739.7 33.9 %all-to-all-start = ((bf16[8,64,768]{2,1,0:T(8,128)(2,1)}), bf16[8,64,768]{2,1,0:T(8,128)(2,1)S(1)}, u32[]{:S(2)}, u32[]{:S(2)}) async-start(bf16[8,64,768]{2,1,0:T(8,128)(2,1)} %bitcast.55), calls=%async_computation.3 | async-start | bytes 1572864 | tf_op jit(solution)/shard_map/all_to_all | solution.py:469
  774.5 76.4 %all-to-all-start.1 = ((bf16[8,64,2304]{2,1,0:T(8,128)(2,1)}), bf16[8,64,2304]{2,1,0:T(8,128)(2,1)S(1)}, u32[]{:S(2)}, u32[]{:S(2)}) async-start(bf16[8,64,2304]{2,1,0:T(8,128)(2,1)} %pad_maximum_fusion.3), calls=%async_computation.4 | async-start | bytes 4718592 | tf_op jit(solution)/shard_map/all_to_all | solution.py:469
  782.2 50.9 %collective-permute-start.53 = (bf16[128,2048]{1,0:T(8,128)(2,1)}, bf16[128,2048]{1,0:T(8,128)(2,1)}, u32[]{:S(2)}, u32[]{:S(2)}) collective-permute-start(bf16[128,2048]{1,0:T(8,128)(2,1)} %fusion.56), channel_id=1, source_target_pairs={{0,16},{8,24},{16,0},{24,8},{1,17},{9,25},{17,1},{25,9},{2,18},{10... | collective-permute-start | bytes 1572872 | tf_op jit(solution)/shard_map/ppermute | solution.py:376
  783.9 49.2 %collective-permute-start.58 = (f32[4,256]{1,0:T(4,128)S(1)}, f32[4,256]{1,0:T(4,128)S(1)}, u32[]{:S(2)}, u32[]{:S(2)}) collective-permute-start(f32[4,256]{1,0:T(4,128)S(1)} %fusion.76), channel_id=1, source_target_pairs={{0,4},{1,5},{2,6},{3,7},{4,0},{5,1},{6,2},{7,3},{8,12},{9,13},{10,... | collective-permute-start | bytes 12296 | tf_op jit(solution)/shard_map/ppermute | solution.py:376
  (86 other events, 1312.6 us)
Sparse Core Ops, SparseCore 0:
  9.6 49.5 all-gather.4
  126.5 46.7 all-gather.8
  339.2 46.7 reduce-scatter.3
  391.7 45.2 all-gather.6
  462.8 48.7 reduce-scatter.5
  711.0 56.4 reduce-scatter.7

commit v3 on v2

--- a/solution.py
+++ b/solution.py
@@ -10,6 +10,7 @@
 
 HEAD = 128
 SLABS = 4
+LANES = 128
 
 
 eps = 1e-06
@@ -444,11 +445,13 @@
 
 
 def total_seq(value):
+    shape = value.shape
+    value = value.reshape(-1, LANES)
     flip = 1
     while flip < lax.axis_size("seq"):
         value = value + swap(value, "seq", flip)
         flip *= 2
-    return value
+    return value.reshape(shape)
 
 
 def share_of_total(rows):
@@ -464,11 +467,35 @@
     return rows[0]
 
 
-def rows_home(summed, seq_count):
-    lead, width = summed.shape
-    return lax.all_to_all(
-        summed.reshape(seq_count, lead // seq_count, width), "seq", split_axis=0, concat_axis=0
-    ).astype(jnp.float32)
+def settle_kernel(index_ref, *refs, groups, width, count):
+    in_refs, out_refs = refs[:count], refs[count:]
+    for flip, in_ref in enumerate(in_refs):
+        source = index_ref[0] ^ flip
+        for at, out_ref in enumerate(out_refs):
+            for group in range(groups):
+                column = (at * groups + group) * width
+                place = pl.multiple_of((group * count + source) * width, width)
+                out_ref[:, pl.ds(place, width)] = in_ref[:, column : column + width].astype(jnp.float32)
+
+
+def rows_home(summed, groups, width):
+    pieces = exchanged(summed, "seq", 0)
+    count = len(pieces)
+    rows, total = pieces[0].shape
+    outs = total // (groups * width)
+    step = min(16, rows)
+    wide = count * groups * width
+    return pl.pallas_call(
+        functools.partial(settle_kernel, groups=groups, width=width, count=count),
+        grid_spec=pltpu.PrefetchScalarGridSpec(
+            num_scalar_prefetch=1,
+            grid=(rows // step,),
+            in_specs=[pl.BlockSpec((step, total), lambda r, index: (r, 0))] * count,
+            out_specs=[pl.BlockSpec((step, wide), lambda r, index: (r, 0))] * outs,
+        ),
+        out_shape=[jax.ShapeDtypeStruct((rows, wide), jnp.float32)] * outs,
+        name="settle",
+    )(lax.axis_index("seq").reshape(1), *pieces)
 
 
 QUERY_BLOCK = 256
@@ -725,8 +752,8 @@
     d_gate_up = jnp.concatenate([d_gate, d_up], 1)
     d_hidden_part = jnp.einsum("nf,df->nd", d_gate_up, w_hidden, preferred_element_type=jnp.float32).astype(low)
     d_hidden_sum = scatter_seq(d_hidden_part.reshape(row_count, row_len, model_width))
+    hidden_part = jnp.einsum("nd,nf->df", hidden_low, d_gate_up, preferred_element_type=jnp.float32).astype(low)
     down_part = jnp.einsum("nf,nd->fd", inner_low, d_branch_all, preferred_element_type=jnp.float32).astype(low)
-    hidden_part = jnp.einsum("nd,nf->df", hidden_low, d_gate_up, preferred_element_type=jnp.float32).astype(low)
     down_grad = sum_dp(*shares_for(down_part))
     hidden_own = sum_dp(*shares_for(hidden_part)).astype(low)
     d_hidden = grad_out + d_hidden_sum.astype(jnp.float32).reshape(tok_count, model_width)
@@ -734,25 +761,14 @@
     attn_gain_term = jnp.sum(d_hidden * attn_unit, 0)
     d_attn = norm_back(d_hidden * gain_attn, attn_unit, attn_inv).astype(low)
     d_mixed = jnp.einsum("nd,fd->nf", d_attn, wo_full, preferred_element_type=jnp.float32).astype(low)
-    d_mixed = placed(
-        exchanged(d_mixed.reshape(row_count, piece_len, feature_count), "seq", 2), seq_at, 1, seq_count
-    )
-    d_attn_own = placed(
-        exchanged(d_attn.reshape(row_count, piece_len, model_width), "seq", 2), seq_at, 1, seq_count
-    ).reshape(all_count, -1)
+    mixed_pieces = exchanged(d_mixed.reshape(row_count, piece_len, feature_count), "seq", 2)
+    d_mixed = placed(mixed_pieces, seq_at, 1, seq_count)
+    attn_pieces = exchanged(d_attn.reshape(row_count, piece_len, model_width), "seq", 2)
+    d_attn_own = placed(attn_pieces, seq_at, 1, seq_count).reshape(all_count, -1)
 
     out_part = jnp.einsum("nf,nd->fd", mixed_all, d_attn_own, preferred_element_type=jnp.float32).astype(low)
     out_own = sum_dp(*shares_for(out_part)).astype(low)
-    home = rows_home(jnp.concatenate([hidden_own, out_own], 1), seq_count)
-    home_rows = home.shape[1]
-    out_grad = home[..., 2 * own_hidden :].transpose(1, 0, 2).reshape(home_rows, feature_count)
-    hidden_home = (
-        home[..., : 2 * own_hidden]
-        .reshape(seq_count, home_rows, 2, dp_count, own_hidden // dp_count)
-        .transpose(2, 1, 3, 0, 4)
-        .reshape(2, home_rows, own_hidden * seq_count)
-    )
-    gate_grad, up_grad = hidden_home[0], hidden_home[1]
+    gate_grad, up_grad = rows_home(hidden_own, dp_count, own_hidden // dp_count)
 
     dq_gained, dk_gained, d_value, dots, gain_terms = attend_back(
         qkv_rows, inverses, tables, norm_gains, ids_all, (*kept, log_total), d_mixed, head_size, scale
@@ -770,17 +786,12 @@
     d_value = d_value.reshape(all_count, own_features)
     d_qkv = jnp.concatenate([dq_pre, dk_pre, d_value], 1)
     d_tokens_part = jnp.einsum("nf,df->nd", d_qkv, w_qkv, preferred_element_type=jnp.float32).astype(low)
-    d_tokens = d_hidden + scatter_seq(d_tokens_part.reshape(row_count, row_len, model_width)).astype(
-        jnp.float32
-    ).reshape(tok_count, model_width)
-
+    d_qkv, d_tokens_part = lax.optimization_barrier((d_qkv, d_tokens_part))
+    d_tokens_sum = scatter_seq(d_tokens_part.reshape(row_count, row_len, model_width))
+    d_tokens = d_hidden + d_tokens_sum.astype(jnp.float32).reshape(tok_count, model_width)
     qkv_part = jnp.einsum("nd,nf->df", tokens_all, d_qkv, preferred_element_type=jnp.float32).astype(low)
-    attn_home = rows_home(sum_dp(*shares_for(qkv_part)).astype(low), seq_count)
-    attn_home = (
-        attn_home.reshape(seq_count, home_rows, 3, own_features)
-        .transpose(2, 1, 0, 3)
-        .reshape(3, home_rows, feature_count)
-    )
+    qkv_own = sum_dp(*shares_for(qkv_part)).astype(low)
+    attn_home = rows_home(jnp.concatenate([qkv_own, out_own], 1), 1, own_features)
     zeros = jnp.zeros((feature_count,), jnp.float32)
     gains = jnp.stack(
         [
@@ -800,7 +811,7 @@
         attn_home[0],
         attn_home[1],
         attn_home[2],
-        out_grad,
+        attn_home[3],
         gate_grad,
         up_grad,
         down_grad,

time: 893 us -> 787 us (0.88)
  waiting for transfers between devices: 459 us -> 385 us
  local copies, waits for them, and re-layouts: 142 us -> 99 us
  other arithmetic: 63.2 us -> 42.5 us
  starting transfers between devices: 77.7 us -> 94.1 us
    ppermute x61 -> x75, waiting for transfers between devices: 333 us -> 283 us  [swap(): lax.ppermute(value, axis, [(at, at ^ flip) for at in range(lax.axis_size(...]
    ppermute x61 -> x75, starting transfers between devices: 69 us -> 93.4 us  [swap(): lax.ppermute(value, axis, [(at, at ^ flip) for at in range(lax.axis_size(...]
    all_to_all x2 -> x0, waiting for transfers between devices: 21.7 us -> none  [rows_home(): lax.all_to_all(summed.reshape(seq_count, lead // seq_count, width), 'seq'...]
    slice x10 -> x0, local copies, waits for them, and re-layouts: 20.1 us -> none  [the longest x3 9.76 us: shards_by_feature(): gate_grad, up_grad = (hidden_home[0], hidden_home[1])]
    unnamed x93 -> x95, local copies, waits for them, and re-layouts: 29 us -> 26 us
  transfers between devices with their start and end apart: 69 -> 81, of which waited for: 36 -> 35; matrix products, arithmetic and copies ran while one was open for 25% -> 18% of each run, Pallas kernels for 2% -> 3%
where the time goes in v3:
time: 787 us; the launch traced here: 776 us
  waiting for transfers between devices  385 us (49%)
  matrix products  107 us (14%)
  local copies, waits for them, and re-layouts  99 us (13%)
  starting transfers between devices  94.1 us (12%)
  other arithmetic  42.5 us (5%)
  Pallas kernels  32.8 us (4%)
  between operations  15.8 us (2%)
    ppermute x75, waiting for transfers between devices, swap(): lax.ppermute(value, axis, [(at, at ^ flip) for at in range(lax.axis_size(...  283 us
    ppermute x75, starting transfers between devices, swap(): lax.ppermute(value, axis, [(at, at ^ flip) for at in range(lax.axis_size(...  93.4 us
    all_gather x2, waiting for transfers between devices, gather_seq(): return lax.all_gather(piece, 'seq', axis=1, tiled=True)  54.8 us
    reduce_scatter x3, waiting for transfers between devices, scatter_seq(): return lax.psum_scatter(partial, 'seq', scatter_dimension=1, tiled=True)  46.5 us
    unnamed x95, local copies, waits for them, and re-layouts  26 us
    dynamic_update_slice x16, local copies, waits for them, and re-layouts, gather_dp(): whole = lax.dynamic_update_slice_in_dim(whole, part, place, 0)  20.1 us
    dynamic_update_slice x20, local copies, waits for them, and re-layouts, placed(): lax.dynamic_update_slice_in_dim(whole, piece, (index ^ flip) * width, axis)  17.4 us
  transfers between devices with their start and end apart: 81, of which 35 were waited for; matrix products, arithmetic and copies ran while one was open for 18% of the time, Pallas kernels for 3%

profile of v3, /device:TPU:0, one launch (start us, length us, event | category | flops | bytes accessed | tf_op | source)
XLA Modules:
  0.0 775.5 jit_solution(9112970501798582137)
XLA Ops:
  15.7 16.2 %collective-permute-done = bf16[512,768]{1,0:T(8,128)(2,1)} collective-permute-done((bf16[512,768]{1,0:T(8,128)(2,1)}, bf16[512,768]{1,0:T(8,128)(2,1)}, u32[]{:S(2)}, u32[]{:S(2)}) %collective-permute-start) | collective-permute-done | bytes 786464 | tf_op jit(solution)/shard_map/ppermute | solution.py:377
  49.3 10.0 %all-gather.5.cloned.1.call-done = bf16[1,1024,2048]{2,1,0:T(8,128)(2,1)} async-done(((bf16[1,128,2048]{2,1,0:T(8,128)(2,1)}), bf16[1,1024,2048]{2,1,0:T(8,128)(2,1)}) %all-gather.5.cloned.1.call-update) | async-done | bytes 4194320 | tf_op jit(solution)/shard_map/all_gather | solution.py:369
  80.1 10.3 %attend.1 = (bf16[1,1024,256]{2,1,0:T(8,128)(2,1)}, bf16[1,1024,256]{2,1,0:T(8,128)(2,1)}, bf16[1,1024,256]{2,1,0:T(8,128)(2,1)}, bf16[1,1024,256]{2,1,0:T(8,128)(2,1)}, f32[1,2,1024,1]{3,2,1,0:T(8,128)}) custom-call(f32[1,1024,768]{2,1,0:T(8,128)} %bitcast.360, f32[1,1024,768]{2,1,0:T(8,128)} %bitcast.361, f32[1,1024,768]{2,1,0:T(8,128)} %bitcast.362, ...), custom_call_target="tpu_custom_call" | custom-call | tf_op jit(solution)/shard_map/attend/pallas_call | solution.py:608
  102.6 15.6 %collective-permute-done.10 = bf16[512,1024]{1,0:T(8,128)(2,1)S(1)} collective-permute-done((bf16[512,1024]{1,0:T(8,128)(2,1)S(1)}, bf16[512,1024]{1,0:T(8,128)(2,1)S(1)}, u32[]{:S(2)}, u32[]{:S(2)}) %collective-permute-start.10) | collective-permute-done | bytes 1048608 | tf_op jit(solution)/shard_map/ppermute | solution.py:377
  154.1 53.7 %collective-permute-done.19 = bf16[256,2048]{1,0:T(8,128)(2,1)S(1)} collective-permute-done((bf16[256,2048]{1,0:T(8,128)(2,1)}, bf16[256,2048]{1,0:T(8,128)(2,1)S(1)}, u32[]{:S(2)}, u32[]{:S(2)}) %collective-permute-start.19) | collective-permute-done | bytes 1048608 | tf_op jit(solution)/shard_map/ppermute | solution.py:377
  233.4 10.5 %collective-permute-done.17 = bf16[256,2048]{1,0:T(8,128)(2,1)S(1)} collective-permute-done((bf16[256,2048]{1,0:T(8,128)(2,1)S(1)}, bf16[256,2048]{1,0:T(8,128)(2,1)S(1)}, u32[]{:S(2)}, u32[]{:S(2)}) %collective-permute-start.17) | collective-permute-done | bytes 1048608 | tf_op jit(solution)/shard_map/ppermute | solution.py:377
  256.5 13.4 %multiply_reduce_fusion = (f32[1024]{0:T(1024)S(1)}, f32[1024,2048]{1,0:T(8,128)S(1)}) fusion(bf16[2048,2048]{1,0:T(8,128)(2,1)} %constant_dynamic-update-slice_fusion.19, bf16[1,1024,2048]{2,1,0:T(8,128)(2,1)} %all-gather.9.cloned.1.call-done), kind=kOutput, calls=%fused_computation.1 | convolution fusion | flops 8594127872 | bytes 20975616 | tf_op jit(solution)/shard_map/dot_general | solution.py:718
  274.9 12.8 %fusion.91 = f32[1024,2048]{1,0:T(8,128)S(1)} fusion(bf16[1024,2048]{1,0:T(8,128)(2,1)S(1)} %add_convert_fusion, bf16[2048,2048]{1,0:T(8,128)(2,1)} %constant_dynamic-update-slice_fusion.14), kind=kOutput, calls=%fused_computation.306 | convolution fusion | flops 8589934592 | bytes 20971520 | tf_op jit(solution)/shard_map/dot_general | solution.py:726
  291.0 8.2 %convert_bitcast_fusion.1 = bf16[1,1024,2048]{2,1,0:T(8,128)(2,1)} fusion(bf16[1024,1024]{1,0:T(8,128)(2,1)S(1)} %multiply_convert_fusion.2, bf16[1024,2048]{1,0:T(8,128)(2,1)} %constant_dynamic-update-slice_fusion.9), kind=kOutput, calls=%fused_computation.21 | convolution fusion | flops 4297064448 | bytes 10485760 | tf_op jit(solution)/shard_map/dot_general | solution.py:731
  300.0 46.5 %reduce-scatter.4.cloned.1.call-done = bf16[1,128,2048]{2,1,0:T(8,128)(2,1)} async-done(((bf16[1,1024,2048]{2,1,0:T(8,128)(2,1)}), bf16[1,128,2048]{2,1,0:T(8,128)(2,1)}) %reduce-scatter.4.cloned.1.call-update) | async-done | bytes 524304 | tf_op jit(solution)/shard_map/reduce_scatter | solution.py:373
  352.8 44.8 %all-gather.7.cloned.1.call-done = bf16[1,1024,2048]{2,1,0:T(8,128)(2,1)} async-done(((bf16[1,128,2048]{2,1,0:T(8,128)(2,1)}), bf16[1,1024,2048]{2,1,0:T(8,128)(2,1)}) %all-gather.7.cloned.1.call-update) | async-done | bytes 4194320 | tf_op jit(solution)/shard_map/all_gather | solution.py:369
  397.6 11.7 %multiply_convert_fusion.1 = (bf16[1024,1024]{1,0:T(8,128)(2,1)S(1)}, bf16[1024,1024]{1,0:T(8,128)(2,1)S(1)}) fusion(f32[1024,2048]{1,0:T(8,128)} %copy-done.7, bf16[1024,2048]{1,0:T(8,128)(2,1)} %constant_dynamic-update-slice_fusion.9, bf16[1,1024,2048]{2,1,0:T(8,128)(2,1)} %all-gather.7.cloned.1.call-done), kind=kOutput, calls=%fused_computation.20 | convolution fusion | flops 4308598784 | bytes 20971520 | tf_op jit(solution)/shard_map/nd,fd->nf/dot_general | solution.py:749
  411.3 12.7 %convert_bitcast_fusion = bf16[1,1024,2048]{2,1,0:T(8,128)(2,1)} fusion(bf16[2048,2048]{1,0:T(8,128)(2,1)} %constant_dynamic-update-slice_fusion.14, bf16[1024,1024]{1,0:T(8,128)(2,1)S(1)} %get-tuple-element.60, bf16[1024,1024]{1,0:T(8,128)(2,1)S(1)} %get-tuple-element.59), kind=kOutput, calls=%fused_computation.18 | convolution fusion | flops 8600420352 | bytes 16777216 | tf_op jit(solution)/shard_map/nf,df->nd/dot_general | solution.py:753
  424.0 14.0 %convolution_convert_fusion = bf16[2048,2048]{1,0:T(8,128)(2,1)} fusion(bf16[1024,2048]{1,0:T(8,128)(2,1)} %copy-done.11, bf16[1024,1024]{1,0:T(8,128)(2,1)} %copy-done.43, bf16[1024,1024]{1,0:T(8,128)(2,1)} %copy-done.42), kind=kOutput, calls=%fused_computation.2 | convolution fusion | flops 8602517504 | bytes 16777216 | tf_op jit(solution)/shard_map/nd,nf->df/dot_general | solution.py:755
  438.0 7.2 fusion.13
  454.9 18.2 %collective-permute-done.68 = bf16[2,128,2048]{2,1,0:T(8,128)(2,1)} collective-permute-done((bf16[2,128,2048]{2,1,0:T(8,128)(2,1)}, bf16[2,128,2048]{2,1,0:T(8,128)(2,1)}, u32[]{:S(2)}, u32[]{:S(2)}) %collective-permute-start.68) | collective-permute-done | bytes 1048608 | tf_op jit(solution)/shard_map/ppermute | solution.py:377
  476.3 45.6 %collective-permute-done.66 = bf16[2,128,2048]{2,1,0:T(8,128)(2,1)S(1)} collective-permute-done((bf16[2,128,2048]{2,1,0:T(8,128)(2,1)S(1)}, bf16[2,128,2048]{2,1,0:T(8,128)(2,1)S(1)}, u32[]{:S(2)}, u32[]{:S(2)}) %collective-permute-start.66) | collective-permute-done | bytes 1048608 | tf_op jit(solution)/shard_map/ppermute | solution.py:377
  533.3 24.3 %collective-permute-done.56 = bf16[256,2048]{1,0:T(8,128)(2,1)S(1)} collective-permute-done((bf16[256,2048]{1,0:T(8,128)(2,1)S(1)}, bf16[256,2048]{1,0:T(8,128)(2,1)S(1)}, u32[]{:S(2)}, u32[]{:S(2)}) %collective-permute-start.56) | collective-permute-done | bytes 1048608 | tf_op jit(solution)/shard_map/ppermute | solution.py:377
  566.9 11.9 %collective-permute-done.60.refs_2_ = bf16[64,2048]{1,0:T(8,128)(2,1)S(1)} collective-permute-done((bf16[64,2048]{1,0:T(8,128)(2,1)S(1)}, bf16[64,2048]{1,0:T(8,128)(2,1)S(1)}, u32[]{:S(2)}, u32[]{:S(2)}) %collective-permute-start.60) | collective-permute-done | bytes 262176 | tf_op jit(solution)/shard_map/ppermute | solution.py:377
  583.4 16.1 %collective-permute-done.63.refs_5_ = bf16[64,2048]{1,0:T(8,128)(2,1)S(1)} collective-permute-done((bf16[64,2048]{1,0:T(8,128)(2,1)S(1)}, bf16[64,2048]{1,0:T(8,128)(2,1)S(1)}, u32[]{:S(2)}, u32[]{:S(2)}) %collective-permute-start.63) | collective-permute-done | bytes 262176 | tf_op jit(solution)/shard_map/ppermute | solution.py:377
  616.1 10.9 %collective-permute-start.24 = (bf16[1,128,256]{2,1,0:T(8,128)(2,1)S(1)}, bf16[1,128,256]{2,1,0:T(8,128)(2,1)S(1)}, u32[]{:S(2)}, u32[]{:S(2)}) collective-permute-start(bf16[1,128,256]{2,1,0:T(8,128)(2,1)S(1)} %get-tuple-element.128), channel_id=1, source_target_pairs={{0,2},{1,3},{2,0},{3,1},{4,6},{5,7},{6,4},{7,5},{8,10},{9,11},{10,... | collective-permute-start | bytes 196616 | tf_op jit(solution)/shard_map/ppermute | solution.py:377
  645.9 14.5 %attend_back.1 = (f32[1,1024,256]{2,1,0:T(8,128)}, f32[1,1024,256]{2,1,0:T(8,128)}, bf16[1,1024,256]{2,1,0:T(8,128)(2,1)}, f32[1,2,1024,2]{3,2,1,0:T(8,128)}, f32[1,2,256]{2,1,0:T(2,128)}) custom-call(f32[1,1024,768]{2,1,0:T(8,128)} %bitcast.363, f32[1,1024,768]{2,1,0:T(8,128)} %bitcast.364, f32[1,1024,1]{2,1,0:T(8,128)} %copy.52.qinv_ref, ...), custom_call_target="tpu_custom_call" | custom-call | tf_op jit(solution)/shard_map/attend_back/pallas_call | solution.py:623
  710.8 15.2 %collective-permute-done.47 = bf16[256,256]{1,0:T(8,128)(2,1)S(1)} collective-permute-done((bf16[256,256]{1,0:T(8,128)(2,1)S(1)}, bf16[256,256]{1,0:T(8,128)(2,1)S(1)}, u32[]{:S(2)}, u32[]{:S(2)}) %collective-permute-start.47) | collective-permute-done | bytes 131104 | tf_op jit(solution)/shard_map/ppermute | solution.py:377
  750.4 9.6 %collective-permute-done.51.refs_4_ = bf16[64,1024]{1,0:T(8,128)(2,1)S(1)} collective-permute-done((bf16[64,1024]{1,0:T(8,128)(2,1)S(1)}, bf16[64,1024]{1,0:T(8,128)(2,1)S(1)}, u32[]{:S(2)}, u32[]{:S(2)}) %collective-permute-start.51) | collective-permute-done | bytes 131104 | tf_op jit(solution)/shard_map/ppermute | solution.py:377
  (423 shorter events, 305.9 us)
Async XLA Ops:
  7.2 52.0 %all-gather.5.cloned.1.call-start = ((), (), s32[]{:S(2)}) async-start(), calls=%async_computation.3 | async-start | bytes 4718592 | tf_op jit(solution)/shard_map/all_gather | solution.py:369
  7.9 248.6 %all-gather.9.cloned.1.call-start = ((), (), s32[]{:S(2)}) async-start(), calls=%async_computation.8 | async-start | bytes 4718592 | tf_op jit(solution)/shard_map/all_gather | solution.py:717
  15.6 52.4 %collective-permute-start.7 = (s32[8,128]{1,0:T(8,128)S(1)}, s32[8,128]{1,0:T(8,128)S(1)}, u32[]{:S(2)}, u32[]{:S(2)}) collective-permute-start(s32[8,128]{1,0:T(8,128)S(1)} %bitcast.377), channel_id=1, source_target_pairs={{0,1},{1,0},{2,3},{3,2},{4,5},{5,4},{6,7},{7,6},{8,9},{9,8},{10,11... | collective-permute-start | bytes 12296 | tf_op jit(solution)/shard_map/ppermute | solution.py:377
  90.5 256.0 %reduce-scatter.4.cloned.1.call-start = ((), (), s32[]{:S(2)}) async-start(), calls=%async_computation.4 | async-start | bytes 4718592 | tf_op jit(solution)/shard_map/reduce_scatter | solution.py:373
  133.7 118.0 %collective-permute-start.14 = (bf16[2048,1024]{1,0:T(8,128)(2,1)}, bf16[2048,1024]{1,0:T(8,128)(2,1)}, u32[]{:S(2)}, u32[]{:S(2)}) collective-permute-start(bf16[2048,1024]{1,0:T(8,128)(2,1)} %constant_dynamic-update-slice_fusion.21), channel_id=1, source_target_pairs={{0,1},{1,0},{2,3},{3,2},{4,5},{5,4},{6,7},{7,6},{8,9},{9,8},{10,11... | collective-permute-start | bytes 12582920 | tf_op jit(solution)/shard_map/ppermute | solution.py:377
  137.1 77.3 %collective-permute-start.15 = (bf16[512,2048]{1,0:T(8,128)(2,1)}, bf16[512,2048]{1,0:T(8,128)(2,1)S(1)}, u32[]{:S(2)}, u32[]{:S(2)}) collective-permute-start(bf16[512,2048]{1,0:T(8,128)(2,1)} %dynamic-slice_dynamic-update-slice_fusion), channel_id=1, source_target_pairs={{0,8},{8,0},{16,24},{24,16},{1,9},{9,1},{17,25},{25,17},{2,10},{10... | collective-permute-start | bytes 6291464 | tf_op jit(solution)/shard_map/ppermute | solution.py:377
  138.5 86.7 %collective-permute-start.16 = (bf16[512,2048]{1,0:T(8,128)(2,1)}, bf16[512,2048]{1,0:T(8,128)(2,1)}, u32[]{:S(2)}, u32[]{:S(2)}) collective-permute-start(bf16[512,2048]{1,0:T(8,128)(2,1)} %dynamic-slice_dynamic-update-slice_fusion), channel_id=1, source_target_pairs={{0,16},{8,24},{16,0},{24,8},{1,17},{9,25},{17,1},{25,9},{2,18},{10... | collective-permute-start | bytes 6291464 | tf_op jit(solution)/shard_map/ppermute | solution.py:377
  144.5 63.3 %collective-permute-start.19 = (bf16[256,2048]{1,0:T(8,128)(2,1)}, bf16[256,2048]{1,0:T(8,128)(2,1)S(1)}, u32[]{:S(2)}, u32[]{:S(2)}) collective-permute-start(bf16[256,2048]{1,0:T(8,128)(2,1)} %get-tuple-element.56), channel_id=1, source_target_pairs={{0,8},{8,0},{16,24},{24,16},{1,9},{9,1},{17,25},{25,17},{2,10},{10... | collective-permute-start | bytes 3145736 | tf_op jit(solution)/shard_map/ppermute | solution.py:377
  145.0 64.0 %collective-permute-start.20 = (bf16[256,2048]{1,0:T(8,128)(2,1)}, bf16[256,2048]{1,0:T(8,128)(2,1)}, u32[]{:S(2)}, u32[]{:S(2)}) collective-permute-start(bf16[256,2048]{1,0:T(8,128)(2,1)} %get-tuple-element.56), channel_id=1, source_target_pairs={{0,16},{8,24},{16,0},{24,8},{1,17},{9,25},{17,1},{25,9},{2,18},{10... | collective-permute-start | bytes 3145736 | tf_op jit(solution)/shard_map/ppermute | solution.py:377
  299.2 98.4 %all-gather.7.cloned.1.call-start = ((), (), s32[]{:S(2)}) async-start(), calls=%async_computation.5 | async-start | bytes 4718592 | tf_op jit(solution)/shard_map/all_gather | solution.py:369
  352.1 252.8 %reduce-scatter.6.cloned.1.call-start = ((), (), s32[]{:S(2)}) async-start(), calls=%async_computation.6 | async-start | bytes 4718592 | tf_op jit(solution)/shard_map/reduce_scatter | solution.py:373
  438.0 328.2 %reduce-scatter.8.cloned.1.call-start = ((), (), s32[]{:S(2)}) async-start(), calls=%async_computation.7 | async-start | bytes 4718592 | tf_op jit(solution)/shard_map/reduce_scatter | solution.py:373
  450.9 73.0 %collective-permute-start.55 = (bf16[2,256,2048]{2,1,0:T(8,128)(2,1)S(1)}, bf16[2,256,2048]{2,1,0:T(8,128)(2,1)S(1)}, u32[]{:S(2)}, u32[]{:S(2)}) collective-permute-start(bf16[2,256,2048]{2,1,0:T(8,128)(2,1)S(1)} %pad_maximum_fusion.3), channel_id=1, source_target_pairs={{0,8},{8,0},{16,24},{24,16},{1,9},{9,1},{17,25},{25,17},{2,10},{10... | collective-permute-start | bytes 6291464 | tf_op jit(solution)/shard_map/ppermute | solution.py:377
  452.5 69.4 %collective-permute-start.66 = (bf16[2,128,2048]{2,1,0:T(8,128)(2,1)S(1)}, bf16[2,128,2048]{2,1,0:T(8,128)(2,1)S(1)}, u32[]{:S(2)}, u32[]{:S(2)}) collective-permute-start(bf16[2,128,2048]{2,1,0:T(8,128)(2,1)S(1)} %pad_maximum_fusion.7), channel_id=1, source_target_pairs={{0,8},{8,0},{16,24},{24,16},{1,9},{9,1},{17,25},{25,17},{2,10},{10... | collective-permute-start | bytes 3145736 | tf_op jit(solution)/shard_map/ppermute | solution.py:377
  453.3 72.1 %collective-permute-start.57 = (bf16[2,256,2048]{2,1,0:T(8,128)(2,1)S(1)}, bf16[2,256,2048]{2,1,0:T(8,128)(2,1)S(1)}, u32[]{:S(2)}, u32[]{:S(2)}) collective-permute-start(bf16[2,256,2048]{2,1,0:T(8,128)(2,1)S(1)} %pad_maximum_fusion.4), channel_id=1, source_target_pairs={{0,16},{8,24},{16,0},{24,8},{1,17},{9,25},{17,1},{25,9},{2,18},{10... | collective-permute-start | bytes 6291464 | tf_op jit(solution)/shard_map/ppermute | solution.py:377
  474.7 58.4 %collective-permute-start.69 = (bf16[128,2048]{1,0:T(8,128)(2,1)S(1)}, bf16[128,2048]{1,0:T(8,128)(2,1)S(1)}, u32[]{:S(2)}, u32[]{:S(2)}) collective-permute-start(bf16[128,2048]{1,0:T(8,128)(2,1)S(1)} %fusion.57), channel_id=1, source_target_pairs={{0,8},{8,0},{16,24},{24,16},{1,9},{9,1},{17,25},{25,17},{2,10},{10... | collective-permute-start | bytes 1572872 | tf_op jit(solution)/shard_map/ppermute | solution.py:377
  522.4 38.3 %collective-permute-start.67 = (bf16[128,2048]{1,0:T(8,128)(2,1)S(1)}, bf16[128,2048]{1,0:T(8,128)(2,1)S(1)}, u32[]{:S(2)}, u32[]{:S(2)}) collective-permute-start(bf16[128,2048]{1,0:T(8,128)(2,1)S(1)} %fusion.56), channel_id=1, source_target_pairs={{0,16},{8,24},{16,0},{24,8},{1,17},{9,25},{17,1},{25,9},{2,18},{10... | collective-permute-start | bytes 1572872 | tf_op jit(solution)/shard_map/ppermute | solution.py:377
  564.0 35.6 %collective-permute-start.63 = (bf16[64,2048]{1,0:T(8,128)(2,1)S(1)}, bf16[64,2048]{1,0:T(8,128)(2,1)S(1)}, u32[]{:S(2)}, u32[]{:S(2)}) collective-permute-start(bf16[64,2048]{1,0:T(8,128)(2,1)S(1)} %get-tuple-element.94), channel_id=1, source_target_pairs={{0,5},{1,4},{2,7},{3,6},{4,1},{5,0},{6,3},{7,2},{8,13},{9,12},{10,... | collective-permute-start | bytes 786440 | tf_op jit(solution)/shard_map/ppermute | solution.py:377
  565.6 33.9 %collective-permute-start.64 = (bf16[64,2048]{1,0:T(8,128)(2,1)S(1)}, bf16[64,2048]{1,0:T(8,128)(2,1)S(1)}, u32[]{:S(2)}, u32[]{:S(2)}) collective-permute-start(bf16[64,2048]{1,0:T(8,128)(2,1)S(1)} %get-tuple-element.93), channel_id=1, source_target_pairs={{0,6},{1,7},{2,4},{3,5},{4,2},{5,3},{6,0},{7,1},{8,14},{9,15},{10,... | collective-permute-start | bytes 786440 | tf_op jit(solution)/shard_map/ppermute | solution.py:377
  635.7 46.8 %collective-permute-start.39 = (bf16[1,128,256]{2,1,0:T(8,128)(2,1)}, bf16[1,128,256]{2,1,0:T(8,128)(2,1)S(1)}, u32[]{:S(2)}, u32[]{:S(2)}) collective-permute-start(bf16[1,128,256]{2,1,0:T(8,128)(2,1)} %get-tuple-element.119), channel_id=1, source_target_pairs={{0,3},{1,2},{2,1},{3,0},{4,7},{5,6},{6,5},{7,4},{8,11},{9,10},{10,... | collective-permute-start | bytes 196616 | tf_op jit(solution)/shard_map/ppermute | solution.py:377
  640.0 44.0 %collective-permute-start.40 = (bf16[1,128,256]{2,1,0:T(8,128)(2,1)}, bf16[1,128,256]{2,1,0:T(8,128)(2,1)S(1)}, u32[]{:S(2)}, u32[]{:S(2)}) collective-permute-start(bf16[1,128,256]{2,1,0:T(8,128)(2,1)} %get-tuple-element.118), channel_id=1, source_target_pairs={{0,4},{1,5},{2,6},{3,7},{4,0},{5,1},{6,2},{7,3},{8,12},{9,13},{10,... | collective-permute-start | bytes 196616 | tf_op jit(solution)/shard_map/ppermute | solution.py:377
  640.0 44.0 %collective-permute-start.41 = (bf16[1,128,256]{2,1,0:T(8,128)(2,1)}, bf16[1,128,256]{2,1,0:T(8,128)(2,1)S(1)}, u32[]{:S(2)}, u32[]{:S(2)}) collective-permute-start(bf16[1,128,256]{2,1,0:T(8,128)(2,1)} %get-tuple-element.117), channel_id=1, source_target_pairs={{0,5},{1,4},{2,7},{3,6},{4,1},{5,0},{6,3},{7,2},{8,13},{9,12},{10,... | collective-permute-start | bytes 196616 | tf_op jit(solution)/shard_map/ppermute | solution.py:377
  642.7 41.4 %collective-permute-start.42 = (bf16[1,128,256]{2,1,0:T(8,128)(2,1)}, bf16[1,128,256]{2,1,0:T(8,128)(2,1)S(1)}, u32[]{:S(2)}, u32[]{:S(2)}) collective-permute-start(bf16[1,128,256]{2,1,0:T(8,128)(2,1)} %get-tuple-element.116), channel_id=1, source_target_pairs={{0,6},{1,7},{2,4},{3,5},{4,2},{5,3},{6,0},{7,1},{8,14},{9,15},{10,... | collective-permute-start | bytes 196616 | tf_op jit(solution)/shard_map/ppermute | solution.py:377
  706.1 34.0 %collective-permute-start.74 = (f32[1,256]{1,0:T(1,128)S(1)}, f32[1,256]{1,0:T(1,128)S(1)}, u32[]{:S(2)}, u32[]{:S(2)}) collective-permute-start(f32[1,256]{1,0:T(1,128)S(1)} %constant_dynamic-slice_fusion), channel_id=1, source_target_pairs={{0,1},{1,0},{2,3},{3,2},{4,5},{5,4},{6,7},{7,6},{8,9},{9,8},{10,11... | collective-permute-start | bytes 3080 | tf_op jit(solution)/shard_map/ppermute | solution.py:377
  (101 other events, 1366.1 us)
Sparse Core Ops, SparseCore 0:
  9.6 49.5 all-gather.4
  90.6 47.4 all-gather.8
  299.3 47.0 reduce-scatter.3
  352.2 45.3 all-gather.6
  438.1 48.7 reduce-scatter.5
  682.6 51.1 reduce-scatter.7

commit v4 on v3

--- a/solution.py
+++ b/solution.py
@@ -377,14 +377,39 @@
     return lax.ppermute(value, axis, [(at, at ^ flip) for at in range(lax.axis_size(axis))])
 
 
-def placed(pieces, index, axis, count):
-    width = pieces[0].shape[axis]
-    shape = list(pieces[0].shape)
-    shape[axis] = width * count
-    whole = jnp.zeros(shape, pieces[0].dtype)
-    for flip, piece in enumerate(pieces):
-        whole = lax.dynamic_update_slice_in_dim(whole, piece, (index ^ flip) * width, axis)
-    return whole
+def place_kernel(spots_ref, *refs):
+    *in_refs, out_ref, sems = refs
+    copies = []
+    for at, in_ref in enumerate(in_refs):
+        rows, width = in_ref.shape
+        row = pl.multiple_of(spots_ref[2 * at], LANES)
+        column = pl.multiple_of(spots_ref[2 * at + 1], LANES)
+        copies.append(
+            pltpu.make_async_copy(
+                in_ref, out_ref.at[pl.ds(row, rows), pl.ds(column, width)], sems.at[at]
+            )
+        )
+    for copy in copies:
+        copy.start()
+    for copy in copies:
+        copy.wait()
+
+
+def placed(pieces, shape):
+    spots = jnp.stack([jnp.int32(at) for _, row, column in pieces for at in (row, column)])
+    anywhere = pl.BlockSpec(memory_space=pl.ANY)
+    return pl.pallas_call(
+        place_kernel,
+        grid_spec=pltpu.PrefetchScalarGridSpec(
+            num_scalar_prefetch=1,
+            grid=(1,),
+            in_specs=[anywhere] * len(pieces),
+            out_specs=anywhere,
+            scratch_shapes=[pltpu.SemaphoreType.DMA((len(pieces),))],
+        ),
+        out_shape=jax.ShapeDtypeStruct(shape, pieces[0][0].dtype),
+        name="place",
+    )(spots, *[piece for piece, _, _ in pieces])
 
 
 def pieces_for(value, name, split_axis):
@@ -404,21 +429,25 @@
     return swapped(pieces_for(value, name, split_axis), name)
 
 
-def gather_dp(piece):
+def pieces_dp(piece):
     half = piece.shape[0] // 2
     first, second = swap(piece, "dp", 1), swap(piece, "dp", 2)
     top, bottom = swap(first[:half], "dp", 2), swap(second[half:], "dp", 1)
     index = lax.axis_index("dp")
     width = piece.shape[0]
-    whole = placed([piece], index, 0, 4)
-    for part, place in (
+    far = (index ^ 3) * width
+    return [
         (first, (index ^ 1) * width),
         (second, (index ^ 2) * width),
-        (top, (index ^ 3) * width),
-        (bottom, (index ^ 3) * width + half),
-    ):
-        whole = lax.dynamic_update_slice_in_dim(whole, part, place, 0)
-    return whole
+        (top, far),
+        (bottom, far + half),
+    ]
+
+
+def gather_dp(piece):
+    rows, width = piece.shape
+    pieces = [(piece, lax.axis_index("dp") * rows), *pieces_dp(piece)]
+    return placed([(part, row, 0) for part, row in pieces], (4 * rows, width))
 
 
 def sum_dp(sent, kept):
@@ -454,16 +483,15 @@
     return value.reshape(shape)
 
 
-def share_of_total(rows):
-    for name in ("dp", "seq"):
-        flip = lax.axis_size(name) // 2
-        while flip:
-            halves = rows.reshape(2, rows.shape[0] // 2, rows.shape[1])
-            side = lax.axis_index(name) // flip % 2
-            kept = lax.dynamic_index_in_dim(halves, side, 0, False)
-            sent = lax.dynamic_index_in_dim(halves, 1 - side, 0, False)
-            rows = kept + swap(sent, name, flip)
-            flip //= 2
+def share_dp(rows):
+    flip = lax.axis_size("dp") // 2
+    while flip:
+        halves = rows.reshape(2, rows.shape[0] // 2, rows.shape[1])
+        side = lax.axis_index("dp") // flip % 2
+        kept = lax.dynamic_index_in_dim(halves, side, 0, False)
+        sent = lax.dynamic_index_in_dim(halves, 1 - side, 0, False)
+        rows = kept + swap(sent, "dp", flip)
+        flip //= 2
     return rows[0]
 
 
@@ -584,10 +612,20 @@
         gains_ref[0, at : at + 1] = jnp.sum(value * unit, 0, keepdims=True)
         value = value * gain_ref[...]
         out_ref[0] = value
-        dots_ref[0, 0, :, at : at + 1] = jnp.sum(value * unit, -1, keepdims=True)
-
-    turned_back(query_acc, q_ref, qinv_ref, gq_ref, dq_ref, 0)
-    turned_back(key_acc, k_ref, kinv_ref, gk_ref, dk_ref, 1)
+        return jnp.sum(value * unit, -1, keepdims=True)
+
+    query_dot = turned_back(query_acc, q_ref, qinv_ref, gq_ref, dq_ref, 0)
+    key_dot = turned_back(key_acc, k_ref, kinv_ref, gk_ref, dk_ref, 1)
+    lane = lax.broadcasted_iota(jnp.int32, (length, LANES), 1)
+    dots = jnp.where(lane == 0, query_dot, jnp.where(lane == 1, key_dot, 0.0)).T[:8]
+
+    @pl.when(pl.program_id(1) == 0)
+    def _():
+        dots_ref[0] = dots
+
+    @pl.when(pl.program_id(1) != 0)
+    def _():
+        dots_ref[0] += dots
 
 
 def attention_specs(length, heads, head_size):
@@ -629,14 +667,14 @@
             wide(0),
             wide(0),
             wide(0),
-            pl.BlockSpec((1, 1, length, 2), lambda r, h: (r, h, 0, 0)),
+            pl.BlockSpec((1, 8, length), lambda r, h: (r, 0, 0)),
             pl.BlockSpec((1, 2, head_size), lambda r, h: (r, 0, h)),
         ],
         out_shape=[
             jax.ShapeDtypeStruct(shape, jnp.float32),
             jax.ShapeDtypeStruct(shape, jnp.float32),
             jax.ShapeDtypeStruct(shape, jnp.bfloat16),
-            jax.ShapeDtypeStruct((rows, heads, length, 2), jnp.float32),
+            jax.ShapeDtypeStruct((rows, 8, length), jnp.float32),
             jax.ShapeDtypeStruct((rows, 2, heads * head_size), jnp.float32),
         ],
         scratch_shapes=[pltpu.VMEM((length, head_size), jnp.float32)] * 3,
@@ -687,8 +725,15 @@
     )
     core = seq_at % 2
     half = model_width // 2
-    wo_half = gather_dp(lax.dynamic_slice_in_dim(w_out, core * half, half, 1))
-    wo_full = placed([wo_half, swap(wo_half, "seq", 1)], core, 1, 2)
+    out_rows = w_out.shape[0]
+    out_pieces = pieces_dp(lax.dynamic_slice_in_dim(w_out, core * half, half, 1))
+    other_pieces = [(swap(piece, "seq", 1), row) for piece, row in out_pieces]
+    wo_full = placed(
+        [(w_out, lax.axis_index("dp") * out_rows, 0)]
+        + [(piece, row, core * half) for piece, row in out_pieces]
+        + [(piece, row, half - core * half) for piece, row in other_pieces],
+        (feature_count, model_width),
+    )
     w_hidden = gather_dp(jnp.concatenate([own_columns(w, dp_count, seq_count, seq_at) for w in (w_gate, w_up)], 1))
     w_back = gather_dp(
         lax.dynamic_slice_in_dim(
@@ -700,6 +745,7 @@
     gain_attn = g_attn.astype(jnp.float32)
     gain_ffn = g_ffn.astype(jnp.float32)
 
+    tokens_all, ids_all = lax.optimization_barrier((tokens_all, ids_all))
     qkv = jnp.dot(tokens_all, w_qkv, preferred_element_type=jnp.float32)
     query_pre = qkv[:, :own_features]
     key_pre = qkv[:, own_features : 2 * own_features]
@@ -761,11 +807,17 @@
     attn_gain_term = jnp.sum(d_hidden * attn_unit, 0)
     d_attn = norm_back(d_hidden * gain_attn, attn_unit, attn_inv).astype(low)
     d_mixed = jnp.einsum("nd,fd->nf", d_attn, wo_full, preferred_element_type=jnp.float32).astype(low)
-    mixed_pieces = exchanged(d_mixed.reshape(row_count, piece_len, feature_count), "seq", 2)
-    d_mixed = placed(mixed_pieces, seq_at, 1, seq_count)
-    attn_pieces = exchanged(d_attn.reshape(row_count, piece_len, model_width), "seq", 2)
-    d_attn_own = placed(attn_pieces, seq_at, 1, seq_count).reshape(all_count, -1)
-
+
+    def own_columns_of_all(tensor):
+        split = tensor.reshape(row_count, piece_len, seq_count, -1).transpose(2, 0, 1, 3)
+        width = split.shape[-1]
+        split = lax.all_to_all(split.reshape(seq_count, tok_count, width), "seq", split_axis=0, concat_axis=0)
+        split = split.reshape(seq_count, row_count, piece_len, width).transpose(1, 0, 2, 3)
+        return split.reshape(row_count, row_len, width)
+
+    d_mixed = own_columns_of_all(d_mixed)
+    d_mixed, d_attn = lax.optimization_barrier((d_mixed, d_attn))
+    d_attn_own = own_columns_of_all(d_attn).reshape(all_count, -1)
     out_part = jnp.einsum("nf,nd->fd", mixed_all, d_attn_own, preferred_element_type=jnp.float32).astype(low)
     out_own = sum_dp(*shares_for(out_part)).astype(low)
     gate_grad, up_grad = rows_home(hidden_own, dp_count, own_hidden // dp_count)
@@ -773,8 +825,18 @@
     dq_gained, dk_gained, d_value, dots, gain_terms = attend_back(
         qkv_rows, inverses, tables, norm_gains, ids_all, (*kept, log_total), d_mixed, head_size, scale
     )
-    query_gain_term, key_gain_term = jnp.sum(gain_terms, 0)
-    means = total_seq(jnp.sum(dots, 1).reshape(all_count, 2).T) / feature_count
+    norm_terms = lax.dynamic_update_slice_in_dim(
+        jnp.zeros((2, feature_count), jnp.float32), jnp.sum(gain_terms, 0), seq_at * own_features, 1
+    )
+    dots = dots[:, :2].transpose(1, 0, 2).reshape(-1, LANES)
+    stat_rows = dots.shape[0]
+    sums = total_seq(
+        jnp.concatenate(
+            [dots]
+            + [part.reshape(-1, LANES) for part in (norm_terms, attn_gain_term, ffn_gain_term)]
+        )
+    )
+    means = sums[:stat_rows].reshape(2, all_count) / feature_count
 
     def norm_back_wide(gained, pre, at):
         inv = inverse[at][:, None]
@@ -792,19 +854,11 @@
     qkv_part = jnp.einsum("nd,nf->df", tokens_all, d_qkv, preferred_element_type=jnp.float32).astype(low)
     qkv_own = sum_dp(*shares_for(qkv_part)).astype(low)
     attn_home = rows_home(jnp.concatenate([qkv_own, out_own], 1), 1, own_features)
-    zeros = jnp.zeros((feature_count,), jnp.float32)
-    gains = jnp.stack(
-        [
-            lax.dynamic_update_slice_in_dim(zeros, query_gain_term, seq_at * own_features, 0),
-            lax.dynamic_update_slice_in_dim(zeros, key_gain_term, seq_at * own_features, 0),
-            attn_gain_term,
-            ffn_gain_term,
-        ]
-    )
     share = feature_count // (dp_count * seq_count)
-    gains = share_of_total(
-        gains.reshape(4, dp_count * seq_count, share).transpose(1, 0, 2).reshape(dp_count * seq_count, 4 * share)
-    ).reshape(4, share)
+    gains = lax.dynamic_index_in_dim(
+        sums[stat_rows:].reshape(4, dp_count, seq_count, share), seq_at, 2, False
+    )
+    gains = share_dp(gains.transpose(1, 0, 2).reshape(dp_count, 4 * share)).reshape(4, share)
     return (
         result,
         d_tokens.reshape(row_count, piece_len, model_width),

time: 787 us -> 1480 us (1.88)
  Pallas kernels: 32.8 us -> 771 us
  local copies, waits for them, and re-layouts: 99 us -> 58.3 us
  starting transfers between devices: 94.1 us -> 78.8 us
    pallas_call x0 -> x4, Pallas kernels: none -> 738 us  [placed(): pl.pallas_call(place_kernel, grid_spec=pltpu.PrefetchScalarGridSpec(num_s...]
    dynamic_update_slice x39 -> x1, local copies, waits for them, and re-layouts: 39.4 us -> 0.68 us  [shards_by_feature(): lax.dynamic_update_slice_in_dim(jnp.zeros((2, feature_count), jnp.float32...]
    ppermute x75 -> x61, starting transfers between devices: 93.4 us -> 62 us  [swap(): lax.ppermute(value, axis, [(at, at ^ flip) for at in range(lax.axis_size(...]
    all_to_all x0 -> x2, starting transfers between devices: none -> 16.6 us  [own_columns_of_all(): lax.all_to_all(split.reshape(seq_count, tok_count, width), 'seq', split_a...]
    ppermute x75 -> x61, waiting for transfers between devices: 283 us -> 288 us  [swap(): lax.ppermute(value, axis, [(at, at ^ flip) for at in range(lax.axis_size(...]
  transfers between devices with their start and end apart: 81 -> 69, of which waited for: 35 -> 32; matrix products, arithmetic and copies ran while one was open for 18% -> 8% of each run, Pallas kernels for 3% -> 52%
where the time goes in v4:
time: 1480 us; the launch traced here: 1460 us
  Pallas kernels  771 us (52%)
  waiting for transfers between devices  392 us (26%)
  matrix products  94.8 us (6%)
  starting transfers between devices  78.8 us (5%)
  local copies, waits for them, and re-layouts  58.3 us (4%)
  other arithmetic  50.6 us (3%)
  between operations  16.1 us (1%)
    pallas_call x4, Pallas kernels, placed(): pl.pallas_call(place_kernel, grid_spec=pltpu.PrefetchScalarGridSpec(num_s...  738 us
    ppermute x61, waiting for transfers between devices, swap(): lax.ppermute(value, axis, [(at, at ^ flip) for at in range(lax.axis_size(...  288 us
    ppermute x61, starting transfers between devices, swap(): lax.ppermute(value, axis, [(at, at ^ flip) for at in range(lax.axis_size(...  62 us
    reduce_scatter x3, waiting for transfers between devices, scatter_seq(): return lax.psum_scatter(partial, 'seq', scatter_dimension=1, tiled=True)  50 us
    all_gather x2, waiting for transfers between devices, gather_seq(): return lax.all_gather(piece, 'seq', axis=1, tiled=True)  45.5 us
  transfers between devices with their start and end apart: 69, of which 32 were waited for; matrix products, arithmetic and copies ran while one was open for 8% of the time, Pallas kernels for 52%

profile of v4, /device:TPU:0, one launch (start us, length us, event | category | flops | bytes accessed | tf_op | source)
XLA Modules:
  0.0 1461.9 jit_solution(17641720682990468085)
XLA Ops:
  14.5 16.0 %collective-permute-done.3.refs_1_ = bf16[512,768]{1,0:T(8,128)(2,1)S(1)} collective-permute-done((bf16[512,768]{1,0:T(8,128)(2,1)S(1)}, bf16[512,768]{1,0:T(8,128)(2,1)S(1)}, u32[]{:S(2)}, u32[]{:S(2)}) %collective-permute-start.3) | collective-permute-done | bytes 786464 | tf_op jit(solution)/shard_map/ppermute | solution.py:377
  46.3 97.1 %place.4 = bf16[2048,768]{1,0:T(8,128)(2,1)} custom-call(s32[10]{0:T(128)} %stack.224.spots_ref, bf16[512,768]{1,0:T(8,128)(2,1)} %copy-done.25, bf16[512,768]{1,0:T(8,128)(2,1)} %copy-done.31, bf16[512,768]{1,0:T(8,128)(2,1)} %copy-done.32, bf16[256,768]{1,0:T(8,128)(2,1)} %copy-done.39, bf16[256,768]{1,0:T(8,128)(2,1)} %copy-done.40), custom_call_target="tpu_custom_call" | custom-call | tf_op jit(solution)/shard_map/place/pallas_call | solution.py:401
  164.2 10.5 attend.1
  189.3 12.8 collective-permute-done.10.refs_1_
  203.2 53.7 %collective-permute-done.11.refs_2_ = bf16[512,1024]{1,0:T(8,128)(2,1)} collective-permute-done((bf16[512,1024]{1,0:T(8,128)(2,1)}, bf16[512,1024]{1,0:T(8,128)(2,1)}, u32[]{:S(2)}, u32[]{:S(2)}) %collective-permute-start.11) | collective-permute-done | bytes 1048608 | tf_op jit(solution)/shard_map/ppermute | solution.py:377
  258.0 10.1 collective-permute-done.22.refs_1_
  268.2 11.1 collective-permute-done.23.refs_2_
  281.4 9.3 collective-permute-done.12.refs_3_
  303.7 128.9 %place.7 = bf16[1024,2048]{1,0:T(8,128)(2,1)} custom-call(s32[10]{0:T(128)} %stack.236.spots_ref, bf16[256,2048]{1,0:T(8,128)(2,1)} %copy-done.16, bf16[256,2048]{1,0:T(8,128)(2,1)} %copy-done.28, bf16[256,2048]{1,0:T(8,128)(2,1)} %copy-done.29, bf16[128,2048]{1,0:T(8,128)(2,1)} %collective-permute-done.24.refs_3_, ...), custom_call_target="tpu_custom_call" | custom-call | tf_op jit(solution)/shard_map/place/pallas_call | solution.py:401
  432.6 256.0 %place.5 = bf16[2048,2048]{1,0:T(8,128)(2,1)} custom-call(s32[18]{0:T(128)} %stack.230.spots_ref, bf16[512,2048]{1,0:T(8,128)(2,1)} %refs_0_.1, bf16[512,1024]{1,0:T(8,128)(2,1)} %collective-permute-done.10.refs_1_, bf16[512,1024]{1,0:T(8,128)(2,1)} %collective-permute-done.11.refs_2_, bf16[256,1024]{1,0:T(8,128)(2,1)} %collective-permute-done.12.refs_3_, ...), custom_call_target="tpu_custom_call" | custom-call | tf_op jit(solution)/shard_map/place/pallas_call | solution.py:401
  689.6 255.9 %place.6 = bf16[2048,2048]{1,0:T(8,128)(2,1)} custom-call(s32[10]{0:T(128)} %stack.224.spots_ref, bf16[512,2048]{1,0:T(8,128)(2,1)} %copy-done.27, bf16[512,2048]{1,0:T(8,128)(2,1)} %copy-done.13, bf16[512,2048]{1,0:T(8,128)(2,1)} %copy-done.14, bf16[256,2048]{1,0:T(8,128)(2,1)} %copy-done.36, bf16[256,2048]{1,0:T(8,128)(2,1)} %collective-permute-done.21.refs_4_), custom_call_target="tpu_custom_call" | custom-call | tf_op jit(solution)/shard_map/place/pallas_call | solution.py:401
  945.6 13.0 multiply_reduce_fusion
  986.7 50.0 %reduce-scatter.4.cloned.1.call-done = bf16[1,128,2048]{2,1,0:T(8,128)(2,1)} async-done(((bf16[1,1024,2048]{2,1,0:T(8,128)(2,1)}), bf16[1,128,2048]{2,1,0:T(8,128)(2,1)}) %reduce-scatter.4.cloned.1.call-update) | async-done | bytes 524304 | tf_op jit(solution)/shard_map/reduce_scatter | solution.py:373
  1042.4 45.4 %all-gather.7.cloned.1.call-done = bf16[1,1024,2048]{2,1,0:T(8,128)(2,1)} async-done(((bf16[1,128,2048]{2,1,0:T(8,128)(2,1)}), bf16[1,1024,2048]{2,1,0:T(8,128)(2,1)}) %all-gather.7.cloned.1.call-update) | async-done | bytes 4194320 | tf_op jit(solution)/shard_map/all_gather | solution.py:369
  1087.9 11.7 multiply_convert_fusion.1
  1101.6 12.8 convert_bitcast_fusion
  1124.4 9.8 convolution_convert_fusion
  1150.9 58.8 %collective-permute-done.55 = bf16[2,128,2048]{2,1,0:T(8,128)(2,1)S(1)} collective-permute-done((bf16[2,128,2048]{2,1,0:T(8,128)(2,1)S(1)}, bf16[2,128,2048]{2,1,0:T(8,128)(2,1)S(1)}, u32[]{:S(2)}, u32[]{:S(2)}) %collective-permute-start.55) | collective-permute-done | bytes 1048608 | tf_op jit(solution)/shard_map/ppermute | solution.py:377
  1242.8 14.9 %attend_back.1 = (f32[1,1024,256]{2,1,0:T(8,128)}, f32[1,1024,256]{2,1,0:T(8,128)}, bf16[1,1024,256]{2,1,0:T(8,128)(2,1)}, f32[1,8,1024]{2,1,0:T(8,128)}, f32[1,2,256]{2,1,0:T(2,128)}) custom-call(f32[1,1024,768]{2,1,0:T(8,128)} %bitcast.306, f32[1,1024,768]{2,1,0:T(8,128)} %bitcast.307, f32[1,1024,1]{2,1,0:T(8,128)} %copy.50.qinv_ref, ...), custom_call_target="tpu_custom_call" | custom-call | tf_op jit(solution)/shard_map/attend_back/pallas_call | solution.py:661
  1311.3 15.7 %collective-permute-done.49.refs_2_ = bf16[64,2048]{1,0:T(8,128)(2,1)S(1)} collective-permute-done((bf16[64,2048]{1,0:T(8,128)(2,1)S(1)}, bf16[64,2048]{1,0:T(8,128)(2,1)S(1)}, u32[]{:S(2)}, u32[]{:S(2)}) %collective-permute-start.49) | collective-permute-done | bytes 262176 | tf_op jit(solution)/shard_map/ppermute | solution.py:377
  1327.5 11.8 collective-permute-done.50.refs_3_
  1342.3 12.5 collective-permute-done.53.refs_6_
  1366.6 12.5 all-to-all-start.1
  1388.1 13.2 collective-permute-done.29
  (400 shorter events, 302.4 us)
Async XLA Ops:
  7.2 136.2 %all-gather.5.cloned.1.call-start = ((), (), s32[]{:S(2)}) async-start(), calls=%async_computation.5 | async-start | bytes 4718592 | tf_op jit(solution)/shard_map/all_gather | solution.py:369
  7.9 937.6 %all-gather.9.cloned.1.call-start = ((), (), s32[]{:S(2)}) async-start(), calls=%async_computation.10 | async-start | bytes 4718592 | tf_op jit(solution)/shard_map/all_gather | solution.py:763
  174.6 862.1 %reduce-scatter.4.cloned.1.call-start = ((), (), s32[]{:S(2)}) async-start(), calls=%async_computation.6 | async-start | bytes 4718592 | tf_op jit(solution)/shard_map/reduce_scatter | solution.py:373
  183.8 95.6 %collective-permute-start.18 = (bf16[512,2048]{1,0:T(8,128)(2,1)S(1)}, bf16[512,2048]{1,0:T(8,128)(2,1)S(1)}, u32[]{:S(2)}, u32[]{:S(2)}) collective-permute-start(bf16[512,2048]{1,0:T(8,128)(2,1)S(1)} %dynamic-slice_dynamic-update-slice_fusion.refs_0_), channel_id=1, source_target_pairs={{0,8},{8,0},{16,24},{24,16},{1,9},{9,1},{17,25},{25,17},{2,10},{10... | collective-permute-start | bytes 6291464 | tf_op jit(solution)/shard_map/ppermute | solution.py:377
  185.9 104.9 %collective-permute-start.19 = (bf16[512,2048]{1,0:T(8,128)(2,1)S(1)}, bf16[512,2048]{1,0:T(8,128)(2,1)S(1)}, u32[]{:S(2)}, u32[]{:S(2)}) collective-permute-start(bf16[512,2048]{1,0:T(8,128)(2,1)S(1)} %dynamic-slice_dynamic-update-slice_fusion.refs_0_), channel_id=1, source_target_pairs={{0,16},{8,24},{16,0},{24,8},{1,17},{9,25},{17,1},{25,9},{2,18},{10... | collective-permute-start | bytes 6291464 | tf_op jit(solution)/shard_map/ppermute | solution.py:377
  185.9 71.1 %collective-permute-start.11 = (bf16[512,1024]{1,0:T(8,128)(2,1)}, bf16[512,1024]{1,0:T(8,128)(2,1)}, u32[]{:S(2)}, u32[]{:S(2)}) collective-permute-start(bf16[512,1024]{1,0:T(8,128)(2,1)} %constant_dynamic-slice_fusion.14), channel_id=1, source_target_pairs={{0,16},{8,24},{16,0},{24,8},{1,17},{9,25},{17,1},{25,9},{2,18},{10... | collective-permute-start | bytes 3145736 | tf_op jit(solution)/shard_map/ppermute | solution.py:377
  189.2 79.0 %collective-permute-start.22 = (bf16[256,2048]{1,0:T(8,128)(2,1)S(1)}, bf16[256,2048]{1,0:T(8,128)(2,1)S(1)}, u32[]{:S(2)}, u32[]{:S(2)}) collective-permute-start(bf16[256,2048]{1,0:T(8,128)(2,1)S(1)} %constant_dynamic-slice_fusion.13.refs_0_), channel_id=1, source_target_pairs={{0,8},{8,0},{16,24},{24,16},{1,9},{9,1},{17,25},{25,17},{2,10},{10... | collective-permute-start | bytes 3145736 | tf_op jit(solution)/shard_map/ppermute | solution.py:377
  202.1 77.2 %collective-permute-start.23 = (bf16[256,2048]{1,0:T(8,128)(2,1)S(1)}, bf16[256,2048]{1,0:T(8,128)(2,1)S(1)}, u32[]{:S(2)}, u32[]{:S(2)}) collective-permute-start(bf16[256,2048]{1,0:T(8,128)(2,1)S(1)} %constant_dynamic-slice_fusion.13.refs_0_), channel_id=1, source_target_pairs={{0,16},{8,24},{16,0},{24,8},{1,17},{9,25},{17,1},{25,9},{2,18},{10... | collective-permute-start | bytes 3145736 | tf_op jit(solution)/shard_map/ppermute | solution.py:377
  290.7 141.9 %collective-permute-start.15 = (bf16[512,1024]{1,0:T(8,128)(2,1)}, bf16[512,1024]{1,0:T(8,128)(2,1)}, u32[]{:S(2)}, u32[]{:S(2)}) collective-permute-start(bf16[512,1024]{1,0:T(8,128)(2,1)} %collective-permute-done.11.refs_2_), channel_id=1, source_target_pairs={{0,1},{1,0},{2,3},{3,2},{4,5},{5,4},{6,7},{7,6},{8,9},{9,8},{10,11... | collective-permute-start | bytes 3145736 | tf_op jit(solution)/shard_map/ppermute | solution.py:377
  293.1 395.5 %collective-permute-start.20 = (bf16[256,2048]{1,0:T(8,128)(2,1)}, bf16[256,2048]{1,0:T(8,128)(2,1)S(1)}, u32[]{:S(2)}, u32[]{:S(2)}) collective-permute-start(bf16[256,2048]{1,0:T(8,128)(2,1)} %slice.182), channel_id=1, source_target_pairs={{0,16},{8,24},{16,0},{24,8},{1,17},{9,25},{17,1},{25,9},{2,18},{10... | collective-permute-start | bytes 3145736 | tf_op jit(solution)/shard_map/ppermute | solution.py:377
  301.9 386.7 %collective-permute-start.21 = (bf16[256,2048]{1,0:T(8,128)(2,1)}, bf16[256,2048]{1,0:T(8,128)(2,1)}, u32[]{:S(2)}, u32[]{:S(2)}) collective-permute-start(bf16[256,2048]{1,0:T(8,128)(2,1)} %slice.183), channel_id=1, source_target_pairs={{0,8},{8,0},{16,24},{24,16},{1,9},{9,1},{17,25},{25,17},{2,10},{10... | collective-permute-start | bytes 3145736 | tf_op jit(solution)/shard_map/ppermute | solution.py:377
  302.0 130.6 %collective-permute-start.16 = (bf16[256,1024]{1,0:T(8,128)(2,1)}, bf16[256,1024]{1,0:T(8,128)(2,1)}, u32[]{:S(2)}, u32[]{:S(2)}) collective-permute-start(bf16[256,1024]{1,0:T(8,128)(2,1)} %collective-permute-done.12.refs_3_), channel_id=1, source_target_pairs={{0,1},{1,0},{2,3},{3,2},{4,5},{5,4},{6,7},{7,6},{8,9},{9,8},{10,11... | collective-permute-start | bytes 1572872 | tf_op jit(solution)/shard_map/ppermute | solution.py:377
  302.0 130.6 %collective-permute-start.17 = (bf16[256,1024]{1,0:T(8,128)(2,1)}, bf16[256,1024]{1,0:T(8,128)(2,1)}, u32[]{:S(2)}, u32[]{:S(2)}) collective-permute-start(bf16[256,1024]{1,0:T(8,128)(2,1)} %collective-permute-done.13.refs_4_), channel_id=1, source_target_pairs={{0,1},{1,0},{2,3},{3,2},{4,5},{5,4},{6,7},{7,6},{8,9},{9,8},{10,11... | collective-permute-start | bytes 1572872 | tf_op jit(solution)/shard_map/ppermute | solution.py:377
  986.0 101.9 %all-gather.7.cloned.1.call-start = ((), (), s32[]{:S(2)}) async-start(), calls=%async_computation.7 | async-start | bytes 4718592 | tf_op jit(solution)/shard_map/all_gather | solution.py:369
  1042.4 170.1 %reduce-scatter.6.cloned.1.call-start = ((), (), s32[]{:S(2)}) async-start(), calls=%async_computation.8 | async-start | bytes 4718592 | tf_op jit(solution)/shard_map/reduce_scatter | solution.py:373
  1138.6 91.5 %collective-permute-start.44 = (bf16[2,256,2048]{2,1,0:T(8,128)(2,1)}, bf16[2,256,2048]{2,1,0:T(8,128)(2,1)}, u32[]{:S(2)}, u32[]{:S(2)}) collective-permute-start(bf16[2,256,2048]{2,1,0:T(8,128)(2,1)} %pad_maximum_fusion.3), channel_id=1, source_target_pairs={{0,8},{8,0},{16,24},{24,16},{1,9},{9,1},{17,25},{25,17},{2,10},{10... | collective-permute-start | bytes 6291464 | tf_op jit(solution)/shard_map/ppermute | solution.py:377
  1140.1 69.6 %collective-permute-start.55 = (bf16[2,128,2048]{2,1,0:T(8,128)(2,1)S(1)}, bf16[2,128,2048]{2,1,0:T(8,128)(2,1)S(1)}, u32[]{:S(2)}, u32[]{:S(2)}) collective-permute-start(bf16[2,128,2048]{2,1,0:T(8,128)(2,1)S(1)} %pad_maximum_fusion.7), channel_id=1, source_target_pairs={{0,8},{8,0},{16,24},{24,16},{1,9},{9,1},{17,25},{25,17},{2,10},{10... | collective-permute-start | bytes 3145736 | tf_op jit(solution)/shard_map/ppermute | solution.py:377
  1142.3 120.4 %collective-permute-start.46 = (bf16[2,256,2048]{2,1,0:T(8,128)(2,1)}, bf16[2,256,2048]{2,1,0:T(8,128)(2,1)}, u32[]{:S(2)}, u32[]{:S(2)}) collective-permute-start(bf16[2,256,2048]{2,1,0:T(8,128)(2,1)} %pad_maximum_fusion.4), channel_id=1, source_target_pairs={{0,16},{8,24},{16,0},{24,8},{1,17},{9,25},{17,1},{25,9},{2,18},{10... | collective-permute-start | bytes 6291464 | tf_op jit(solution)/shard_map/ppermute | solution.py:377
  1149.5 78.0 %collective-permute-start.58 = (bf16[128,2048]{1,0:T(8,128)(2,1)}, bf16[128,2048]{1,0:T(8,128)(2,1)}, u32[]{:S(2)}, u32[]{:S(2)}) collective-permute-start(bf16[128,2048]{1,0:T(8,128)(2,1)} %fusion.50), channel_id=1, source_target_pairs={{0,8},{8,0},{16,24},{24,16},{1,9},{9,1},{17,25},{25,17},{2,10},{10... | collective-permute-start | bytes 1572872 | tf_op jit(solution)/shard_map/ppermute | solution.py:377
  1211.0 68.0 %collective-permute-start.56 = (bf16[128,2048]{1,0:T(8,128)(2,1)}, bf16[128,2048]{1,0:T(8,128)(2,1)}, u32[]{:S(2)}, u32[]{:S(2)}) collective-permute-start(bf16[128,2048]{1,0:T(8,128)(2,1)} %fusion.49), channel_id=1, source_target_pairs={{0,16},{8,24},{16,0},{24,8},{1,17},{9,25},{17,1},{25,9},{2,18},{10... | collective-permute-start | bytes 1572872 | tf_op jit(solution)/shard_map/ppermute | solution.py:377
  1227.5 224.9 %reduce-scatter.8.cloned.1.call-start = ((), (), s32[]{:S(2)}) async-start(), calls=%async_computation.9 | async-start | bytes 4718592 | tf_op jit(solution)/shard_map/reduce_scatter | solution.py:373
  1308.7 46.1 %collective-permute-start.53 = (bf16[64,2048]{1,0:T(8,128)(2,1)S(1)}, bf16[64,2048]{1,0:T(8,128)(2,1)S(1)}, u32[]{:S(2)}, u32[]{:S(2)}) collective-permute-start(bf16[64,2048]{1,0:T(8,128)(2,1)S(1)} %get-tuple-element.97), channel_id=1, source_target_pairs={{0,6},{1,7},{2,4},{3,5},{4,2},{5,3},{6,0},{7,1},{8,14},{9,15},{10,... | collective-permute-start | bytes 786440 | tf_op jit(solution)/shard_map/ppermute | solution.py:377
  1339.3 45.1 %collective-permute-start.31 = (bf16[2,256,768]{2,1,0:T(8,128)(2,1)}, bf16[2,256,768]{2,1,0:T(8,128)(2,1)S(1)}, u32[]{:S(2)}, u32[]{:S(2)}) collective-permute-start(bf16[2,256,768]{2,1,0:T(8,128)(2,1)} %pad_maximum_fusion.11), channel_id=1, source_target_pairs={{0,16},{8,24},{16,0},{24,8},{1,17},{9,25},{17,1},{25,9},{2,18},{10... | collective-permute-start | bytes 2359304 | tf_op jit(solution)/shard_map/ppermute | solution.py:377
  1382.9 44.0 %collective-permute-start.60 = (f32[1,256]{1,0:T(1,128)S(1)}, f32[1,256]{1,0:T(1,128)S(1)}, u32[]{:S(2)}, u32[]{:S(2)}) collective-permute-start(f32[1,256]{1,0:T(1,128)S(1)} %constant_dynamic-slice_fusion), channel_id=1, source_target_pairs={{0,8},{8,0},{16,24},{24,16},{1,9},{9,1},{17,25},{25,17},{2,10},{10... | collective-permute-start | bytes 3080 | tf_op jit(solution)/shard_map/ppermute | solution.py:377
  (112 other events, 1979.7 us)
Sparse Core Ops, SparseCore 0:
  9.6 49.7 all-gather.4
  174.8 47.1 all-gather.8
  986.1 50.5 reduce-scatter.3
  1042.5 45.3 all-gather.6
  1114.5 48.7 reduce-scatter.5
  1279.1 71.6 reduce-scatter.7

commit v5 on v4

--- a/solution.py
+++ b/solution.py
@@ -397,14 +397,16 @@
 
 def placed(pieces, shape):
     spots = jnp.stack([jnp.int32(at) for _, row, column in pieces for at in (row, column)])
-    anywhere = pl.BlockSpec(memory_space=pl.ANY)
     return pl.pallas_call(
         place_kernel,
         grid_spec=pltpu.PrefetchScalarGridSpec(
             num_scalar_prefetch=1,
             grid=(1,),
-            in_specs=[anywhere] * len(pieces),
-            out_specs=anywhere,
+            in_specs=[
+                pl.BlockSpec(piece.shape, lambda at, spots: (0, 0), pipeline_mode=pl.Buffered(1))
+                for piece, _, _ in pieces
+            ],
+            out_specs=pl.BlockSpec(memory_space=pl.ANY),
             scratch_shapes=[pltpu.SemaphoreType.DMA((len(pieces),))],
         ),
         out_shape=jax.ShapeDtypeStruct(shape, pieces[0][0].dtype),

time: 1480 us -> 773 us (0.52)
  Pallas kernels: 771 us -> 57.1 us
    pallas_call x4, Pallas kernels: 738 us -> 24.1 us  [placed(): pl.pallas_call(place_kernel, grid_spec=pltpu.PrefetchScalarGridSpec(num_s...]
  transfers between devices with their start and end apart: 69 -> 69, of which waited for: 32 -> 36; matrix products, arithmetic and copies ran while one was open for 8% -> 15% of each run, Pallas kernels for 52% -> 6%
where the time goes in v5:
time: 773 us; the launch traced here: 759 us
  waiting for transfers between devices  397 us (51%)
  matrix products  94.7 us (12%)
  starting transfers between devices  87.1 us (11%)
  local copies, waits for them, and re-layouts  57.1 us (7%)
  Pallas kernels  57.1 us (7%)
  other arithmetic  50.6 us (7%)
  between operations  16 us (2%)
    ppermute x61, waiting for transfers between devices, swap(): lax.ppermute(value, axis, [(at, at ^ flip) for at in range(lax.axis_size(...  285 us
    ppermute x61, starting transfers between devices, swap(): lax.ppermute(value, axis, [(at, at ^ flip) for at in range(lax.axis_size(...  70.2 us
    all_gather x2, waiting for transfers between devices, gather_seq(): return lax.all_gather(piece, 'seq', axis=1, tiled=True)  54.3 us
    reduce_scatter x3, waiting for transfers between devices, scatter_seq(): return lax.psum_scatter(partial, 'seq', scatter_dimension=1, tiled=True)  48.2 us
    unnamed x141, local copies, waits for them, and re-layouts  26.1 us
    pallas_call x4, Pallas kernels, placed(): pl.pallas_call(place_kernel, grid_spec=pltpu.PrefetchScalarGridSpec(num_s...  24.1 us
    all_to_all x2, starting transfers between devices, own_columns_of_all(): lax.all_to_all(split.reshape(seq_count, tok_count, width), 'seq', split_a...  16.6 us
  transfers between devices with their start and end apart: 69, of which 36 were waited for; matrix products, arithmetic and copies ran while one was open for 15% of the time, Pallas kernels for 6%

profile of v5, /device:TPU:0, one launch (start us, length us, event | category | flops | bytes accessed | tf_op | source)
XLA Modules:
  0.0 759.3 jit_solution(3703123400851684523)
XLA Ops:
  14.5 16.0 %collective-permute-done.3.refs_1_ = bf16[512,768]{1,0:T(8,128)(2,1)S(1)} collective-permute-done((bf16[512,768]{1,0:T(8,128)(2,1)S(1)}, bf16[512,768]{1,0:T(8,128)(2,1)S(1)}, u32[]{:S(2)}, u32[]{:S(2)}) %collective-permute-start.3) | collective-permute-done | bytes 786464 | tf_op jit(solution)/shard_map/ppermute | solution.py:377
  50.5 8.9 %all-gather.5.cloned.1.call-done = bf16[1,1024,2048]{2,1,0:T(8,128)(2,1)} async-done(((bf16[1,128,2048]{2,1,0:T(8,128)(2,1)}), bf16[1,1024,2048]{2,1,0:T(8,128)(2,1)}) %all-gather.5.cloned.1.call-update) | async-done | bytes 4194320 | tf_op jit(solution)/shard_map/all_gather | solution.py:369
  79.1 10.5 %attend.1 = (bf16[1,1024,256]{2,1,0:T(8,128)(2,1)}, bf16[1,1024,256]{2,1,0:T(8,128)(2,1)}, bf16[1,1024,256]{2,1,0:T(8,128)(2,1)}, bf16[1,1024,256]{2,1,0:T(8,128)(2,1)}, f32[1,2,1024,1]{3,2,1,0:T(8,128)}) custom-call(f32[1,1024,768]{2,1,0:T(8,128)} %bitcast.303, f32[1,1024,768]{2,1,0:T(8,128)} %bitcast.304, f32[1,1024,768]{2,1,0:T(8,128)} %bitcast.305, ...), custom_call_target="tpu_custom_call" | custom-call | tf_op jit(solution)/shard_map/attend/pallas_call | solution.py:648
  105.7 11.4 %collective-permute-done.10.refs_1_ = bf16[512,1024]{1,0:T(8,128)(2,1)} collective-permute-done((bf16[512,1024]{1,0:T(8,128)(2,1)}, bf16[512,1024]{1,0:T(8,128)(2,1)}, u32[]{:S(2)}, u32[]{:S(2)}) %collective-permute-start.10) | collective-permute-done | bytes 1048608 | tf_op jit(solution)/shard_map/ppermute | solution.py:377
  119.7 52.2 %collective-permute-done.11.refs_2_ = bf16[512,1024]{1,0:T(8,128)(2,1)} collective-permute-done((bf16[512,1024]{1,0:T(8,128)(2,1)}, bf16[512,1024]{1,0:T(8,128)(2,1)}, u32[]{:S(2)}, u32[]{:S(2)}) %collective-permute-start.11) | collective-permute-done | bytes 1048608 | tf_op jit(solution)/shard_map/ppermute | solution.py:377
  181.5 12.7 %collective-permute-done.23.refs_2_ = bf16[256,2048]{1,0:T(8,128)(2,1)S(1)} collective-permute-done((bf16[256,2048]{1,0:T(8,128)(2,1)S(1)}, bf16[256,2048]{1,0:T(8,128)(2,1)S(1)}, u32[]{:S(2)}, u32[]{:S(2)}) %collective-permute-start.23) | collective-permute-done | bytes 1048608 | tf_op jit(solution)/shard_map/ppermute | solution.py:377
  224.2 7.5 place.5
  244.8 13.0 %multiply_reduce_fusion = (f32[1024]{0:T(1024)S(1)}, f32[1024,2048]{1,0:T(8,128)S(1)}) fusion(bf16[2048,2048]{1,0:T(8,128)(2,1)} %place.5, bf16[1,1024,2048]{2,1,0:T(8,128)(2,1)} %all-gather.9.cloned.1.call-done), kind=kOutput, calls=%fused_computation.1 | convolution fusion | flops 8594127872 | bytes 20975616 | tf_op jit(solution)/shard_map/dot_general | solution.py:766
  264.5 8.9 %fusion.76 = f32[1024,2048]{1,0:T(8,128)S(1)} fusion(bf16[1024,2048]{1,0:T(8,128)(2,1)S(1)} %add_convert_fusion, bf16[2048,2048]{1,0:T(8,128)(2,1)S(1)} %copy-done.8), kind=kOutput, calls=%fused_computation.238 | convolution fusion | flops 8589934592 | bytes 20971520 | tf_op jit(solution)/shard_map/dot_general | solution.py:774
  286.0 48.1 %reduce-scatter.4.cloned.1.call-done = bf16[1,128,2048]{2,1,0:T(8,128)(2,1)} async-done(((bf16[1,1024,2048]{2,1,0:T(8,128)(2,1)}), bf16[1,128,2048]{2,1,0:T(8,128)(2,1)}) %reduce-scatter.4.cloned.1.call-update) | async-done | bytes 524304 | tf_op jit(solution)/shard_map/reduce_scatter | solution.py:373
  339.8 45.4 %all-gather.7.cloned.1.call-done = bf16[1,1024,2048]{2,1,0:T(8,128)(2,1)} async-done(((bf16[1,128,2048]{2,1,0:T(8,128)(2,1)}), bf16[1,1024,2048]{2,1,0:T(8,128)(2,1)}) %all-gather.7.cloned.1.call-update) | async-done | bytes 4194320 | tf_op jit(solution)/shard_map/all_gather | solution.py:369
  385.3 11.7 %multiply_convert_fusion.1 = (bf16[1024,1024]{1,0:T(8,128)(2,1)S(1)}, bf16[1024,1024]{1,0:T(8,128)(2,1)S(1)}) fusion(f32[1024,2048]{1,0:T(8,128)} %copy-done.9, bf16[1024,2048]{1,0:T(8,128)(2,1)} %place.7, bf16[1,1024,2048]{2,1,0:T(8,128)(2,1)} %all-gather.7.cloned.1.call-done), kind=kOutput, calls=%fused_computation.16 | convolution fusion | flops 4308598784 | bytes 20971520 | tf_op jit(solution)/shard_map/nd,fd->nf/dot_general | solution.py:797
  398.9 12.8 %convert_bitcast_fusion = bf16[1,1024,2048]{2,1,0:T(8,128)(2,1)} fusion(bf16[2048,2048]{1,0:T(8,128)(2,1)} %place.6, bf16[1024,1024]{1,0:T(8,128)(2,1)S(1)} %get-tuple-element.64, bf16[1024,1024]{1,0:T(8,128)(2,1)S(1)} %get-tuple-element.63), kind=kOutput, calls=%fused_computation.14 | convolution fusion | flops 8600420352 | bytes 16777216 | tf_op jit(solution)/shard_map/nf,df->nd/dot_general | solution.py:801
  421.8 9.8 %convolution_convert_fusion = bf16[2048,2048]{1,0:T(8,128)(2,1)S(1)} fusion(bf16[1024,2048]{1,0:T(8,128)(2,1)S(1)} %copy-done.22, bf16[1024,1024]{1,0:T(8,128)(2,1)} %copy-done.65, bf16[1024,1024]{1,0:T(8,128)(2,1)S(1)} %copy-done.64), kind=kOutput, calls=%fused_computation.2 | convolution fusion | flops 8602517504 | bytes 16777216 | tf_op jit(solution)/shard_map/nd,nf->df/dot_general | solution.py:803
  448.3 58.8 %collective-permute-done.55 = bf16[2,128,2048]{2,1,0:T(8,128)(2,1)S(1)} collective-permute-done((bf16[2,128,2048]{2,1,0:T(8,128)(2,1)S(1)}, bf16[2,128,2048]{2,1,0:T(8,128)(2,1)S(1)}, u32[]{:S(2)}, u32[]{:S(2)}) %collective-permute-start.55) | collective-permute-done | bytes 1048608 | tf_op jit(solution)/shard_map/ppermute | solution.py:377
  531.9 8.3 %all-to-all-done = bf16[8,128,256]{2,1,0:T(8,128)(2,1)} async-done(((bf16[8,128,256]{2,1,0:T(8,128)(2,1)}), bf16[8,128,256]{2,1,0:T(8,128)(2,1)}, u32[]{:S(2)}, u32[]{:S(2)}) %all-to-all-start) | async-done | bytes 524320 | tf_op jit(solution)/shard_map/all_to_all | solution.py:816
  540.2 14.9 %attend_back.1 = (f32[1,1024,256]{2,1,0:T(8,128)}, f32[1,1024,256]{2,1,0:T(8,128)}, bf16[1,1024,256]{2,1,0:T(8,128)(2,1)}, f32[1,8,1024]{2,1,0:T(8,128)}, f32[1,2,256]{2,1,0:T(2,128)}) custom-call(f32[1,1024,768]{2,1,0:T(8,128)} %bitcast.306, f32[1,1024,768]{2,1,0:T(8,128)} %bitcast.307, f32[1,1024,1]{2,1,0:T(8,128)} %copy.50.qinv_ref, ...), custom_call_target="tpu_custom_call" | custom-call | tf_op jit(solution)/shard_map/attend_back/pallas_call | solution.py:663
  577.7 7.5 collective-permute-done.45
  608.7 15.7 %collective-permute-done.49.refs_2_ = bf16[64,2048]{1,0:T(8,128)(2,1)S(1)} collective-permute-done((bf16[64,2048]{1,0:T(8,128)(2,1)S(1)}, bf16[64,2048]{1,0:T(8,128)(2,1)S(1)}, u32[]{:S(2)}, u32[]{:S(2)}) %collective-permute-start.49) | collective-permute-done | bytes 262176 | tf_op jit(solution)/shard_map/ppermute | solution.py:377
  624.8 11.8 %collective-permute-done.50.refs_3_ = bf16[64,2048]{1,0:T(8,128)(2,1)S(1)} collective-permute-done((bf16[64,2048]{1,0:T(8,128)(2,1)S(1)}, bf16[64,2048]{1,0:T(8,128)(2,1)S(1)}, u32[]{:S(2)}, u32[]{:S(2)}) %collective-permute-start.50) | collective-permute-done | bytes 262176 | tf_op jit(solution)/shard_map/ppermute | solution.py:377
  639.7 12.5 %collective-permute-done.53.refs_6_ = bf16[64,2048]{1,0:T(8,128)(2,1)S(1)} collective-permute-done((bf16[64,2048]{1,0:T(8,128)(2,1)S(1)}, bf16[64,2048]{1,0:T(8,128)(2,1)S(1)}, u32[]{:S(2)}, u32[]{:S(2)}) %collective-permute-start.53) | collective-permute-done | bytes 262176 | tf_op jit(solution)/shard_map/ppermute | solution.py:377
  664.0 12.5 %all-to-all-start.1 = ((bf16[8,128,256]{2,1,0:T(8,128)(2,1)}), bf16[8,128,256]{2,1,0:T(8,128)(2,1)S(1)}, u32[]{:S(2)}, u32[]{:S(2)}) async-start(bf16[8,128,256]{2,1,0:T(8,128)(2,1)} %bitcast.301), calls=%async_computation.4 | async-start | bytes 1048576 | tf_op jit(solution)/shard_map/all_to_all | solution.py:816
  685.5 13.2 %collective-permute-done.29 = bf16[2,256,768]{2,1,0:T(8,128)(2,1)S(1)} collective-permute-done((bf16[2,256,768]{2,1,0:T(8,128)(2,1)S(1)}, bf16[2,256,768]{2,1,0:T(8,128)(2,1)S(1)}, u32[]{:S(2)}, u32[]{:S(2)}) %collective-permute-start.29) | collective-permute-done | bytes 786464 | tf_op jit(solution)/shard_map/ppermute | solution.py:377
  735.8 9.1 %collective-permute-done.41.refs_5_ = bf16[64,1024]{1,0:T(8,128)(2,1)S(1)} collective-permute-done((bf16[64,1024]{1,0:T(8,128)(2,1)S(1)}, bf16[64,1024]{1,0:T(8,128)(2,1)S(1)}, u32[]{:S(2)}, u32[]{:S(2)}) %collective-permute-start.41) | collective-permute-done | bytes 131104 | tf_op jit(solution)/shard_map/ppermute | solution.py:377
  (400 shorter events, 310.1 us)
Async XLA Ops:
  7.2 52.2 %all-gather.5.cloned.1.call-start = ((), (), s32[]{:S(2)}) async-start(), calls=%async_computation.5 | async-start | bytes 4718592 | tf_op jit(solution)/shard_map/all_gather | solution.py:369
  7.9 236.9 %all-gather.9.cloned.1.call-start = ((), (), s32[]{:S(2)}) async-start(), calls=%async_computation.10 | async-start | bytes 4718592 | tf_op jit(solution)/shard_map/all_gather | solution.py:765
  89.6 244.5 %reduce-scatter.4.cloned.1.call-start = ((), (), s32[]{:S(2)}) async-start(), calls=%async_computation.6 | async-start | bytes 4718592 | tf_op jit(solution)/shard_map/reduce_scatter | solution.py:373
  100.2 95.5 %collective-permute-start.18 = (bf16[512,2048]{1,0:T(8,128)(2,1)S(1)}, bf16[512,2048]{1,0:T(8,128)(2,1)S(1)}, u32[]{:S(2)}, u32[]{:S(2)}) collective-permute-start(bf16[512,2048]{1,0:T(8,128)(2,1)S(1)} %dynamic-slice_dynamic-update-slice_fusion.refs_0_), channel_id=1, source_target_pairs={{0,8},{8,0},{16,24},{24,16},{1,9},{9,1},{17,25},{25,17},{2,10},{10... | collective-permute-start | bytes 6291464 | tf_op jit(solution)/shard_map/ppermute | solution.py:377
  100.8 106.3 %collective-permute-start.19 = (bf16[512,2048]{1,0:T(8,128)(2,1)S(1)}, bf16[512,2048]{1,0:T(8,128)(2,1)S(1)}, u32[]{:S(2)}, u32[]{:S(2)}) collective-permute-start(bf16[512,2048]{1,0:T(8,128)(2,1)S(1)} %dynamic-slice_dynamic-update-slice_fusion.refs_0_), channel_id=1, source_target_pairs={{0,16},{8,24},{16,0},{24,8},{1,17},{9,25},{17,1},{25,9},{2,18},{10... | collective-permute-start | bytes 6291464 | tf_op jit(solution)/shard_map/ppermute | solution.py:377
  102.3 69.6 %collective-permute-start.11 = (bf16[512,1024]{1,0:T(8,128)(2,1)}, bf16[512,1024]{1,0:T(8,128)(2,1)}, u32[]{:S(2)}, u32[]{:S(2)}) collective-permute-start(bf16[512,1024]{1,0:T(8,128)(2,1)} %constant_dynamic-slice_fusion.14), channel_id=1, source_target_pairs={{0,16},{8,24},{16,0},{24,8},{1,17},{9,25},{17,1},{25,9},{2,18},{10... | collective-permute-start | bytes 3145736 | tf_op jit(solution)/shard_map/ppermute | solution.py:377
  104.1 77.3 %collective-permute-start.22 = (bf16[256,2048]{1,0:T(8,128)(2,1)S(1)}, bf16[256,2048]{1,0:T(8,128)(2,1)S(1)}, u32[]{:S(2)}, u32[]{:S(2)}) collective-permute-start(bf16[256,2048]{1,0:T(8,128)(2,1)S(1)} %constant_dynamic-slice_fusion.13.refs_0_), channel_id=1, source_target_pairs={{0,8},{8,0},{16,24},{24,16},{1,9},{9,1},{17,25},{25,17},{2,10},{10... | collective-permute-start | bytes 3145736 | tf_op jit(solution)/shard_map/ppermute | solution.py:377
  117.1 77.1 %collective-permute-start.23 = (bf16[256,2048]{1,0:T(8,128)(2,1)S(1)}, bf16[256,2048]{1,0:T(8,128)(2,1)S(1)}, u32[]{:S(2)}, u32[]{:S(2)}) collective-permute-start(bf16[256,2048]{1,0:T(8,128)(2,1)S(1)} %constant_dynamic-slice_fusion.13.refs_0_), channel_id=1, source_target_pairs={{0,16},{8,24},{16,0},{24,8},{1,17},{9,25},{17,1},{25,9},{2,18},{10... | collective-permute-start | bytes 3145736 | tf_op jit(solution)/shard_map/ppermute | solution.py:377
  181.4 36.0 %collective-permute-start.14 = (bf16[512,1024]{1,0:T(8,128)(2,1)}, bf16[512,1024]{1,0:T(8,128)(2,1)}, u32[]{:S(2)}, u32[]{:S(2)}) collective-permute-start(bf16[512,1024]{1,0:T(8,128)(2,1)} %collective-permute-done.10.refs_1_), channel_id=1, source_target_pairs={{0,1},{1,0},{2,3},{3,2},{4,5},{5,4},{6,7},{7,6},{8,9},{9,8},{10,11... | collective-permute-start | bytes 3145736 | tf_op jit(solution)/shard_map/ppermute | solution.py:377
  285.2 100.0 %all-gather.7.cloned.1.call-start = ((), (), s32[]{:S(2)}) async-start(), calls=%async_computation.7 | async-start | bytes 4718592 | tf_op jit(solution)/shard_map/all_gather | solution.py:369
  339.8 170.1 %reduce-scatter.6.cloned.1.call-start = ((), (), s32[]{:S(2)}) async-start(), calls=%async_computation.8 | async-start | bytes 4718592 | tf_op jit(solution)/shard_map/reduce_scatter | solution.py:373
  435.9 91.6 %collective-permute-start.44 = (bf16[2,256,2048]{2,1,0:T(8,128)(2,1)}, bf16[2,256,2048]{2,1,0:T(8,128)(2,1)}, u32[]{:S(2)}, u32[]{:S(2)}) collective-permute-start(bf16[2,256,2048]{2,1,0:T(8,128)(2,1)} %pad_maximum_fusion.3), channel_id=1, source_target_pairs={{0,8},{8,0},{16,24},{24,16},{1,9},{9,1},{17,25},{25,17},{2,10},{10... | collective-permute-start | bytes 6291464 | tf_op jit(solution)/shard_map/ppermute | solution.py:377
  437.5 69.6 %collective-permute-start.55 = (bf16[2,128,2048]{2,1,0:T(8,128)(2,1)S(1)}, bf16[2,128,2048]{2,1,0:T(8,128)(2,1)S(1)}, u32[]{:S(2)}, u32[]{:S(2)}) collective-permute-start(bf16[2,128,2048]{2,1,0:T(8,128)(2,1)S(1)} %pad_maximum_fusion.7), channel_id=1, source_target_pairs={{0,8},{8,0},{16,24},{24,16},{1,9},{9,1},{17,25},{25,17},{2,10},{10... | collective-permute-start | bytes 3145736 | tf_op jit(solution)/shard_map/ppermute | solution.py:377
  439.6 120.4 %collective-permute-start.46 = (bf16[2,256,2048]{2,1,0:T(8,128)(2,1)}, bf16[2,256,2048]{2,1,0:T(8,128)(2,1)}, u32[]{:S(2)}, u32[]{:S(2)}) collective-permute-start(bf16[2,256,2048]{2,1,0:T(8,128)(2,1)} %pad_maximum_fusion.4), channel_id=1, source_target_pairs={{0,16},{8,24},{16,0},{24,8},{1,17},{9,25},{17,1},{25,9},{2,18},{10... | collective-permute-start | bytes 6291464 | tf_op jit(solution)/shard_map/ppermute | solution.py:377
  446.9 78.1 %collective-permute-start.58 = (bf16[128,2048]{1,0:T(8,128)(2,1)}, bf16[128,2048]{1,0:T(8,128)(2,1)}, u32[]{:S(2)}, u32[]{:S(2)}) collective-permute-start(bf16[128,2048]{1,0:T(8,128)(2,1)} %fusion.50), channel_id=1, source_target_pairs={{0,8},{8,0},{16,24},{24,16},{1,9},{9,1},{17,25},{25,17},{2,10},{10... | collective-permute-start | bytes 1572872 | tf_op jit(solution)/shard_map/ppermute | solution.py:377
  508.4 68.0 %collective-permute-start.56 = (bf16[128,2048]{1,0:T(8,128)(2,1)}, bf16[128,2048]{1,0:T(8,128)(2,1)}, u32[]{:S(2)}, u32[]{:S(2)}) collective-permute-start(bf16[128,2048]{1,0:T(8,128)(2,1)} %fusion.49), channel_id=1, source_target_pairs={{0,16},{8,24},{16,0},{24,8},{1,17},{9,25},{17,1},{25,9},{2,18},{10... | collective-permute-start | bytes 1572872 | tf_op jit(solution)/shard_map/ppermute | solution.py:377
  524.9 224.9 %reduce-scatter.8.cloned.1.call-start = ((), (), s32[]{:S(2)}) async-start(), calls=%async_computation.9 | async-start | bytes 4718592 | tf_op jit(solution)/shard_map/reduce_scatter | solution.py:373
  595.9 40.8 %collective-permute-start.50 = (bf16[64,2048]{1,0:T(8,128)(2,1)S(1)}, bf16[64,2048]{1,0:T(8,128)(2,1)S(1)}, u32[]{:S(2)}, u32[]{:S(2)}) collective-permute-start(bf16[64,2048]{1,0:T(8,128)(2,1)S(1)} %get-tuple-element.95), channel_id=1, source_target_pairs={{0,3},{1,2},{2,1},{3,0},{4,7},{5,6},{6,5},{7,4},{8,11},{9,10},{10,... | collective-permute-start | bytes 786440 | tf_op jit(solution)/shard_map/ppermute | solution.py:377
  597.1 42.6 %collective-permute-start.51 = (bf16[64,2048]{1,0:T(8,128)(2,1)S(1)}, bf16[64,2048]{1,0:T(8,128)(2,1)S(1)}, u32[]{:S(2)}, u32[]{:S(2)}) collective-permute-start(bf16[64,2048]{1,0:T(8,128)(2,1)S(1)} %get-tuple-element.96), channel_id=1, source_target_pairs={{0,4},{1,5},{2,6},{3,7},{4,0},{5,1},{6,2},{7,3},{8,12},{9,13},{10,... | collective-permute-start | bytes 786440 | tf_op jit(solution)/shard_map/ppermute | solution.py:377
  598.8 40.9 %collective-permute-start.52 = (bf16[64,2048]{1,0:T(8,128)(2,1)S(1)}, bf16[64,2048]{1,0:T(8,128)(2,1)S(1)}, u32[]{:S(2)}, u32[]{:S(2)}) collective-permute-start(bf16[64,2048]{1,0:T(8,128)(2,1)S(1)} %get-tuple-element.98), channel_id=1, source_target_pairs={{0,5},{1,4},{2,7},{3,6},{4,1},{5,0},{6,3},{7,2},{8,13},{9,12},{10,... | collective-permute-start | bytes 786440 | tf_op jit(solution)/shard_map/ppermute | solution.py:377
  606.1 46.1 %collective-permute-start.53 = (bf16[64,2048]{1,0:T(8,128)(2,1)S(1)}, bf16[64,2048]{1,0:T(8,128)(2,1)S(1)}, u32[]{:S(2)}, u32[]{:S(2)}) collective-permute-start(bf16[64,2048]{1,0:T(8,128)(2,1)S(1)} %get-tuple-element.97), channel_id=1, source_target_pairs={{0,6},{1,7},{2,4},{3,5},{4,2},{5,3},{6,0},{7,1},{8,14},{9,15},{10,... | collective-permute-start | bytes 786440 | tf_op jit(solution)/shard_map/ppermute | solution.py:377
  636.7 45.1 %collective-permute-start.31 = (bf16[2,256,768]{2,1,0:T(8,128)(2,1)}, bf16[2,256,768]{2,1,0:T(8,128)(2,1)S(1)}, u32[]{:S(2)}, u32[]{:S(2)}) collective-permute-start(bf16[2,256,768]{2,1,0:T(8,128)(2,1)} %pad_maximum_fusion.11), channel_id=1, source_target_pairs={{0,16},{8,24},{16,0},{24,8},{1,17},{9,25},{17,1},{25,9},{2,18},{10... | collective-permute-start | bytes 2359304 | tf_op jit(solution)/shard_map/ppermute | solution.py:377
  664.0 36.0 %all-to-all-start.1 = ((bf16[8,128,256]{2,1,0:T(8,128)(2,1)}), bf16[8,128,256]{2,1,0:T(8,128)(2,1)S(1)}, u32[]{:S(2)}, u32[]{:S(2)}) async-start(bf16[8,128,256]{2,1,0:T(8,128)(2,1)} %bitcast.301), calls=%async_computation.4 | async-start | bytes 1048576 | tf_op jit(solution)/shard_map/all_to_all | solution.py:816
  680.3 44.0 %collective-permute-start.60 = (f32[1,256]{1,0:T(1,128)S(1)}, f32[1,256]{1,0:T(1,128)S(1)}, u32[]{:S(2)}, u32[]{:S(2)}) collective-permute-start(f32[1,256]{1,0:T(1,128)S(1)} %constant_dynamic-slice_fusion), channel_id=1, source_target_pairs={{0,8},{8,0},{16,24},{24,16},{1,9},{9,1},{17,25},{25,17},{2,10},{10... | collective-permute-start | bytes 3080 | tf_op jit(solution)/shard_map/ppermute | solution.py:377
  (112 other events, 1654.8 us)
Sparse Core Ops, SparseCore 0:
  9.6 49.7 all-gather.4
  89.7 46.6 all-gather.8
  285.4 48.7 reduce-scatter.3
  339.9 45.3 all-gather.6
  411.9 48.7 reduce-scatter.5
  576.5 71.6 reduce-scatter.7

commit v6 on v5

--- a/solution.py
+++ b/solution.py
@@ -4,6 +4,7 @@
 import jax.numpy as jnp
 from jax import lax
 from jax.experimental import pallas as pl
+from jax.experimental.layout import Layout, with_layout_constraint
 from jax.experimental.pallas import tpu as pltpu
 from jax.sharding import PartitionSpec as P
 
@@ -475,6 +476,11 @@
     return sent, kept
 
 
+def stored_turned(matrix, after):
+    matrix, after = lax.optimization_barrier((matrix, after))
+    return with_layout_constraint(matrix.T, Layout((0, 1))), after
+
+
 def total_seq(value):
     shape = value.shape
     value = value.reshape(-1, LANES)
@@ -777,6 +783,8 @@
     active = gate * sigma
     inner_low = (active * up_proj).astype(low)
     branch_part = jnp.dot(inner_low, w_back, preferred_element_type=jnp.float32).astype(low)
+    w_hidden_turned, branch_part = stored_turned(w_hidden, branch_part)
+    w_back_turned, branch_part = stored_turned(w_back, branch_part)
     branch = (
         scatter_seq(branch_part.reshape(row_count, row_len, model_width))
         .astype(jnp.float32)
@@ -794,11 +802,11 @@
     ffn_gain_term = jnp.sum(grad_out * branch_unit, 0)
     d_branch = norm_back(grad_out * gain_ffn, branch_unit, branch_inv).astype(low)
     d_branch_all = gather_seq(d_branch.reshape(row_count, piece_len, model_width)).reshape(all_count, model_width)
-    d_inner = jnp.einsum("nd,fd->nf", d_branch_all, w_back, preferred_element_type=jnp.float32)
+    d_inner = jnp.dot(d_branch_all, w_back_turned, preferred_element_type=jnp.float32)
     d_gate = (d_inner * up_proj * sigma * (1.0 + gate * (1.0 - sigma))).astype(low)
     d_up = (d_inner * active).astype(low)
     d_gate_up = jnp.concatenate([d_gate, d_up], 1)
-    d_hidden_part = jnp.einsum("nf,df->nd", d_gate_up, w_hidden, preferred_element_type=jnp.float32).astype(low)
+    d_hidden_part = jnp.dot(d_gate_up, w_hidden_turned, preferred_element_type=jnp.float32).astype(low)
     d_hidden_sum = scatter_seq(d_hidden_part.reshape(row_count, row_len, model_width))
     hidden_part = jnp.einsum("nd,nf->df", hidden_low, d_gate_up, preferred_element_type=jnp.float32).astype(low)
     down_part = jnp.einsum("nf,nd->fd", inner_low, d_branch_all, preferred_element_type=jnp.float32).astype(low)

time: 773 us -> 749 us (0.969)
  waiting for transfers between devices: 397 us -> 358 us
  local copies, waits for them, and re-layouts: 57.1 us -> 77.9 us
    optimization_barrier x0 -> x2, local copies, waits for them, and re-layouts: none -> 19 us  [stored_turned(): matrix, after = lax.optimization_barrier((matrix, after))]
    all_gather x2, waiting for transfers between devices: 54.3 us -> 35.4 us  [gather_seq(): return lax.all_gather(piece, 'seq', axis=1, tiled=True)]
    ppermute x61, waiting for transfers between devices: 285 us -> 273 us  [swap(): lax.ppermute(value, axis, [(at, at ^ flip) for at in range(lax.axis_size(...]
    all_to_all x2, waiting for transfers between devices: 8.3 us -> 0.01 us  [own_columns_of_all(): lax.all_to_all(split.reshape(seq_count, tok_count, width), 'seq', split_a...]
    unnamed x141 -> x153, local copies, waits for them, and re-layouts: 26.1 us -> 28 us
  transfers between devices with their start and end apart: 69 -> 69, of which waited for: 36 -> 37; matrix products, arithmetic and copies ran while one was open for 15% -> 18% of each run, Pallas kernels for 6% -> 6%
where the time goes in v6:
time: 749 us; the launch traced here: 735 us
  waiting for transfers between devices  358 us (48%)
  matrix products  92.6 us (12%)
  starting transfers between devices  82.3 us (11%)
  local copies, waits for them, and re-layouts  77.9 us (10%)
  Pallas kernels  57.1 us (8%)
  other arithmetic  51.8 us (7%)
  between operations  15.8 us (2%)
    ppermute x61, waiting for transfers between devices, swap(): lax.ppermute(value, axis, [(at, at ^ flip) for at in range(lax.axis_size(...  273 us
    ppermute x61, starting transfers between devices, swap(): lax.ppermute(value, axis, [(at, at ^ flip) for at in range(lax.axis_size(...  67.2 us
    reduce_scatter x3, waiting for transfers between devices, scatter_seq(): return lax.psum_scatter(partial, 'seq', scatter_dimension=1, tiled=True)  48.2 us
    all_gather x2, waiting for transfers between devices, gather_seq(): return lax.all_gather(piece, 'seq', axis=1, tiled=True)  35.4 us
    unnamed x153, local copies, waits for them, and re-layouts  28 us
    pallas_call x4, Pallas kernels, placed(): pl.pallas_call(place_kernel, grid_spec=pltpu.PrefetchScalarGridSpec(num_s...  24 us
    optimization_barrier x2, local copies, waits for them, and re-layouts, stored_turned(): matrix, after = lax.optimization_barrier((matrix, after))  19 us
    pallas_call x1, Pallas kernels, attend_back(): pl.pallas_call(functools.partial(attend_back_kernel, scale=scale), grid=(...  15 us
  transfers between devices with their start and end apart: 69, of which 37 were waited for; matrix products, arithmetic and copies ran while one was open for 18% of the time, Pallas kernels for 6%

profile of v6, /device:TPU:0, one launch (start us, length us, event | category | flops | bytes accessed | tf_op | source)
XLA Modules:
  0.0 735.2 jit_solution(17736626578292462129)
XLA Ops:
  14.5 16.0 %collective-permute-done.3.refs_1_ = bf16[512,768]{1,0:T(8,128)(2,1)S(1)} collective-permute-done((bf16[512,768]{1,0:T(8,128)(2,1)S(1)}, bf16[512,768]{1,0:T(8,128)(2,1)S(1)}, u32[]{:S(2)}, u32[]{:S(2)}) %collective-permute-start.3) | collective-permute-done | bytes 786464 | tf_op jit(solution)/shard_map/ppermute | solution.py:378
  50.5 8.9 %all-gather.5.cloned.1.call-done = bf16[1,1024,2048]{2,1,0:T(8,128)(2,1)} async-done(((bf16[1,128,2048]{2,1,0:T(8,128)(2,1)}), bf16[1,1024,2048]{2,1,0:T(8,128)(2,1)}) %all-gather.5.cloned.1.call-update) | async-done | bytes 4194320 | tf_op jit(solution)/shard_map/all_gather | solution.py:370
  79.1 10.5 %attend.1 = (bf16[1,1024,256]{2,1,0:T(8,128)(2,1)}, bf16[1,1024,256]{2,1,0:T(8,128)(2,1)}, bf16[1,1024,256]{2,1,0:T(8,128)(2,1)}, bf16[1,1024,256]{2,1,0:T(8,128)(2,1)}, f32[1,2,1024,1]{3,2,1,0:T(8,128)}) custom-call(f32[1,1024,768]{2,1,0:T(8,128)} %bitcast.310, f32[1,1024,768]{2,1,0:T(8,128)} %bitcast.311, f32[1,1024,768]{2,1,0:T(8,128)} %bitcast.312, ...), custom_call_target="tpu_custom_call" | custom-call | tf_op jit(solution)/shard_map/attend/pallas_call | solution.py:654
  105.7 11.4 %collective-permute-done.10.refs_1_ = bf16[512,1024]{1,0:T(8,128)(2,1)} collective-permute-done((bf16[512,1024]{1,0:T(8,128)(2,1)}, bf16[512,1024]{1,0:T(8,128)(2,1)}, u32[]{:S(2)}, u32[]{:S(2)}) %collective-permute-start.10) | collective-permute-done | bytes 1048608 | tf_op jit(solution)/shard_map/ppermute | solution.py:378
  119.7 52.2 %collective-permute-done.11.refs_2_ = bf16[512,1024]{1,0:T(8,128)(2,1)} collective-permute-done((bf16[512,1024]{1,0:T(8,128)(2,1)}, bf16[512,1024]{1,0:T(8,128)(2,1)}, u32[]{:S(2)}, u32[]{:S(2)}) %collective-permute-start.11) | collective-permute-done | bytes 1048608 | tf_op jit(solution)/shard_map/ppermute | solution.py:378
  183.2 11.0 %collective-permute-done.19.refs_2_ = bf16[256,2048]{1,0:T(8,128)(2,1)S(1)} collective-permute-done((bf16[256,2048]{1,0:T(8,128)(2,1)S(1)}, bf16[256,2048]{1,0:T(8,128)(2,1)S(1)}, u32[]{:S(2)}, u32[]{:S(2)}) %collective-permute-start.19) | collective-permute-done | bytes 1048608 | tf_op jit(solution)/shard_map/ppermute | solution.py:378
  224.6 7.5 %place.5 = bf16[2048,2048]{1,0:T(8,128)(2,1)} custom-call(s32[18]{0:T(128)} %stack.230.spots_ref, bf16[512,2048]{1,0:T(8,128)(2,1)} %refs_0_.1, bf16[512,1024]{1,0:T(8,128)(2,1)} %collective-permute-done.10.refs_1_, bf16[512,1024]{1,0:T(8,128)(2,1)} %collective-permute-done.11.refs_2_, bf16[256,1024]{1,0:T(8,128)(2,1)} %copy-done.40, ...), custom_call_target="tpu_custom_call" | custom-call | tf_op jit(solution)/shard_map/place/pallas_call | solution.py:401
  243.8 13.3 %multiply_reduce_fusion = (f32[1024]{0:T(1024)S(1)}, f32[1024,2048]{1,0:T(8,128)S(1)}) fusion(bf16[2048,2048]{1,0:T(8,128)(2,1)} %place.5, bf16[1,1024,2048]{2,1,0:T(8,128)(2,1)} %all-gather.9.cloned.1.call-done), kind=kOutput, calls=%fused_computation.3 | convolution fusion | flops 8594127872 | bytes 20975616 | tf_op jit(solution)/shard_map/dot_general | solution.py:772
  263.6 8.9 %fusion.81 = f32[1024,2048]{1,0:T(8,128)S(1)} fusion(bf16[1024,2048]{1,0:T(8,128)(2,1)S(1)} %add_convert_fusion, bf16[2048,2048]{1,0:T(8,128)(2,1)S(1)} %copy-done.4), kind=kOutput, calls=%fused_computation.241 | convolution fusion | flops 8589934592 | bytes 20971520 | tf_op jit(solution)/shard_map/dot_general | solution.py:780
  284.8 48.2 %reduce-scatter.4.cloned.1.call-done = bf16[1,128,2048]{2,1,0:T(8,128)(2,1)} async-done(((bf16[1,1024,2048]{2,1,0:T(8,128)(2,1)}), bf16[1,128,2048]{2,1,0:T(8,128)(2,1)}) %reduce-scatter.4.cloned.1.call-update) | async-done | bytes 524304 | tf_op jit(solution)/shard_map/reduce_scatter | solution.py:374
  345.1 12.5 %copy.60 = bf16[2048,2048]{0,1:T(8,128)(2,1)} copy(bf16[2048,2048]{1,0:T(8,128)(2,1)} %place.7) | data formatting | bytes 16777216 | tf_op jit(solution)/shard_map/optimization_barrier | solution.py:480
  357.6 26.5 %all-gather.7.cloned.1.call-done = bf16[1,1024,2048]{2,1,0:T(8,128)(2,1)} async-done(((bf16[1,128,2048]{2,1,0:T(8,128)(2,1)}), bf16[1,1024,2048]{2,1,0:T(8,128)(2,1)}) %all-gather.7.cloned.1.call-update) | async-done | bytes 4194320 | tf_op jit(solution)/shard_map/all_gather | solution.py:370
  384.1 11.7 %multiply_convert_fusion.1 = (bf16[1024,1024]{1,0:T(8,128)(2,1)S(1)}, bf16[1024,1024]{1,0:T(8,128)(2,1)S(1)}) fusion(f32[1024,2048]{1,0:T(8,128)} %copy-done.10, bf16[1024,2048]{0,1:T(8,128)(2,1)} %copy.57, bf16[1,1024,2048]{2,1,0:T(8,128)(2,1)} %all-gather.7.cloned.1.call-done), kind=kOutput, calls=%fused_computation.19 | convolution fusion | flops 4308598784 | bytes 20971520 | tf_op jit(solution)/shard_map/dot_general | solution.py:805
  397.9 10.5 %convert_bitcast_fusion = bf16[1,1024,2048]{2,1,0:T(8,128)(2,1)} fusion(bf16[2048,2048]{0,1:T(8,128)(2,1)S(1)} %copy-done.11, bf16[1024,1024]{1,0:T(8,128)(2,1)S(1)} %get-tuple-element.72, bf16[1024,1024]{1,0:T(8,128)(2,1)S(1)} %get-tuple-element.71), kind=kOutput, calls=%fused_computation.17 | convolution fusion | flops 8600420352 | bytes 16777216 | tf_op jit(solution)/shard_map/dot_general | solution.py:809
  418.5 9.8 %convolution_convert_fusion = bf16[2048,2048]{1,0:T(8,128)(2,1)S(1)} fusion(bf16[1024,2048]{1,0:T(8,128)(2,1)S(1)} %copy-done.23, bf16[1024,1024]{1,0:T(8,128)(2,1)} %copy-done.71, bf16[1024,1024]{1,0:T(8,128)(2,1)S(1)} %copy-done.70), kind=kOutput, calls=%fused_computation.4 | convolution fusion | flops 8602517504 | bytes 16777216 | tf_op jit(solution)/shard_map/nd,nf->df/dot_general | solution.py:811
  445.0 9.5 %collective-permute-done.57 = bf16[2,128,2048]{2,1,0:T(8,128)(2,1)S(1)} collective-permute-done((bf16[2,128,2048]{2,1,0:T(8,128)(2,1)S(1)}, bf16[2,128,2048]{2,1,0:T(8,128)(2,1)S(1)}, u32[]{:S(2)}, u32[]{:S(2)}) %collective-permute-start.57) | collective-permute-done | bytes 1048608 | tf_op jit(solution)/shard_map/ppermute | solution.py:378
  474.5 35.6 %collective-permute-done.56 = bf16[128,2048]{1,0:T(8,128)(2,1)} collective-permute-done((bf16[128,2048]{1,0:T(8,128)(2,1)}, bf16[128,2048]{1,0:T(8,128)(2,1)}, u32[]{:S(2)}, u32[]{:S(2)}) %collective-permute-start.56) | collective-permute-done | bytes 524320 | tf_op jit(solution)/shard_map/ppermute | solution.py:378
  516.9 15.0 %attend_back.1 = (f32[1,1024,256]{2,1,0:T(8,128)}, f32[1,1024,256]{2,1,0:T(8,128)}, bf16[1,1024,256]{2,1,0:T(8,128)(2,1)}, f32[1,8,1024]{2,1,0:T(8,128)}, f32[1,2,256]{2,1,0:T(2,128)}) custom-call(f32[1,1024,768]{2,1,0:T(8,128)} %bitcast.313, f32[1,1024,768]{2,1,0:T(8,128)} %bitcast.314, f32[1,1024,1]{2,1,0:T(8,128)} %copy.54.qinv_ref, ...), custom_call_target="tpu_custom_call" | custom-call | tf_op jit(solution)/shard_map/attend_back/pallas_call | solution.py:669
  584.5 16.8 %collective-permute-done.52.refs_5_ = bf16[64,2048]{1,0:T(8,128)(2,1)S(1)} collective-permute-done((bf16[64,2048]{1,0:T(8,128)(2,1)S(1)}, bf16[64,2048]{1,0:T(8,128)(2,1)S(1)}, u32[]{:S(2)}, u32[]{:S(2)}) %collective-permute-start.52) | collective-permute-done | bytes 262176 | tf_op jit(solution)/shard_map/ppermute | solution.py:378
  605.3 15.1 %collective-permute-done.50.refs_3_ = bf16[64,2048]{1,0:T(8,128)(2,1)S(1)} collective-permute-done((bf16[64,2048]{1,0:T(8,128)(2,1)S(1)}, bf16[64,2048]{1,0:T(8,128)(2,1)S(1)}, u32[]{:S(2)}, u32[]{:S(2)}) %collective-permute-start.50) | collective-permute-done | bytes 262176 | tf_op jit(solution)/shard_map/ppermute | solution.py:378
  620.5 11.6 %collective-permute-done.51.refs_4_ = bf16[64,2048]{1,0:T(8,128)(2,1)S(1)} collective-permute-done((bf16[64,2048]{1,0:T(8,128)(2,1)S(1)}, bf16[64,2048]{1,0:T(8,128)(2,1)S(1)}, u32[]{:S(2)}, u32[]{:S(2)}) %collective-permute-start.51) | collective-permute-done | bytes 262176 | tf_op jit(solution)/shard_map/ppermute | solution.py:378
  641.9 10.7 %all-to-all-start.1 = ((bf16[8,128,256]{2,1,0:T(8,128)(2,1)}), bf16[8,128,256]{2,1,0:T(8,128)(2,1)S(1)}, u32[]{:S(2)}, u32[]{:S(2)}) async-start(bf16[8,128,256]{2,1,0:T(8,128)(2,1)} %bitcast.308), calls=%async_computation.4 | async-start | bytes 1048576 | tf_op jit(solution)/shard_map/all_to_all | solution.py:824
  662.2 12.7 %collective-permute-done.31 = bf16[2,256,768]{2,1,0:T(8,128)(2,1)S(1)} collective-permute-done((bf16[2,256,768]{2,1,0:T(8,128)(2,1)S(1)}, bf16[2,256,768]{2,1,0:T(8,128)(2,1)S(1)}, u32[]{:S(2)}, u32[]{:S(2)}) %collective-permute-start.31) | collective-permute-done | bytes 786464 | tf_op jit(solution)/shard_map/ppermute | solution.py:378
  712.0 9.1 %collective-permute-done.41.refs_5_ = bf16[64,1024]{1,0:T(8,128)(2,1)S(1)} collective-permute-done((bf16[64,1024]{1,0:T(8,128)(2,1)S(1)}, bf16[64,1024]{1,0:T(8,128)(2,1)S(1)}, u32[]{:S(2)}, u32[]{:S(2)}) %collective-permute-start.41) | collective-permute-done | bytes 131104 | tf_op jit(solution)/shard_map/ppermute | solution.py:378
  (414 shorter events, 324.3 us)
Async XLA Ops:
  7.2 52.2 %all-gather.5.cloned.1.call-start = ((), (), s32[]{:S(2)}) async-start(), calls=%async_computation.5 | async-start | bytes 4718592 | tf_op jit(solution)/shard_map/all_gather | solution.py:370
  7.9 235.8 %all-gather.9.cloned.1.call-start = ((), (), s32[]{:S(2)}) async-start(), calls=%async_computation.10 | async-start | bytes 4718592 | tf_op jit(solution)/shard_map/all_gather | solution.py:771
  89.6 243.4 %reduce-scatter.4.cloned.1.call-start = ((), (), s32[]{:S(2)}) async-start(), calls=%async_computation.6 | async-start | bytes 4718592 | tf_op jit(solution)/shard_map/reduce_scatter | solution.py:374
  100.2 95.6 %collective-permute-start.22 = (bf16[512,2048]{1,0:T(8,128)(2,1)S(1)}, bf16[512,2048]{1,0:T(8,128)(2,1)S(1)}, u32[]{:S(2)}, u32[]{:S(2)}) collective-permute-start(bf16[512,2048]{1,0:T(8,128)(2,1)S(1)} %dynamic-slice_dynamic-update-slice_fusion.refs_0_), channel_id=1, source_target_pairs={{0,8},{8,0},{16,24},{24,16},{1,9},{9,1},{17,25},{25,17},{2,10},{10... | collective-permute-start | bytes 6291464 | tf_op jit(solution)/shard_map/ppermute | solution.py:378
  100.8 104.7 %collective-permute-start.23 = (bf16[512,2048]{1,0:T(8,128)(2,1)S(1)}, bf16[512,2048]{1,0:T(8,128)(2,1)S(1)}, u32[]{:S(2)}, u32[]{:S(2)}) collective-permute-start(bf16[512,2048]{1,0:T(8,128)(2,1)S(1)} %dynamic-slice_dynamic-update-slice_fusion.refs_0_), channel_id=1, source_target_pairs={{0,16},{8,24},{16,0},{24,8},{1,17},{9,25},{17,1},{25,9},{2,18},{10... | collective-permute-start | bytes 6291464 | tf_op jit(solution)/shard_map/ppermute | solution.py:378
  102.3 69.6 %collective-permute-start.11 = (bf16[512,1024]{1,0:T(8,128)(2,1)}, bf16[512,1024]{1,0:T(8,128)(2,1)}, u32[]{:S(2)}, u32[]{:S(2)}) collective-permute-start(bf16[512,1024]{1,0:T(8,128)(2,1)} %constant_dynamic-slice_fusion.14), channel_id=1, source_target_pairs={{0,16},{8,24},{16,0},{24,8},{1,17},{9,25},{17,1},{25,9},{2,18},{10... | collective-permute-start | bytes 3145736 | tf_op jit(solution)/shard_map/ppermute | solution.py:378
  104.1 77.6 %collective-permute-start.18 = (bf16[256,2048]{1,0:T(8,128)(2,1)S(1)}, bf16[256,2048]{1,0:T(8,128)(2,1)S(1)}, u32[]{:S(2)}, u32[]{:S(2)}) collective-permute-start(bf16[256,2048]{1,0:T(8,128)(2,1)S(1)} %constant_dynamic-slice_fusion.13.refs_0_), channel_id=1, source_target_pairs={{0,8},{8,0},{16,24},{24,16},{1,9},{9,1},{17,25},{25,17},{2,10},{10... | collective-permute-start | bytes 3145736 | tf_op jit(solution)/shard_map/ppermute | solution.py:378
  117.1 77.1 %collective-permute-start.19 = (bf16[256,2048]{1,0:T(8,128)(2,1)S(1)}, bf16[256,2048]{1,0:T(8,128)(2,1)S(1)}, u32[]{:S(2)}, u32[]{:S(2)}) collective-permute-start(bf16[256,2048]{1,0:T(8,128)(2,1)S(1)} %constant_dynamic-slice_fusion.13.refs_0_), channel_id=1, source_target_pairs={{0,16},{8,24},{16,0},{24,8},{1,17},{9,25},{17,1},{25,9},{2,18},{10... | collective-permute-start | bytes 3145736 | tf_op jit(solution)/shard_map/ppermute | solution.py:378
  171.9 33.6 %collective-permute-start.12 = (bf16[256,1024]{1,0:T(8,128)(2,1)S(1)}, bf16[256,1024]{1,0:T(8,128)(2,1)S(1)}, u32[]{:S(2)}, u32[]{:S(2)}) collective-permute-start(bf16[256,1024]{1,0:T(8,128)(2,1)S(1)} %slice.180), channel_id=1, source_target_pairs={{0,16},{8,24},{16,0},{24,8},{1,17},{9,25},{17,1},{25,9},{2,18},{10... | collective-permute-start | bytes 1572872 | tf_op jit(solution)/shard_map/ppermute | solution.py:378
  284.0 100.1 %all-gather.7.cloned.1.call-start = ((), (), s32[]{:S(2)}) async-start(), calls=%async_computation.7 | async-start | bytes 4718592 | tf_op jit(solution)/shard_map/all_gather | solution.py:370
  338.6 120.8 %reduce-scatter.6.cloned.1.call-start = ((), (), s32[]{:S(2)}) async-start(), calls=%async_computation.8 | async-start | bytes 4718592 | tf_op jit(solution)/shard_map/reduce_scatter | solution.py:374
  434.2 78.3 %collective-permute-start.46 = (bf16[2,256,2048]{2,1,0:T(8,128)(2,1)}, bf16[2,256,2048]{2,1,0:T(8,128)(2,1)}, u32[]{:S(2)}, u32[]{:S(2)}) collective-permute-start(bf16[2,256,2048]{2,1,0:T(8,128)(2,1)} %pad_maximum_fusion.4), channel_id=1, source_target_pairs={{0,16},{8,24},{16,0},{24,8},{1,17},{9,25},{17,1},{25,9},{2,18},{10... | collective-permute-start | bytes 6291464 | tf_op jit(solution)/shard_map/ppermute | solution.py:378
  436.3 101.7 %collective-permute-start.44 = (bf16[2,256,2048]{2,1,0:T(8,128)(2,1)}, bf16[2,256,2048]{2,1,0:T(8,128)(2,1)}, u32[]{:S(2)}, u32[]{:S(2)}) collective-permute-start(bf16[2,256,2048]{2,1,0:T(8,128)(2,1)} %pad_maximum_fusion.3), channel_id=1, source_target_pairs={{0,8},{8,0},{16,24},{24,16},{1,9},{9,1},{17,25},{25,17},{2,10},{10... | collective-permute-start | bytes 6291464 | tf_op jit(solution)/shard_map/ppermute | solution.py:378
  443.5 66.6 %collective-permute-start.56 = (bf16[128,2048]{1,0:T(8,128)(2,1)}, bf16[128,2048]{1,0:T(8,128)(2,1)}, u32[]{:S(2)}, u32[]{:S(2)}) collective-permute-start(bf16[128,2048]{1,0:T(8,128)(2,1)} %fusion.54), channel_id=1, source_target_pairs={{0,16},{8,24},{16,0},{24,8},{1,17},{9,25},{17,1},{25,9},{2,18},{10... | collective-permute-start | bytes 1572872 | tf_op jit(solution)/shard_map/ppermute | solution.py:378
  457.9 96.3 %collective-permute-start.58 = (bf16[128,2048]{1,0:T(8,128)(2,1)}, bf16[128,2048]{1,0:T(8,128)(2,1)}, u32[]{:S(2)}, u32[]{:S(2)}) collective-permute-start(bf16[128,2048]{1,0:T(8,128)(2,1)} %fusion.55), channel_id=1, source_target_pairs={{0,8},{8,0},{16,24},{24,16},{1,9},{9,1},{17,25},{25,17},{2,10},{10... | collective-permute-start | bytes 1572872 | tf_op jit(solution)/shard_map/ppermute | solution.py:378
  470.2 46.7 %all-to-all-start = ((bf16[8,128,256]{2,1,0:T(8,128)(2,1)}), bf16[8,128,256]{2,1,0:T(8,128)(2,1)}, u32[]{:S(2)}, u32[]{:S(2)}) async-start(bf16[8,128,256]{2,1,0:T(8,128)(2,1)} %bitcast.322), calls=%async_computation.2 | async-start | bytes 1048576 | tf_op jit(solution)/shard_map/all_to_all | solution.py:824
  474.4 251.5 %reduce-scatter.8.cloned.1.call-start = ((), (), s32[]{:S(2)}) async-start(), calls=%async_computation.9 | async-start | bytes 4718592 | tf_op jit(solution)/shard_map/reduce_scatter | solution.py:374
  570.9 30.4 %collective-permute-start.52 = (bf16[64,2048]{1,0:T(8,128)(2,1)S(1)}, bf16[64,2048]{1,0:T(8,128)(2,1)S(1)}, u32[]{:S(2)}, u32[]{:S(2)}) collective-permute-start(bf16[64,2048]{1,0:T(8,128)(2,1)S(1)} %get-tuple-element.106), channel_id=1, source_target_pairs={{0,5},{1,4},{2,7},{3,6},{4,1},{5,0},{6,3},{7,2},{8,13},{9,12},{10,... | collective-permute-start | bytes 786440 | tf_op jit(solution)/shard_map/ppermute | solution.py:378
  577.2 43.3 %collective-permute-start.50 = (bf16[64,2048]{1,0:T(8,128)(2,1)S(1)}, bf16[64,2048]{1,0:T(8,128)(2,1)S(1)}, u32[]{:S(2)}, u32[]{:S(2)}) collective-permute-start(bf16[64,2048]{1,0:T(8,128)(2,1)S(1)} %get-tuple-element.103), channel_id=1, source_target_pairs={{0,3},{1,2},{2,1},{3,0},{4,7},{5,6},{6,5},{7,4},{8,11},{9,10},{10,... | collective-permute-start | bytes 786440 | tf_op jit(solution)/shard_map/ppermute | solution.py:378
  601.3 30.8 %collective-permute-start.51 = (bf16[64,2048]{1,0:T(8,128)(2,1)S(1)}, bf16[64,2048]{1,0:T(8,128)(2,1)S(1)}, u32[]{:S(2)}, u32[]{:S(2)}) collective-permute-start(bf16[64,2048]{1,0:T(8,128)(2,1)S(1)} %get-tuple-element.104), channel_id=1, source_target_pairs={{0,4},{1,5},{2,6},{3,7},{4,0},{5,1},{6,2},{7,3},{8,12},{9,13},{10,... | collective-permute-start | bytes 786440 | tf_op jit(solution)/shard_map/ppermute | solution.py:378
  601.3 34.7 %collective-permute-start.54 = (bf16[64,2048]{1,0:T(8,128)(2,1)S(1)}, bf16[64,2048]{1,0:T(8,128)(2,1)S(1)}, u32[]{:S(2)}, u32[]{:S(2)}) collective-permute-start(bf16[64,2048]{1,0:T(8,128)(2,1)S(1)} %get-tuple-element.99), channel_id=1, source_target_pairs={{0,7},{1,6},{2,5},{3,4},{4,3},{5,2},{6,1},{7,0},{8,15},{9,14},{10,... | collective-permute-start | bytes 786440 | tf_op jit(solution)/shard_map/ppermute | solution.py:378
  602.6 54.9 %collective-permute-start.29 = (bf16[2,256,768]{2,1,0:T(8,128)(2,1)}, bf16[2,256,768]{2,1,0:T(8,128)(2,1)S(1)}, u32[]{:S(2)}, u32[]{:S(2)}) collective-permute-start(bf16[2,256,768]{2,1,0:T(8,128)(2,1)} %pad_maximum_fusion.10), channel_id=1, source_target_pairs={{0,8},{8,0},{16,24},{24,16},{1,9},{9,1},{17,25},{25,17},{2,10},{10... | collective-permute-start | bytes 2359304 | tf_op jit(solution)/shard_map/ppermute | solution.py:378
  641.9 34.3 %all-to-all-start.1 = ((bf16[8,128,256]{2,1,0:T(8,128)(2,1)}), bf16[8,128,256]{2,1,0:T(8,128)(2,1)S(1)}, u32[]{:S(2)}, u32[]{:S(2)}) async-start(bf16[8,128,256]{2,1,0:T(8,128)(2,1)} %bitcast.308), calls=%async_computation.4 | async-start | bytes 1048576 | tf_op jit(solution)/shard_map/all_to_all | solution.py:824
  656.5 43.8 %collective-permute-start.60 = (f32[1,256]{1,0:T(1,128)S(1)}, f32[1,256]{1,0:T(1,128)S(1)}, u32[]{:S(2)}, u32[]{:S(2)}) collective-permute-start(f32[1,256]{1,0:T(1,128)S(1)} %constant_dynamic-slice_fusion), channel_id=1, source_target_pairs={{0,8},{8,0},{16,24},{24,16},{1,9},{9,1},{17,25},{25,17},{2,10},{10... | collective-permute-start | bytes 3080 | tf_op jit(solution)/shard_map/ppermute | solution.py:378
  (118 other events, 1708.5 us)
Sparse Core Ops, SparseCore 0:
  9.6 49.7 all-gather.4
  89.7 46.6 all-gather.8
  284.2 48.7 reduce-scatter.3
  338.8 45.3 all-gather.6
  408.5 48.7 reduce-scatter.5
  554.3 73.3 reduce-scatter.7

commit v7 on v6

--- a/solution.py
+++ b/solution.py
@@ -378,8 +378,8 @@
     return lax.ppermute(value, axis, [(at, at ^ flip) for at in range(lax.axis_size(axis))])
 
 
-def place_kernel(spots_ref, *refs):
-    *in_refs, out_ref, sems = refs
+def place_kernel(spots_ref, *refs, count):
+    in_refs, (out_ref, sems) = refs[:count], refs[-2:]
     copies = []
     for at, in_ref in enumerate(in_refs):
         rows, width = in_ref.shape
@@ -396,23 +396,27 @@
         copy.wait()
 
 
-def placed(pieces, shape):
+def placed(pieces, shape, whole=None):
     spots = jnp.stack([jnp.int32(at) for _, row, column in pieces for at in (row, column)])
+    outside = pl.BlockSpec(memory_space=pl.ANY)
+    given = [] if whole is None else [whole]
     return pl.pallas_call(
-        place_kernel,
+        functools.partial(place_kernel, count=len(pieces)),
         grid_spec=pltpu.PrefetchScalarGridSpec(
             num_scalar_prefetch=1,
             grid=(1,),
             in_specs=[
                 pl.BlockSpec(piece.shape, lambda at, spots: (0, 0), pipeline_mode=pl.Buffered(1))
                 for piece, _, _ in pieces
-            ],
-            out_specs=pl.BlockSpec(memory_space=pl.ANY),
+            ]
+            + [outside] * len(given),
+            out_specs=outside,
             scratch_shapes=[pltpu.SemaphoreType.DMA((len(pieces),))],
         ),
         out_shape=jax.ShapeDtypeStruct(shape, pieces[0][0].dtype),
+        input_output_aliases={1 + len(pieces): 0} if given else {},
         name="place",
-    )(spots, *[piece for piece, _, _ in pieces])
+    )(spots, *[piece for piece, _, _ in pieces], *given)
 
 
 def pieces_for(value, name, split_axis):
@@ -450,7 +454,9 @@
 def gather_dp(piece):
     rows, width = piece.shape
     pieces = [(piece, lax.axis_index("dp") * rows), *pieces_dp(piece)]
-    return placed([(part, row, 0) for part, row in pieces], (4 * rows, width))
+    pieces = [(part, row, 0) for part, row in pieces]
+    whole = placed(pieces[:3], (4 * rows, width))
+    return placed(pieces[3:], (4 * rows, width), whole)
 
 
 def sum_dp(sent, kept):

time: 749 us -> 749 us (level)
  waiting for transfers between devices: 358 us -> 349 us
    pallas_call x4 -> x7, Pallas kernels: 24 us -> 30.8 us  [placed(): pl.pallas_call(functools.partial(place_kernel, count=len(pieces)), grid_s...]
  transfers between devices with their start and end apart: 69 -> 69, of which waited for: 37 -> 35; matrix products, arithmetic and copies ran while one was open for 18% -> 18% of each run, Pallas kernels for 6% -> 7%
where the time goes in v7:
time: 749 us; the launch traced here: 735 us
  waiting for transfers between devices  349 us (47%)
  matrix products  92.5 us (12%)
  starting transfers between devices  82.3 us (11%)
  local copies, waits for them, and re-layouts  77.9 us (10%)
  Pallas kernels  64 us (9%)
  other arithmetic  53 us (7%)
  between operations  15.8 us (2%)
    ppermute x61, waiting for transfers between devices, swap(): lax.ppermute(value, axis, [(at, at ^ flip) for at in range(lax.axis_size(...  269 us
    ppermute x61, starting transfers between devices, swap(): lax.ppermute(value, axis, [(at, at ^ flip) for at in range(lax.axis_size(...  67.2 us
    reduce_scatter x3, waiting for transfers between devices, scatter_seq(): return lax.psum_scatter(partial, 'seq', scatter_dimension=1, tiled=True)  46.9 us
    all_gather x2, waiting for transfers between devices, gather_seq(): return lax.all_gather(piece, 'seq', axis=1, tiled=True)  33.2 us
    pallas_call x7, Pallas kernels, placed(): pl.pallas_call(functools.partial(place_kernel, count=len(pieces)), grid_s...  30.8 us
    unnamed x153, local copies, waits for them, and re-layouts  28 us
    optimization_barrier x2, local copies, waits for them, and re-layouts, stored_turned(): matrix, after = lax.optimization_barrier((matrix, after))  19 us
    pallas_call x1, Pallas kernels, attend_back(): pl.pallas_call(functools.partial(attend_back_kernel, scale=scale), grid=(...  15 us
  transfers between devices with their start and end apart: 69, of which 35 were waited for; matrix products, arithmetic and copies ran while one was open for 18% of the time, Pallas kernels for 7%

profile of v7, /device:TPU:0, one launch (start us, length us, event | category | flops | bytes accessed | tf_op | source)
XLA Modules:
  0.0 735.0 jit_solution(15979230305358737282)
XLA Ops:
  14.5 16.0 %collective-permute-done.3.refs_1_ = bf16[512,768]{1,0:T(8,128)(2,1)S(1)} collective-permute-done((bf16[512,768]{1,0:T(8,128)(2,1)S(1)}, bf16[512,768]{1,0:T(8,128)(2,1)S(1)}, u32[]{:S(2)}, u32[]{:S(2)}) %collective-permute-start.3) | collective-permute-done | bytes 786464 | tf_op jit(solution)/shard_map/ppermute | solution.py:378
  79.1 10.5 %attend.1 = (bf16[1,1024,256]{2,1,0:T(8,128)(2,1)}, bf16[1,1024,256]{2,1,0:T(8,128)(2,1)}, bf16[1,1024,256]{2,1,0:T(8,128)(2,1)}, bf16[1,1024,256]{2,1,0:T(8,128)(2,1)}, f32[1,2,1024,1]{3,2,1,0:T(8,128)}) custom-call(f32[1,1024,768]{2,1,0:T(8,128)} %bitcast.310, f32[1,1024,768]{2,1,0:T(8,128)} %bitcast.311, f32[1,1024,768]{2,1,0:T(8,128)} %bitcast.312, ...), custom_call_target="tpu_custom_call" | custom-call | tf_op jit(solution)/shard_map/attend/pallas_call | solution.py:660
  105.7 11.4 %collective-permute-done.10.refs_1_ = bf16[512,1024]{1,0:T(8,128)(2,1)} collective-permute-done((bf16[512,1024]{1,0:T(8,128)(2,1)}, bf16[512,1024]{1,0:T(8,128)(2,1)}, u32[]{:S(2)}, u32[]{:S(2)}) %collective-permute-start.10) | collective-permute-done | bytes 1048608 | tf_op jit(solution)/shard_map/ppermute | solution.py:378
  119.7 52.2 %collective-permute-done.11.refs_2_ = bf16[512,1024]{1,0:T(8,128)(2,1)} collective-permute-done((bf16[512,1024]{1,0:T(8,128)(2,1)}, bf16[512,1024]{1,0:T(8,128)(2,1)}, u32[]{:S(2)}, u32[]{:S(2)}) %collective-permute-start.11) | collective-permute-done | bytes 1048608 | tf_op jit(solution)/shard_map/ppermute | solution.py:378
  174.4 7.3 collective-permute-done.18.refs_1_
  183.2 11.0 %collective-permute-done.20.refs_2_ = bf16[256,2048]{1,0:T(8,128)(2,1)S(1)} collective-permute-done((bf16[256,2048]{1,0:T(8,128)(2,1)S(1)}, bf16[256,2048]{1,0:T(8,128)(2,1)S(1)}, u32[]{:S(2)}, u32[]{:S(2)}) %collective-permute-start.20) | collective-permute-done | bytes 1048608 | tf_op jit(solution)/shard_map/ppermute | solution.py:378
  233.7 7.6 %place.9 = bf16[2048,2048]{1,0:T(8,128)(2,1)} custom-call(s32[18]{0:T(128)} %stack.238.spots_ref, bf16[512,2048]{1,0:T(8,128)(2,1)} %refs_0_.1, bf16[512,1024]{1,0:T(8,128)(2,1)} %collective-permute-done.10.refs_1_, bf16[512,1024]{1,0:T(8,128)(2,1)} %collective-permute-done.11.refs_2_, bf16[256,1024]{1,0:T(8,128)(2,1)} %copy-done.40, ...), custom_call_target="tpu_custom_call" | custom-call | tf_op jit(solution)/shard_map/place/pallas_call | solution.py:403
  244.9 13.3 %multiply_reduce_fusion = (f32[1024]{0:T(1024)S(1)}, f32[1024,2048]{1,0:T(8,128)S(1)}) fusion(bf16[2048,2048]{1,0:T(8,128)(2,1)} %place.9, bf16[1,1024,2048]{2,1,0:T(8,128)(2,1)} %all-gather.9.cloned.1.call-done), kind=kOutput, calls=%fused_computation.3 | convolution fusion | flops 8594127872 | bytes 20975616 | tf_op jit(solution)/shard_map/dot_general | solution.py:778
  264.7 8.9 %fusion.83 = f32[1024,2048]{1,0:T(8,128)S(1)} fusion(bf16[1024,2048]{1,0:T(8,128)(2,1)S(1)} %add_convert_fusion, bf16[2048,2048]{1,0:T(8,128)(2,1)S(1)} %copy-done.4), kind=kOutput, calls=%fused_computation.247 | convolution fusion | flops 8589934592 | bytes 20971520 | tf_op jit(solution)/shard_map/dot_general | solution.py:786
  285.9 46.9 %reduce-scatter.4.cloned.1.call-done = bf16[1,128,2048]{2,1,0:T(8,128)(2,1)} async-done(((bf16[1,1024,2048]{2,1,0:T(8,128)(2,1)}), bf16[1,128,2048]{2,1,0:T(8,128)(2,1)}) %reduce-scatter.4.cloned.1.call-update) | async-done | bytes 524304 | tf_op jit(solution)/shard_map/reduce_scatter | solution.py:374
  345.0 12.5 %copy.63 = bf16[2048,2048]{0,1:T(8,128)(2,1)} copy(bf16[2048,2048]{1,0:T(8,128)(2,1)} %place.13) | data formatting | bytes 16777216 | tf_op jit(solution)/shard_map/optimization_barrier | solution.py:486
  357.5 26.5 %all-gather.7.cloned.1.call-done = bf16[1,1024,2048]{2,1,0:T(8,128)(2,1)} async-done(((bf16[1,128,2048]{2,1,0:T(8,128)(2,1)}), bf16[1,1024,2048]{2,1,0:T(8,128)(2,1)}) %all-gather.7.cloned.1.call-update) | async-done | bytes 4194320 | tf_op jit(solution)/shard_map/all_gather | solution.py:370
  384.0 11.7 %multiply_convert_fusion.1 = (bf16[1024,1024]{1,0:T(8,128)(2,1)S(1)}, bf16[1024,1024]{1,0:T(8,128)(2,1)S(1)}) fusion(f32[1024,2048]{1,0:T(8,128)} %copy-done.11, bf16[1024,2048]{0,1:T(8,128)(2,1)} %copy.60, bf16[1,1024,2048]{2,1,0:T(8,128)(2,1)} %all-gather.7.cloned.1.call-done), kind=kOutput, calls=%fused_computation.19 | convolution fusion | flops 4308598784 | bytes 20971520 | tf_op jit(solution)/shard_map/dot_general | solution.py:811
  397.7 10.5 %convert_bitcast_fusion = bf16[1,1024,2048]{2,1,0:T(8,128)(2,1)} fusion(bf16[2048,2048]{0,1:T(8,128)(2,1)S(1)} %copy-done.12, bf16[1024,1024]{1,0:T(8,128)(2,1)S(1)} %get-tuple-element.72, bf16[1024,1024]{1,0:T(8,128)(2,1)S(1)} %get-tuple-element.71), kind=kOutput, calls=%fused_computation.17 | convolution fusion | flops 8600420352 | bytes 16777216 | tf_op jit(solution)/shard_map/dot_general | solution.py:815
  418.3 9.8 %convolution_convert_fusion = bf16[2048,2048]{1,0:T(8,128)(2,1)S(1)} fusion(bf16[1024,2048]{1,0:T(8,128)(2,1)S(1)} %copy-done.23, bf16[1024,1024]{1,0:T(8,128)(2,1)} %copy-done.71, bf16[1024,1024]{1,0:T(8,128)(2,1)S(1)} %copy-done.70), kind=kOutput, calls=%fused_computation.4 | convolution fusion | flops 8602517504 | bytes 16777216 | tf_op jit(solution)/shard_map/nd,nf->df/dot_general | solution.py:817
  444.8 9.5 %collective-permute-done.57 = bf16[2,128,2048]{2,1,0:T(8,128)(2,1)S(1)} collective-permute-done((bf16[2,128,2048]{2,1,0:T(8,128)(2,1)S(1)}, bf16[2,128,2048]{2,1,0:T(8,128)(2,1)S(1)}, u32[]{:S(2)}, u32[]{:S(2)}) %collective-permute-start.57) | collective-permute-done | bytes 1048608 | tf_op jit(solution)/shard_map/ppermute | solution.py:378
  474.3 35.6 %collective-permute-done.56 = bf16[128,2048]{1,0:T(8,128)(2,1)} collective-permute-done((bf16[128,2048]{1,0:T(8,128)(2,1)}, bf16[128,2048]{1,0:T(8,128)(2,1)}, u32[]{:S(2)}, u32[]{:S(2)}) %collective-permute-start.56) | collective-permute-done | bytes 524320 | tf_op jit(solution)/shard_map/ppermute | solution.py:378
  516.8 15.0 %attend_back.1 = (f32[1,1024,256]{2,1,0:T(8,128)}, f32[1,1024,256]{2,1,0:T(8,128)}, bf16[1,1024,256]{2,1,0:T(8,128)(2,1)}, f32[1,8,1024]{2,1,0:T(8,128)}, f32[1,2,256]{2,1,0:T(2,128)}) custom-call(f32[1,1024,768]{2,1,0:T(8,128)} %bitcast.313, f32[1,1024,768]{2,1,0:T(8,128)} %bitcast.314, f32[1,1024,1]{2,1,0:T(8,128)} %copy.57.qinv_ref, ...), custom_call_target="tpu_custom_call" | custom-call | tf_op jit(solution)/shard_map/attend_back/pallas_call | solution.py:675
  584.4 16.8 %collective-permute-done.52.refs_5_ = bf16[64,2048]{1,0:T(8,128)(2,1)S(1)} collective-permute-done((bf16[64,2048]{1,0:T(8,128)(2,1)S(1)}, bf16[64,2048]{1,0:T(8,128)(2,1)S(1)}, u32[]{:S(2)}, u32[]{:S(2)}) %collective-permute-start.52) | collective-permute-done | bytes 262176 | tf_op jit(solution)/shard_map/ppermute | solution.py:378
  605.2 15.1 %collective-permute-done.50.refs_3_ = bf16[64,2048]{1,0:T(8,128)(2,1)S(1)} collective-permute-done((bf16[64,2048]{1,0:T(8,128)(2,1)S(1)}, bf16[64,2048]{1,0:T(8,128)(2,1)S(1)}, u32[]{:S(2)}, u32[]{:S(2)}) %collective-permute-start.50) | collective-permute-done | bytes 262176 | tf_op jit(solution)/shard_map/ppermute | solution.py:378
  620.3 11.6 %collective-permute-done.51.refs_4_ = bf16[64,2048]{1,0:T(8,128)(2,1)S(1)} collective-permute-done((bf16[64,2048]{1,0:T(8,128)(2,1)S(1)}, bf16[64,2048]{1,0:T(8,128)(2,1)S(1)}, u32[]{:S(2)}, u32[]{:S(2)}) %collective-permute-start.51) | collective-permute-done | bytes 262176 | tf_op jit(solution)/shard_map/ppermute | solution.py:378
  641.8 10.7 %all-to-all-start.1 = ((bf16[8,128,256]{2,1,0:T(8,128)(2,1)}), bf16[8,128,256]{2,1,0:T(8,128)(2,1)S(1)}, u32[]{:S(2)}, u32[]{:S(2)}) async-start(bf16[8,128,256]{2,1,0:T(8,128)(2,1)} %bitcast.308), calls=%async_computation.4 | async-start | bytes 1048576 | tf_op jit(solution)/shard_map/all_to_all | solution.py:830
  662.0 12.7 %collective-permute-done.31 = bf16[2,256,768]{2,1,0:T(8,128)(2,1)S(1)} collective-permute-done((bf16[2,256,768]{2,1,0:T(8,128)(2,1)S(1)}, bf16[2,256,768]{2,1,0:T(8,128)(2,1)S(1)}, u32[]{:S(2)}, u32[]{:S(2)}) %collective-permute-start.31) | collective-permute-done | bytes 786464 | tf_op jit(solution)/shard_map/ppermute | solution.py:378
  711.8 9.1 %collective-permute-done.41.refs_5_ = bf16[64,1024]{1,0:T(8,128)(2,1)S(1)} collective-permute-done((bf16[64,1024]{1,0:T(8,128)(2,1)S(1)}, bf16[64,1024]{1,0:T(8,128)(2,1)S(1)}, u32[]{:S(2)}, u32[]{:S(2)}) %collective-permute-start.41) | collective-permute-done | bytes 131104 | tf_op jit(solution)/shard_map/ppermute | solution.py:378
  (419 shorter events, 326.9 us)
Async XLA Ops:
  7.2 52.2 %all-gather.5.cloned.1.call-start = ((), (), s32[]{:S(2)}) async-start(), calls=%async_computation.5 | async-start | bytes 4718592 | tf_op jit(solution)/shard_map/all_gather | solution.py:370
  7.9 237.0 %all-gather.9.cloned.1.call-start = ((), (), s32[]{:S(2)}) async-start(), calls=%async_computation.10 | async-start | bytes 4718592 | tf_op jit(solution)/shard_map/all_gather | solution.py:777
  89.6 243.2 %reduce-scatter.4.cloned.1.call-start = ((), (), s32[]{:S(2)}) async-start(), calls=%async_computation.6 | async-start | bytes 4718592 | tf_op jit(solution)/shard_map/reduce_scatter | solution.py:374
  100.2 95.6 %collective-permute-start.22 = (bf16[512,2048]{1,0:T(8,128)(2,1)S(1)}, bf16[512,2048]{1,0:T(8,128)(2,1)S(1)}, u32[]{:S(2)}, u32[]{:S(2)}) collective-permute-start(bf16[512,2048]{1,0:T(8,128)(2,1)S(1)} %dynamic-slice_dynamic-update-slice_fusion.refs_0_), channel_id=1, source_target_pairs={{0,8},{8,0},{16,24},{24,16},{1,9},{9,1},{17,25},{25,17},{2,10},{10... | collective-permute-start | bytes 6291464 | tf_op jit(solution)/shard_map/ppermute | solution.py:378
  100.8 104.7 %collective-permute-start.24 = (bf16[512,2048]{1,0:T(8,128)(2,1)S(1)}, bf16[512,2048]{1,0:T(8,128)(2,1)S(1)}, u32[]{:S(2)}, u32[]{:S(2)}) collective-permute-start(bf16[512,2048]{1,0:T(8,128)(2,1)S(1)} %dynamic-slice_dynamic-update-slice_fusion.refs_0_), channel_id=1, source_target_pairs={{0,16},{8,24},{16,0},{24,8},{1,17},{9,25},{17,1},{25,9},{2,18},{10... | collective-permute-start | bytes 6291464 | tf_op jit(solution)/shard_map/ppermute | solution.py:378
  102.3 69.6 %collective-permute-start.11 = (bf16[512,1024]{1,0:T(8,128)(2,1)}, bf16[512,1024]{1,0:T(8,128)(2,1)}, u32[]{:S(2)}, u32[]{:S(2)}) collective-permute-start(bf16[512,1024]{1,0:T(8,128)(2,1)} %constant_dynamic-slice_fusion.14), channel_id=1, source_target_pairs={{0,16},{8,24},{16,0},{24,8},{1,17},{9,25},{17,1},{25,9},{2,18},{10... | collective-permute-start | bytes 3145736 | tf_op jit(solution)/shard_map/ppermute | solution.py:378
  104.1 77.6 %collective-permute-start.18 = (bf16[256,2048]{1,0:T(8,128)(2,1)S(1)}, bf16[256,2048]{1,0:T(8,128)(2,1)S(1)}, u32[]{:S(2)}, u32[]{:S(2)}) collective-permute-start(bf16[256,2048]{1,0:T(8,128)(2,1)S(1)} %constant_dynamic-slice_fusion.13.refs_0_), channel_id=1, source_target_pairs={{0,8},{8,0},{16,24},{24,16},{1,9},{9,1},{17,25},{25,17},{2,10},{10... | collective-permute-start | bytes 3145736 | tf_op jit(solution)/shard_map/ppermute | solution.py:378
  117.1 77.1 %collective-permute-start.20 = (bf16[256,2048]{1,0:T(8,128)(2,1)S(1)}, bf16[256,2048]{1,0:T(8,128)(2,1)S(1)}, u32[]{:S(2)}, u32[]{:S(2)}) collective-permute-start(bf16[256,2048]{1,0:T(8,128)(2,1)S(1)} %constant_dynamic-slice_fusion.13.refs_0_), channel_id=1, source_target_pairs={{0,16},{8,24},{16,0},{24,8},{1,17},{9,25},{17,1},{25,9},{2,18},{10... | collective-permute-start | bytes 3145736 | tf_op jit(solution)/shard_map/ppermute | solution.py:378
  171.9 33.6 %collective-permute-start.12 = (bf16[256,1024]{1,0:T(8,128)(2,1)S(1)}, bf16[256,1024]{1,0:T(8,128)(2,1)S(1)}, u32[]{:S(2)}, u32[]{:S(2)}) collective-permute-start(bf16[256,1024]{1,0:T(8,128)(2,1)S(1)} %slice.180), channel_id=1, source_target_pairs={{0,16},{8,24},{16,0},{24,8},{1,17},{9,25},{17,1},{25,9},{2,18},{10... | collective-permute-start | bytes 1572872 | tf_op jit(solution)/shard_map/ppermute | solution.py:378
  285.2 98.8 %all-gather.7.cloned.1.call-start = ((), (), s32[]{:S(2)}) async-start(), calls=%async_computation.7 | async-start | bytes 4718592 | tf_op jit(solution)/shard_map/all_gather | solution.py:370
  338.5 120.8 %reduce-scatter.6.cloned.1.call-start = ((), (), s32[]{:S(2)}) async-start(), calls=%async_computation.8 | async-start | bytes 4718592 | tf_op jit(solution)/shard_map/reduce_scatter | solution.py:374
  434.1 78.3 %collective-permute-start.46 = (bf16[2,256,2048]{2,1,0:T(8,128)(2,1)}, bf16[2,256,2048]{2,1,0:T(8,128)(2,1)}, u32[]{:S(2)}, u32[]{:S(2)}) collective-permute-start(bf16[2,256,2048]{2,1,0:T(8,128)(2,1)} %pad_maximum_fusion.4), channel_id=1, source_target_pairs={{0,16},{8,24},{16,0},{24,8},{1,17},{9,25},{17,1},{25,9},{2,18},{10... | collective-permute-start | bytes 6291464 | tf_op jit(solution)/shard_map/ppermute | solution.py:378
  436.1 101.7 %collective-permute-start.44 = (bf16[2,256,2048]{2,1,0:T(8,128)(2,1)}, bf16[2,256,2048]{2,1,0:T(8,128)(2,1)}, u32[]{:S(2)}, u32[]{:S(2)}) collective-permute-start(bf16[2,256,2048]{2,1,0:T(8,128)(2,1)} %pad_maximum_fusion.3), channel_id=1, source_target_pairs={{0,8},{8,0},{16,24},{24,16},{1,9},{9,1},{17,25},{25,17},{2,10},{10... | collective-permute-start | bytes 6291464 | tf_op jit(solution)/shard_map/ppermute | solution.py:378
  443.3 66.6 %collective-permute-start.56 = (bf16[128,2048]{1,0:T(8,128)(2,1)}, bf16[128,2048]{1,0:T(8,128)(2,1)}, u32[]{:S(2)}, u32[]{:S(2)}) collective-permute-start(bf16[128,2048]{1,0:T(8,128)(2,1)} %fusion.54), channel_id=1, source_target_pairs={{0,16},{8,24},{16,0},{24,8},{1,17},{9,25},{17,1},{25,9},{2,18},{10... | collective-permute-start | bytes 1572872 | tf_op jit(solution)/shard_map/ppermute | solution.py:378
  457.8 96.3 %collective-permute-start.58 = (bf16[128,2048]{1,0:T(8,128)(2,1)}, bf16[128,2048]{1,0:T(8,128)(2,1)}, u32[]{:S(2)}, u32[]{:S(2)}) collective-permute-start(bf16[128,2048]{1,0:T(8,128)(2,1)} %fusion.55), channel_id=1, source_target_pairs={{0,8},{8,0},{16,24},{24,16},{1,9},{9,1},{17,25},{25,17},{2,10},{10... | collective-permute-start | bytes 1572872 | tf_op jit(solution)/shard_map/ppermute | solution.py:378
  470.1 46.7 %all-to-all-start = ((bf16[8,128,256]{2,1,0:T(8,128)(2,1)}), bf16[8,128,256]{2,1,0:T(8,128)(2,1)}, u32[]{:S(2)}, u32[]{:S(2)}) async-start(bf16[8,128,256]{2,1,0:T(8,128)(2,1)} %bitcast.322), calls=%async_computation.2 | async-start | bytes 1048576 | tf_op jit(solution)/shard_map/all_to_all | solution.py:830
  474.2 251.5 %reduce-scatter.8.cloned.1.call-start = ((), (), s32[]{:S(2)}) async-start(), calls=%async_computation.9 | async-start | bytes 4718592 | tf_op jit(solution)/shard_map/reduce_scatter | solution.py:374
  570.8 30.4 %collective-permute-start.52 = (bf16[64,2048]{1,0:T(8,128)(2,1)S(1)}, bf16[64,2048]{1,0:T(8,128)(2,1)S(1)}, u32[]{:S(2)}, u32[]{:S(2)}) collective-permute-start(bf16[64,2048]{1,0:T(8,128)(2,1)S(1)} %get-tuple-element.106), channel_id=1, source_target_pairs={{0,5},{1,4},{2,7},{3,6},{4,1},{5,0},{6,3},{7,2},{8,13},{9,12},{10,... | collective-permute-start | bytes 786440 | tf_op jit(solution)/shard_map/ppermute | solution.py:378
  577.0 43.3 %collective-permute-start.50 = (bf16[64,2048]{1,0:T(8,128)(2,1)S(1)}, bf16[64,2048]{1,0:T(8,128)(2,1)S(1)}, u32[]{:S(2)}, u32[]{:S(2)}) collective-permute-start(bf16[64,2048]{1,0:T(8,128)(2,1)S(1)} %get-tuple-element.103), channel_id=1, source_target_pairs={{0,3},{1,2},{2,1},{3,0},{4,7},{5,6},{6,5},{7,4},{8,11},{9,10},{10,... | collective-permute-start | bytes 786440 | tf_op jit(solution)/shard_map/ppermute | solution.py:378
  601.1 30.8 %collective-permute-start.51 = (bf16[64,2048]{1,0:T(8,128)(2,1)S(1)}, bf16[64,2048]{1,0:T(8,128)(2,1)S(1)}, u32[]{:S(2)}, u32[]{:S(2)}) collective-permute-start(bf16[64,2048]{1,0:T(8,128)(2,1)S(1)} %get-tuple-element.104), channel_id=1, source_target_pairs={{0,4},{1,5},{2,6},{3,7},{4,0},{5,1},{6,2},{7,3},{8,12},{9,13},{10,... | collective-permute-start | bytes 786440 | tf_op jit(solution)/shard_map/ppermute | solution.py:378
  601.2 34.7 %collective-permute-start.54 = (bf16[64,2048]{1,0:T(8,128)(2,1)S(1)}, bf16[64,2048]{1,0:T(8,128)(2,1)S(1)}, u32[]{:S(2)}, u32[]{:S(2)}) collective-permute-start(bf16[64,2048]{1,0:T(8,128)(2,1)S(1)} %get-tuple-element.99), channel_id=1, source_target_pairs={{0,7},{1,6},{2,5},{3,4},{4,3},{5,2},{6,1},{7,0},{8,15},{9,14},{10,... | collective-permute-start | bytes 786440 | tf_op jit(solution)/shard_map/ppermute | solution.py:378
  602.5 54.9 %collective-permute-start.29 = (bf16[2,256,768]{2,1,0:T(8,128)(2,1)}, bf16[2,256,768]{2,1,0:T(8,128)(2,1)S(1)}, u32[]{:S(2)}, u32[]{:S(2)}) collective-permute-start(bf16[2,256,768]{2,1,0:T(8,128)(2,1)} %pad_maximum_fusion.10), channel_id=1, source_target_pairs={{0,8},{8,0},{16,24},{24,16},{1,9},{9,1},{17,25},{25,17},{2,10},{10... | collective-permute-start | bytes 2359304 | tf_op jit(solution)/shard_map/ppermute | solution.py:378
  641.8 34.3 %all-to-all-start.1 = ((bf16[8,128,256]{2,1,0:T(8,128)(2,1)}), bf16[8,128,256]{2,1,0:T(8,128)(2,1)S(1)}, u32[]{:S(2)}, u32[]{:S(2)}) async-start(bf16[8,128,256]{2,1,0:T(8,128)(2,1)} %bitcast.308), calls=%async_computation.4 | async-start | bytes 1048576 | tf_op jit(solution)/shard_map/all_to_all | solution.py:830
  656.3 43.8 %collective-permute-start.60 = (f32[1,256]{1,0:T(1,128)S(1)}, f32[1,256]{1,0:T(1,128)S(1)}, u32[]{:S(2)}, u32[]{:S(2)}) collective-permute-start(f32[1,256]{1,0:T(1,128)S(1)} %constant_dynamic-slice_fusion), channel_id=1, source_target_pairs={{0,8},{8,0},{16,24},{24,16},{1,9},{9,1},{17,25},{25,17},{2,10},{10... | collective-permute-start | bytes 3080 | tf_op jit(solution)/shard_map/ppermute | solution.py:378
  (118 other events, 1751.1 us)
Sparse Core Ops, SparseCore 0:
  9.6 49.7 all-gather.4
  89.7 46.6 all-gather.8
  285.3 47.4 reduce-scatter.3
  338.6 45.3 all-gather.6
  408.4 48.7 reduce-scatter.5
  554.2 73.3 reduce-scatter.7

commit v8 on v7

--- a/solution.py
+++ b/solution.py
@@ -438,16 +438,15 @@
 
 def pieces_dp(piece):
     half = piece.shape[0] // 2
-    first, second = swap(piece, "dp", 1), swap(piece, "dp", 2)
-    top, bottom = swap(first[:half], "dp", 2), swap(second[half:], "dp", 1)
+    halves = piece[:half], piece[half:]
+    first = [swap(part, "dp", 1) for part in halves]
+    second = [swap(part, "dp", 2) for part in halves]
+    far = swap(first[0], "dp", 2), swap(second[1], "dp", 1)
     index = lax.axis_index("dp")
-    width = piece.shape[0]
-    far = (index ^ 3) * width
     return [
-        (first, (index ^ 1) * width),
-        (second, (index ^ 2) * width),
-        (top, far),
-        (bottom, far + half),
+        (part, (2 * (index ^ flip) + side) * half)
+        for flip, parts in ((1, first), (2, second), (3, far))
+        for side, part in enumerate(parts)
     ]
 
 
@@ -455,8 +454,8 @@
     rows, width = piece.shape
     pieces = [(piece, lax.axis_index("dp") * rows), *pieces_dp(piece)]
     pieces = [(part, row, 0) for part, row in pieces]
-    whole = placed(pieces[:3], (4 * rows, width))
-    return placed(pieces[3:], (4 * rows, width), whole)
+    whole = placed(pieces[:5], (4 * rows, width))
+    return placed(pieces[5:], (4 * rows, width), whole)
 
 
 def sum_dp(sent, kept):
@@ -814,10 +813,12 @@
     d_gate_up = jnp.concatenate([d_gate, d_up], 1)
     d_hidden_part = jnp.dot(d_gate_up, w_hidden_turned, preferred_element_type=jnp.float32).astype(low)
     d_hidden_sum = scatter_seq(d_hidden_part.reshape(row_count, row_len, model_width))
-    hidden_part = jnp.einsum("nd,nf->df", hidden_low, d_gate_up, preferred_element_type=jnp.float32).astype(low)
+    gate_part = jnp.einsum("nd,nf->df", hidden_low, d_gate, preferred_element_type=jnp.float32).astype(low)
+    up_part = jnp.einsum("nd,nf->df", hidden_low, d_up, preferred_element_type=jnp.float32).astype(low)
     down_part = jnp.einsum("nf,nd->fd", inner_low, d_branch_all, preferred_element_type=jnp.float32).astype(low)
     down_grad = sum_dp(*shares_for(down_part))
-    hidden_own = sum_dp(*shares_for(hidden_part)).astype(low)
+    gate_own = sum_dp(*shares_for(gate_part)).astype(low)
+    up_own = sum_dp(*shares_for(up_part)).astype(low)
     d_hidden = grad_out + d_hidden_sum.astype(jnp.float32).reshape(tok_count, model_width)
 
     attn_gain_term = jnp.sum(d_hidden * attn_unit, 0)
@@ -836,7 +837,8 @@
     d_attn_own = own_columns_of_all(d_attn).reshape(all_count, -1)
     out_part = jnp.einsum("nf,nd->fd", mixed_all, d_attn_own, preferred_element_type=jnp.float32).astype(low)
     out_own = sum_dp(*shares_for(out_part)).astype(low)
-    gate_grad, up_grad = rows_home(hidden_own, dp_count, own_hidden // dp_count)
+    (gate_grad,) = rows_home(gate_own, dp_count, own_hidden // dp_count)
+    (up_grad,) = rows_home(up_own, dp_count, own_hidden // dp_count)
 
     dq_gained, dk_gained, d_value, dots, gain_terms = attend_back(
         qkv_rows, inverses, tables, norm_gains, ids_all, (*kept, log_total), d_mixed, head_size, scale

time: 749 us -> 726 us (0.969)
  waiting for transfers between devices: 349 us -> 302 us
  starting transfers between devices: 82.3 us -> 104 us
    ppermute x61 -> x82, waiting for transfers between devices: 269 us -> 209 us  [swap(): lax.ppermute(value, axis, [(at, at ^ flip) for at in range(lax.axis_size(...]
    ppermute x61 -> x82, starting transfers between devices: 67.2 us -> 92.9 us  [swap(): lax.ppermute(value, axis, [(at, at ^ flip) for at in range(lax.axis_size(...]
    unnamed x153 -> x173, local copies, waits for them, and re-layouts: 28 us -> 29.2 us
  transfers between devices with their start and end apart: 69 -> 90, of which waited for: 35 -> 42; matrix products, arithmetic and copies ran while one was open for 18% -> 19% of each run, Pallas kernels for 7% -> 8%
where the time goes in v8:
time: 726 us; the launch traced here: 713 us
  waiting for transfers between devices  302 us (42%)
  starting transfers between devices  104 us (14%)
  matrix products  92.6 us (13%)
  local copies, waits for them, and re-layouts  77.5 us (11%)
  Pallas kernels  66.5 us (9%)
  other arithmetic  54.5 us (8%)
  between operations  16.2 us (2%)
    ppermute x82, waiting for transfers between devices, swap(): lax.ppermute(value, axis, [(at, at ^ flip) for at in range(lax.axis_size(...  209 us
    ppermute x82, starting transfers between devices, swap(): lax.ppermute(value, axis, [(at, at ^ flip) for at in range(lax.axis_size(...  92.9 us
    reduce_scatter x3, waiting for transfers between devices, scatter_seq(): return lax.psum_scatter(partial, 'seq', scatter_dimension=1, tiled=True)  49 us
    all_gather x2, waiting for transfers between devices, gather_seq(): return lax.all_gather(piece, 'seq', axis=1, tiled=True)  38.3 us
    pallas_call x7, Pallas kernels, placed(): pl.pallas_call(functools.partial(place_kernel, count=len(pieces)), grid_s...  30.8 us
    unnamed x173, local copies, waits for them, and re-layouts  29.2 us
    optimization_barrier x2, local copies, waits for them, and re-layouts, stored_turned(): matrix, after = lax.optimization_barrier((matrix, after))  18.7 us
    pallas_call x1, Pallas kernels, attend_back(): pl.pallas_call(functools.partial(attend_back_kernel, scale=scale), grid=(...  14.9 us
  transfers between devices with their start and end apart: 90, of which 42 were waited for; matrix products, arithmetic and copies ran while one was open for 19% of the time, Pallas kernels for 8%

profile of v8, /device:TPU:0, one launch (start us, length us, event | category | flops | bytes accessed | tf_op | source)
XLA Modules:
  0.0 713.2 jit_solution(9614011252799781188)
XLA Ops:
  15.9 7.9 %collective-permute-done.3.refs_1_ = bf16[256,768]{1,0:T(8,128)(2,1)S(1)} collective-permute-done((bf16[256,768]{1,0:T(8,128)(2,1)S(1)}, bf16[256,768]{1,0:T(8,128)(2,1)S(1)}, u32[]{:S(2)}, u32[]{:S(2)}) %collective-permute-start.3) | collective-permute-done | bytes 393248 | tf_op jit(solution)/shard_map/ppermute | solution.py:378
  47.8 11.6 %all-gather.5.cloned.1.call-done = bf16[1,1024,2048]{2,1,0:T(8,128)(2,1)} async-done(((bf16[1,128,2048]{2,1,0:T(8,128)(2,1)}), bf16[1,1024,2048]{2,1,0:T(8,128)(2,1)}) %all-gather.5.cloned.1.call-update) | async-done | bytes 4194320 | tf_op jit(solution)/shard_map/all_gather | solution.py:370
  79.1 10.5 %attend.1 = (bf16[1,1024,256]{2,1,0:T(8,128)(2,1)}, bf16[1,1024,256]{2,1,0:T(8,128)(2,1)}, bf16[1,1024,256]{2,1,0:T(8,128)(2,1)}, bf16[1,1024,256]{2,1,0:T(8,128)(2,1)}, f32[1,2,1024,1]{3,2,1,0:T(8,128)}) custom-call(f32[1,1024,768]{2,1,0:T(8,128)} %bitcast.349, f32[1,1024,768]{2,1,0:T(8,128)} %bitcast.350, f32[1,1024,768]{2,1,0:T(8,128)} %bitcast.351, ...), custom_call_target="tpu_custom_call" | custom-call | tf_op jit(solution)/shard_map/attend/pallas_call | solution.py:659
  106.6 12.2 %collective-permute-done.12.refs_1_ = bf16[256,1024]{1,0:T(8,128)(2,1)} collective-permute-done((bf16[256,1024]{1,0:T(8,128)(2,1)}, bf16[256,1024]{1,0:T(8,128)(2,1)}, u32[]{:S(2)}, u32[]{:S(2)}) %collective-permute-start.12) | collective-permute-done | bytes 524320 | tf_op jit(solution)/shard_map/ppermute | solution.py:378
  122.8 7.2 %collective-permute-done.24.refs_1_ = bf16[128,2048]{1,0:T(8,128)(2,1)} collective-permute-done((bf16[128,2048]{1,0:T(8,128)(2,1)S(1)}, bf16[128,2048]{1,0:T(8,128)(2,1)}, u32[]{:S(2)}, u32[]{:S(2)}) %collective-permute-start.24) | collective-permute-done | bytes 524320 | tf_op jit(solution)/shard_map/ppermute | solution.py:378
  133.6 7.6 %collective-permute-done.28.refs_2_ = bf16[128,2048]{1,0:T(8,128)(2,1)S(1)} collective-permute-done((bf16[128,2048]{1,0:T(8,128)(2,1)S(1)}, bf16[128,2048]{1,0:T(8,128)(2,1)S(1)}, u32[]{:S(2)}, u32[]{:S(2)}) %collective-permute-start.28) | collective-permute-done | bytes 524320 | tf_op jit(solution)/shard_map/ppermute | solution.py:378
  144.5 7.4 %collective-permute-done.16.refs_5_ = bf16[256,1024]{1,0:T(8,128)(2,1)} collective-permute-done((bf16[256,1024]{1,0:T(8,128)(2,1)}, bf16[256,1024]{1,0:T(8,128)(2,1)}, u32[]{:S(2)}, u32[]{:S(2)}) %collective-permute-start.16) | collective-permute-done | bytes 524320 | tf_op jit(solution)/shard_map/ppermute | solution.py:378
  159.3 15.5 %collective-permute-done.30.refs_1_ = bf16[256,2048]{1,0:T(8,128)(2,1)S(1)} collective-permute-done((bf16[256,2048]{1,0:T(8,128)(2,1)S(1)}, bf16[256,2048]{1,0:T(8,128)(2,1)S(1)}, u32[]{:S(2)}, u32[]{:S(2)}) %collective-permute-start.30) | collective-permute-done | bytes 1048608 | tf_op jit(solution)/shard_map/ppermute | solution.py:378
  179.0 18.5 %collective-permute-done.34.refs_2_ = bf16[256,2048]{1,0:T(8,128)(2,1)} collective-permute-done((bf16[256,2048]{1,0:T(8,128)(2,1)S(1)}, bf16[256,2048]{1,0:T(8,128)(2,1)}, u32[]{:S(2)}, u32[]{:S(2)}) %collective-permute-start.34) | collective-permute-done | bytes 1048608 | tf_op jit(solution)/shard_map/ppermute | solution.py:378
  200.5 11.1 %collective-permute-done.25.refs_0_ = bf16[128,2048]{1,0:T(8,128)(2,1)S(1)} collective-permute-done((bf16[128,2048]{1,0:T(8,128)(2,1)}, bf16[128,2048]{1,0:T(8,128)(2,1)S(1)}, u32[]{:S(2)}, u32[]{:S(2)}) %collective-permute-start.25) | collective-permute-done | bytes 524320 | tf_op jit(solution)/shard_map/ppermute | solution.py:378
  230.8 7.6 %place.9 = bf16[2048,2048]{1,0:T(8,128)(2,1)} custom-call(s32[26]{0:T(128)} %stack.298.spots_ref, bf16[512,2048]{1,0:T(8,128)(2,1)} %refs_0_.1, bf16[256,1024]{1,0:T(8,128)(2,1)} %collective-permute-done.12.refs_1_, bf16[256,1024]{1,0:T(8,128)(2,1)} %collective-permute-done.13.refs_2_, bf16[256,1024]{1,0:T(8,128)(2,1)} %copy-done.36, ...), custom_call_target="tpu_custom_call" | custom-call | tf_op jit(solution)/shard_map/place/pallas_call | solution.py:403
  242.0 12.8 %multiply_reduce_fusion = (f32[1024]{0:T(1024)S(1)}, f32[1024,2048]{1,0:T(8,128)S(1)}) fusion(bf16[2048,2048]{1,0:T(8,128)(2,1)} %place.9, bf16[1,1024,2048]{2,1,0:T(8,128)(2,1)} %all-gather.9.cloned.1.call-done), kind=kOutput, calls=%fused_computation.3 | convolution fusion | flops 8594127872 | bytes 20975616 | tf_op jit(solution)/shard_map/dot_general | solution.py:777
  261.2 8.9 %fusion.104 = f32[1024,2048]{1,0:T(8,128)S(1)} fusion(bf16[1024,2048]{1,0:T(8,128)(2,1)S(1)} %add_convert_fusion, bf16[2048,2048]{1,0:T(8,128)(2,1)S(1)} %copy-done.4), kind=kOutput, calls=%fused_computation.300 | convolution fusion | flops 8589934592 | bytes 20971520 | tf_op jit(solution)/shard_map/dot_general | solution.py:785
  282.6 49.0 %reduce-scatter.4.cloned.1.call-done = bf16[1,128,2048]{2,1,0:T(8,128)(2,1)} async-done(((bf16[1,1024,2048]{2,1,0:T(8,128)(2,1)}), bf16[1,128,2048]{2,1,0:T(8,128)(2,1)}) %reduce-scatter.4.cloned.1.call-update) | async-done | bytes 524304 | tf_op jit(solution)/shard_map/reduce_scatter | solution.py:374
  343.7 12.3 %copy.63 = bf16[2048,2048]{0,1:T(8,128)(2,1)} copy(bf16[2048,2048]{1,0:T(8,128)(2,1)} %place.13) | data formatting | bytes 16777216 | tf_op jit(solution)/shard_map/optimization_barrier | solution.py:485
  356.1 26.7 %all-gather.7.cloned.1.call-done = bf16[1,1024,2048]{2,1,0:T(8,128)(2,1)} async-done(((bf16[1,128,2048]{2,1,0:T(8,128)(2,1)}), bf16[1,1024,2048]{2,1,0:T(8,128)(2,1)}) %all-gather.7.cloned.1.call-update) | async-done | bytes 4194320 | tf_op jit(solution)/shard_map/all_gather | solution.py:370
  382.8 11.7 %multiply_convert_fusion.1 = (bf16[1024,1024]{1,0:T(8,128)(2,1)S(1)}, bf16[1024,1024]{1,0:T(8,128)(2,1)S(1)}) fusion(f32[1024,2048]{1,0:T(8,128)} %copy-done.10, bf16[1024,2048]{0,1:T(8,128)(2,1)} %copy.60, bf16[1,1024,2048]{2,1,0:T(8,128)(2,1)} %all-gather.7.cloned.1.call-done), kind=kOutput, calls=%fused_computation.18 | convolution fusion | flops 4308598784 | bytes 20971520 | tf_op jit(solution)/shard_map/dot_general | solution.py:810
  396.5 10.5 %convert_bitcast_fusion = bf16[1,1024,2048]{2,1,0:T(8,128)(2,1)} fusion(bf16[2048,2048]{0,1:T(8,128)(2,1)S(1)} %copy-done.11, bf16[1024,1024]{1,0:T(8,128)(2,1)S(1)} %get-tuple-element.68, bf16[1024,1024]{1,0:T(8,128)(2,1)S(1)} %get-tuple-element.67), kind=kOutput, calls=%fused_computation.16 | convolution fusion | flops 8600420352 | bytes 16777216 | tf_op jit(solution)/shard_map/dot_general | solution.py:814
  446.5 18.6 %collective-permute-done.67 = bf16[2,256,1024]{2,1,0:T(8,128)(2,1)S(1)} collective-permute-done((bf16[2,256,1024]{2,1,0:T(8,128)(2,1)S(1)}, bf16[2,256,1024]{2,1,0:T(8,128)(2,1)S(1)}, u32[]{:S(2)}, u32[]{:S(2)}) %collective-permute-start.67) | collective-permute-done | bytes 1048608 | tf_op jit(solution)/shard_map/ppermute | solution.py:378
  501.4 14.9 %attend_back.1 = (f32[1,1024,256]{2,1,0:T(8,128)}, f32[1,1024,256]{2,1,0:T(8,128)}, bf16[1,1024,256]{2,1,0:T(8,128)(2,1)}, f32[1,8,1024]{2,1,0:T(8,128)}, f32[1,2,256]{2,1,0:T(2,128)}) custom-call(f32[1,1024,768]{2,1,0:T(8,128)} %bitcast.352, f32[1,1024,768]{2,1,0:T(8,128)} %bitcast.353, f32[1,1024,1]{2,1,0:T(8,128)} %copy.57.qinv_ref, ...), custom_call_target="tpu_custom_call" | custom-call | tf_op jit(solution)/shard_map/attend_back/pallas_call | solution.py:674
  583.9 11.1 %collective-permute-start.60 = (bf16[64,1024]{1,0:T(8,128)(2,1)}, bf16[64,1024]{1,0:T(8,128)(2,1)}, u32[]{:S(2)}, u32[]{:S(2)}) collective-permute-start(bf16[64,1024]{1,0:T(8,128)(2,1)} %get-tuple-element.121), channel_id=1, source_target_pairs={{0,3},{1,2},{2,1},{3,0},{4,7},{5,6},{6,5},{7,4},{8,11},{9,10},{10,... | collective-permute-start | bytes 393224 | tf_op jit(solution)/shard_map/ppermute | solution.py:378
  607.0 13.0 %collective-permute-done.61.refs_4_ = bf16[64,1024]{1,0:T(8,128)(2,1)} collective-permute-done((bf16[64,1024]{1,0:T(8,128)(2,1)}, bf16[64,1024]{1,0:T(8,128)(2,1)}, u32[]{:S(2)}, u32[]{:S(2)}) %collective-permute-start.61) | collective-permute-done | bytes 131104 | tf_op jit(solution)/shard_map/ppermute | solution.py:378
  639.7 12.8 %collective-permute-done.41 = bf16[2,256,768]{2,1,0:T(8,128)(2,1)S(1)} collective-permute-done((bf16[2,256,768]{2,1,0:T(8,128)(2,1)S(1)}, bf16[2,256,768]{2,1,0:T(8,128)(2,1)S(1)}, u32[]{:S(2)}, u32[]{:S(2)}) %collective-permute-start.41) | collective-permute-done | bytes 786464 | tf_op jit(solution)/shard_map/ppermute | solution.py:378
  689.7 9.1 %collective-permute-done.51.refs_5_ = bf16[64,1024]{1,0:T(8,128)(2,1)S(1)} collective-permute-done((bf16[64,1024]{1,0:T(8,128)(2,1)S(1)}, bf16[64,1024]{1,0:T(8,128)(2,1)S(1)}, u32[]{:S(2)}, u32[]{:S(2)}) %collective-permute-start.51) | collective-permute-done | bytes 131104 | tf_op jit(solution)/shard_map/ppermute | solution.py:378
  (489 shorter events, 368.8 us)
Async XLA Ops:
  7.2 52.2 %all-gather.5.cloned.1.call-start = ((), (), s32[]{:S(2)}) async-start(), calls=%async_computation.5 | async-start | bytes 4718592 | tf_op jit(solution)/shard_map/all_gather | solution.py:370
  7.9 234.1 %all-gather.9.cloned.1.call-start = ((), (), s32[]{:S(2)}) async-start(), calls=%async_computation.10 | async-start | bytes 4718592 | tf_op jit(solution)/shard_map/all_gather | solution.py:776
  89.6 242.0 %reduce-scatter.4.cloned.1.call-start = ((), (), s32[]{:S(2)}) async-start(), calls=%async_computation.6 | async-start | bytes 4718592 | tf_op jit(solution)/shard_map/reduce_scatter | solution.py:374
  152.8 44.6 %collective-permute-start.34 = (bf16[256,2048]{1,0:T(8,128)(2,1)S(1)}, bf16[256,2048]{1,0:T(8,128)(2,1)}, u32[]{:S(2)}, u32[]{:S(2)}) collective-permute-start(bf16[256,2048]{1,0:T(8,128)(2,1)S(1)} %get-tuple-element.107), channel_id=1, source_target_pairs={{0,8},{8,0},{16,24},{24,16},{1,9},{9,1},{17,25},{25,17},{2,10},{10... | collective-permute-start | bytes 3145736 | tf_op jit(solution)/shard_map/ppermute | solution.py:378
  155.2 45.3 %collective-permute-start.35 = (bf16[256,2048]{1,0:T(8,128)(2,1)S(1)}, bf16[256,2048]{1,0:T(8,128)(2,1)}, u32[]{:S(2)}, u32[]{:S(2)}) collective-permute-start(bf16[256,2048]{1,0:T(8,128)(2,1)S(1)} %get-tuple-element.108), channel_id=1, source_target_pairs={{0,16},{8,24},{16,0},{24,8},{1,17},{9,25},{17,1},{25,9},{2,18},{10... | collective-permute-start | bytes 3145736 | tf_op jit(solution)/shard_map/ppermute | solution.py:378
  158.4 53.2 %collective-permute-start.25 = (bf16[128,2048]{1,0:T(8,128)(2,1)}, bf16[128,2048]{1,0:T(8,128)(2,1)S(1)}, u32[]{:S(2)}, u32[]{:S(2)}) collective-permute-start(bf16[128,2048]{1,0:T(8,128)(2,1)} %collective-permute-done.24.refs_1_), channel_id=1, source_target_pairs={{0,16},{8,24},{16,0},{24,8},{1,17},{9,25},{17,1},{25,9},{2,18},{10... | collective-permute-start | bytes 1572872 | tf_op jit(solution)/shard_map/ppermute | solution.py:378
  174.8 37.6 %collective-permute-start.27 = (bf16[128,2048]{1,0:T(8,128)(2,1)S(1)}, bf16[128,2048]{1,0:T(8,128)(2,1)S(1)}, u32[]{:S(2)}, u32[]{:S(2)}) collective-permute-start(bf16[128,2048]{1,0:T(8,128)(2,1)S(1)} %collective-permute-done.26.refs_4_), channel_id=1, source_target_pairs={{0,8},{8,0},{16,24},{24,16},{1,9},{9,1},{17,25},{25,17},{2,10},{10... | collective-permute-start | bytes 1572872 | tf_op jit(solution)/shard_map/ppermute | solution.py:378
  178.0 60.4 %collective-permute-start.31 = (bf16[256,2048]{1,0:T(8,128)(2,1)S(1)}, bf16[256,2048]{1,0:T(8,128)(2,1)}, u32[]{:S(2)}, u32[]{:S(2)}) collective-permute-start(bf16[256,2048]{1,0:T(8,128)(2,1)S(1)} %collective-permute-done.30.refs_1_), channel_id=1, source_target_pairs={{0,16},{8,24},{16,0},{24,8},{1,17},{9,25},{17,1},{25,9},{2,18},{10... | collective-permute-start | bytes 3145736 | tf_op jit(solution)/shard_map/ppermute | solution.py:378
  197.4 41.0 %collective-permute-start.33 = (bf16[256,2048]{1,0:T(8,128)(2,1)}, bf16[256,2048]{1,0:T(8,128)(2,1)}, u32[]{:S(2)}, u32[]{:S(2)}) collective-permute-start(bf16[256,2048]{1,0:T(8,128)(2,1)} %collective-permute-done.32.refs_4_), channel_id=1, source_target_pairs={{0,8},{8,0},{16,24},{24,16},{1,9},{9,1},{17,25},{25,17},{2,10},{10... | collective-permute-start | bytes 3145736 | tf_op jit(solution)/shard_map/ppermute | solution.py:378
  281.9 100.9 %all-gather.7.cloned.1.call-start = ((), (), s32[]{:S(2)}) async-start(), calls=%async_computation.7 | async-start | bytes 4718592 | tf_op jit(solution)/shard_map/all_gather | solution.py:370
  337.3 133.8 %reduce-scatter.6.cloned.1.call-start = ((), (), s32[]{:S(2)}) async-start(), calls=%async_computation.8 | async-start | bytes 4718592 | tf_op jit(solution)/shard_map/reduce_scatter | solution.py:374
  423.9 41.2 %collective-permute-start.67 = (bf16[2,256,1024]{2,1,0:T(8,128)(2,1)S(1)}, bf16[2,256,1024]{2,1,0:T(8,128)(2,1)S(1)}, u32[]{:S(2)}, u32[]{:S(2)}) collective-permute-start(bf16[2,256,1024]{2,1,0:T(8,128)(2,1)S(1)} %pad_maximum_fusion.5), channel_id=1, source_target_pairs={{0,16},{8,24},{16,0},{24,8},{1,17},{9,25},{17,1},{25,9},{2,18},{10... | collective-permute-start | bytes 3145736 | tf_op jit(solution)/shard_map/ppermute | solution.py:378
  424.6 42.3 %collective-permute-start.65 = (bf16[2,256,1024]{2,1,0:T(8,128)(2,1)S(1)}, bf16[2,256,1024]{2,1,0:T(8,128)(2,1)S(1)}, u32[]{:S(2)}, u32[]{:S(2)}) collective-permute-start(bf16[2,256,1024]{2,1,0:T(8,128)(2,1)S(1)} %pad_maximum_fusion.4), channel_id=1, source_target_pairs={{0,8},{8,0},{16,24},{24,16},{1,9},{9,1},{17,25},{25,17},{2,10},{10... | collective-permute-start | bytes 3145736 | tf_op jit(solution)/shard_map/ppermute | solution.py:378
  433.8 53.8 %collective-permute-start.56 = (bf16[2,256,1024]{2,1,0:T(8,128)(2,1)}, bf16[2,256,1024]{2,1,0:T(8,128)(2,1)}, u32[]{:S(2)}, u32[]{:S(2)}) collective-permute-start(bf16[2,256,1024]{2,1,0:T(8,128)(2,1)} %pad_maximum_fusion.3), channel_id=1, source_target_pairs={{0,16},{8,24},{16,0},{24,8},{1,17},{9,25},{17,1},{25,9},{2,18},{10... | collective-permute-start | bytes 3145736 | tf_op jit(solution)/shard_map/ppermute | solution.py:378
  440.9 51.0 %collective-permute-start.54 = (bf16[2,256,1024]{2,1,0:T(8,128)(2,1)}, bf16[2,256,1024]{2,1,0:T(8,128)(2,1)}, u32[]{:S(2)}, u32[]{:S(2)}) collective-permute-start(bf16[2,256,1024]{2,1,0:T(8,128)(2,1)} %pad_maximum_fusion.2), channel_id=1, source_target_pairs={{0,8},{8,0},{16,24},{24,16},{1,9},{9,1},{17,25},{25,17},{2,10},{10... | collective-permute-start | bytes 3145736 | tf_op jit(solution)/shard_map/ppermute | solution.py:378
  443.7 105.4 %collective-permute-start.77 = (bf16[128,2048]{1,0:T(8,128)(2,1)}, bf16[128,2048]{1,0:T(8,128)(2,1)}, u32[]{:S(2)}, u32[]{:S(2)}) collective-permute-start(bf16[128,2048]{1,0:T(8,128)(2,1)} %fusion.65), channel_id=1, source_target_pairs={{0,16},{8,24},{16,0},{24,8},{1,17},{9,25},{17,1},{25,9},{2,18},{10... | collective-permute-start | bytes 1572872 | tf_op jit(solution)/shard_map/ppermute | solution.py:378
  465.0 86.2 %collective-permute-start.79 = (bf16[128,2048]{1,0:T(8,128)(2,1)}, bf16[128,2048]{1,0:T(8,128)(2,1)}, u32[]{:S(2)}, u32[]{:S(2)}) collective-permute-start(bf16[128,2048]{1,0:T(8,128)(2,1)} %fusion.66), channel_id=1, source_target_pairs={{0,8},{8,0},{16,24},{24,16},{1,9},{9,1},{17,25},{25,17},{2,10},{10... | collective-permute-start | bytes 1572872 | tf_op jit(solution)/shard_map/ppermute | solution.py:378
  467.0 50.9 %collective-permute-start.68 = (bf16[256,1024]{1,0:T(8,128)(2,1)}, bf16[256,1024]{1,0:T(8,128)(2,1)}, u32[]{:S(2)}, u32[]{:S(2)}) collective-permute-start(bf16[256,1024]{1,0:T(8,128)(2,1)} %fusion.64), channel_id=1, source_target_pairs={{0,8},{8,0},{16,24},{24,16},{1,9},{9,1},{17,25},{25,17},{2,10},{10... | collective-permute-start | bytes 1572872 | tf_op jit(solution)/shard_map/ppermute | solution.py:378
  486.1 217.5 %reduce-scatter.8.cloned.1.call-start = ((), (), s32[]{:S(2)}) async-start(), calls=%async_computation.9 | async-start | bytes 4718592 | tf_op jit(solution)/shard_map/reduce_scatter | solution.py:374
  487.6 34.3 %collective-permute-start.66 = (bf16[256,1024]{1,0:T(8,128)(2,1)}, bf16[256,1024]{1,0:T(8,128)(2,1)}, u32[]{:S(2)}, u32[]{:S(2)}) collective-permute-start(bf16[256,1024]{1,0:T(8,128)(2,1)} %fusion.63), channel_id=1, source_target_pairs={{0,16},{8,24},{16,0},{24,8},{1,17},{9,25},{17,1},{25,9},{2,18},{10... | collective-permute-start | bytes 1572872 | tf_op jit(solution)/shard_map/ppermute | solution.py:378
  492.0 34.2 %collective-permute-start.57 = (bf16[256,1024]{1,0:T(8,128)(2,1)}, bf16[256,1024]{1,0:T(8,128)(2,1)}, u32[]{:S(2)}, u32[]{:S(2)}) collective-permute-start(bf16[256,1024]{1,0:T(8,128)(2,1)} %fusion.62), channel_id=1, source_target_pairs={{0,8},{8,0},{16,24},{24,16},{1,9},{9,1},{17,25},{25,17},{2,10},{10... | collective-permute-start | bytes 1572872 | tf_op jit(solution)/shard_map/ppermute | solution.py:378
  564.0 36.7 %collective-permute-start.62 = (bf16[64,1024]{1,0:T(8,128)(2,1)S(1)}, bf16[64,1024]{1,0:T(8,128)(2,1)S(1)}, u32[]{:S(2)}, u32[]{:S(2)}) collective-permute-start(bf16[64,1024]{1,0:T(8,128)(2,1)S(1)} %get-tuple-element.124), channel_id=1, source_target_pairs={{0,5},{1,4},{2,7},{3,6},{4,1},{5,0},{6,3},{7,2},{8,13},{9,12},{10,... | collective-permute-start | bytes 393224 | tf_op jit(solution)/shard_map/ppermute | solution.py:378
  601.5 34.1 %collective-permute-start.39 = (bf16[2,256,768]{2,1,0:T(8,128)(2,1)}, bf16[2,256,768]{2,1,0:T(8,128)(2,1)S(1)}, u32[]{:S(2)}, u32[]{:S(2)}) collective-permute-start(bf16[2,256,768]{2,1,0:T(8,128)(2,1)} %pad_maximum_fusion.9), channel_id=1, source_target_pairs={{0,8},{8,0},{16,24},{24,16},{1,9},{9,1},{17,25},{25,17},{2,10},{10... | collective-permute-start | bytes 2359304 | tf_op jit(solution)/shard_map/ppermute | solution.py:378
  634.5 43.3 %collective-permute-start.81 = (f32[1,256]{1,0:T(1,128)S(1)}, f32[1,256]{1,0:T(1,128)S(1)}, u32[]{:S(2)}, u32[]{:S(2)}) collective-permute-start(f32[1,256]{1,0:T(1,128)S(1)} %constant_dynamic-slice_fusion.3), channel_id=1, source_target_pairs={{0,8},{8,0},{16,24},{24,16},{1,9},{9,1},{17,25},{25,17},{2,10},{10... | collective-permute-start | bytes 3080 | tf_op jit(solution)/shard_map/ppermute | solution.py:378
  (149 other events, 2654.2 us)
Sparse Core Ops, SparseCore 0:
  9.6 49.7 all-gather.4
  89.7 46.6 all-gather.8
  282.0 49.5 reduce-scatter.3
  337.4 45.3 all-gather.6
  407.1 48.7 reduce-scatter.5
  540.2 84.7 reduce-scatter.7

commit v9 on v7

--- a/solution.py
+++ b/solution.py
@@ -814,10 +814,12 @@
     d_gate_up = jnp.concatenate([d_gate, d_up], 1)
     d_hidden_part = jnp.dot(d_gate_up, w_hidden_turned, preferred_element_type=jnp.float32).astype(low)
     d_hidden_sum = scatter_seq(d_hidden_part.reshape(row_count, row_len, model_width))
-    hidden_part = jnp.einsum("nd,nf->df", hidden_low, d_gate_up, preferred_element_type=jnp.float32).astype(low)
+    gate_part = jnp.einsum("nd,nf->df", hidden_low, d_gate, preferred_element_type=jnp.float32).astype(low)
+    up_part = jnp.einsum("nd,nf->df", hidden_low, d_up, preferred_element_type=jnp.float32).astype(low)
     down_part = jnp.einsum("nf,nd->fd", inner_low, d_branch_all, preferred_element_type=jnp.float32).astype(low)
     down_grad = sum_dp(*shares_for(down_part))
-    hidden_own = sum_dp(*shares_for(hidden_part)).astype(low)
+    gate_own = sum_dp(*shares_for(gate_part)).astype(low)
+    up_own = sum_dp(*shares_for(up_part)).astype(low)
     d_hidden = grad_out + d_hidden_sum.astype(jnp.float32).reshape(tok_count, model_width)
 
     attn_gain_term = jnp.sum(d_hidden * attn_unit, 0)
@@ -832,11 +834,8 @@
         return split.reshape(row_count, row_len, width)
 
     d_mixed = own_columns_of_all(d_mixed)
-    d_mixed, d_attn = lax.optimization_barrier((d_mixed, d_attn))
-    d_attn_own = own_columns_of_all(d_attn).reshape(all_count, -1)
-    out_part = jnp.einsum("nf,nd->fd", mixed_all, d_attn_own, preferred_element_type=jnp.float32).astype(low)
-    out_own = sum_dp(*shares_for(out_part)).astype(low)
-    gate_grad, up_grad = rows_home(hidden_own, dp_count, own_hidden // dp_count)
+    (gate_grad,) = rows_home(gate_own, dp_count, own_hidden // dp_count)
+    (up_grad,) = rows_home(up_own, dp_count, own_hidden // dp_count)
 
     dq_gained, dk_gained, d_value, dots, gain_terms = attend_back(
         qkv_rows, inverses, tables, norm_gains, ids_all, (*kept, log_total), d_mixed, head_size, scale
@@ -865,9 +864,13 @@
     d_qkv = jnp.concatenate([dq_pre, dk_pre, d_value], 1)
     d_tokens_part = jnp.einsum("nf,df->nd", d_qkv, w_qkv, preferred_element_type=jnp.float32).astype(low)
     d_qkv, d_tokens_part = lax.optimization_barrier((d_qkv, d_tokens_part))
+    qkv_part = jnp.einsum("nd,nf->df", tokens_all, d_qkv, preferred_element_type=jnp.float32).astype(low)
+    d_attn, qkv_part = lax.optimization_barrier((d_attn, qkv_part))
+    d_attn_own = own_columns_of_all(d_attn).reshape(all_count, -1)
+    out_part = jnp.einsum("nf,nd->fd", mixed_all, d_attn_own, preferred_element_type=jnp.float32).astype(low)
+    out_own = sum_dp(*shares_for(out_part)).astype(low)
     d_tokens_sum = scatter_seq(d_tokens_part.reshape(row_count, row_len, model_width))
     d_tokens = d_hidden + d_tokens_sum.astype(jnp.float32).reshape(tok_count, model_width)
-    qkv_part = jnp.einsum("nd,nf->df", tokens_all, d_qkv, preferred_element_type=jnp.float32).astype(low)
     qkv_own = sum_dp(*shares_for(qkv_part)).astype(low)
     attn_home = rows_home(jnp.concatenate([qkv_own, out_own], 1), 1, own_features)
     share = feature_count // (dp_count * seq_count)

time: 749 us -> 725 us (0.968)
  waiting for transfers between devices: 349 us -> 302 us
  starting transfers between devices: 82.3 us -> 98.5 us
    ppermute x61 -> x72, waiting for transfers between devices: 269 us -> 216 us  [swap(): lax.ppermute(value, axis, [(at, at ^ flip) for at in range(lax.axis_size(...]
    ppermute x61 -> x72, starting transfers between devices: 67.2 us -> 87.9 us  [swap(): lax.ppermute(value, axis, [(at, at ^ flip) for at in range(lax.axis_size(...]
    unnamed x153 -> x167, local copies, waits for them, and re-layouts: 28 us -> 28.7 us
  transfers between devices with their start and end apart: 69 -> 80, of which waited for: 35 -> 35; matrix products, arithmetic and copies ran while one was open for 18% -> 19% of each run, Pallas kernels for 7% -> 8%
where the time goes in v9:
time: 725 us; the launch traced here: 711 us
  waiting for transfers between devices  302 us (42%)
  starting transfers between devices  98.5 us (14%)
  matrix products  92.7 us (13%)
  local copies, waits for them, and re-layouts  78.2 us (11%)
  Pallas kernels  66.5 us (9%)
  other arithmetic  56.4 us (8%)
  between operations  16.2 us (2%)
    ppermute x72, waiting for transfers between devices, swap(): lax.ppermute(value, axis, [(at, at ^ flip) for at in range(lax.axis_size(...  216 us
    ppermute x72, starting transfers between devices, swap(): lax.ppermute(value, axis, [(at, at ^ flip) for at in range(lax.axis_size(...  87.9 us
    reduce_scatter x3, waiting for transfers between devices, scatter_seq(): return lax.psum_scatter(partial, 'seq', scatter_dimension=1, tiled=True)  46.9 us
    all_gather x2, waiting for transfers between devices, gather_seq(): return lax.all_gather(piece, 'seq', axis=1, tiled=True)  33.1 us
    pallas_call x7, Pallas kernels, placed(): pl.pallas_call(functools.partial(place_kernel, count=len(pieces)), grid_s...  30.8 us
    unnamed x167, local copies, waits for them, and re-layouts  28.7 us
    optimization_barrier x2, local copies, waits for them, and re-layouts, stored_turned(): matrix, after = lax.optimization_barrier((matrix, after))  19 us
    pallas_call x1, Pallas kernels, attend_back(): pl.pallas_call(functools.partial(attend_back_kernel, scale=scale), grid=(...  14.8 us
  transfers between devices with their start and end apart: 80, of which 35 were waited for; matrix products, arithmetic and copies ran while one was open for 19% of the time, Pallas kernels for 8%

profile of v9, /device:TPU:0, one launch (start us, length us, event | category | flops | bytes accessed | tf_op | source)
XLA Modules:
  0.0 710.6 jit_solution(4827453666493334783)
XLA Ops:
  14.5 16.0 %collective-permute-done.3.refs_1_ = bf16[512,768]{1,0:T(8,128)(2,1)S(1)} collective-permute-done((bf16[512,768]{1,0:T(8,128)(2,1)S(1)}, bf16[512,768]{1,0:T(8,128)(2,1)S(1)}, u32[]{:S(2)}, u32[]{:S(2)}) %collective-permute-start.3) | collective-permute-done | bytes 786464 | tf_op jit(solution)/shard_map/ppermute | solution.py:378
  52.8 6.7 all-gather.5.cloned.1.call-done
  79.1 10.5 %attend.1 = (bf16[1,1024,256]{2,1,0:T(8,128)(2,1)}, bf16[1,1024,256]{2,1,0:T(8,128)(2,1)}, bf16[1,1024,256]{2,1,0:T(8,128)(2,1)}, bf16[1,1024,256]{2,1,0:T(8,128)(2,1)}, f32[1,2,1024,1]{3,2,1,0:T(8,128)}) custom-call(f32[1,1024,768]{2,1,0:T(8,128)} %bitcast.345, f32[1,1024,768]{2,1,0:T(8,128)} %bitcast.346, f32[1,1024,768]{2,1,0:T(8,128)} %bitcast.347, ...), custom_call_target="tpu_custom_call" | custom-call | tf_op jit(solution)/shard_map/attend/pallas_call | solution.py:660
  105.7 11.4 %collective-permute-done.10.refs_1_ = bf16[512,1024]{1,0:T(8,128)(2,1)} collective-permute-done((bf16[512,1024]{1,0:T(8,128)(2,1)}, bf16[512,1024]{1,0:T(8,128)(2,1)}, u32[]{:S(2)}, u32[]{:S(2)}) %collective-permute-start.10) | collective-permute-done | bytes 1048608 | tf_op jit(solution)/shard_map/ppermute | solution.py:378
  119.7 52.2 %collective-permute-done.11.refs_2_ = bf16[512,1024]{1,0:T(8,128)(2,1)} collective-permute-done((bf16[512,1024]{1,0:T(8,128)(2,1)}, bf16[512,1024]{1,0:T(8,128)(2,1)}, u32[]{:S(2)}, u32[]{:S(2)}) %collective-permute-start.11) | collective-permute-done | bytes 1048608 | tf_op jit(solution)/shard_map/ppermute | solution.py:378
  174.4 7.3 %collective-permute-done.18.refs_1_ = bf16[256,2048]{1,0:T(8,128)(2,1)S(1)} collective-permute-done((bf16[256,2048]{1,0:T(8,128)(2,1)S(1)}, bf16[256,2048]{1,0:T(8,128)(2,1)S(1)}, u32[]{:S(2)}, u32[]{:S(2)}) %collective-permute-start.18) | collective-permute-done | bytes 1048608 | tf_op jit(solution)/shard_map/ppermute | solution.py:378
  183.2 11.0 %collective-permute-done.20.refs_2_ = bf16[256,2048]{1,0:T(8,128)(2,1)S(1)} collective-permute-done((bf16[256,2048]{1,0:T(8,128)(2,1)S(1)}, bf16[256,2048]{1,0:T(8,128)(2,1)S(1)}, u32[]{:S(2)}, u32[]{:S(2)}) %collective-permute-start.20) | collective-permute-done | bytes 1048608 | tf_op jit(solution)/shard_map/ppermute | solution.py:378
  198.4 7.1 collective-permute-done.12.refs_3_
  233.7 7.5 %place.9 = bf16[2048,2048]{1,0:T(8,128)(2,1)} custom-call(s32[18]{0:T(128)} %stack.274.spots_ref, bf16[512,2048]{1,0:T(8,128)(2,1)} %refs_0_.1, bf16[512,1024]{1,0:T(8,128)(2,1)} %collective-permute-done.10.refs_1_, bf16[512,1024]{1,0:T(8,128)(2,1)} %collective-permute-done.11.refs_2_, bf16[256,1024]{1,0:T(8,128)(2,1)} %copy-done.43, ...), custom_call_target="tpu_custom_call" | custom-call | tf_op jit(solution)/shard_map/place/pallas_call | solution.py:403
  244.9 12.9 %multiply_reduce_fusion = (f32[1024]{0:T(1024)S(1)}, f32[1024,2048]{1,0:T(8,128)S(1)}) fusion(bf16[2048,2048]{1,0:T(8,128)(2,1)} %place.9, bf16[1,1024,2048]{2,1,0:T(8,128)(2,1)} %all-gather.9.cloned.1.call-done), kind=kOutput, calls=%fused_computation.3 | convolution fusion | flops 8594127872 | bytes 20975616 | tf_op jit(solution)/shard_map/dot_general | solution.py:778
  264.3 8.9 %fusion.101 = f32[1024,2048]{1,0:T(8,128)S(1)} fusion(bf16[1024,2048]{1,0:T(8,128)(2,1)S(1)} %add_convert_fusion, bf16[2048,2048]{1,0:T(8,128)(2,1)S(1)} %copy-done.4), kind=kOutput, calls=%fused_computation.295 | convolution fusion | flops 8589934592 | bytes 20971520 | tf_op jit(solution)/shard_map/dot_general | solution.py:786
  278.4 6.5 convolution_convert_fusion.3
  285.7 46.9 %reduce-scatter.4.cloned.1.call-done = bf16[1,128,2048]{2,1,0:T(8,128)(2,1)} async-done(((bf16[1,1024,2048]{2,1,0:T(8,128)(2,1)}), bf16[1,128,2048]{2,1,0:T(8,128)(2,1)}) %reduce-scatter.4.cloned.1.call-update) | async-done | bytes 524304 | tf_op jit(solution)/shard_map/reduce_scatter | solution.py:374
  344.7 12.6 %copy.63 = bf16[2048,2048]{0,1:T(8,128)(2,1)} copy(bf16[2048,2048]{1,0:T(8,128)(2,1)} %place.13) | data formatting | bytes 16777216 | tf_op jit(solution)/shard_map/optimization_barrier | solution.py:486
  357.3 26.4 %all-gather.7.cloned.1.call-done = bf16[1,1024,2048]{2,1,0:T(8,128)(2,1)} async-done(((bf16[1,128,2048]{2,1,0:T(8,128)(2,1)}), bf16[1,1024,2048]{2,1,0:T(8,128)(2,1)}) %all-gather.7.cloned.1.call-update) | async-done | bytes 4194320 | tf_op jit(solution)/shard_map/all_gather | solution.py:370
  383.7 11.7 %multiply_convert_fusion.1 = (bf16[1024,1024]{1,0:T(8,128)(2,1)S(1)}, bf16[1024,1024]{1,0:T(8,128)(2,1)S(1)}) fusion(f32[1024,2048]{1,0:T(8,128)} %copy-done.9, bf16[1024,2048]{0,1:T(8,128)(2,1)} %copy.60, bf16[1,1024,2048]{2,1,0:T(8,128)(2,1)} %all-gather.7.cloned.1.call-done), kind=kOutput, calls=%fused_computation.18 | convolution fusion | flops 4308598784 | bytes 20971520 | tf_op jit(solution)/shard_map/dot_general | solution.py:811
  397.5 10.5 %convert_bitcast_fusion = bf16[1,1024,2048]{2,1,0:T(8,128)(2,1)} fusion(bf16[2048,2048]{0,1:T(8,128)(2,1)S(1)} %copy-done.10, bf16[1024,1024]{1,0:T(8,128)(2,1)S(1)} %get-tuple-element.68, bf16[1024,1024]{1,0:T(8,128)(2,1)S(1)} %get-tuple-element.67), kind=kOutput, calls=%fused_computation.16 | convolution fusion | flops 8600420352 | bytes 16777216 | tf_op jit(solution)/shard_map/dot_general | solution.py:815
  408.2 7.0 fusion.19
  447.5 18.6 %collective-permute-done.57 = bf16[2,256,1024]{2,1,0:T(8,128)(2,1)S(1)} collective-permute-done((bf16[2,256,1024]{2,1,0:T(8,128)(2,1)S(1)}, bf16[2,256,1024]{2,1,0:T(8,128)(2,1)S(1)}, u32[]{:S(2)}, u32[]{:S(2)}) %collective-permute-start.57) | collective-permute-done | bytes 1048608 | tf_op jit(solution)/shard_map/ppermute | solution.py:378
  502.4 14.8 %attend_back.1 = (f32[1,1024,256]{2,1,0:T(8,128)}, f32[1,1024,256]{2,1,0:T(8,128)}, bf16[1,1024,256]{2,1,0:T(8,128)(2,1)}, f32[1,8,1024]{2,1,0:T(8,128)}, f32[1,2,256]{2,1,0:T(2,128)}) custom-call(f32[1,1024,768]{2,1,0:T(8,128)} %bitcast.348, f32[1,1024,768]{2,1,0:T(8,128)} %bitcast.349, f32[1,1024,1]{2,1,0:T(8,128)} %copy.57.qinv_ref, ...), custom_call_target="tpu_custom_call" | custom-call | tf_op jit(solution)/shard_map/attend_back/pallas_call | solution.py:675
  584.9 11.1 %collective-permute-start.50 = (bf16[64,1024]{1,0:T(8,128)(2,1)}, bf16[64,1024]{1,0:T(8,128)(2,1)}, u32[]{:S(2)}, u32[]{:S(2)}) collective-permute-start(bf16[64,1024]{1,0:T(8,128)(2,1)} %get-tuple-element.115), channel_id=1, source_target_pairs={{0,3},{1,2},{2,1},{3,0},{4,7},{5,6},{6,5},{7,4},{8,11},{9,10},{10,... | collective-permute-start | bytes 393224 | tf_op jit(solution)/shard_map/ppermute | solution.py:378
  607.9 13.0 %collective-permute-done.51.refs_4_ = bf16[64,1024]{1,0:T(8,128)(2,1)} collective-permute-done((bf16[64,1024]{1,0:T(8,128)(2,1)}, bf16[64,1024]{1,0:T(8,128)(2,1)}, u32[]{:S(2)}, u32[]{:S(2)}) %collective-permute-start.51) | collective-permute-done | bytes 131104 | tf_op jit(solution)/shard_map/ppermute | solution.py:378
  640.0 7.2 %collective-permute-done.31 = bf16[2,256,768]{2,1,0:T(8,128)(2,1)} collective-permute-done((bf16[2,256,768]{2,1,0:T(8,128)(2,1)}, bf16[2,256,768]{2,1,0:T(8,128)(2,1)}, u32[]{:S(2)}, u32[]{:S(2)}) %collective-permute-start.31) | collective-permute-done | bytes 786464 | tf_op jit(solution)/shard_map/ppermute | solution.py:378
  686.8 9.5 %collective-permute-done.41.refs_5_ = bf16[64,1024]{1,0:T(8,128)(2,1)S(1)} collective-permute-done((bf16[64,1024]{1,0:T(8,128)(2,1)S(1)}, bf16[64,1024]{1,0:T(8,128)(2,1)S(1)}, u32[]{:S(2)}, u32[]{:S(2)}) %collective-permute-start.41) | collective-permute-done | bytes 131104 | tf_op jit(solution)/shard_map/ppermute | solution.py:378
  (468 shorter events, 347.0 us)
Async XLA Ops:
  7.2 52.2 %all-gather.5.cloned.1.call-start = ((), (), s32[]{:S(2)}) async-start(), calls=%async_computation.5 | async-start | bytes 4718592 | tf_op jit(solution)/shard_map/all_gather | solution.py:370
  7.9 236.9 %all-gather.9.cloned.1.call-start = ((), (), s32[]{:S(2)}) async-start(), calls=%async_computation.10 | async-start | bytes 4718592 | tf_op jit(solution)/shard_map/all_gather | solution.py:777
  89.6 243.0 %reduce-scatter.4.cloned.1.call-start = ((), (), s32[]{:S(2)}) async-start(), calls=%async_computation.6 | async-start | bytes 4718592 | tf_op jit(solution)/shard_map/reduce_scatter | solution.py:374
  100.2 95.6 %collective-permute-start.22 = (bf16[512,2048]{1,0:T(8,128)(2,1)S(1)}, bf16[512,2048]{1,0:T(8,128)(2,1)S(1)}, u32[]{:S(2)}, u32[]{:S(2)}) collective-permute-start(bf16[512,2048]{1,0:T(8,128)(2,1)S(1)} %dynamic-slice_dynamic-update-slice_fusion.refs_0_), channel_id=1, source_target_pairs={{0,8},{8,0},{16,24},{24,16},{1,9},{9,1},{17,25},{25,17},{2,10},{10... | collective-permute-start | bytes 6291464 | tf_op jit(solution)/shard_map/ppermute | solution.py:378
  100.8 104.7 %collective-permute-start.24 = (bf16[512,2048]{1,0:T(8,128)(2,1)S(1)}, bf16[512,2048]{1,0:T(8,128)(2,1)S(1)}, u32[]{:S(2)}, u32[]{:S(2)}) collective-permute-start(bf16[512,2048]{1,0:T(8,128)(2,1)S(1)} %dynamic-slice_dynamic-update-slice_fusion.refs_0_), channel_id=1, source_target_pairs={{0,16},{8,24},{16,0},{24,8},{1,17},{9,25},{17,1},{25,9},{2,18},{10... | collective-permute-start | bytes 6291464 | tf_op jit(solution)/shard_map/ppermute | solution.py:378
  102.3 69.6 %collective-permute-start.11 = (bf16[512,1024]{1,0:T(8,128)(2,1)}, bf16[512,1024]{1,0:T(8,128)(2,1)}, u32[]{:S(2)}, u32[]{:S(2)}) collective-permute-start(bf16[512,1024]{1,0:T(8,128)(2,1)} %constant_dynamic-slice_fusion.14), channel_id=1, source_target_pairs={{0,16},{8,24},{16,0},{24,8},{1,17},{9,25},{17,1},{25,9},{2,18},{10... | collective-permute-start | bytes 3145736 | tf_op jit(solution)/shard_map/ppermute | solution.py:378
  104.1 77.6 %collective-permute-start.18 = (bf16[256,2048]{1,0:T(8,128)(2,1)S(1)}, bf16[256,2048]{1,0:T(8,128)(2,1)S(1)}, u32[]{:S(2)}, u32[]{:S(2)}) collective-permute-start(bf16[256,2048]{1,0:T(8,128)(2,1)S(1)} %constant_dynamic-slice_fusion.13.refs_0_), channel_id=1, source_target_pairs={{0,8},{8,0},{16,24},{24,16},{1,9},{9,1},{17,25},{25,17},{2,10},{10... | collective-permute-start | bytes 3145736 | tf_op jit(solution)/shard_map/ppermute | solution.py:378
  117.1 77.1 %collective-permute-start.20 = (bf16[256,2048]{1,0:T(8,128)(2,1)S(1)}, bf16[256,2048]{1,0:T(8,128)(2,1)S(1)}, u32[]{:S(2)}, u32[]{:S(2)}) collective-permute-start(bf16[256,2048]{1,0:T(8,128)(2,1)S(1)} %constant_dynamic-slice_fusion.13.refs_0_), channel_id=1, source_target_pairs={{0,16},{8,24},{16,0},{24,8},{1,17},{9,25},{17,1},{25,9},{2,18},{10... | collective-permute-start | bytes 3145736 | tf_op jit(solution)/shard_map/ppermute | solution.py:378
  171.9 33.6 %collective-permute-start.12 = (bf16[256,1024]{1,0:T(8,128)(2,1)S(1)}, bf16[256,1024]{1,0:T(8,128)(2,1)S(1)}, u32[]{:S(2)}, u32[]{:S(2)}) collective-permute-start(bf16[256,1024]{1,0:T(8,128)(2,1)S(1)} %slice.198), channel_id=1, source_target_pairs={{0,16},{8,24},{16,0},{24,8},{1,17},{9,25},{17,1},{25,9},{2,18},{10... | collective-permute-start | bytes 1572872 | tf_op jit(solution)/shard_map/ppermute | solution.py:378
  284.9 98.8 %all-gather.7.cloned.1.call-start = ((), (), s32[]{:S(2)}) async-start(), calls=%async_computation.7 | async-start | bytes 4718592 | tf_op jit(solution)/shard_map/all_gather | solution.py:370
  338.3 133.8 %reduce-scatter.6.cloned.1.call-start = ((), (), s32[]{:S(2)}) async-start(), calls=%async_computation.8 | async-start | bytes 4718592 | tf_op jit(solution)/shard_map/reduce_scatter | solution.py:374
  424.9 41.2 %collective-permute-start.57 = (bf16[2,256,1024]{2,1,0:T(8,128)(2,1)S(1)}, bf16[2,256,1024]{2,1,0:T(8,128)(2,1)S(1)}, u32[]{:S(2)}, u32[]{:S(2)}) collective-permute-start(bf16[2,256,1024]{2,1,0:T(8,128)(2,1)S(1)} %pad_maximum_fusion.5), channel_id=1, source_target_pairs={{0,16},{8,24},{16,0},{24,8},{1,17},{9,25},{17,1},{25,9},{2,18},{10... | collective-permute-start | bytes 3145736 | tf_op jit(solution)/shard_map/ppermute | solution.py:378
  425.7 42.4 %collective-permute-start.55 = (bf16[2,256,1024]{2,1,0:T(8,128)(2,1)S(1)}, bf16[2,256,1024]{2,1,0:T(8,128)(2,1)S(1)}, u32[]{:S(2)}, u32[]{:S(2)}) collective-permute-start(bf16[2,256,1024]{2,1,0:T(8,128)(2,1)S(1)} %pad_maximum_fusion.4), channel_id=1, source_target_pairs={{0,8},{8,0},{16,24},{24,16},{1,9},{9,1},{17,25},{25,17},{2,10},{10... | collective-permute-start | bytes 3145736 | tf_op jit(solution)/shard_map/ppermute | solution.py:378
  434.8 53.8 %collective-permute-start.46 = (bf16[2,256,1024]{2,1,0:T(8,128)(2,1)}, bf16[2,256,1024]{2,1,0:T(8,128)(2,1)}, u32[]{:S(2)}, u32[]{:S(2)}) collective-permute-start(bf16[2,256,1024]{2,1,0:T(8,128)(2,1)} %pad_maximum_fusion.3), channel_id=1, source_target_pairs={{0,16},{8,24},{16,0},{24,8},{1,17},{9,25},{17,1},{25,9},{2,18},{10... | collective-permute-start | bytes 3145736 | tf_op jit(solution)/shard_map/ppermute | solution.py:378
  442.0 51.0 %collective-permute-start.44 = (bf16[2,256,1024]{2,1,0:T(8,128)(2,1)}, bf16[2,256,1024]{2,1,0:T(8,128)(2,1)}, u32[]{:S(2)}, u32[]{:S(2)}) collective-permute-start(bf16[2,256,1024]{2,1,0:T(8,128)(2,1)} %pad_maximum_fusion.2), channel_id=1, source_target_pairs={{0,8},{8,0},{16,24},{24,16},{1,9},{9,1},{17,25},{25,17},{2,10},{10... | collective-permute-start | bytes 3145736 | tf_op jit(solution)/shard_map/ppermute | solution.py:378
  444.7 105.3 %collective-permute-start.67 = (bf16[128,2048]{1,0:T(8,128)(2,1)}, bf16[128,2048]{1,0:T(8,128)(2,1)}, u32[]{:S(2)}, u32[]{:S(2)}) collective-permute-start(bf16[128,2048]{1,0:T(8,128)(2,1)} %fusion.65), channel_id=1, source_target_pairs={{0,16},{8,24},{16,0},{24,8},{1,17},{9,25},{17,1},{25,9},{2,18},{10... | collective-permute-start | bytes 1572872 | tf_op jit(solution)/shard_map/ppermute | solution.py:378
  466.1 86.1 %collective-permute-start.69 = (bf16[128,2048]{1,0:T(8,128)(2,1)}, bf16[128,2048]{1,0:T(8,128)(2,1)}, u32[]{:S(2)}, u32[]{:S(2)}) collective-permute-start(bf16[128,2048]{1,0:T(8,128)(2,1)} %fusion.66), channel_id=1, source_target_pairs={{0,8},{8,0},{16,24},{24,16},{1,9},{9,1},{17,25},{25,17},{2,10},{10... | collective-permute-start | bytes 1572872 | tf_op jit(solution)/shard_map/ppermute | solution.py:378
  468.0 50.8 %collective-permute-start.58 = (bf16[256,1024]{1,0:T(8,128)(2,1)}, bf16[256,1024]{1,0:T(8,128)(2,1)}, u32[]{:S(2)}, u32[]{:S(2)}) collective-permute-start(bf16[256,1024]{1,0:T(8,128)(2,1)} %fusion.64), channel_id=1, source_target_pairs={{0,8},{8,0},{16,24},{24,16},{1,9},{9,1},{17,25},{25,17},{2,10},{10... | collective-permute-start | bytes 1572872 | tf_op jit(solution)/shard_map/ppermute | solution.py:378
  487.1 214.0 %reduce-scatter.8.cloned.1.call-start = ((), (), s32[]{:S(2)}) async-start(), calls=%async_computation.9 | async-start | bytes 4718592 | tf_op jit(solution)/shard_map/reduce_scatter | solution.py:374
  488.6 34.2 %collective-permute-start.56 = (bf16[256,1024]{1,0:T(8,128)(2,1)}, bf16[256,1024]{1,0:T(8,128)(2,1)}, u32[]{:S(2)}, u32[]{:S(2)}) collective-permute-start(bf16[256,1024]{1,0:T(8,128)(2,1)} %fusion.63), channel_id=1, source_target_pairs={{0,16},{8,24},{16,0},{24,8},{1,17},{9,25},{17,1},{25,9},{2,18},{10... | collective-permute-start | bytes 1572872 | tf_op jit(solution)/shard_map/ppermute | solution.py:378
  493.0 34.2 %collective-permute-start.47 = (bf16[256,1024]{1,0:T(8,128)(2,1)}, bf16[256,1024]{1,0:T(8,128)(2,1)}, u32[]{:S(2)}, u32[]{:S(2)}) collective-permute-start(bf16[256,1024]{1,0:T(8,128)(2,1)} %fusion.62), channel_id=1, source_target_pairs={{0,8},{8,0},{16,24},{24,16},{1,9},{9,1},{17,25},{25,17},{2,10},{10... | collective-permute-start | bytes 1572872 | tf_op jit(solution)/shard_map/ppermute | solution.py:378
  564.9 36.8 %collective-permute-start.52 = (bf16[64,1024]{1,0:T(8,128)(2,1)S(1)}, bf16[64,1024]{1,0:T(8,128)(2,1)S(1)}, u32[]{:S(2)}, u32[]{:S(2)}) collective-permute-start(bf16[64,1024]{1,0:T(8,128)(2,1)S(1)} %get-tuple-element.118), channel_id=1, source_target_pairs={{0,5},{1,4},{2,7},{3,6},{4,1},{5,0},{6,3},{7,2},{8,13},{9,12},{10,... | collective-permute-start | bytes 393224 | tf_op jit(solution)/shard_map/ppermute | solution.py:378
  602.3 33.6 %collective-permute-start.29 = (bf16[2,256,768]{2,1,0:T(8,128)(2,1)}, bf16[2,256,768]{2,1,0:T(8,128)(2,1)S(1)}, u32[]{:S(2)}, u32[]{:S(2)}) collective-permute-start(bf16[2,256,768]{2,1,0:T(8,128)(2,1)} %pad_maximum_fusion.9), channel_id=1, source_target_pairs={{0,8},{8,0},{16,24},{24,16},{1,9},{9,1},{17,25},{25,17},{2,10},{10... | collective-permute-start | bytes 2359304 | tf_op jit(solution)/shard_map/ppermute | solution.py:378
  634.9 41.4 %collective-permute-start.71 = (f32[1,256]{1,0:T(1,128)S(1)}, f32[1,256]{1,0:T(1,128)S(1)}, u32[]{:S(2)}, u32[]{:S(2)}) collective-permute-start(f32[1,256]{1,0:T(1,128)S(1)} %constant_dynamic-slice_fusion), channel_id=1, source_target_pairs={{0,8},{8,0},{16,24},{24,16},{1,9},{9,1},{17,25},{25,17},{2,10},{10... | collective-permute-start | bytes 3080 | tf_op jit(solution)/shard_map/ppermute | solution.py:378
  (136 other events, 2047.3 us)
Sparse Core Ops, SparseCore 0:
  9.6 49.7 all-gather.4
  89.7 46.6 all-gather.8
  285.1 47.4 reduce-scatter.3
  338.4 45.2 all-gather.6
  408.1 48.7 reduce-scatter.5
  541.2 84.8 reduce-scatter.7

commit v10 on v9

--- a/solution.py
+++ b/solution.py
@@ -862,17 +862,18 @@
     dk_pre = norm_back_wide(dk_gained, key_pre, 1)
     d_value = d_value.reshape(all_count, own_features)
     d_qkv = jnp.concatenate([dq_pre, dk_pre, d_value], 1)
+    qkv_part = jnp.einsum("nd,nf->df", tokens_all, d_qkv, preferred_element_type=jnp.float32).astype(low)
+    d_qkv, qkv_part = lax.optimization_barrier((d_qkv, qkv_part))
     d_tokens_part = jnp.einsum("nf,df->nd", d_qkv, w_qkv, preferred_element_type=jnp.float32).astype(low)
-    d_qkv, d_tokens_part = lax.optimization_barrier((d_qkv, d_tokens_part))
-    qkv_part = jnp.einsum("nd,nf->df", tokens_all, d_qkv, preferred_element_type=jnp.float32).astype(low)
-    d_attn, qkv_part = lax.optimization_barrier((d_attn, qkv_part))
+    d_attn, d_tokens_part = lax.optimization_barrier((d_attn, d_tokens_part))
+    d_tokens_sum = scatter_seq(d_tokens_part.reshape(row_count, row_len, model_width))
+    d_tokens = d_hidden + d_tokens_sum.astype(jnp.float32).reshape(tok_count, model_width)
+    qkv_own = sum_dp(*shares_for(qkv_part)).astype(low)
+    query_grad, key_grad, value_grad = rows_home(qkv_own, 1, own_features)
     d_attn_own = own_columns_of_all(d_attn).reshape(all_count, -1)
     out_part = jnp.einsum("nf,nd->fd", mixed_all, d_attn_own, preferred_element_type=jnp.float32).astype(low)
     out_own = sum_dp(*shares_for(out_part)).astype(low)
-    d_tokens_sum = scatter_seq(d_tokens_part.reshape(row_count, row_len, model_width))
-    d_tokens = d_hidden + d_tokens_sum.astype(jnp.float32).reshape(tok_count, model_width)
-    qkv_own = sum_dp(*shares_for(qkv_part)).astype(low)
-    attn_home = rows_home(jnp.concatenate([qkv_own, out_own], 1), 1, own_features)
+    (out_grad,) = rows_home(out_own, 1, own_features)
     share = feature_count // (dp_count * seq_count)
     gains = lax.dynamic_index_in_dim(
         sums[stat_rows:].reshape(4, dp_count, seq_count, share), seq_at, 2, False
@@ -881,10 +882,10 @@
     return (
         result,
         d_tokens.reshape(row_count, piece_len, model_width),
-        attn_home[0],
-        attn_home[1],
-        attn_home[2],
-        attn_home[3],
+        query_grad,
+        key_grad,
+        value_grad,
+        out_grad,
         gate_grad,
         up_grad,
         down_grad,

time: 725 us -> 729 us (level)
  waiting for transfers between devices: 302 us -> 281 us
  starting transfers between devices: 98.5 us -> 115 us
    ppermute x72 -> x79, waiting for transfers between devices: 216 us -> 187 us  [swap(): lax.ppermute(value, axis, [(at, at ^ flip) for at in range(lax.axis_size(...]
    ppermute x72 -> x79, starting transfers between devices: 87.9 us -> 104 us  [swap(): lax.ppermute(value, axis, [(at, at ^ flip) for at in range(lax.axis_size(...]
    all_to_all x2, waiting for transfers between devices: 5.53 us -> 13.5 us  [own_columns_of_all(): lax.all_to_all(split.reshape(seq_count, tok_count, width), 'seq', split_a...]
    unnamed x167 -> x177, local copies, waits for them, and re-layouts: 28.7 us -> 32 us
  transfers between devices with their start and end apart: 80 -> 87, of which waited for: 35 -> 33; matrix products, arithmetic and copies ran while one was open for 19% -> 20% of each run, Pallas kernels for 8% -> 8%
where the time goes in v10:
time: 729 us; the launch traced here: 718 us
  waiting for transfers between devices  281 us (39%)
  starting transfers between devices  115 us (16%)
  matrix products  94.2 us (13%)
  local copies, waits for them, and re-layouts  84.4 us (12%)
  Pallas kernels  69.5 us (10%)
  other arithmetic  57.8 us (8%)
  between operations  16.1 us (2%)
    ppermute x79, waiting for transfers between devices, swap(): lax.ppermute(value, axis, [(at, at ^ flip) for at in range(lax.axis_size(...  187 us
    ppermute x79, starting transfers between devices, swap(): lax.ppermute(value, axis, [(at, at ^ flip) for at in range(lax.axis_size(...  104 us
    reduce_scatter x3, waiting for transfers between devices, scatter_seq(): return lax.psum_scatter(partial, 'seq', scatter_dimension=1, tiled=True)  46.9 us
    all_gather x2, waiting for transfers between devices, gather_seq(): return lax.all_gather(piece, 'seq', axis=1, tiled=True)  33.1 us
    unnamed x177, local copies, waits for them, and re-layouts  32 us
    pallas_call x7, Pallas kernels, placed(): pl.pallas_call(functools.partial(place_kernel, count=len(pieces)), grid_s...  30.8 us
    optimization_barrier x2, local copies, waits for them, and re-layouts, stored_turned(): matrix, after = lax.optimization_barrier((matrix, after))  18.9 us
    pallas_call x1, Pallas kernels, attend_back(): pl.pallas_call(functools.partial(attend_back_kernel, scale=scale), grid=(...  15.1 us
  transfers between devices with their start and end apart: 87, of which 33 were waited for; matrix products, arithmetic and copies ran while one was open for 20% of the time, Pallas kernels for 8%

profile of v10, /device:TPU:0, one launch (start us, length us, event | category | flops | bytes accessed | tf_op | source)
XLA Modules:
  0.0 717.6 jit_solution(13531305308016914836)
XLA Ops:
  14.5 16.0 %collective-permute-done.3.refs_1_ = bf16[512,768]{1,0:T(8,128)(2,1)S(1)} collective-permute-done((bf16[512,768]{1,0:T(8,128)(2,1)S(1)}, bf16[512,768]{1,0:T(8,128)(2,1)S(1)}, u32[]{:S(2)}, u32[]{:S(2)}) %collective-permute-start.3) | collective-permute-done | bytes 786464 | tf_op jit(solution)/shard_map/ppermute | solution.py:378
  52.8 6.6 all-gather.5.cloned.1.call-done
  79.1 10.5 %attend.1 = (bf16[1,1024,256]{2,1,0:T(8,128)(2,1)}, bf16[1,1024,256]{2,1,0:T(8,128)(2,1)}, bf16[1,1024,256]{2,1,0:T(8,128)(2,1)}, bf16[1,1024,256]{2,1,0:T(8,128)(2,1)}, f32[1,2,1024,1]{3,2,1,0:T(8,128)}) custom-call(f32[1,1024,768]{2,1,0:T(8,128)} %bitcast.345, f32[1,1024,768]{2,1,0:T(8,128)} %bitcast.346, f32[1,1024,768]{2,1,0:T(8,128)} %bitcast.347, ...), custom_call_target="tpu_custom_call" | custom-call | tf_op jit(solution)/shard_map/attend/pallas_call | solution.py:660
  105.7 11.4 %collective-permute-done.10.refs_1_ = bf16[512,1024]{1,0:T(8,128)(2,1)} collective-permute-done((bf16[512,1024]{1,0:T(8,128)(2,1)}, bf16[512,1024]{1,0:T(8,128)(2,1)}, u32[]{:S(2)}, u32[]{:S(2)}) %collective-permute-start.10) | collective-permute-done | bytes 1048608 | tf_op jit(solution)/shard_map/ppermute | solution.py:378
  119.7 52.2 %collective-permute-done.11.refs_2_ = bf16[512,1024]{1,0:T(8,128)(2,1)} collective-permute-done((bf16[512,1024]{1,0:T(8,128)(2,1)}, bf16[512,1024]{1,0:T(8,128)(2,1)}, u32[]{:S(2)}, u32[]{:S(2)}) %collective-permute-start.11) | collective-permute-done | bytes 1048608 | tf_op jit(solution)/shard_map/ppermute | solution.py:378
  174.4 7.3 %collective-permute-done.18.refs_1_ = bf16[256,2048]{1,0:T(8,128)(2,1)S(1)} collective-permute-done((bf16[256,2048]{1,0:T(8,128)(2,1)S(1)}, bf16[256,2048]{1,0:T(8,128)(2,1)S(1)}, u32[]{:S(2)}, u32[]{:S(2)}) %collective-permute-start.18) | collective-permute-done | bytes 1048608 | tf_op jit(solution)/shard_map/ppermute | solution.py:378
  183.2 11.0 %collective-permute-done.20.refs_2_ = bf16[256,2048]{1,0:T(8,128)(2,1)S(1)} collective-permute-done((bf16[256,2048]{1,0:T(8,128)(2,1)S(1)}, bf16[256,2048]{1,0:T(8,128)(2,1)S(1)}, u32[]{:S(2)}, u32[]{:S(2)}) %collective-permute-start.20) | collective-permute-done | bytes 1048608 | tf_op jit(solution)/shard_map/ppermute | solution.py:378
  198.4 7.1 collective-permute-done.12.refs_3_
  233.7 7.5 %place.9 = bf16[2048,2048]{1,0:T(8,128)(2,1)} custom-call(s32[18]{0:T(128)} %stack.274.spots_ref, bf16[512,2048]{1,0:T(8,128)(2,1)} %refs_0_.1, bf16[512,1024]{1,0:T(8,128)(2,1)} %collective-permute-done.10.refs_1_, bf16[512,1024]{1,0:T(8,128)(2,1)} %collective-permute-done.11.refs_2_, bf16[256,1024]{1,0:T(8,128)(2,1)} %copy-done.44, ...), custom_call_target="tpu_custom_call" | custom-call | tf_op jit(solution)/shard_map/place/pallas_call | solution.py:403
  244.8 13.3 %multiply_reduce_fusion = (f32[1024]{0:T(1024)S(1)}, f32[1024,2048]{1,0:T(8,128)S(1)}) fusion(bf16[2048,2048]{1,0:T(8,128)(2,1)} %place.9, bf16[1,1024,2048]{2,1,0:T(8,128)(2,1)} %all-gather.9.cloned.1.call-done), kind=kOutput, calls=%fused_computation.3 | convolution fusion | flops 8594127872 | bytes 20975616 | tf_op jit(solution)/shard_map/dot_general | solution.py:778
  264.5 8.9 %fusion.117 = f32[1024,2048]{1,0:T(8,128)S(1)} fusion(bf16[1024,2048]{1,0:T(8,128)(2,1)S(1)} %add_convert_fusion, bf16[2048,2048]{1,0:T(8,128)(2,1)S(1)} %copy-done.4), kind=kOutput, calls=%fused_computation.334 | convolution fusion | flops 8589934592 | bytes 20971520 | tf_op jit(solution)/shard_map/dot_general | solution.py:786
  285.7 46.9 %reduce-scatter.4.cloned.1.call-done = bf16[1,128,2048]{2,1,0:T(8,128)(2,1)} async-done(((bf16[1,1024,2048]{2,1,0:T(8,128)(2,1)}), bf16[1,128,2048]{2,1,0:T(8,128)(2,1)}) %reduce-scatter.4.cloned.1.call-update) | async-done | bytes 524304 | tf_op jit(solution)/shard_map/reduce_scatter | solution.py:374
  344.8 12.5 %copy.63 = bf16[2048,2048]{0,1:T(8,128)(2,1)} copy(bf16[2048,2048]{1,0:T(8,128)(2,1)} %place.13) | data formatting | bytes 16777216 | tf_op jit(solution)/shard_map/optimization_barrier | solution.py:486
  357.3 26.5 %all-gather.7.cloned.1.call-done = bf16[1,1024,2048]{2,1,0:T(8,128)(2,1)} async-done(((bf16[1,128,2048]{2,1,0:T(8,128)(2,1)}), bf16[1,1024,2048]{2,1,0:T(8,128)(2,1)}) %all-gather.7.cloned.1.call-update) | async-done | bytes 4194320 | tf_op jit(solution)/shard_map/all_gather | solution.py:370
  383.8 11.7 %multiply_convert_fusion.1 = (bf16[1024,1024]{1,0:T(8,128)(2,1)S(1)}, bf16[1024,1024]{1,0:T(8,128)(2,1)S(1)}) fusion(f32[1024,2048]{1,0:T(8,128)} %copy-done.10, bf16[1024,2048]{0,1:T(8,128)(2,1)} %copy.60, bf16[1,1024,2048]{2,1,0:T(8,128)(2,1)} %all-gather.7.cloned.1.call-done), kind=kOutput, calls=%fused_computation.18 | convolution fusion | flops 4308598784 | bytes 20971520 | tf_op jit(solution)/shard_map/dot_general | solution.py:811
  397.5 10.5 %convert_bitcast_fusion = bf16[1,1024,2048]{2,1,0:T(8,128)(2,1)} fusion(bf16[2048,2048]{0,1:T(8,128)(2,1)S(1)} %copy-done.11, bf16[1024,1024]{1,0:T(8,128)(2,1)S(1)} %get-tuple-element.66, bf16[1024,1024]{1,0:T(8,128)(2,1)S(1)} %get-tuple-element.65), kind=kOutput, calls=%fused_computation.16 | convolution fusion | flops 8600420352 | bytes 16777216 | tf_op jit(solution)/shard_map/dot_general | solution.py:815
  408.2 7.0 fusion.19
  447.6 18.5 %collective-permute-done.64 = bf16[2,256,1024]{2,1,0:T(8,128)(2,1)S(1)} collective-permute-done((bf16[2,256,1024]{2,1,0:T(8,128)(2,1)S(1)}, bf16[2,256,1024]{2,1,0:T(8,128)(2,1)S(1)}, u32[]{:S(2)}, u32[]{:S(2)}) %collective-permute-start.64) | collective-permute-done | bytes 1048608 | tf_op jit(solution)/shard_map/ppermute | solution.py:378
  472.8 6.5 convolution_convert_fusion.5
  499.9 15.1 %attend_back.1 = (f32[1,1024,256]{2,1,0:T(8,128)}, f32[1,1024,256]{2,1,0:T(8,128)}, bf16[1,1024,256]{2,1,0:T(8,128)(2,1)}, f32[1,8,1024]{2,1,0:T(8,128)}, f32[1,2,256]{2,1,0:T(2,128)}) custom-call(f32[1,1024,768]{2,1,0:T(8,128)} %bitcast.348, f32[1,1024,768]{2,1,0:T(8,128)} %bitcast.349, f32[1,1024,1]{2,1,0:T(8,128)} %copy.57.qinv_ref, ...), custom_call_target="tpu_custom_call" | custom-call | tf_op jit(solution)/shard_map/attend_back/pallas_call | solution.py:675
  564.8 6.7 collective-permute-done.70.refs_5_
  592.0 11.5 %collective-permute-start.56 = (bf16[64,1024]{1,0:T(8,128)(2,1)S(1)}, bf16[64,1024]{1,0:T(8,128)(2,1)S(1)}, u32[]{:S(2)}, u32[]{:S(2)}) collective-permute-start(bf16[64,1024]{1,0:T(8,128)(2,1)S(1)} %copy-done.52), channel_id=1, source_target_pairs={{0,2},{1,3},{2,0},{3,1},{4,6},{5,7},{6,4},{7,5},{8,10},{9,11},{10,... | collective-permute-start | bytes 393224 | tf_op jit(solution)/shard_map/ppermute | solution.py:378
  633.0 6.7 all-to-all-start.1
  644.2 11.0 %all-to-all-done.1 = bf16[8,128,256]{2,1,0:T(8,128)(2,1)} async-done(((bf16[8,128,256]{2,1,0:T(8,128)(2,1)}), bf16[8,128,256]{2,1,0:T(8,128)(2,1)}, u32[]{:S(2)}, u32[]{:S(2)}) %all-to-all-start.1) | async-done | bytes 524320 | tf_op jit(solution)/shard_map/all_to_all | solution.py:832
  (494 shorter events, 358.5 us)
Async XLA Ops:
  7.2 52.2 %all-gather.5.cloned.1.call-start = ((), (), s32[]{:S(2)}) async-start(), calls=%async_computation.5 | async-start | bytes 4718592 | tf_op jit(solution)/shard_map/all_gather | solution.py:370
  7.9 236.8 %all-gather.9.cloned.1.call-start = ((), (), s32[]{:S(2)}) async-start(), calls=%async_computation.10 | async-start | bytes 4718592 | tf_op jit(solution)/shard_map/all_gather | solution.py:777
  89.6 243.0 %reduce-scatter.4.cloned.1.call-start = ((), (), s32[]{:S(2)}) async-start(), calls=%async_computation.6 | async-start | bytes 4718592 | tf_op jit(solution)/shard_map/reduce_scatter | solution.py:374
  100.2 95.6 %collective-permute-start.22 = (bf16[512,2048]{1,0:T(8,128)(2,1)S(1)}, bf16[512,2048]{1,0:T(8,128)(2,1)S(1)}, u32[]{:S(2)}, u32[]{:S(2)}) collective-permute-start(bf16[512,2048]{1,0:T(8,128)(2,1)S(1)} %dynamic-slice_dynamic-update-slice_fusion.refs_0_), channel_id=1, source_target_pairs={{0,8},{8,0},{16,24},{24,16},{1,9},{9,1},{17,25},{25,17},{2,10},{10... | collective-permute-start | bytes 6291464 | tf_op jit(solution)/shard_map/ppermute | solution.py:378
  100.8 104.7 %collective-permute-start.24 = (bf16[512,2048]{1,0:T(8,128)(2,1)S(1)}, bf16[512,2048]{1,0:T(8,128)(2,1)S(1)}, u32[]{:S(2)}, u32[]{:S(2)}) collective-permute-start(bf16[512,2048]{1,0:T(8,128)(2,1)S(1)} %dynamic-slice_dynamic-update-slice_fusion.refs_0_), channel_id=1, source_target_pairs={{0,16},{8,24},{16,0},{24,8},{1,17},{9,25},{17,1},{25,9},{2,18},{10... | collective-permute-start | bytes 6291464 | tf_op jit(solution)/shard_map/ppermute | solution.py:378
  102.3 69.6 %collective-permute-start.11 = (bf16[512,1024]{1,0:T(8,128)(2,1)}, bf16[512,1024]{1,0:T(8,128)(2,1)}, u32[]{:S(2)}, u32[]{:S(2)}) collective-permute-start(bf16[512,1024]{1,0:T(8,128)(2,1)} %constant_dynamic-slice_fusion.6), channel_id=1, source_target_pairs={{0,16},{8,24},{16,0},{24,8},{1,17},{9,25},{17,1},{25,9},{2,18},{10... | collective-permute-start | bytes 3145736 | tf_op jit(solution)/shard_map/ppermute | solution.py:378
  104.1 77.6 %collective-permute-start.18 = (bf16[256,2048]{1,0:T(8,128)(2,1)S(1)}, bf16[256,2048]{1,0:T(8,128)(2,1)S(1)}, u32[]{:S(2)}, u32[]{:S(2)}) collective-permute-start(bf16[256,2048]{1,0:T(8,128)(2,1)S(1)} %constant_dynamic-slice_fusion.5.refs_0_), channel_id=1, source_target_pairs={{0,8},{8,0},{16,24},{24,16},{1,9},{9,1},{17,25},{25,17},{2,10},{10... | collective-permute-start | bytes 3145736 | tf_op jit(solution)/shard_map/ppermute | solution.py:378
  117.1 77.1 %collective-permute-start.20 = (bf16[256,2048]{1,0:T(8,128)(2,1)S(1)}, bf16[256,2048]{1,0:T(8,128)(2,1)S(1)}, u32[]{:S(2)}, u32[]{:S(2)}) collective-permute-start(bf16[256,2048]{1,0:T(8,128)(2,1)S(1)} %constant_dynamic-slice_fusion.5.refs_0_), channel_id=1, source_target_pairs={{0,16},{8,24},{16,0},{24,8},{1,17},{9,25},{17,1},{25,9},{2,18},{10... | collective-permute-start | bytes 3145736 | tf_op jit(solution)/shard_map/ppermute | solution.py:378
  171.9 33.6 %collective-permute-start.12 = (bf16[256,1024]{1,0:T(8,128)(2,1)S(1)}, bf16[256,1024]{1,0:T(8,128)(2,1)S(1)}, u32[]{:S(2)}, u32[]{:S(2)}) collective-permute-start(bf16[256,1024]{1,0:T(8,128)(2,1)S(1)} %slice.198), channel_id=1, source_target_pairs={{0,16},{8,24},{16,0},{24,8},{1,17},{9,25},{17,1},{25,9},{2,18},{10... | collective-permute-start | bytes 1572872 | tf_op jit(solution)/shard_map/ppermute | solution.py:378
  285.0 98.8 %all-gather.7.cloned.1.call-start = ((), (), s32[]{:S(2)}) async-start(), calls=%async_computation.7 | async-start | bytes 4718592 | tf_op jit(solution)/shard_map/all_gather | solution.py:370
  338.3 131.0 %reduce-scatter.6.cloned.1.call-start = ((), (), s32[]{:S(2)}) async-start(), calls=%async_computation.8 | async-start | bytes 4718592 | tf_op jit(solution)/shard_map/reduce_scatter | solution.py:374
  424.8 41.3 %collective-permute-start.64 = (bf16[2,256,1024]{2,1,0:T(8,128)(2,1)S(1)}, bf16[2,256,1024]{2,1,0:T(8,128)(2,1)S(1)}, u32[]{:S(2)}, u32[]{:S(2)}) collective-permute-start(bf16[2,256,1024]{2,1,0:T(8,128)(2,1)S(1)} %pad_maximum_fusion.5), channel_id=1, source_target_pairs={{0,16},{8,24},{16,0},{24,8},{1,17},{9,25},{17,1},{25,9},{2,18},{10... | collective-permute-start | bytes 3145736 | tf_op jit(solution)/shard_map/ppermute | solution.py:378
  426.5 57.4 %collective-permute-start.62 = (bf16[2,256,1024]{2,1,0:T(8,128)(2,1)}, bf16[2,256,1024]{2,1,0:T(8,128)(2,1)}, u32[]{:S(2)}, u32[]{:S(2)}) collective-permute-start(bf16[2,256,1024]{2,1,0:T(8,128)(2,1)} %pad_maximum_fusion.4), channel_id=1, source_target_pairs={{0,8},{8,0},{16,24},{24,16},{1,9},{9,1},{17,25},{25,17},{2,10},{10... | collective-permute-start | bytes 3145736 | tf_op jit(solution)/shard_map/ppermute | solution.py:378
  435.3 54.0 %collective-permute-start.53 = (bf16[2,256,1024]{2,1,0:T(8,128)(2,1)}, bf16[2,256,1024]{2,1,0:T(8,128)(2,1)}, u32[]{:S(2)}, u32[]{:S(2)}) collective-permute-start(bf16[2,256,1024]{2,1,0:T(8,128)(2,1)} %pad_maximum_fusion.3), channel_id=1, source_target_pairs={{0,16},{8,24},{16,0},{24,8},{1,17},{9,25},{17,1},{25,9},{2,18},{10... | collective-permute-start | bytes 3145736 | tf_op jit(solution)/shard_map/ppermute | solution.py:378
  442.0 51.7 %collective-permute-start.51 = (bf16[2,256,1024]{2,1,0:T(8,128)(2,1)}, bf16[2,256,1024]{2,1,0:T(8,128)(2,1)}, u32[]{:S(2)}, u32[]{:S(2)}) collective-permute-start(bf16[2,256,1024]{2,1,0:T(8,128)(2,1)} %pad_maximum_fusion.2), channel_id=1, source_target_pairs={{0,8},{8,0},{16,24},{24,16},{1,9},{9,1},{17,25},{25,17},{2,10},{10... | collective-permute-start | bytes 3145736 | tf_op jit(solution)/shard_map/ppermute | solution.py:378
  444.8 112.2 %collective-permute-start.74 = (bf16[128,2048]{1,0:T(8,128)(2,1)}, bf16[128,2048]{1,0:T(8,128)(2,1)}, u32[]{:S(2)}, u32[]{:S(2)}) collective-permute-start(bf16[128,2048]{1,0:T(8,128)(2,1)} %fusion.65), channel_id=1, source_target_pairs={{0,16},{8,24},{16,0},{24,8},{1,17},{9,25},{17,1},{25,9},{2,18},{10... | collective-permute-start | bytes 1572872 | tf_op jit(solution)/shard_map/ppermute | solution.py:378
  466.1 93.0 %collective-permute-start.76 = (bf16[128,2048]{1,0:T(8,128)(2,1)}, bf16[128,2048]{1,0:T(8,128)(2,1)}, u32[]{:S(2)}, u32[]{:S(2)}) collective-permute-start(bf16[128,2048]{1,0:T(8,128)(2,1)} %fusion.66), channel_id=1, source_target_pairs={{0,8},{8,0},{16,24},{24,16},{1,9},{9,1},{17,25},{25,17},{2,10},{10... | collective-permute-start | bytes 1572872 | tf_op jit(solution)/shard_map/ppermute | solution.py:378
  483.9 224.5 %reduce-scatter.8.cloned.1.call-start = ((), (), s32[]{:S(2)}) async-start(), calls=%async_computation.9 | async-start | bytes 4718592 | tf_op jit(solution)/shard_map/reduce_scatter | solution.py:374
  483.9 40.6 %collective-permute-start.65 = (bf16[256,1024]{1,0:T(8,128)(2,1)}, bf16[256,1024]{1,0:T(8,128)(2,1)}, u32[]{:S(2)}, u32[]{:S(2)}) collective-permute-start(bf16[256,1024]{1,0:T(8,128)(2,1)} %fusion.64), channel_id=1, source_target_pairs={{0,8},{8,0},{16,24},{24,16},{1,9},{9,1},{17,25},{25,17},{2,10},{10... | collective-permute-start | bytes 1572872 | tf_op jit(solution)/shard_map/ppermute | solution.py:378
  489.3 56.0 %collective-permute-start.63 = (bf16[256,1024]{1,0:T(8,128)(2,1)}, bf16[256,1024]{1,0:T(8,128)(2,1)}, u32[]{:S(2)}, u32[]{:S(2)}) collective-permute-start(bf16[256,1024]{1,0:T(8,128)(2,1)} %fusion.63), channel_id=1, source_target_pairs={{0,16},{8,24},{16,0},{24,8},{1,17},{9,25},{17,1},{25,9},{2,18},{10... | collective-permute-start | bytes 1572872 | tf_op jit(solution)/shard_map/ppermute | solution.py:378
  571.8 38.0 %collective-permute-start.59 = (bf16[64,1024]{1,0:T(8,128)(2,1)S(1)}, bf16[64,1024]{1,0:T(8,128)(2,1)S(1)}, u32[]{:S(2)}, u32[]{:S(2)}) collective-permute-start(bf16[64,1024]{1,0:T(8,128)(2,1)S(1)} %get-tuple-element.116), channel_id=1, source_target_pairs={{0,5},{1,4},{2,7},{3,6},{4,1},{5,0},{6,3},{7,2},{8,13},{9,12},{10,... | collective-permute-start | bytes 393224 | tf_op jit(solution)/shard_map/ppermute | solution.py:378
  577.6 32.2 %collective-permute-start.77 = (f32[2,256]{1,0:T(2,128)S(1)}, f32[2,256]{1,0:T(2,128)S(1)}, u32[]{:S(2)}, u32[]{:S(2)}) collective-permute-start(f32[2,256]{1,0:T(2,128)S(1)} %fusion.110), channel_id=1, source_target_pairs={{0,16},{8,24},{16,0},{24,8},{1,17},{9,25},{17,1},{25,9},{2,18},{10... | collective-permute-start | bytes 6152 | tf_op jit(solution)/shard_map/ppermute | solution.py:378
  580.0 30.2 %collective-permute-start.60 = (bf16[64,1024]{1,0:T(8,128)(2,1)S(1)}, bf16[64,1024]{1,0:T(8,128)(2,1)S(1)}, u32[]{:S(2)}, u32[]{:S(2)}) collective-permute-start(bf16[64,1024]{1,0:T(8,128)(2,1)S(1)} %get-tuple-element.115), channel_id=1, source_target_pairs={{0,6},{1,7},{2,4},{3,5},{4,2},{5,3},{6,0},{7,1},{8,14},{9,15},{10,... | collective-permute-start | bytes 393224 | tf_op jit(solution)/shard_map/ppermute | solution.py:378
  583.7 32.6 %collective-permute-start.55 = (bf16[64,1024]{1,0:T(8,128)(2,1)S(1)}, bf16[64,1024]{1,0:T(8,128)(2,1)S(1)}, u32[]{:S(2)}, u32[]{:S(2)}) collective-permute-start(bf16[64,1024]{1,0:T(8,128)(2,1)S(1)} %copy-done.53), channel_id=1, source_target_pairs={{0,1},{1,0},{2,3},{3,2},{4,5},{5,4},{6,7},{7,6},{8,9},{9,8},{10,11... | collective-permute-start | bytes 393224 | tf_op jit(solution)/shard_map/ppermute | solution.py:378
  (147 other events, 2104.0 us)
Sparse Core Ops, SparseCore 0:
  9.6 49.7 all-gather.4
  89.7 46.6 all-gather.8
  285.1 47.5 reduce-scatter.3
  338.4 45.3 all-gather.6
  408.2 48.7 reduce-scatter.5
  545.4 78.8 reduce-scatter.7

commit v11 on v10

--- a/solution.py
+++ b/solution.py
@@ -12,6 +12,7 @@
 HEAD = 128
 SLABS = 4
 LANES = 128
+MEBI = 1 << 20
 
 
 eps = 1e-06
@@ -415,6 +416,10 @@
         ),
         out_shape=jax.ShapeDtypeStruct(shape, pieces[0][0].dtype),
         input_output_aliases={1 + len(pieces): 0} if given else {},
+        compiler_params=pltpu.CompilerParams(
+            vmem_limit_bytes=MEBI
+            + sum(piece.size * piece.dtype.itemsize for piece, _, _ in pieces)
+        ),
         name="place",
     )(spots, *[piece for piece, _, _ in pieces], *given)
 
@@ -536,6 +541,7 @@
             out_specs=[pl.BlockSpec((step, wide), lambda r, index: (r, 0))] * outs,
         ),
         out_shape=[jax.ShapeDtypeStruct((rows, wide), jnp.float32)] * outs,
+        compiler_params=pltpu.CompilerParams(vmem_limit_bytes=8 * MEBI),
         name="settle",
     )(lax.axis_index("seq").reshape(1), *pieces)
 

time: 729 us -> 720 us (0.988)
  Pallas kernels: 69.5 us -> 42.6 us
  waiting for transfers between devices: 281 us -> 293 us
  local copies, waits for them, and re-layouts: 84.4 us -> 95.4 us
    pallas_call x7, Pallas kernels: 30.8 us -> 10.5 us  [placed(): pl.pallas_call(functools.partial(place_kernel, count=len(pieces)), grid_s...]
    unnamed x177 -> x165, local copies, waits for them, and re-layouts: 32 us -> 43.6 us
    ppermute x79, waiting for transfers between devices: 187 us -> 196 us  [swap(): lax.ppermute(value, axis, [(at, at ^ flip) for at in range(lax.axis_size(...]
  transfers between devices with their start and end apart: 87 -> 87, of which waited for: 33 -> 37; matrix products, arithmetic and copies ran while one was open for 20% -> 20% of each run, Pallas kernels for 8% -> 5%
where the time goes in v11:
time: 720 us; the launch traced here: 711 us
  waiting for transfers between devices  293 us (41%)
  starting transfers between devices  111 us (15%)
  local copies, waits for them, and re-layouts  95.4 us (13%)
  matrix products  93.4 us (13%)
  other arithmetic  59.3 us (8%)
  Pallas kernels  42.6 us (6%)
  between operations  16 us (2%)
    ppermute x79, waiting for transfers between devices, swap(): lax.ppermute(value, axis, [(at, at ^ flip) for at in range(lax.axis_size(...  196 us
    ppermute x79, starting transfers between devices, swap(): lax.ppermute(value, axis, [(at, at ^ flip) for at in range(lax.axis_size(...  100 us
    reduce_scatter x3, waiting for transfers between devices, scatter_seq(): return lax.psum_scatter(partial, 'seq', scatter_dimension=1, tiled=True)  48.2 us
    unnamed x165, local copies, waits for them, and re-layouts  43.6 us
    all_gather x2, waiting for transfers between devices, gather_seq(): return lax.all_gather(piece, 'seq', axis=1, tiled=True)  36.1 us
    optimization_barrier x2, local copies, waits for them, and re-layouts, stored_turned(): matrix, after = lax.optimization_barrier((matrix, after))  19 us
    pallas_call x1, Pallas kernels, attend_back(): pl.pallas_call(functools.partial(attend_back_kernel, scale=scale), grid=(...  14.8 us
  transfers between devices with their start and end apart: 87, of which 37 were waited for; matrix products, arithmetic and copies ran while one was open for 20% of the time, Pallas kernels for 5%

profile of v11, /device:TPU:0, one launch (start us, length us, event | category | flops | bytes accessed | tf_op | source)
XLA Modules:
  0.0 710.8 jit_solution(1298451716028105273)
XLA Ops:
  14.5 16.0 %collective-permute-done.3.refs_1_ = bf16[512,768]{1,0:T(8,128)(2,1)S(1)} collective-permute-done((bf16[512,768]{1,0:T(8,128)(2,1)S(1)}, bf16[512,768]{1,0:T(8,128)(2,1)S(1)}, u32[]{:S(2)}, u32[]{:S(2)}) %collective-permute-start.3) | collective-permute-done | bytes 786464 | tf_op jit(solution)/shard_map/ppermute | solution.py:379
  49.8 9.6 %all-gather.5.cloned.1.call-done = bf16[1,1024,2048]{2,1,0:T(8,128)(2,1)} async-done(((bf16[1,128,2048]{2,1,0:T(8,128)(2,1)}), bf16[1,1024,2048]{2,1,0:T(8,128)(2,1)}) %all-gather.5.cloned.1.call-update) | async-done | bytes 4194320 | tf_op jit(solution)/shard_map/all_gather | solution.py:371
  80.8 10.5 %attend.1 = (bf16[1,1024,256]{2,1,0:T(8,128)(2,1)}, bf16[1,1024,256]{2,1,0:T(8,128)(2,1)}, bf16[1,1024,256]{2,1,0:T(8,128)(2,1)}, bf16[1,1024,256]{2,1,0:T(8,128)(2,1)}, f32[1,2,1024,1]{3,2,1,0:T(8,128)}) custom-call(f32[1,1024,768]{2,1,0:T(8,128)} %bitcast.345, f32[1,1024,768]{2,1,0:T(8,128)} %bitcast.346, f32[1,1024,768]{2,1,0:T(8,128)} %bitcast.347, ...), custom_call_target="tpu_custom_call" | custom-call | tf_op jit(solution)/shard_map/attend/pallas_call | solution.py:666
  107.8 11.4 %collective-permute-done.10.refs_1_ = bf16[512,1024]{1,0:T(8,128)(2,1)} collective-permute-done((bf16[512,1024]{1,0:T(8,128)(2,1)}, bf16[512,1024]{1,0:T(8,128)(2,1)}, u32[]{:S(2)}, u32[]{:S(2)}) %collective-permute-start.10) | collective-permute-done | bytes 1048608 | tf_op jit(solution)/shard_map/ppermute | solution.py:379
  121.8 52.3 %collective-permute-done.11.refs_2_ = bf16[512,1024]{1,0:T(8,128)(2,1)} collective-permute-done((bf16[512,1024]{1,0:T(8,128)(2,1)}, bf16[512,1024]{1,0:T(8,128)(2,1)}, u32[]{:S(2)}, u32[]{:S(2)}) %collective-permute-start.11) | collective-permute-done | bytes 1048608 | tf_op jit(solution)/shard_map/ppermute | solution.py:379
  176.6 7.2 %collective-permute-done.18.refs_1_ = bf16[256,2048]{1,0:T(8,128)(2,1)S(1)} collective-permute-done((bf16[256,2048]{1,0:T(8,128)(2,1)S(1)}, bf16[256,2048]{1,0:T(8,128)(2,1)S(1)}, u32[]{:S(2)}, u32[]{:S(2)}) %collective-permute-start.18) | collective-permute-done | bytes 1048608 | tf_op jit(solution)/shard_map/ppermute | solution.py:379
  185.3 11.1 %collective-permute-done.20.refs_2_ = bf16[256,2048]{1,0:T(8,128)(2,1)S(1)} collective-permute-done((bf16[256,2048]{1,0:T(8,128)(2,1)S(1)}, bf16[256,2048]{1,0:T(8,128)(2,1)S(1)}, u32[]{:S(2)}, u32[]{:S(2)}) %collective-permute-start.20) | collective-permute-done | bytes 1048608 | tf_op jit(solution)/shard_map/ppermute | solution.py:379
  200.6 7.1 collective-permute-done.12.refs_3_
  245.6 12.8 %multiply_reduce_fusion = (f32[1024]{0:T(1024)S(1)}, f32[1024,2048]{1,0:T(8,128)S(1)}) fusion(bf16[2048,2048]{1,0:T(8,128)(2,1)} %copy-done.6, bf16[1,1024,2048]{2,1,0:T(8,128)(2,1)} %all-gather.9.cloned.1.call-done), kind=kOutput, calls=%fused_computation.3 | convolution fusion | flops 8594127872 | bytes 20975616 | tf_op jit(solution)/shard_map/dot_general | solution.py:784
  264.8 8.9 %fusion.117 = f32[1024,2048]{1,0:T(8,128)S(1)} fusion(bf16[1024,2048]{1,0:T(8,128)(2,1)S(1)} %add_convert_fusion, bf16[2048,2048]{1,0:T(8,128)(2,1)S(1)} %copy-done.3), kind=kOutput, calls=%fused_computation.334 | convolution fusion | flops 8589934592 | bytes 20971520 | tf_op jit(solution)/shard_map/dot_general | solution.py:792
  285.8 48.2 %reduce-scatter.4.cloned.1.call-done = bf16[1,128,2048]{2,1,0:T(8,128)(2,1)} async-done(((bf16[1,1024,2048]{2,1,0:T(8,128)(2,1)}), bf16[1,128,2048]{2,1,0:T(8,128)(2,1)}) %reduce-scatter.4.cloned.1.call-update) | async-done | bytes 524304 | tf_op jit(solution)/shard_map/reduce_scatter | solution.py:375
  339.7 6.6 copy.60
  346.4 12.3 %copy.63 = bf16[2048,2048]{0,1:T(8,128)(2,1)} copy(bf16[2048,2048]{1,0:T(8,128)(2,1)} %copy-done.2) | data formatting | bytes 16777216 | tf_op jit(solution)/shard_map/optimization_barrier | solution.py:491
  358.7 26.5 %all-gather.7.cloned.1.call-done = bf16[1,1024,2048]{2,1,0:T(8,128)(2,1)} async-done(((bf16[1,128,2048]{2,1,0:T(8,128)(2,1)}), bf16[1,1024,2048]{2,1,0:T(8,128)(2,1)}) %all-gather.7.cloned.1.call-update) | async-done | bytes 4194320 | tf_op jit(solution)/shard_map/all_gather | solution.py:371
  385.2 11.7 %multiply_convert_fusion.1 = (bf16[1024,1024]{1,0:T(8,128)(2,1)S(1)}, bf16[1024,1024]{1,0:T(8,128)(2,1)S(1)}) fusion(f32[1024,2048]{1,0:T(8,128)} %copy-done.32, bf16[1024,2048]{0,1:T(8,128)(2,1)} %copy.60, bf16[1,1024,2048]{2,1,0:T(8,128)(2,1)} %all-gather.7.cloned.1.call-done), kind=kOutput, calls=%fused_computation.18 | convolution fusion | flops 4308598784 | bytes 20971520 | tf_op jit(solution)/shard_map/dot_general | solution.py:817
  398.9 10.5 %convert_bitcast_fusion = bf16[1,1024,2048]{2,1,0:T(8,128)(2,1)} fusion(bf16[2048,2048]{0,1:T(8,128)(2,1)S(1)} %copy-done.33, bf16[1024,1024]{1,0:T(8,128)(2,1)S(1)} %get-tuple-element.66, bf16[1024,1024]{1,0:T(8,128)(2,1)S(1)} %get-tuple-element.65), kind=kOutput, calls=%fused_computation.16 | convolution fusion | flops 8600420352 | bytes 16777216 | tf_op jit(solution)/shard_map/dot_general | solution.py:821
  409.6 7.0 fusion.19
  449.0 18.4 %collective-permute-done.64 = bf16[2,256,1024]{2,1,0:T(8,128)(2,1)S(1)} collective-permute-done((bf16[2,256,1024]{2,1,0:T(8,128)(2,1)S(1)}, bf16[2,256,1024]{2,1,0:T(8,128)(2,1)S(1)}, u32[]{:S(2)}, u32[]{:S(2)}) %collective-permute-start.64) | collective-permute-done | bytes 1048608 | tf_op jit(solution)/shard_map/ppermute | solution.py:379
  472.9 6.3 convolution_convert_fusion.5
  499.7 14.8 %attend_back.1 = (f32[1,1024,256]{2,1,0:T(8,128)}, f32[1,1024,256]{2,1,0:T(8,128)}, bf16[1,1024,256]{2,1,0:T(8,128)(2,1)}, f32[1,8,1024]{2,1,0:T(8,128)}, f32[1,2,256]{2,1,0:T(2,128)}) custom-call(f32[1,1024,768]{2,1,0:T(8,128)} %bitcast.348, f32[1,1024,768]{2,1,0:T(8,128)} %bitcast.349, f32[1,1024,1]{2,1,0:T(8,128)} %copy.57.qinv_ref, ...), custom_call_target="tpu_custom_call" | custom-call | tf_op jit(solution)/shard_map/attend_back/pallas_call | solution.py:681
  591.4 11.1 %collective-permute-start.56 = (bf16[64,1024]{1,0:T(8,128)(2,1)S(1)}, bf16[64,1024]{1,0:T(8,128)(2,1)S(1)}, u32[]{:S(2)}, u32[]{:S(2)}) collective-permute-start(bf16[64,1024]{1,0:T(8,128)(2,1)S(1)} %copy-done.64), channel_id=1, source_target_pairs={{0,2},{1,3},{2,0},{3,1},{4,6},{5,7},{6,4},{7,5},{8,10},{9,11},{10,... | collective-permute-start | bytes 393224 | tf_op jit(solution)/shard_map/ppermute | solution.py:379
  602.5 6.2 collective-permute-done.59.refs_5_
  609.0 7.0 collective-permute-start.58
  642.7 8.9 %all-to-all-done.1 = bf16[8,128,256]{2,1,0:T(8,128)(2,1)S(1)} async-done(((bf16[8,128,256]{2,1,0:T(8,128)(2,1)}), bf16[8,128,256]{2,1,0:T(8,128)(2,1)S(1)}, u32[]{:S(2)}, u32[]{:S(2)}) %all-to-all-start.1) | async-done | bytes 524320 | tf_op jit(solution)/shard_map/all_to_all | solution.py:838
  (482 shorter events, 352.2 us)
Async XLA Ops:
  7.2 52.2 %all-gather.5.cloned.1.call-start = ((), (), s32[]{:S(2)}) async-start(), calls=%async_computation.5 | async-start | bytes 4718592 | tf_op jit(solution)/shard_map/all_gather | solution.py:371
  7.9 237.7 %all-gather.9.cloned.1.call-start = ((), (), s32[]{:S(2)}) async-start(), calls=%async_computation.10 | async-start | bytes 4718592 | tf_op jit(solution)/shard_map/all_gather | solution.py:783
  91.3 242.7 %reduce-scatter.4.cloned.1.call-start = ((), (), s32[]{:S(2)}) async-start(), calls=%async_computation.6 | async-start | bytes 4718592 | tf_op jit(solution)/shard_map/reduce_scatter | solution.py:375
  102.3 95.6 %collective-permute-start.22 = (bf16[512,2048]{1,0:T(8,128)(2,1)S(1)}, bf16[512,2048]{1,0:T(8,128)(2,1)S(1)}, u32[]{:S(2)}, u32[]{:S(2)}) collective-permute-start(bf16[512,2048]{1,0:T(8,128)(2,1)S(1)} %dynamic-slice_dynamic-update-slice_fusion.refs_0_), channel_id=1, source_target_pairs={{0,8},{8,0},{16,24},{24,16},{1,9},{9,1},{17,25},{25,17},{2,10},{10... | collective-permute-start | bytes 6291464 | tf_op jit(solution)/shard_map/ppermute | solution.py:379
  103.0 104.7 %collective-permute-start.24 = (bf16[512,2048]{1,0:T(8,128)(2,1)S(1)}, bf16[512,2048]{1,0:T(8,128)(2,1)S(1)}, u32[]{:S(2)}, u32[]{:S(2)}) collective-permute-start(bf16[512,2048]{1,0:T(8,128)(2,1)S(1)} %dynamic-slice_dynamic-update-slice_fusion.refs_0_), channel_id=1, source_target_pairs={{0,16},{8,24},{16,0},{24,8},{1,17},{9,25},{17,1},{25,9},{2,18},{10... | collective-permute-start | bytes 6291464 | tf_op jit(solution)/shard_map/ppermute | solution.py:379
  104.4 69.6 %collective-permute-start.11 = (bf16[512,1024]{1,0:T(8,128)(2,1)}, bf16[512,1024]{1,0:T(8,128)(2,1)}, u32[]{:S(2)}, u32[]{:S(2)}) collective-permute-start(bf16[512,1024]{1,0:T(8,128)(2,1)} %constant_dynamic-slice_fusion.6), channel_id=1, source_target_pairs={{0,16},{8,24},{16,0},{24,8},{1,17},{9,25},{17,1},{25,9},{2,18},{10... | collective-permute-start | bytes 3145736 | tf_op jit(solution)/shard_map/ppermute | solution.py:379
  106.3 77.5 %collective-permute-start.18 = (bf16[256,2048]{1,0:T(8,128)(2,1)S(1)}, bf16[256,2048]{1,0:T(8,128)(2,1)S(1)}, u32[]{:S(2)}, u32[]{:S(2)}) collective-permute-start(bf16[256,2048]{1,0:T(8,128)(2,1)S(1)} %constant_dynamic-slice_fusion.5.refs_0_), channel_id=1, source_target_pairs={{0,8},{8,0},{16,24},{24,16},{1,9},{9,1},{17,25},{25,17},{2,10},{10... | collective-permute-start | bytes 3145736 | tf_op jit(solution)/shard_map/ppermute | solution.py:379
  119.2 77.2 %collective-permute-start.20 = (bf16[256,2048]{1,0:T(8,128)(2,1)S(1)}, bf16[256,2048]{1,0:T(8,128)(2,1)S(1)}, u32[]{:S(2)}, u32[]{:S(2)}) collective-permute-start(bf16[256,2048]{1,0:T(8,128)(2,1)S(1)} %constant_dynamic-slice_fusion.5.refs_0_), channel_id=1, source_target_pairs={{0,16},{8,24},{16,0},{24,8},{1,17},{9,25},{17,1},{25,9},{2,18},{10... | collective-permute-start | bytes 3145736 | tf_op jit(solution)/shard_map/ppermute | solution.py:379
  174.0 33.6 %collective-permute-start.12 = (bf16[256,1024]{1,0:T(8,128)(2,1)S(1)}, bf16[256,1024]{1,0:T(8,128)(2,1)S(1)}, u32[]{:S(2)}, u32[]{:S(2)}) collective-permute-start(bf16[256,1024]{1,0:T(8,128)(2,1)S(1)} %slice.198), channel_id=1, source_target_pairs={{0,16},{8,24},{16,0},{24,8},{1,17},{9,25},{17,1},{25,9},{2,18},{10... | collective-permute-start | bytes 1572872 | tf_op jit(solution)/shard_map/ppermute | solution.py:379
  285.0 100.1 %all-gather.7.cloned.1.call-start = ((), (), s32[]{:S(2)}) async-start(), calls=%async_computation.7 | async-start | bytes 4718592 | tf_op jit(solution)/shard_map/all_gather | solution.py:371
  339.7 129.7 %reduce-scatter.6.cloned.1.call-start = ((), (), s32[]{:S(2)}) async-start(), calls=%async_computation.8 | async-start | bytes 4718592 | tf_op jit(solution)/shard_map/reduce_scatter | solution.py:375
  427.3 40.1 %collective-permute-start.64 = (bf16[2,256,1024]{2,1,0:T(8,128)(2,1)S(1)}, bf16[2,256,1024]{2,1,0:T(8,128)(2,1)S(1)}, u32[]{:S(2)}, u32[]{:S(2)}) collective-permute-start(bf16[2,256,1024]{2,1,0:T(8,128)(2,1)S(1)} %pad_maximum_fusion.5), channel_id=1, source_target_pairs={{0,16},{8,24},{16,0},{24,8},{1,17},{9,25},{17,1},{25,9},{2,18},{10... | collective-permute-start | bytes 3145736 | tf_op jit(solution)/shard_map/ppermute | solution.py:379
  429.1 55.3 %collective-permute-start.62 = (bf16[2,256,1024]{2,1,0:T(8,128)(2,1)}, bf16[2,256,1024]{2,1,0:T(8,128)(2,1)}, u32[]{:S(2)}, u32[]{:S(2)}) collective-permute-start(bf16[2,256,1024]{2,1,0:T(8,128)(2,1)} %pad_maximum_fusion.4), channel_id=1, source_target_pairs={{0,8},{8,0},{16,24},{24,16},{1,9},{9,1},{17,25},{25,17},{2,10},{10... | collective-permute-start | bytes 3145736 | tf_op jit(solution)/shard_map/ppermute | solution.py:379
  438.2 51.8 %collective-permute-start.53 = (bf16[2,256,1024]{2,1,0:T(8,128)(2,1)}, bf16[2,256,1024]{2,1,0:T(8,128)(2,1)}, u32[]{:S(2)}, u32[]{:S(2)}) collective-permute-start(bf16[2,256,1024]{2,1,0:T(8,128)(2,1)} %pad_maximum_fusion.3), channel_id=1, source_target_pairs={{0,16},{8,24},{16,0},{24,8},{1,17},{9,25},{17,1},{25,9},{2,18},{10... | collective-permute-start | bytes 3145736 | tf_op jit(solution)/shard_map/ppermute | solution.py:379
  443.3 50.1 %collective-permute-start.51 = (bf16[2,256,1024]{2,1,0:T(8,128)(2,1)}, bf16[2,256,1024]{2,1,0:T(8,128)(2,1)}, u32[]{:S(2)}, u32[]{:S(2)}) collective-permute-start(bf16[2,256,1024]{2,1,0:T(8,128)(2,1)} %pad_maximum_fusion.2), channel_id=1, source_target_pairs={{0,8},{8,0},{16,24},{24,16},{1,9},{9,1},{17,25},{25,17},{2,10},{10... | collective-permute-start | bytes 3145736 | tf_op jit(solution)/shard_map/ppermute | solution.py:379
  446.2 110.1 %collective-permute-start.74 = (bf16[128,2048]{1,0:T(8,128)(2,1)}, bf16[128,2048]{1,0:T(8,128)(2,1)}, u32[]{:S(2)}, u32[]{:S(2)}) collective-permute-start(bf16[128,2048]{1,0:T(8,128)(2,1)} %fusion.65), channel_id=1, source_target_pairs={{0,16},{8,24},{16,0},{24,8},{1,17},{9,25},{17,1},{25,9},{2,18},{10... | collective-permute-start | bytes 1572872 | tf_op jit(solution)/shard_map/ppermute | solution.py:379
  467.4 92.0 %collective-permute-start.76 = (bf16[128,2048]{1,0:T(8,128)(2,1)}, bf16[128,2048]{1,0:T(8,128)(2,1)}, u32[]{:S(2)}, u32[]{:S(2)}) collective-permute-start(bf16[128,2048]{1,0:T(8,128)(2,1)} %fusion.66), channel_id=1, source_target_pairs={{0,8},{8,0},{16,24},{24,16},{1,9},{9,1},{17,25},{25,17},{2,10},{10... | collective-permute-start | bytes 1572872 | tf_op jit(solution)/shard_map/ppermute | solution.py:379
  484.4 217.2 %reduce-scatter.8.cloned.1.call-start = ((), (), s32[]{:S(2)}) async-start(), calls=%async_computation.9 | async-start | bytes 4718592 | tf_op jit(solution)/shard_map/reduce_scatter | solution.py:375
  484.4 38.4 %collective-permute-start.65 = (bf16[256,1024]{1,0:T(8,128)(2,1)}, bf16[256,1024]{1,0:T(8,128)(2,1)}, u32[]{:S(2)}, u32[]{:S(2)}) collective-permute-start(bf16[256,1024]{1,0:T(8,128)(2,1)} %fusion.64), channel_id=1, source_target_pairs={{0,8},{8,0},{16,24},{24,16},{1,9},{9,1},{17,25},{25,17},{2,10},{10... | collective-permute-start | bytes 1572872 | tf_op jit(solution)/shard_map/ppermute | solution.py:379
  490.0 53.6 %collective-permute-start.63 = (bf16[256,1024]{1,0:T(8,128)(2,1)}, bf16[256,1024]{1,0:T(8,128)(2,1)}, u32[]{:S(2)}, u32[]{:S(2)}) collective-permute-start(bf16[256,1024]{1,0:T(8,128)(2,1)} %fusion.63), channel_id=1, source_target_pairs={{0,16},{8,24},{16,0},{24,8},{1,17},{9,25},{17,1},{25,9},{2,18},{10... | collective-permute-start | bytes 1572872 | tf_op jit(solution)/shard_map/ppermute | solution.py:379
  571.4 37.4 %collective-permute-start.59 = (bf16[64,1024]{1,0:T(8,128)(2,1)S(1)}, bf16[64,1024]{1,0:T(8,128)(2,1)S(1)}, u32[]{:S(2)}, u32[]{:S(2)}) collective-permute-start(bf16[64,1024]{1,0:T(8,128)(2,1)S(1)} %get-tuple-element.116), channel_id=1, source_target_pairs={{0,5},{1,4},{2,7},{3,6},{4,1},{5,0},{6,3},{7,2},{8,13},{9,12},{10,... | collective-permute-start | bytes 393224 | tf_op jit(solution)/shard_map/ppermute | solution.py:379
  576.2 32.7 %collective-permute-start.77 = (f32[2,256]{1,0:T(2,128)S(1)}, f32[2,256]{1,0:T(2,128)S(1)}, u32[]{:S(2)}, u32[]{:S(2)}) collective-permute-start(f32[2,256]{1,0:T(2,128)S(1)} %fusion.110), channel_id=1, source_target_pairs={{0,16},{8,24},{16,0},{24,8},{1,17},{9,25},{17,1},{25,9},{2,18},{10... | collective-permute-start | bytes 6152 | tf_op jit(solution)/shard_map/ppermute | solution.py:379
  579.4 29.7 %collective-permute-start.60 = (bf16[64,1024]{1,0:T(8,128)(2,1)S(1)}, bf16[64,1024]{1,0:T(8,128)(2,1)S(1)}, u32[]{:S(2)}, u32[]{:S(2)}) collective-permute-start(bf16[64,1024]{1,0:T(8,128)(2,1)S(1)} %get-tuple-element.115), channel_id=1, source_target_pairs={{0,6},{1,7},{2,4},{3,5},{4,2},{5,3},{6,0},{7,1},{8,14},{9,15},{10,... | collective-permute-start | bytes 393224 | tf_op jit(solution)/shard_map/ppermute | solution.py:379
  583.1 32.9 %collective-permute-start.55 = (bf16[64,1024]{1,0:T(8,128)(2,1)S(1)}, bf16[64,1024]{1,0:T(8,128)(2,1)S(1)}, u32[]{:S(2)}, u32[]{:S(2)}) collective-permute-start(bf16[64,1024]{1,0:T(8,128)(2,1)S(1)} %copy-done.65), channel_id=1, source_target_pairs={{0,1},{1,0},{2,3},{3,2},{4,5},{5,4},{6,7},{7,6},{8,9},{9,8},{10,11... | collective-permute-start | bytes 393224 | tf_op jit(solution)/shard_map/ppermute | solution.py:379
  (141 other events, 1929.9 us)
Sparse Core Ops, SparseCore 0:
  9.6 49.7 all-gather.4
  91.4 46.6 all-gather.8
  285.2 48.7 reduce-scatter.3
  339.8 45.3 all-gather.6
  409.6 48.7 reduce-scatter.5
  543.8 78.1 reduce-scatter.7

commit v12 on v11

--- a/solution.py
+++ b/solution.py
@@ -785,8 +785,10 @@
     attn_inv_all = inverse_rms(attn_out)
     hidden_all = tokens_all.astype(jnp.float32) + attn_out * attn_inv_all * gain_attn
     hidden_low = hidden_all.astype(low)
-    attn_inv = own_piece(attn_inv_all)
-    attn_unit = own_piece(attn_out) * attn_inv
+    hidden_low, attn_inv, attn_own = lax.optimization_barrier(
+        (hidden_low, own_piece(attn_inv_all), own_piece(attn_out))
+    )
+    attn_unit = attn_own * attn_inv
     hidden_state = tokens.reshape(tok_count, model_width).astype(jnp.float32) + attn_unit * gain_attn
 
     gate_up = jnp.dot(hidden_low, w_hidden, preferred_element_type=jnp.float32)
@@ -871,7 +873,6 @@
     qkv_part = jnp.einsum("nd,nf->df", tokens_all, d_qkv, preferred_element_type=jnp.float32).astype(low)
     d_qkv, qkv_part = lax.optimization_barrier((d_qkv, qkv_part))
     d_tokens_part = jnp.einsum("nf,df->nd", d_qkv, w_qkv, preferred_element_type=jnp.float32).astype(low)
-    d_attn, d_tokens_part = lax.optimization_barrier((d_attn, d_tokens_part))
     d_tokens_sum = scatter_seq(d_tokens_part.reshape(row_count, row_len, model_width))
     d_tokens = d_hidden + d_tokens_sum.astype(jnp.float32).reshape(tok_count, model_width)
     qkv_own = sum_dp(*shares_for(qkv_part)).astype(low)

time: 720 us -> 728 us (1.011)
  waiting for transfers between devices: 293 us -> 310 us
    ppermute x79, waiting for transfers between devices: 196 us -> 221 us  [swap(): lax.ppermute(value, axis, [(at, at ^ flip) for at in range(lax.axis_size(...]
    unnamed x165 -> x149, local copies, waits for them, and re-layouts: 43.6 us -> 42 us
  transfers between devices with their start and end apart: 87 -> 87, of which waited for: 37 -> 33; matrix products, arithmetic and copies ran while one was open for 20% -> 19% of each run, Pallas kernels for 5% -> 4%
where the time goes in v12:
time: 728 us; the launch traced here: 720 us
  waiting for transfers between devices  310 us (43%)
  starting transfers between devices  112 us (15%)
  matrix products  93.7 us (13%)
  local copies, waits for them, and re-layouts  92.3 us (13%)
  other arithmetic  52.9 us (7%)
  Pallas kernels  42.6 us (6%)
  between operations  16 us (2%)
    ppermute x79, waiting for transfers between devices, swap(): lax.ppermute(value, axis, [(at, at ^ flip) for at in range(lax.axis_size(...  221 us
    ppermute x79, starting transfers between devices, swap(): lax.ppermute(value, axis, [(at, at ^ flip) for at in range(lax.axis_size(...  103 us
    reduce_scatter x3, waiting for transfers between devices, scatter_seq(): return lax.psum_scatter(partial, 'seq', scatter_dimension=1, tiled=True)  48 us
    unnamed x149, local copies, waits for them, and re-layouts  42 us
    all_gather x2, waiting for transfers between devices, gather_seq(): return lax.all_gather(piece, 'seq', axis=1, tiled=True)  36.1 us
    optimization_barrier x2, local copies, waits for them, and re-layouts, stored_turned(): matrix, after = lax.optimization_barrier((matrix, after))  19 us
    pallas_call x1, Pallas kernels, attend_back(): pl.pallas_call(functools.partial(attend_back_kernel, scale=scale), grid=(...  14.8 us
  transfers between devices with their start and end apart: 87, of which 33 were waited for; matrix products, arithmetic and copies ran while one was open for 19% of the time, Pallas kernels for 4%

profile of v12, /device:TPU:0, one launch (start us, length us, event | category | flops | bytes accessed | tf_op | source)
XLA Modules:
  0.0 719.5 jit_solution(6952808721557158247)
XLA Ops:
  14.5 16.0 %collective-permute-done.3.refs_1_ = bf16[512,768]{1,0:T(8,128)(2,1)S(1)} collective-permute-done((bf16[512,768]{1,0:T(8,128)(2,1)S(1)}, bf16[512,768]{1,0:T(8,128)(2,1)S(1)}, u32[]{:S(2)}, u32[]{:S(2)}) %collective-permute-start.3) | collective-permute-done | bytes 786464 | tf_op jit(solution)/shard_map/ppermute | solution.py:379
  49.8 9.7 %all-gather.5.cloned.1.call-done = bf16[1,1024,2048]{2,1,0:T(8,128)(2,1)} async-done(((bf16[1,128,2048]{2,1,0:T(8,128)(2,1)}), bf16[1,1024,2048]{2,1,0:T(8,128)(2,1)}) %all-gather.5.cloned.1.call-update) | async-done | bytes 4194320 | tf_op jit(solution)/shard_map/all_gather | solution.py:371
  80.8 10.5 %attend.1 = (bf16[1,1024,256]{2,1,0:T(8,128)(2,1)}, bf16[1,1024,256]{2,1,0:T(8,128)(2,1)}, bf16[1,1024,256]{2,1,0:T(8,128)(2,1)}, bf16[1,1024,256]{2,1,0:T(8,128)(2,1)}, f32[1,2,1024,1]{3,2,1,0:T(8,128)}) custom-call(f32[1,1024,768]{2,1,0:T(8,128)} %bitcast.360, f32[1,1024,768]{2,1,0:T(8,128)} %bitcast.361, f32[1,1024,768]{2,1,0:T(8,128)} %bitcast.362, ...), custom_call_target="tpu_custom_call" | custom-call | tf_op jit(solution)/shard_map/attend/pallas_call | solution.py:666
  107.6 11.4 %collective-permute-done.10.refs_1_ = bf16[512,1024]{1,0:T(8,128)(2,1)} collective-permute-done((bf16[512,1024]{1,0:T(8,128)(2,1)}, bf16[512,1024]{1,0:T(8,128)(2,1)}, u32[]{:S(2)}, u32[]{:S(2)}) %collective-permute-start.10) | collective-permute-done | bytes 1048608 | tf_op jit(solution)/shard_map/ppermute | solution.py:379
  121.6 52.2 %collective-permute-done.11.refs_2_ = bf16[512,1024]{1,0:T(8,128)(2,1)} collective-permute-done((bf16[512,1024]{1,0:T(8,128)(2,1)}, bf16[512,1024]{1,0:T(8,128)(2,1)}, u32[]{:S(2)}, u32[]{:S(2)}) %collective-permute-start.11) | collective-permute-done | bytes 1048608 | tf_op jit(solution)/shard_map/ppermute | solution.py:379
  176.4 7.2 %collective-permute-done.18.refs_1_ = bf16[256,2048]{1,0:T(8,128)(2,1)S(1)} collective-permute-done((bf16[256,2048]{1,0:T(8,128)(2,1)S(1)}, bf16[256,2048]{1,0:T(8,128)(2,1)S(1)}, u32[]{:S(2)}, u32[]{:S(2)}) %collective-permute-start.18) | collective-permute-done | bytes 1048608 | tf_op jit(solution)/shard_map/ppermute | solution.py:379
  185.2 11.0 %collective-permute-done.20.refs_2_ = bf16[256,2048]{1,0:T(8,128)(2,1)S(1)} collective-permute-done((bf16[256,2048]{1,0:T(8,128)(2,1)S(1)}, bf16[256,2048]{1,0:T(8,128)(2,1)S(1)}, u32[]{:S(2)}, u32[]{:S(2)}) %collective-permute-start.20) | collective-permute-done | bytes 1048608 | tf_op jit(solution)/shard_map/ppermute | solution.py:379
  200.4 7.0 collective-permute-done.12.refs_3_
  245.6 12.8 %multiply_reduce_fusion = (f32[1024]{0:T(1024)S(1)}, f32[1024,2048]{1,0:T(8,128)S(1)}) fusion(bf16[2048,2048]{1,0:T(8,128)(2,1)} %copy-done.5, bf16[1,1024,2048]{2,1,0:T(8,128)(2,1)} %all-gather.9.cloned.1.call-done), kind=kOutput, calls=%fused_computation.3 | convolution fusion | flops 8594127872 | bytes 20975616 | tf_op jit(solution)/shard_map/dot_general | solution.py:784
  261.9 8.9 %fusion.118 = f32[1024,2048]{1,0:T(8,128)S(1)} fusion(bf16[1024,2048]{1,0:T(8,128)(2,1)S(1)} %add_convert_fusion, bf16[2048,2048]{1,0:T(8,128)(2,1)S(1)} %bitcast.359), kind=kOutput, calls=%fused_computation.336 | convolution fusion | flops 8589934592 | bytes 20971520 | tf_op jit(solution)/shard_map/dot_general | solution.py:794
  282.7 48.0 %reduce-scatter.4.cloned.1.call-done = bf16[1,128,2048]{2,1,0:T(8,128)(2,1)} async-done(((bf16[1,1024,2048]{2,1,0:T(8,128)(2,1)}), bf16[1,128,2048]{2,1,0:T(8,128)(2,1)}) %reduce-scatter.4.cloned.1.call-update) | async-done | bytes 524304 | tf_op jit(solution)/shard_map/reduce_scatter | solution.py:375
  335.8 6.6 copy.60
  342.4 12.4 %copy.63 = bf16[2048,2048]{0,1:T(8,128)(2,1)} copy(bf16[2048,2048]{1,0:T(8,128)(2,1)} %copy-done.2) | data formatting | bytes 16777216 | tf_op jit(solution)/shard_map/optimization_barrier | solution.py:491
  354.8 26.4 %all-gather.7.cloned.1.call-done = bf16[1,1024,2048]{2,1,0:T(8,128)(2,1)} async-done(((bf16[1,128,2048]{2,1,0:T(8,128)(2,1)}), bf16[1,1024,2048]{2,1,0:T(8,128)(2,1)}) %all-gather.7.cloned.1.call-update) | async-done | bytes 4194320 | tf_op jit(solution)/shard_map/all_gather | solution.py:371
  381.2 11.7 %multiply_convert_fusion.1 = (bf16[1024,1024]{1,0:T(8,128)(2,1)S(1)}, bf16[1024,1024]{1,0:T(8,128)(2,1)S(1)}) fusion(f32[1024,2048]{1,0:T(8,128)} %copy-done.30, bf16[1024,2048]{0,1:T(8,128)(2,1)} %copy.60, bf16[1,1024,2048]{2,1,0:T(8,128)(2,1)} %all-gather.7.cloned.1.call-done), kind=kOutput, calls=%fused_computation.19 | convolution fusion | flops 4308598784 | bytes 20971520 | tf_op jit(solution)/shard_map/dot_general | solution.py:819
  395.0 10.6 %convert_bitcast_fusion.1 = bf16[1,1024,2048]{2,1,0:T(8,128)(2,1)} fusion(bf16[2048,2048]{0,1:T(8,128)(2,1)S(1)} %copy-done.31, bf16[1024,1024]{1,0:T(8,128)(2,1)S(1)} %get-tuple-element.68, bf16[1024,1024]{1,0:T(8,128)(2,1)S(1)} %get-tuple-element.67), kind=kOutput, calls=%fused_computation.17 | convolution fusion | flops 8600420352 | bytes 16777216 | tf_op jit(solution)/shard_map/dot_general | solution.py:823
  405.8 7.4 %fusion.19 = bf16[1024,2048]{1,0:T(8,128)(2,1)S(1)} fusion(bf16[1024,1024]{1,0:T(8,128)(2,1)} %copy-done.50, bf16[1,1024,2048]{2,1,0:T(8,128)(2,1)} %all-gather.7.cloned.1.call-done), kind=kOutput, calls=%fused_computation.23 | convolution fusion | flops 4297064448 | bytes 10485760 | tf_op jit(solution)/shard_map/nf,nd->fd/dot_general | solution.py:827
  445.5 18.5 %collective-permute-done.64 = bf16[2,256,1024]{2,1,0:T(8,128)(2,1)S(1)} collective-permute-done((bf16[2,256,1024]{2,1,0:T(8,128)(2,1)S(1)}, bf16[2,256,1024]{2,1,0:T(8,128)(2,1)S(1)}, u32[]{:S(2)}, u32[]{:S(2)}) %collective-permute-start.64) | collective-permute-done | bytes 1048608 | tf_op jit(solution)/shard_map/ppermute | solution.py:379
  497.9 14.8 %attend_back.1 = (f32[1,1024,256]{2,1,0:T(8,128)}, f32[1,1024,256]{2,1,0:T(8,128)}, bf16[1,1024,256]{2,1,0:T(8,128)(2,1)}, f32[1,8,1024]{2,1,0:T(8,128)}, f32[1,2,256]{2,1,0:T(2,128)}) custom-call(f32[1,1024,768]{2,1,0:T(8,128)} %bitcast.363, f32[1,1024,768]{2,1,0:T(8,128)} %bitcast.364, f32[1,1024,1]{2,1,0:T(8,128)} %copy.57.qinv_ref, ...), custom_call_target="tpu_custom_call" | custom-call | tf_op jit(solution)/shard_map/attend_back/pallas_call | solution.py:681
  574.2 9.5 %collective-permute-done.67.refs_2_ = bf16[64,1024]{1,0:T(8,128)(2,1)S(1)} collective-permute-done((bf16[64,1024]{1,0:T(8,128)(2,1)S(1)}, bf16[64,1024]{1,0:T(8,128)(2,1)S(1)}, u32[]{:S(2)}, u32[]{:S(2)}) %collective-permute-start.67) | collective-permute-done | bytes 131104 | tf_op jit(solution)/shard_map/ppermute | solution.py:379
  589.0 10.7 %collective-permute-done.69.refs_4_ = bf16[64,1024]{1,0:T(8,128)(2,1)S(1)} collective-permute-done((bf16[64,1024]{1,0:T(8,128)(2,1)S(1)}, bf16[64,1024]{1,0:T(8,128)(2,1)S(1)}, u32[]{:S(2)}, u32[]{:S(2)}) %collective-permute-start.69) | collective-permute-done | bytes 131104 | tf_op jit(solution)/shard_map/ppermute | solution.py:379
  602.9 12.9 %collective-permute-start.57 = (bf16[64,1024]{1,0:T(8,128)(2,1)S(1)}, bf16[64,1024]{1,0:T(8,128)(2,1)S(1)}, u32[]{:S(2)}, u32[]{:S(2)}) collective-permute-start(bf16[64,1024]{1,0:T(8,128)(2,1)S(1)} %get-tuple-element.117), channel_id=1, source_target_pairs={{0,3},{1,2},{2,1},{3,0},{4,7},{5,6},{6,5},{7,4},{8,11},{9,10},{10,... | collective-permute-start | bytes 393224 | tf_op jit(solution)/shard_map/ppermute | solution.py:379
  624.5 10.8 %collective-permute-done.58.refs_4_ = bf16[64,1024]{1,0:T(8,128)(2,1)S(1)} collective-permute-done((bf16[64,1024]{1,0:T(8,128)(2,1)S(1)}, bf16[64,1024]{1,0:T(8,128)(2,1)S(1)}, u32[]{:S(2)}, u32[]{:S(2)}) %collective-permute-start.58) | collective-permute-done | bytes 131104 | tf_op jit(solution)/shard_map/ppermute | solution.py:379
  656.7 14.6 %collective-permute-done.43 = bf16[256,256]{1,0:T(8,128)(2,1)S(1)} collective-permute-done((bf16[256,256]{1,0:T(8,128)(2,1)S(1)}, bf16[256,256]{1,0:T(8,128)(2,1)S(1)}, u32[]{:S(2)}, u32[]{:S(2)}) %collective-permute-start.43) | collective-permute-done | bytes 131104 | tf_op jit(solution)/shard_map/ppermute | solution.py:379
  (469 shorter events, 341.7 us)
Async XLA Ops:
  7.2 52.2 %all-gather.5.cloned.1.call-start = ((), (), s32[]{:S(2)}) async-start(), calls=%async_computation.5 | async-start | bytes 4718592 | tf_op jit(solution)/shard_map/all_gather | solution.py:371
  7.9 237.6 %all-gather.9.cloned.1.call-start = ((), (), s32[]{:S(2)}) async-start(), calls=%async_computation.10 | async-start | bytes 4718592 | tf_op jit(solution)/shard_map/all_gather | solution.py:783
  91.3 239.5 %reduce-scatter.4.cloned.1.call-start = ((), (), s32[]{:S(2)}) async-start(), calls=%async_computation.6 | async-start | bytes 4718592 | tf_op jit(solution)/shard_map/reduce_scatter | solution.py:375
  102.1 95.6 %collective-permute-start.22 = (bf16[512,2048]{1,0:T(8,128)(2,1)S(1)}, bf16[512,2048]{1,0:T(8,128)(2,1)S(1)}, u32[]{:S(2)}, u32[]{:S(2)}) collective-permute-start(bf16[512,2048]{1,0:T(8,128)(2,1)S(1)} %dynamic-slice_dynamic-update-slice_fusion.refs_0_), channel_id=1, source_target_pairs={{0,8},{8,0},{16,24},{24,16},{1,9},{9,1},{17,25},{25,17},{2,10},{10... | collective-permute-start | bytes 6291464 | tf_op jit(solution)/shard_map/ppermute | solution.py:379
  102.8 104.7 %collective-permute-start.24 = (bf16[512,2048]{1,0:T(8,128)(2,1)S(1)}, bf16[512,2048]{1,0:T(8,128)(2,1)S(1)}, u32[]{:S(2)}, u32[]{:S(2)}) collective-permute-start(bf16[512,2048]{1,0:T(8,128)(2,1)S(1)} %dynamic-slice_dynamic-update-slice_fusion.refs_0_), channel_id=1, source_target_pairs={{0,16},{8,24},{16,0},{24,8},{1,17},{9,25},{17,1},{25,9},{2,18},{10... | collective-permute-start | bytes 6291464 | tf_op jit(solution)/shard_map/ppermute | solution.py:379
  104.2 69.6 %collective-permute-start.11 = (bf16[512,1024]{1,0:T(8,128)(2,1)}, bf16[512,1024]{1,0:T(8,128)(2,1)}, u32[]{:S(2)}, u32[]{:S(2)}) collective-permute-start(bf16[512,1024]{1,0:T(8,128)(2,1)} %constant_dynamic-slice_fusion.7), channel_id=1, source_target_pairs={{0,16},{8,24},{16,0},{24,8},{1,17},{9,25},{17,1},{25,9},{2,18},{10... | collective-permute-start | bytes 3145736 | tf_op jit(solution)/shard_map/ppermute | solution.py:379
  106.1 77.6 %collective-permute-start.18 = (bf16[256,2048]{1,0:T(8,128)(2,1)S(1)}, bf16[256,2048]{1,0:T(8,128)(2,1)S(1)}, u32[]{:S(2)}, u32[]{:S(2)}) collective-permute-start(bf16[256,2048]{1,0:T(8,128)(2,1)S(1)} %constant_dynamic-slice_fusion.5.refs_0_), channel_id=1, source_target_pairs={{0,8},{8,0},{16,24},{24,16},{1,9},{9,1},{17,25},{25,17},{2,10},{10... | collective-permute-start | bytes 3145736 | tf_op jit(solution)/shard_map/ppermute | solution.py:379
  119.0 77.1 %collective-permute-start.20 = (bf16[256,2048]{1,0:T(8,128)(2,1)S(1)}, bf16[256,2048]{1,0:T(8,128)(2,1)S(1)}, u32[]{:S(2)}, u32[]{:S(2)}) collective-permute-start(bf16[256,2048]{1,0:T(8,128)(2,1)S(1)} %constant_dynamic-slice_fusion.5.refs_0_), channel_id=1, source_target_pairs={{0,16},{8,24},{16,0},{24,8},{1,17},{9,25},{17,1},{25,9},{2,18},{10... | collective-permute-start | bytes 3145736 | tf_op jit(solution)/shard_map/ppermute | solution.py:379
  282.1 99.1 %all-gather.7.cloned.1.call-start = ((), (), s32[]{:S(2)}) async-start(), calls=%async_computation.7 | async-start | bytes 4718592 | tf_op jit(solution)/shard_map/all_gather | solution.py:371
  335.7 131.5 %reduce-scatter.6.cloned.1.call-start = ((), (), s32[]{:S(2)}) async-start(), calls=%async_computation.8 | async-start | bytes 4718592 | tf_op jit(solution)/shard_map/reduce_scatter | solution.py:375
  423.5 40.5 %collective-permute-start.64 = (bf16[2,256,1024]{2,1,0:T(8,128)(2,1)S(1)}, bf16[2,256,1024]{2,1,0:T(8,128)(2,1)S(1)}, u32[]{:S(2)}, u32[]{:S(2)}) collective-permute-start(bf16[2,256,1024]{2,1,0:T(8,128)(2,1)S(1)} %pad_maximum_fusion.5), channel_id=1, source_target_pairs={{0,16},{8,24},{16,0},{24,8},{1,17},{9,25},{17,1},{25,9},{2,18},{10... | collective-permute-start | bytes 3145736 | tf_op jit(solution)/shard_map/ppermute | solution.py:379
  425.3 57.3 %collective-permute-start.62 = (bf16[2,256,1024]{2,1,0:T(8,128)(2,1)}, bf16[2,256,1024]{2,1,0:T(8,128)(2,1)}, u32[]{:S(2)}, u32[]{:S(2)}) collective-permute-start(bf16[2,256,1024]{2,1,0:T(8,128)(2,1)} %pad_maximum_fusion.4), channel_id=1, source_target_pairs={{0,8},{8,0},{16,24},{24,16},{1,9},{9,1},{17,25},{25,17},{2,10},{10... | collective-permute-start | bytes 3145736 | tf_op jit(solution)/shard_map/ppermute | solution.py:379
  434.8 52.2 %collective-permute-start.53 = (bf16[2,256,1024]{2,1,0:T(8,128)(2,1)}, bf16[2,256,1024]{2,1,0:T(8,128)(2,1)}, u32[]{:S(2)}, u32[]{:S(2)}) collective-permute-start(bf16[2,256,1024]{2,1,0:T(8,128)(2,1)} %pad_maximum_fusion.3), channel_id=1, source_target_pairs={{0,16},{8,24},{16,0},{24,8},{1,17},{9,25},{17,1},{25,9},{2,18},{10... | collective-permute-start | bytes 3145736 | tf_op jit(solution)/shard_map/ppermute | solution.py:379
  439.9 51.9 %collective-permute-start.51 = (bf16[2,256,1024]{2,1,0:T(8,128)(2,1)}, bf16[2,256,1024]{2,1,0:T(8,128)(2,1)}, u32[]{:S(2)}, u32[]{:S(2)}) collective-permute-start(bf16[2,256,1024]{2,1,0:T(8,128)(2,1)} %pad_maximum_fusion.2), channel_id=1, source_target_pairs={{0,8},{8,0},{16,24},{24,16},{1,9},{9,1},{17,25},{25,17},{2,10},{10... | collective-permute-start | bytes 3145736 | tf_op jit(solution)/shard_map/ppermute | solution.py:379
  442.7 105.0 %collective-permute-start.74 = (bf16[128,2048]{1,0:T(8,128)(2,1)}, bf16[128,2048]{1,0:T(8,128)(2,1)}, u32[]{:S(2)}, u32[]{:S(2)}) collective-permute-start(bf16[128,2048]{1,0:T(8,128)(2,1)} %fusion.65), channel_id=1, source_target_pairs={{0,16},{8,24},{16,0},{24,8},{1,17},{9,25},{17,1},{25,9},{2,18},{10... | collective-permute-start | bytes 1572872 | tf_op jit(solution)/shard_map/ppermute | solution.py:379
  464.0 87.2 %collective-permute-start.76 = (bf16[128,2048]{1,0:T(8,128)(2,1)}, bf16[128,2048]{1,0:T(8,128)(2,1)}, u32[]{:S(2)}, u32[]{:S(2)}) collective-permute-start(bf16[128,2048]{1,0:T(8,128)(2,1)} %fusion.66), channel_id=1, source_target_pairs={{0,8},{8,0},{16,24},{24,16},{1,9},{9,1},{17,25},{25,17},{2,10},{10... | collective-permute-start | bytes 1572872 | tf_op jit(solution)/shard_map/ppermute | solution.py:379
  482.6 227.6 %reduce-scatter.8.cloned.1.call-start = ((), (), s32[]{:S(2)}) async-start(), calls=%async_computation.9 | async-start | bytes 4718592 | tf_op jit(solution)/shard_map/reduce_scatter | solution.py:375
  482.7 39.6 %collective-permute-start.65 = (bf16[256,1024]{1,0:T(8,128)(2,1)}, bf16[256,1024]{1,0:T(8,128)(2,1)}, u32[]{:S(2)}, u32[]{:S(2)}) collective-permute-start(bf16[256,1024]{1,0:T(8,128)(2,1)} %fusion.64), channel_id=1, source_target_pairs={{0,8},{8,0},{16,24},{24,16},{1,9},{9,1},{17,25},{25,17},{2,10},{10... | collective-permute-start | bytes 1572872 | tf_op jit(solution)/shard_map/ppermute | solution.py:379
  487.1 56.5 %collective-permute-start.63 = (bf16[256,1024]{1,0:T(8,128)(2,1)}, bf16[256,1024]{1,0:T(8,128)(2,1)}, u32[]{:S(2)}, u32[]{:S(2)}) collective-permute-start(bf16[256,1024]{1,0:T(8,128)(2,1)} %fusion.63), channel_id=1, source_target_pairs={{0,16},{8,24},{16,0},{24,8},{1,17},{9,25},{17,1},{25,9},{2,18},{10... | collective-permute-start | bytes 1572872 | tf_op jit(solution)/shard_map/ppermute | solution.py:379
  520.8 39.2 %collective-permute-start.54 = (bf16[256,1024]{1,0:T(8,128)(2,1)}, bf16[256,1024]{1,0:T(8,128)(2,1)}, u32[]{:S(2)}, u32[]{:S(2)}) collective-permute-start(bf16[256,1024]{1,0:T(8,128)(2,1)} %fusion.62), channel_id=1, source_target_pairs={{0,8},{8,0},{16,24},{24,16},{1,9},{9,1},{17,25},{25,17},{2,10},{10... | collective-permute-start | bytes 1572872 | tf_op jit(solution)/shard_map/ppermute | solution.py:379
  527.4 36.2 %collective-permute-start.52 = (bf16[256,1024]{1,0:T(8,128)(2,1)}, bf16[256,1024]{1,0:T(8,128)(2,1)}, u32[]{:S(2)}, u32[]{:S(2)}) collective-permute-start(bf16[256,1024]{1,0:T(8,128)(2,1)} %fusion.61), channel_id=1, source_target_pairs={{0,16},{8,24},{16,0},{24,8},{1,17},{9,25},{17,1},{25,9},{2,18},{10... | collective-permute-start | bytes 1572872 | tf_op jit(solution)/shard_map/ppermute | solution.py:379
  556.3 80.8 %all-to-all-start.1 = ((bf16[8,128,256]{2,1,0:T(8,128)(2,1)}), bf16[8,128,256]{2,1,0:T(8,128)(2,1)S(1)}, u32[]{:S(2)}, u32[]{:S(2)}) async-start(bf16[8,128,256]{2,1,0:T(8,128)(2,1)} %bitcast.356), calls=%async_computation.4 | async-start | bytes 1048576 | tf_op jit(solution)/shard_map/all_to_all | solution.py:840
  569.2 51.6 %collective-permute-start.59 = (bf16[64,1024]{1,0:T(8,128)(2,1)S(1)}, bf16[64,1024]{1,0:T(8,128)(2,1)S(1)}, u32[]{:S(2)}, u32[]{:S(2)}) collective-permute-start(bf16[64,1024]{1,0:T(8,128)(2,1)S(1)} %get-tuple-element.120), channel_id=1, source_target_pairs={{0,5},{1,4},{2,7},{3,6},{4,1},{5,0},{6,3},{7,2},{8,13},{9,12},{10,... | collective-permute-start | bytes 393224 | tf_op jit(solution)/shard_map/ppermute | solution.py:379
  583.7 37.1 %collective-permute-start.60 = (bf16[64,1024]{1,0:T(8,128)(2,1)S(1)}, bf16[64,1024]{1,0:T(8,128)(2,1)S(1)}, u32[]{:S(2)}, u32[]{:S(2)}) collective-permute-start(bf16[64,1024]{1,0:T(8,128)(2,1)S(1)} %get-tuple-element.119), channel_id=1, source_target_pairs={{0,6},{1,7},{2,4},{3,5},{4,2},{5,3},{6,0},{7,1},{8,14},{9,15},{10,... | collective-permute-start | bytes 393224 | tf_op jit(solution)/shard_map/ppermute | solution.py:379
  (134 other events, 1723.6 us)
Sparse Core Ops, SparseCore 0:
  9.6 49.7 all-gather.4
  91.4 46.6 all-gather.8
  282.2 48.5 reduce-scatter.3
  335.8 45.3 all-gather.6
  405.7 48.7 reduce-scatter.5
  543.7 94.0 reduce-scatter.7
